TPU v7x, 32 devices: a whole 2x2x4 slice. The times are simulated.
32 devices in a mesh: pipe: 2 (over y), expert: 16 (over z, x, core).
Axes of the slice: x: 2, y: 2, z: 4, core: 2. Of those that a mesh axis runs over, the one named last changes fastest.
Arguments:
- bwd_input: bfloat16 [2, 2048, 2048], P('pipe', 'expert'), may hold values from -6 to 6
- out_grad: bfloat16 [2, 2048, 2048], P('pipe', 'expert'), may hold values from -6 to 6
- norm_gain: float32 [2, 2048], P('pipe'), may hold values from 0.1 to 1.9
- up_weight: bfloat16 [2, 16, 2048, 768], P('pipe', 'expert'), may hold values from -0.125 to 0.125
- down_weight: bfloat16 [2, 16, 768, 2048], P('pipe', 'expert'), may hold values from -0.21875 to 0.21875
- bwd_routes: int32 [2, 2048, 8], P('pipe', 'expert'), may hold values from 0 to 15, all different within a row; in each aligned block of 128 rows (0 to 127, 128 to 255, ..., all dimensions but the last counted through in order) at most 80 rows name the same one
- bwd_gates: bfloat16 [2, 2048, 8], P('pipe', 'expert'), may hold values from 0.19921875 to 1
Outputs:
- prev_grad: bfloat16 [2, 2048, 2048], P('pipe', 'expert')
Inputs may be any that keep to these rules, and one draw needn't show every extreme that they name: `bwd_routes`: A token's 8 routes name different experts. Among the 128 tokens of one index of expert (aligned blocks of rows, sections taken in order) at most 80 name any one expert, and in every draw some expert is named by exactly 80 tokens of some block.
All inputs are finite; a program needn't handle non-finite values.
Results may differ from a plain program's by a relative error of at most 0.0053.
Values may be sent and summed in bfloat16 or wider, within the bound.
No kernel may reach another device: no remote copies, remote signals or barrier semaphores. Data moves between devices by JAX's collectives and lax.ppermute only.
A program may use at most 128 MiB of HBM per device.

v0:
```python
import jax
import jax.numpy as jnp
from jax import lax
from jax.sharding import PartitionSpec as P

epsilon = 1e-06


def passed_along(shard, axis, by):
    length = lax.axis_size(axis)
    return lax.ppermute(shard, axis, [(i, (i + by) % length) for i in range(length)])


def normalize(inputs, gain_row):
    values = inputs.astype(jnp.float32)
    scaling = lax.rsqrt(jnp.mean(values * values, axis=-1, keepdims=True) + epsilon)
    return ((values * scaling * gain_row[None, :]).astype(jnp.bfloat16), values, scaling)


def norm_back(values, scaling, gain_row, d_normed):
    weighted = gain_row[None, :] * d_normed
    inner_mean = jnp.mean(values * weighted, axis=-1, keepdims=True)
    return scaling * weighted - values * (scaling * scaling * scaling) * inner_mean


def hidden_grad(grad_block, down_matrix):
    return lax.dot_general(
        grad_block, down_matrix, (((1,), (1,)), ((), ())), preferred_element_type=jnp.float32
    )


def finish_backward(row_block, d_hidden, up_matrix):
    before = jnp.dot(row_block, up_matrix, preferred_element_type=jnp.float32)
    sigmoid_of = jax.nn.sigmoid(before)
    d_before = (d_hidden * sigmoid_of * (1.0 + before * (1.0 - sigmoid_of))).astype(jnp.bfloat16)
    return lax.dot_general(
        d_before, up_matrix, (((1,), (1,)), ((), ())), preferred_element_type=jnp.float32
    ).astype(jnp.bfloat16)


def slot_tables(routes, experts, capacity):
    chosen = routes[:, :, None] == jnp.arange(experts, dtype=jnp.int32)[None, None, :]
    member = jnp.sum(chosen.astype(jnp.int32), axis=1)
    rank_in = jnp.cumsum(member, axis=0) - member
    slot_of = jnp.sum(jnp.where(chosen, rank_in[:, None, :], 0), axis=2)
    places = (member[None, :, :] == 1) & (
        rank_in[None, :, :] == jnp.arange(capacity, dtype=jnp.int32)[:, None, None]
    )
    dispatch = jnp.transpose(places, (2, 0, 1)).astype(jnp.bfloat16)
    return (dispatch, routes * capacity + slot_of)


def pack_rows(dispatch, source_rows):
    return jnp.einsum(
        "ect,td->ecd", dispatch, source_rows, preferred_element_type=jnp.float32
    ).astype(jnp.bfloat16)


def combine(returned, flat_index, gates):
    flat_rows = returned.reshape(-1, returned.shape[-1])
    picked = jnp.take(flat_rows, flat_index, axis=0)
    return jnp.sum(gates.astype(jnp.float32)[:, :, None] * picked.astype(jnp.float32), axis=1)


def shards(bwd_input, out_grad, norm_gain, up_weight, down_weight, bwd_routes, bwd_gates):
    up_matrix = up_weight[0, 0]
    down_matrix = down_weight[0, 0]
    gain_row = norm_gain[0]
    experts = lax.axis_size("expert")
    tokens_here = bwd_input.shape[1]
    model_width = bwd_input.shape[2]
    top_count = bwd_routes.shape[2]
    capacity = min(tokens_here, tokens_here * top_count * 5 // (4 * experts))
    normed_bwd, values_bwd, scaling_bwd = normalize(bwd_input[0], gain_row)
    grad_rows = out_grad[0]
    dispatch_bwd, index_bwd = slot_tables(bwd_routes[0], experts, capacity)
    send_rows = pack_rows(dispatch_bwd, normed_bwd)
    send_grad = pack_rows(dispatch_bwd, grad_rows)
    pieces = (
        lax.all_to_all(send_rows, "expert", split_axis=0, concat_axis=0, tiled=True),
        lax.all_to_all(send_grad, "expert", split_axis=0, concat_axis=0, tiled=True),
    )
    d_part = hidden_grad(pieces[1].reshape(-1, model_width), down_matrix)
    back_rows = finish_backward(pieces[0].reshape(-1, model_width), d_part, up_matrix).reshape(
        pieces[0].shape
    )
    returned_bwd = lax.all_to_all(back_rows, "expert", split_axis=0, concat_axis=0, tiled=True)
    d_normed = combine(returned_bwd, index_bwd, bwd_gates[0])
    input_grad = (
        grad_rows.astype(jnp.float32) + norm_back(values_bwd, scaling_bwd, gain_row, d_normed)
    ).astype(jnp.bfloat16)
    return passed_along(input_grad[None], "pipe", -1)


def solution(mesh):
    return jax.shard_map(
        shards,
        mesh=mesh,
        in_specs=(
            P("pipe", "expert", None),
            P("pipe", "expert", None),
            P("pipe", None),
            P("pipe", "expert", None, None),
            P("pipe", "expert", None, None),
            P("pipe", "expert", None),
            P("pipe", "expert", None),
        ),
        out_specs=P("pipe", "expert", None),
        check_vma=False,
    )
```

profile of v0, /device:TPU:14, one launch (start us, length us, event | category | flops | bytes accessed | tf_op | source)
XLA Modules:
  0.0 417.6 jit_solution(14847885434170356171)
XLA Ops:
  0.0 0.0 copy-start
  0.0 0.9 convert_reduce_fusion
  0.9 0.1 copy.20
  1.0 0.2 reduce_window_sum.11
  1.2 0.1 copy.24
  1.2 1.2 fusion.9
  2.5 5.0 %convolution_convert_fusion.1 = bf16[16,80,2048]{2,1,0:T(8,128)(2,1)} fusion(bf16[1,128,2048]{2,1,0:T(8,128)(2,1)} %param.7, f32[2048]{0:T(1024)} %bitcast.70, f32[128]{0:T(128)S(1)} %get-tuple-element.6, s32[16,128]{1,0:T(8,128)S(1)} %copy.24, pred[16,128]{1,0:T(8,128)(4,1)S(1)} %compare_bitcast_fusion), kind=kOutput, calls=%fused_computation.4 | convolution fusion | flops 675086336 | bytes 5786112 | tf_op jit(solution)/shard_map/ect,td->ecd/dot_general | solution.py:54
  7.5 6.2 %all-to-all-start.1 = ((bf16[16,80,2048]{2,1,0:T(8,128)(2,1)}), bf16[16,80,2048]{2,1,0:T(8,128)(2,1)}, u32[]{:S(2)}, u32[]{:S(2)}) async-start(bf16[16,80,2048]{2,1,0:T(8,128)(2,1)} %convolution_convert_fusion.1), calls=%async_computation.1 | async-start | bytes 10485760 | tf_op jit(solution)/shard_map/all_to_all | solution.py:80
  13.7 4.9 %convolution_convert_fusion.2 = bf16[16,80,2048]{2,1,0:T(8,128)(2,1)} fusion(bf16[1,128,2048]{2,1,0:T(8,128)(2,1)} %param.8, s32[16,128]{1,0:T(8,128)S(1)} %copy.24, pred[16,128]{1,0:T(8,128)(4,1)S(1)} %compare_bitcast_fusion), kind=kOutput, calls=%fused_computation.5 | convolution fusion | flops 674037760 | bytes 5777408 | tf_op jit(solution)/shard_map/ect,td->ecd/dot_general | solution.py:54
  18.6 109.9 %all-to-all-done.1 = bf16[16,80,2048]{2,1,0:T(8,128)(2,1)} async-done(((bf16[16,80,2048]{2,1,0:T(8,128)(2,1)}), bf16[16,80,2048]{2,1,0:T(8,128)(2,1)}, u32[]{:S(2)}, u32[]{:S(2)}) %all-to-all-start.1) | async-done | bytes 5242912 | tf_op jit(solution)/shard_map/all_to_all | solution.py:80
  128.5 5.1 %all-to-all-start = ((bf16[16,80,2048]{2,1,0:T(8,128)(2,1)}), bf16[16,80,2048]{2,1,0:T(8,128)(2,1)}, u32[]{:S(2)}, u32[]{:S(2)}) async-start(bf16[16,80,2048]{2,1,0:T(8,128)(2,1)} %convolution_convert_fusion.2), calls=%async_computation | async-start | bytes 10485760 | tf_op jit(solution)/shard_map/all_to_all | solution.py:81
  133.6 0.0 copy-done
  133.6 8.6 %fusion.3 = f32[1280,768]{1,0:T(8,128)} fusion(bf16[1280,2048]{1,0:T(8,128)(2,1)} %bitcast.11, bf16[1,1,2048,768]{3,2,1,0:T(8,128)(2,1)S(1)} %copy-done), kind=kOutput, calls=%fused_computation.10 | convolution fusion | flops 4026531840 | bytes 12320768 | tf_op jit(solution)/shard_map/dot_general | solution.py:33
  142.2 106.2 %all-to-all-done = bf16[16,80,2048]{2,1,0:T(8,128)(2,1)} async-done(((bf16[16,80,2048]{2,1,0:T(8,128)(2,1)}), bf16[16,80,2048]{2,1,0:T(8,128)(2,1)}, u32[]{:S(2)}, u32[]{:S(2)}) %all-to-all-start) | async-done | bytes 5242912 | tf_op jit(solution)/shard_map/all_to_all | solution.py:81
  248.4 9.6 %fusion.1 = bf16[1280,768]{1,0:T(8,128)(2,1)S(1)} fusion(f32[1280,768]{1,0:T(8,128)} %fusion.3, bf16[1280,2048]{1,0:T(8,128)(2,1)} %bitcast.8, bf16[1,1,768,2048]{3,2,1,0:T(8,128)(2,1)} %param.11), kind=kOutput, calls=%fused_computation.8 | convolution fusion | flops 4035379200 | bytes 14286848 | tf_op jit(solution)/shard_map/dot_general | solution.py:27
  258.0 6.1 %convolution_convert_fusion = bf16[1280,2048]{1,0:T(8,128)(2,1)} fusion(bf16[1280,768]{1,0:T(8,128)(2,1)S(1)} %fusion.1, bf16[1,1,2048,768]{3,2,1,0:T(8,128)(2,1)S(1)} %copy-done), kind=kOutput, calls=%fused_computation.2 | convolution fusion | flops 4029153280 | bytes 10354688 | tf_op jit(solution)/shard_map/dot_general | solution.py:36
  264.1 5.2 %all-to-all-start.2 = ((bf16[16,80,2048]{2,1,0:T(8,128)(2,1)}), bf16[16,80,2048]{2,1,0:T(8,128)(2,1)}, u32[]{:S(2)}, u32[]{:S(2)}) async-start(bf16[16,80,2048]{2,1,0:T(8,128)(2,1)} %bitcast.68), calls=%async_computation.2 | async-start | bytes 10485760 | tf_op jit(solution)/shard_map/all_to_all | solution.py:87
  269.3 0.0 copy-done.4
  269.4 0.1 copy.25
  269.5 0.1 reshape.164
  269.6 0.1 copy.23
  269.7 0.0 copy-done.5
  269.7 0.1 copy.19
  269.8 114.2 %all-to-all-done.2 = bf16[16,80,2048]{2,1,0:T(8,128)(2,1)} async-done(((bf16[16,80,2048]{2,1,0:T(8,128)(2,1)}), bf16[16,80,2048]{2,1,0:T(8,128)(2,1)}, u32[]{:S(2)}, u32[]{:S(2)}) %all-to-all-start.2) | async-done | bytes 5242912 | tf_op jit(solution)/shard_map/all_to_all | solution.py:87
  384.1 12.0 %gather_fusion = bf16[1024,2048]{1,0:T(8,128)(2,1)} fusion(bf16[1280,2048]{1,0:T(8,128)(2,1)} %bitcast.14, s32[1024]{0:T(1024)S(1)} %broadcast_clamp_fusion), kind=kCustom, calls=%fused_computation | custom fusion | bytes 8392704 | tf_op jit(solution)/shard_map/jit(_take)/gather | solution.py:61
  396.1 5.7 %multiply_reduce_fusion = f32[128,2048]{1,0:T(8,128)S(1)} fusion(bf16[1024,2048]{1,0:T(8,128)(2,1)} %gather_fusion, f32[128,8]{1,0:T(8,128)S(1)} %copy.19, pred[128,8]{1,0:T(8,128)(4,1)S(1)} %copy.23), kind=kLoop, calls=%fused_computation.1 | loop fusion | flops 8126464 | bytes 5248000 | tf_op jit(solution)/shard_map/reduce_sum | solution.py:62
  401.8 0.0 copy-done.1
  401.8 0.2 fusion.12
  402.1 0.5 fusion.16
  402.6 0.6 collective-permute-start
  403.2 13.6 %collective-permute-done = bf16[1,128,2048]{2,1,0:T(8,128)(2,1)S(1)} collective-permute-done((bf16[1,128,2048]{2,1,0:T(8,128)(2,1)S(1)}, bf16[1,128,2048]{2,1,0:T(8,128)(2,1)S(1)}, u32[]{:S(2)}, u32[]{:S(2)}) %collective-permute-start) | collective-permute-done | bytes 524320 | tf_op jit(solution)/shard_map/ppermute | solution.py:11
  416.8 0.8 copy.27
  (17 shorter events, 0.2 us)
Async XLA Ops:
  0.0 133.6 %copy-start = (bf16[1,1,2048,768]{3,2,1,0:T(8,128)(2,1)S(1)}, bf16[1,1,2048,768]{3,2,1,0:T(8,128)(2,1)}, u32[]{:S(2)}) copy-start(bf16[1,1,2048,768]{3,2,1,0:T(8,128)(2,1)} %param.10) | copy-start | bytes 9437188
  7.5 121.0 %all-to-all-start.1 = ((bf16[16,80,2048]{2,1,0:T(8,128)(2,1)}), bf16[16,80,2048]{2,1,0:T(8,128)(2,1)}, u32[]{:S(2)}, u32[]{:S(2)}) async-start(bf16[16,80,2048]{2,1,0:T(8,128)(2,1)} %convolution_convert_fusion.1), calls=%async_computation.1 | async-start | bytes 10485760 | tf_op jit(solution)/shard_map/all_to_all | solution.py:80
  128.5 119.8 %all-to-all-start = ((bf16[16,80,2048]{2,1,0:T(8,128)(2,1)}), bf16[16,80,2048]{2,1,0:T(8,128)(2,1)}, u32[]{:S(2)}, u32[]{:S(2)}) async-start(bf16[16,80,2048]{2,1,0:T(8,128)(2,1)} %convolution_convert_fusion.2), calls=%async_computation | async-start | bytes 10485760 | tf_op jit(solution)/shard_map/all_to_all | solution.py:81
  264.1 5.3 %copy-start.4 = (s32[1,128,8]{1,2,0:T(8,128)S(1)}, s32[1,128,8]{1,2,0:T(8,128)}, u32[]{:S(2)}) copy-start(s32[1,128,8]{1,2,0:T(8,128)} %param.12) | copy-start | bytes 12292
  264.1 5.7 %copy-start.5 = (bf16[1,128,8]{1,2,0:T(8,128)(2,1)S(1)}, bf16[1,128,8]{1,2,0:T(8,128)(2,1)}, u32[]{:S(2)}) copy-start(bf16[1,128,8]{1,2,0:T(8,128)(2,1)} %param.13) | copy-start | bytes 6148
  264.1 120.0 %all-to-all-start.2 = ((bf16[16,80,2048]{2,1,0:T(8,128)(2,1)}), bf16[16,80,2048]{2,1,0:T(8,128)(2,1)}, u32[]{:S(2)}, u32[]{:S(2)}) async-start(bf16[16,80,2048]{2,1,0:T(8,128)(2,1)} %bitcast.68), calls=%async_computation.2 | async-start | bytes 10485760 | tf_op jit(solution)/shard_map/all_to_all | solution.py:87
  396.1 5.7 %copy-start.1 = (bf16[1,128,2048]{2,1,0:T(8,128)(2,1)S(1)}, bf16[1,128,2048]{2,1,0:T(8,128)(2,1)}, u32[]{:S(2)}) copy-start(bf16[1,128,2048]{2,1,0:T(8,128)(2,1)} %param.7) | copy-start | bytes 1572868
  396.1 5.7 %copy-start.3 = (f32[1,2048]{1,0:T(1,128)S(1)}, f32[1,2048]{1,0:T(1,128)}, u32[]{:S(2)}) copy-start(f32[1,2048]{1,0:T(1,128)} %param.9) | copy-start | bytes 24580
  396.1 5.9 %copy-start.2 = (bf16[1,128,2048]{2,1,0:T(8,128)(2,1)S(1)}, bf16[1,128,2048]{2,1,0:T(8,128)(2,1)}, u32[]{:S(2)}) copy-start(bf16[1,128,2048]{2,1,0:T(8,128)(2,1)} %param.8) | copy-start | bytes 1572868
  402.6 14.2 %collective-permute-start = (bf16[1,128,2048]{2,1,0:T(8,128)(2,1)S(1)}, bf16[1,128,2048]{2,1,0:T(8,128)(2,1)S(1)}, u32[]{:S(2)}, u32[]{:S(2)}) collective-permute-start(bf16[1,128,2048]{2,1,0:T(8,128)(2,1)S(1)} %fusion.16), channel_id=1, source_target_pairs={{0,16},{16,0},{1,17},{17,1},{2,18},{18,2},{3,19},{19,3},{4,20},{20... | collective-permute-start | bytes 1572872 | tf_op jit(solution)/shard_map/ppermute | solution.py:11
where the time goes:
time: 418 us
  waiting for transfers between devices  344 us (82%)
  matrix products  34.2 us (8%)
  starting transfers between devices  17.1 us (4%)
  local copies, waits for them, and re-layouts  13.5 us (3%)
  other arithmetic  8.8 us (2%)
    all_to_all x1, waiting for transfers between devices, shards(): lax.all_to_all(back_rows, 'expert', split_axis=0, concat_axis=0, tiled=True)  114 us
    all_to_all x1, waiting for transfers between devices, shards(): lax.all_to_all(send_rows, 'expert', split_axis=0, concat_axis=0, tiled=True)  110 us
    all_to_all x1, waiting for transfers between devices, shards(): lax.all_to_all(send_grad, 'expert', split_axis=0, concat_axis=0, tiled=True)  106 us
    ppermute x1, waiting for transfers between devices, passed_along(): lax.ppermute(shard, axis, [(i, (i + by) % length) for i in range(length)])  13.6 us
    gather x1, local copies, waits for them, and re-layouts, combine(): picked = jnp.take(flat_rows, flat_index, axis=0)  12 us
    dot_general x2, matrix products, pack_rows(): jnp.einsum('ect,td->ecd', dispatch, source_rows, preferred_element_type=j...  9.92 us
    dot_general x1, matrix products, hidden_grad(): lax.dot_general(grad_block, down_matrix, (((1,), (1,)), ((), ())), prefer...  9.62 us
    dot_general x1, matrix products, finish_backward(): before = jnp.dot(row_block, up_matrix, preferred_element_type=jnp.float32)  8.62 us
  transfers between devices with their start and end apart: 4, of which 4 were waited for; matrix products, arithmetic and copies ran while one was open for 3% of the time, Pallas kernels for 0%

commit v1 on v0

v1 whole, which is shorter than its diff:
```python
import jax
import jax.numpy as jnp
from jax import lax
from jax.experimental import pallas as pl
from jax.experimental.pallas import tpu as pltpu
from jax.sharding import PartitionSpec as P

epsilon = 1e-06
LANES = 128
NT = (((1,), (1,)), ((), ()))


def pack_kernel(x_ref, g_ref, gain_ref, routes_ref, gates_ref, up_ref, down_ref):
    half, width = up_ref.shape[0], x_ref.shape[1]
    values = x_ref[...].astype(jnp.float32)
    scaling = lax.rsqrt(jnp.mean(values * values, axis=-1, keepdims=True) + epsilon)
    normed = (values * scaling * gain_ref[...]).astype(jnp.bfloat16)
    lanes = up_ref.shape[1] - 2 * width
    lane = lax.broadcasted_iota(jnp.int32, (x_ref.shape[0], lanes), 1)
    dense = jnp.zeros((x_ref.shape[0], lanes), jnp.float32)
    routes, gates = routes_ref[...], gates_ref[...].astype(jnp.float32)
    for k in range(routes.shape[1]):
        dense = dense + jnp.where(lane == routes[:, k : k + 1], gates[:, k : k + 1], 0.0)
    dense = dense.astype(jnp.bfloat16)
    for ref, first in ((up_ref, 0), (down_ref, half)):
        ref[:, :width] = normed[first : first + half]
        ref[:, width : 2 * width] = g_ref[first : first + half, :]
        ref[:, 2 * width :] = dense[first : first + half]


def pack(x, grad, gain, routes, gates, experts):
    rows, width = x.shape
    lanes = -(-experts // LANES) * LANES
    shape = jax.ShapeDtypeStruct((rows // 2, 2 * width + lanes), jnp.bfloat16)
    return pl.pallas_call(
        pack_kernel,
        out_shape=(shape, shape),
        compiler_params=pltpu.CompilerParams(vmem_limit_bytes=40 << 20),
        name="pack",
    )(x, grad, gain, routes, gates)


def expert_kernel(me_ref, a_ref, b_ref, u0_ref, u1_ref, d0_ref, d1_ref, o_ref, n_s, g_s, w_s):
    width = u0_ref.shape[0]
    half = a_ref.shape[0]

    @pl.when(pl.program_id(0) == 0)
    def _():
        lane = lax.broadcasted_iota(jnp.int32, (half, a_ref.shape[1] - 2 * width), 1)
        for ref, first in ((a_ref, 0), (b_ref, half)):
            n_s[first : first + half, :] = ref[:, :width]
            g_s[first : first + half, :] = ref[:, width : 2 * width]
            dense = ref[:, 2 * width :].astype(jnp.float32)
            for i in range(2):
                w_s[first : first + half, i : i + 1] = jnp.sum(
                    jnp.where(lane == me_ref[i], dense, 0.0), axis=-1, keepdims=True
                )

    total = None
    for i, (u_ref, d_ref) in enumerate(((u0_ref, d0_ref), (u1_ref, d1_ref))):
        before = jnp.dot(n_s[...], u_ref[...], preferred_element_type=jnp.float32)
        d_hidden = lax.dot_general(g_s[...], d_ref[...], NT, preferred_element_type=jnp.float32)
        sigmoid_of = jax.nn.sigmoid(before)
        d_before = d_hidden * sigmoid_of * (1.0 + before * (1.0 - sigmoid_of))
        d_before = (d_before * w_s[:, i : i + 1]).astype(jnp.bfloat16)
        part = lax.dot_general(d_before, u_ref[...], NT, preferred_element_type=jnp.float32)
        total = part if total is None else total + part

    @pl.when(pl.program_id(0) == 0)
    def _():
        o_ref[...] = total

    @pl.when(pl.program_id(0) > 0)
    def _():
        o_ref[...] += total


def expert_part(me, a, b, u0, u1, d0, d1):
    half, wide = a.shape
    width, hidden = u0.shape
    chunk = 256
    up = pl.BlockSpec((width, chunk), lambda i: (0, i))
    down = pl.BlockSpec((chunk, width), lambda i: (i, 0))
    rows = pl.BlockSpec((half, wide), lambda i: (0, 0))
    return pl.pallas_call(
        expert_kernel,
        out_shape=jax.ShapeDtypeStruct((2 * half, width), jnp.float32),
        grid=(hidden // chunk,),
        in_specs=[pl.BlockSpec(memory_space=pltpu.SMEM), rows, rows, up, up, down, down],
        out_specs=pl.BlockSpec((2 * half, width), lambda i: (0, 0)),
        scratch_shapes=[
            pltpu.VMEM((2 * half, width), jnp.bfloat16),
            pltpu.VMEM((2 * half, width), jnp.bfloat16),
            pltpu.VMEM((2 * half, LANES), jnp.float32),
        ],
        compiler_params=pltpu.CompilerParams(
            dimension_semantics=("arbitrary",), vmem_limit_bytes=40 << 20
        ),
        cost_estimate=pl.CostEstimate(
            flops=24 * half * width * hidden,
            transcendentals=4 * half * hidden,
            bytes_accessed=8 * width * hidden + 12 * half * width,
        ),
        name="expert_part",
    )(me, a, b, u0, u1, d0, d1)


def finish_kernel(x_ref, g_ref, gain_ref, own_ref, a_ref, b_ref, o_ref):
    half = a_ref.shape[0]
    for ref, first in ((a_ref, 0), (b_ref, half)):
        part = slice(first, first + half)
        values = x_ref[part, :].astype(jnp.float32)
        scaling = lax.rsqrt(jnp.mean(values * values, axis=-1, keepdims=True) + epsilon)
        d_normed = own_ref[part, :].astype(jnp.float32) + ref[...].astype(jnp.float32)
        weighted = gain_ref[...] * d_normed
        inner_mean = jnp.mean(values * weighted, axis=-1, keepdims=True)
        back = scaling * weighted - values * (scaling * scaling * scaling) * inner_mean
        o_ref[part, :] = (g_ref[part, :].astype(jnp.float32) + back).astype(jnp.bfloat16)


def finish(x, grad, gain, own, a, b):
    return pl.pallas_call(
        finish_kernel,
        out_shape=jax.ShapeDtypeStruct(x.shape, jnp.bfloat16),
        compiler_params=pltpu.CompilerParams(vmem_limit_bytes=40 << 20),
        name="finish",
    )(x, grad, gain, own, a, b)


def shards(bwd_input, out_grad, norm_gain, up_weight, down_weight, bwd_routes, bwd_gates):
    experts = lax.axis_size("expert")
    sections = lax.axis_size("pipe")
    chips = experts // 2
    ring = list(range(0, chips, 2)) + list(range(1, chips, 2))[::-1]

    def hop(value, by):
        moves = [(ring[i], ring[(i + by) % chips]) for i in range(chips)]
        return lax.ppermute(value, "expert", [(2 * a + c, 2 * b + c) for a, b in moves for c in (0, 1)])

    def last_hop(value, by):
        moves = [(ring[i], ring[(i + by) % chips]) for i in range(chips)]
        return lax.ppermute(
            value,
            ("pipe", "expert"),
            [
                (s * experts + 2 * a + c, (s - 1) % sections * experts + 2 * b + c)
                for s in range(sections)
                for a, b in moves
                for c in (0, 1)
            ],
        )

    def to_previous(value):
        return lax.ppermute(value, "pipe", [(s, (s - 1) % sections) for s in range(sections)])

    def swap(value):
        return lax.ppermute(value, "expert", [(e, e ^ 1) for e in range(experts)])

    x, grad = bwd_input[0], out_grad[0]
    u0, d0 = up_weight[0, 0], down_weight[0, 0]
    e = lax.axis_index("expert").astype(jnp.int32)
    me = jnp.stack([e, e ^ 1])

    a, b = pack(x, grad, norm_gain, bwd_routes[0], bwd_gates[0], experts)
    a1, b1 = hop(a, 1), hop(b, -1)
    u1, d1 = swap(u0), swap(d0)
    x_out, grad_out, gain_out = to_previous(x), to_previous(grad), to_previous(norm_gain)
    own = to_previous(expert_part(me, a, b, u0, u1, d0, d1).astype(jnp.bfloat16))
    half = a.shape[0]
    sum_a = sum_b = None
    for step in range(1, chips):
        a, b = a1, b1
        if step < chips - 1:
            a1, b1 = hop(a, 1), hop(b, -1)
        part = expert_part(me, a, b, u0, u1, d0, d1)
        part_a, part_b = part[:half], part[half:]
        if step > 1:
            part_a = part_a + sum_a.astype(jnp.float32)
            part_b = part_b + sum_b.astype(jnp.float32)
        move = hop if step < chips - 1 else last_hop
        sum_a = move(part_a.astype(jnp.bfloat16), 1)
        sum_b = move(part_b.astype(jnp.bfloat16), -1)
    return finish(x_out, grad_out, gain_out, own, sum_a, sum_b)[None]


def solution(mesh):
    return jax.shard_map(
        shards,
        mesh=mesh,
        in_specs=(
            P("pipe", "expert", None),
            P("pipe", "expert", None),
            P("pipe", None),
            P("pipe", "expert", None, None),
            P("pipe", "expert", None, None),
            P("pipe", "expert", None),
            P("pipe", "expert", None),
        ),
        out_specs=P("pipe", "expert", None),
        check_vma=False,
    )
```

time: 418 us -> 170 us (0.41)
  the two profiles are of different devices: /device:TPU:14 before, /device:TPU:0 now
where the time goes in v1:
time: 170 us
  Pallas kernels  84.6 us (50%)
  waiting for transfers between devices  39.4 us (23%)
  starting transfers between devices  36.6 us (22%)
  local copies, waits for them, and re-layouts  8.2 us (5%)
    pallas_call x8, Pallas kernels, expert_part(): pl.pallas_call(expert_kernel, out_shape=jax.ShapeDtypeStruct((2 * half, w...  81.6 us
    ppermute x26, starting transfers between devices, hop(): lax.ppermute(value, 'expert', [(2 * a + c, 2 * b + c) for a, b in moves f...  27.7 us
    ppermute x26, waiting for transfers between devices, hop(): lax.ppermute(value, 'expert', [(2 * a + c, 2 * b + c) for a, b in moves f...  24.8 us
    ppermute x4, waiting for transfers between devices, to_previous(): lax.ppermute(value, 'pipe', [(s, (s - 1) % sections) for s in range(secti...  14.6 us
    unnamed x22, local copies, waits for them, and re-layouts  8.16 us
    ppermute x4, starting transfers between devices, to_previous(): lax.ppermute(value, 'pipe', [(s, (s - 1) % sections) for s in range(secti...  5.14 us
  transfers between devices with their start and end apart: 34, of which 7 were waited for; matrix products, arithmetic and copies ran while one was open for 1% of the time, Pallas kernels for 49%

profile of v1, /device:TPU:0, one launch (start us, length us, event | category | flops | bytes accessed | tf_op | source)
XLA Modules:
  0.0 169.8 jit_solution(11230056219157160962)
XLA Ops:
  6.3 2.9 %collective-permute-start.13 = (bf16[64,4224]{1,0:T(8,128)(2,1)}, bf16[64,4224]{1,0:T(8,128)(2,1)}, u32[]{:S(2)}, u32[]{:S(2)}) collective-permute-start(bf16[64,4224]{1,0:T(8,128)(2,1)} %get-tuple-element.8.b_ref), channel_id=1, source_target_pairs={{0,2},{1,3},{4,0},{5,1},{8,4},{9,5},{12,8},{13,9},{14,12},{15,13},... | collective-permute-start | bytes 1622024 | tf_op jit(solution)/shard_map/ppermute | solution.py:138
  9.4 12.7 %collective-permute-done.13.b_ref = bf16[64,4224]{1,0:T(8,128)(2,1)} collective-permute-done((bf16[64,4224]{1,0:T(8,128)(2,1)}, bf16[64,4224]{1,0:T(8,128)(2,1)}, u32[]{:S(2)}, u32[]{:S(2)}) %collective-permute-start.13) | collective-permute-done | bytes 540704 | tf_op jit(solution)/shard_map/ppermute | solution.py:138
  22.1 1.7 collective-permute-start.14
  24.1 1.9 %copy-done = bf16[1,1,2048,768]{3,2,1,0:T(8,128)(2,1)S(1)} copy-done((bf16[1,1,2048,768]{3,2,1,0:T(8,128)(2,1)S(1)}, bf16[1,1,2048,768]{3,2,1,0:T(8,128)(2,1)}, u32[]{:S(2)}) %copy-start) | copy-done | bytes 3145752
  26.0 1.9 %copy-done.2 = bf16[1,1,768,2048]{3,2,1,0:T(8,128)(2,1)S(1)} copy-done((bf16[1,1,768,2048]{3,2,1,0:T(8,128)(2,1)S(1)}, bf16[1,1,768,2048]{3,2,1,0:T(8,128)(2,1)}, u32[]{:S(2)}) %copy-start.2) | copy-done | bytes 3145752
  27.9 10.4 %expert_part.15 = f32[128,2048]{1,0:T(8,128)S(1)} custom-call(s32[2]{0:T(128)S(1)} %pad_add_fusion.me_ref, bf16[64,4224]{1,0:T(8,128)(2,1)} %collective-permute-done.6.a_ref, bf16[64,4224]{1,0:T(8,128)(2,1)} %collective-permute-done.13.b_ref, bf16[2048,768]{1,0:T(8,128)(2,1)S(1)} %bitcast.10, bf16[2048,768]{1,0:T(8,128)(2,1)S(1)} %collective-permute-done.3.u1_ref, ...), custom_call_target="tpu_custom_call" | custom-call | flops 2415919104 | bytes 14155776 | tf_op jit(solution)/shard_map/expert_part/pallas_call | solution.py:85
  38.4 1.8 %collective-permute-start.20 = (bf16[64,2048]{1,0:T(8,128)(2,1)S(1)}, bf16[64,2048]{1,0:T(8,128)(2,1)S(1)}, u32[]{:S(2)}, u32[]{:S(2)}) collective-permute-start(bf16[64,2048]{1,0:T(8,128)(2,1)S(1)} %get-tuple-element.22), channel_id=1, source_target_pairs={{0,4},{1,5},{4,8},{5,9},{8,12},{9,13},{12,14},{13,15},{14,10},{15,... | collective-permute-start | bytes 786440 | tf_op jit(solution)/shard_map/ppermute | solution.py:138
  40.5 1.7 collective-permute-start.15
  42.6 10.1 %expert_part.14 = f32[128,2048]{1,0:T(8,128)S(1)} custom-call(s32[2]{0:T(128)S(1)} %pad_add_fusion.me_ref, bf16[64,4224]{1,0:T(8,128)(2,1)S(1)} %collective-permute-done.7.a_ref, bf16[64,4224]{1,0:T(8,128)(2,1)S(1)} %collective-permute-done.14.b_ref, bf16[2048,768]{1,0:T(8,128)(2,1)S(1)} %bitcast.11, bf16[2048,768]{1,0:T(8,128)(2,1)S(1)} %collective-permute-done.3.u1_ref, ...), custom_call_target="tpu_custom_call" | custom-call | flops 2415919104 | bytes 14155776 | tf_op jit(solution)/shard_map/expert_part/pallas_call | solution.py:85
  52.8 1.8 %collective-permute-start.21 = (bf16[64,2048]{1,0:T(8,128)(2,1)S(1)}, bf16[64,2048]{1,0:T(8,128)(2,1)S(1)}, u32[]{:S(2)}, u32[]{:S(2)}) collective-permute-start(bf16[64,2048]{1,0:T(8,128)(2,1)S(1)} %get-tuple-element.20), channel_id=1, source_target_pairs={{0,4},{1,5},{4,8},{5,9},{8,12},{9,13},{12,14},{13,15},{14,10},{15,... | collective-permute-start | bytes 786440 | tf_op jit(solution)/shard_map/ppermute | solution.py:138
  54.9 6.2 %collective-permute-done.15.b_ref = bf16[64,4224]{1,0:T(8,128)(2,1)S(1)} collective-permute-done((bf16[64,4224]{1,0:T(8,128)(2,1)S(1)}, bf16[64,4224]{1,0:T(8,128)(2,1)S(1)}, u32[]{:S(2)}, u32[]{:S(2)}) %collective-permute-start.15) | collective-permute-done | bytes 540704 | tf_op jit(solution)/shard_map/ppermute | solution.py:138
  61.4 1.8 %collective-permute-start.9 = (bf16[64,4224]{1,0:T(8,128)(2,1)S(1)}, bf16[64,4224]{1,0:T(8,128)(2,1)S(1)}, u32[]{:S(2)}, u32[]{:S(2)}) collective-permute-start(bf16[64,4224]{1,0:T(8,128)(2,1)S(1)} %collective-permute-done.8.a_ref), channel_id=1, source_target_pairs={{0,4},{1,5},{4,8},{5,9},{8,12},{9,13},{12,14},{13,15},{14,10},{15,... | collective-permute-start | bytes 1622024 | tf_op jit(solution)/shard_map/ppermute | solution.py:138
  63.1 10.1 %expert_part.13 = f32[128,2048]{1,0:T(8,128)S(1)} custom-call(s32[2]{0:T(128)S(1)} %pad_add_fusion.me_ref, bf16[64,4224]{1,0:T(8,128)(2,1)S(1)} %collective-permute-done.8.a_ref, bf16[64,4224]{1,0:T(8,128)(2,1)S(1)} %collective-permute-done.15.b_ref, bf16[2048,768]{1,0:T(8,128)(2,1)S(1)} %bitcast.12, bf16[2048,768]{1,0:T(8,128)(2,1)S(1)} %collective-permute-done.3.u1_ref, ...), custom_call_target="tpu_custom_call" | custom-call | flops 2415919104 | bytes 14155776 | tf_op jit(solution)/shard_map/expert_part/pallas_call | solution.py:85
  73.4 1.6 collective-permute-start.22
  76.5 1.8 %collective-permute-start.10 = (bf16[64,4224]{1,0:T(8,128)(2,1)S(1)}, bf16[64,4224]{1,0:T(8,128)(2,1)S(1)}, u32[]{:S(2)}, u32[]{:S(2)}) collective-permute-start(bf16[64,4224]{1,0:T(8,128)(2,1)S(1)} %collective-permute-done.9.a_ref), channel_id=1, source_target_pairs={{0,4},{1,5},{4,8},{5,9},{8,12},{9,13},{12,14},{13,15},{14,10},{15,... | collective-permute-start | bytes 1622024 | tf_op jit(solution)/shard_map/ppermute | solution.py:138
  78.6 10.1 %expert_part.12 = f32[128,2048]{1,0:T(8,128)S(1)} custom-call(s32[2]{0:T(128)S(1)} %pad_add_fusion.me_ref, bf16[64,4224]{1,0:T(8,128)(2,1)S(1)} %collective-permute-done.9.a_ref, bf16[64,4224]{1,0:T(8,128)(2,1)S(1)} %collective-permute-done.16.b_ref, bf16[2048,768]{1,0:T(8,128)(2,1)S(1)} %bitcast.13, bf16[2048,768]{1,0:T(8,128)(2,1)S(1)} %collective-permute-done.3.u1_ref, ...), custom_call_target="tpu_custom_call" | custom-call | flops 2415919104 | bytes 14155776 | tf_op jit(solution)/shard_map/expert_part/pallas_call | solution.py:85
  88.8 1.8 %collective-permute-start.23 = (bf16[64,2048]{1,0:T(8,128)(2,1)S(1)}, bf16[64,2048]{1,0:T(8,128)(2,1)S(1)}, u32[]{:S(2)}, u32[]{:S(2)}) collective-permute-start(bf16[64,2048]{1,0:T(8,128)(2,1)S(1)} %get-tuple-element.16), channel_id=1, source_target_pairs={{0,4},{1,5},{4,8},{5,9},{8,12},{9,13},{12,14},{13,15},{14,10},{15,... | collective-permute-start | bytes 786440 | tf_op jit(solution)/shard_map/ppermute | solution.py:138
  90.9 3.4 %collective-permute-done.10.a_ref = bf16[64,4224]{1,0:T(8,128)(2,1)S(1)} collective-permute-done((bf16[64,4224]{1,0:T(8,128)(2,1)S(1)}, bf16[64,4224]{1,0:T(8,128)(2,1)S(1)}, u32[]{:S(2)}, u32[]{:S(2)}) %collective-permute-start.10) | collective-permute-done | bytes 540704 | tf_op jit(solution)/shard_map/ppermute | solution.py:138
  94.2 1.5 collective-permute-start.11
  96.3 10.1 %expert_part.11 = f32[128,2048]{1,0:T(8,128)S(1)} custom-call(s32[2]{0:T(128)S(1)} %pad_add_fusion.me_ref, bf16[64,4224]{1,0:T(8,128)(2,1)S(1)} %collective-permute-done.10.a_ref, bf16[64,4224]{1,0:T(8,128)(2,1)S(1)} %collective-permute-done.17.b_ref, bf16[2048,768]{1,0:T(8,128)(2,1)S(1)} %bitcast.14, bf16[2048,768]{1,0:T(8,128)(2,1)S(1)} %collective-permute-done.3.u1_ref, ...), custom_call_target="tpu_custom_call" | custom-call | flops 2415919104 | bytes 14155776 | tf_op jit(solution)/shard_map/expert_part/pallas_call | solution.py:85
  106.5 1.6 collective-permute-start.24
  111.4 1.5 collective-permute-start.12
  113.5 10.3 %expert_part.10 = f32[128,2048]{1,0:T(8,128)S(1)} custom-call(s32[2]{0:T(128)S(1)} %pad_add_fusion.me_ref, bf16[64,4224]{1,0:T(8,128)(2,1)S(1)} %collective-permute-done.11.a_ref, bf16[64,4224]{1,0:T(8,128)(2,1)S(1)} %collective-permute-done.18.b_ref, bf16[2048,768]{1,0:T(8,128)(2,1)S(1)} %bitcast.15, bf16[2048,768]{1,0:T(8,128)(2,1)S(1)} %collective-permute-done.3.u1_ref, ...), custom_call_target="tpu_custom_call" | custom-call | flops 2415919104 | bytes 14155776 | tf_op jit(solution)/shard_map/expert_part/pallas_call | solution.py:85
  123.9 1.6 collective-permute-start.25
  126.0 10.4 %expert_part.8 = f32[128,2048]{1,0:T(8,128)S(1)} custom-call(s32[2]{0:T(128)S(1)} %pad_add_fusion.me_ref, bf16[64,4224]{1,0:T(8,128)(2,1)} %get-tuple-element.7.a_ref, bf16[64,4224]{1,0:T(8,128)(2,1)} %get-tuple-element.8.b_ref, bf16[2048,768]{1,0:T(8,128)(2,1)S(1)} %bitcast.16, bf16[2048,768]{1,0:T(8,128)(2,1)S(1)} %collective-permute-done.3.u1_ref, ...), custom_call_target="tpu_custom_call" | custom-call | flops 2415919104 | bytes 14155776 | tf_op jit(solution)/shard_map/expert_part/pallas_call | solution.py:85
  136.5 1.6 collective-permute-start.1
  138.6 10.1 %expert_part.9 = f32[128,2048]{1,0:T(8,128)S(1)} custom-call(s32[2]{0:T(128)S(1)} %pad_add_fusion.me_ref, bf16[64,4224]{1,0:T(8,128)(2,1)S(1)} %collective-permute-done.12.a_ref, bf16[64,4224]{1,0:T(8,128)(2,1)S(1)} %collective-permute-done.19.b_ref, bf16[2048,768]{1,0:T(8,128)(2,1)S(1)} %bitcast.17, bf16[2048,768]{1,0:T(8,128)(2,1)S(1)} %collective-permute-done.3.u1_ref, ...), custom_call_target="tpu_custom_call" | custom-call | flops 2415919104 | bytes 14155776 | tf_op jit(solution)/shard_map/expert_part/pallas_call | solution.py:85
  148.7 1.6 collective-permute-start.5
  150.4 1.6 collective-permute-start.26
  152.7 1.7 %collective-permute-start.33 = (bf16[64,2048]{1,0:T(8,128)(2,1)S(1)}, bf16[64,2048]{1,0:T(8,128)(2,1)S(1)}, u32[]{:S(2)}, u32[]{:S(2)}) collective-permute-start(bf16[64,2048]{1,0:T(8,128)(2,1)S(1)} %get-tuple-element.9), channel_id=1, source_target_pairs={{0,18},{1,19},{4,16},{5,17},{8,20},{9,21},{12,24},{13,25},{14,28},... | collective-permute-start | bytes 786440 | tf_op jit(solution)/shard_map/ppermute | solution.py:142
  154.4 13.9 %collective-permute-done.5.own_ref = bf16[128,2048]{1,0:T(8,128)(2,1)S(1)} collective-permute-done((bf16[128,2048]{1,0:T(8,128)(2,1)S(1)}, bf16[128,2048]{1,0:T(8,128)(2,1)S(1)}, u32[]{:S(2)}, u32[]{:S(2)}) %collective-permute-start.5) | collective-permute-done | bytes 524320 | tf_op jit(solution)/shard_map/ppermute | solution.py:154
  168.3 1.5 finish.1
  (78 shorter events, 16.9 us)
Async XLA Ops:
  0.0 24.1 %collective-permute-start.3 = (bf16[2048,768]{1,0:T(8,128)(2,1)}, bf16[2048,768]{1,0:T(8,128)(2,1)S(1)}, u32[]{:S(2)}, u32[]{:S(2)}) collective-permute-start(bf16[2048,768]{1,0:T(8,128)(2,1)} %bitcast.9), channel_id=1, source_target_pairs={{0,1},{1,0},{2,3},{3,2},{4,5},{5,4},{6,7},{7,6},{8,9},{9,8},{10,11... | collective-permute-start | bytes 9437192 | tf_op jit(solution)/shard_map/ppermute | solution.py:157
  0.5 23.7 %collective-permute-start.4 = (bf16[768,2048]{1,0:T(8,128)(2,1)}, bf16[768,2048]{1,0:T(8,128)(2,1)}, u32[]{:S(2)}, u32[]{:S(2)}) collective-permute-start(bf16[768,2048]{1,0:T(8,128)(2,1)} %bitcast.18), channel_id=1, source_target_pairs={{0,1},{1,0},{2,3},{3,2},{4,5},{5,4},{6,7},{7,6},{8,9},{9,8},{10,11... | collective-permute-start | bytes 9437192 | tf_op jit(solution)/shard_map/ppermute | solution.py:157
  6.3 15.8 %collective-permute-start.13 = (bf16[64,4224]{1,0:T(8,128)(2,1)}, bf16[64,4224]{1,0:T(8,128)(2,1)}, u32[]{:S(2)}, u32[]{:S(2)}) collective-permute-start(bf16[64,4224]{1,0:T(8,128)(2,1)} %get-tuple-element.8.b_ref), channel_id=1, source_target_pairs={{0,2},{1,3},{4,0},{5,1},{8,4},{9,5},{12,8},{13,9},{14,12},{15,13},... | collective-permute-start | bytes 1622024 | tf_op jit(solution)/shard_map/ppermute | solution.py:138
  9.2 14.5 %collective-permute-start.6 = (bf16[64,4224]{1,0:T(8,128)(2,1)}, bf16[64,4224]{1,0:T(8,128)(2,1)}, u32[]{:S(2)}, u32[]{:S(2)}) collective-permute-start(bf16[64,4224]{1,0:T(8,128)(2,1)} %get-tuple-element.7.a_ref), channel_id=1, source_target_pairs={{0,4},{1,5},{4,8},{5,9},{8,12},{9,13},{12,14},{13,15},{14,10},{15,... | collective-permute-start | bytes 1622024 | tf_op jit(solution)/shard_map/ppermute | solution.py:138
  22.1 18.4 %collective-permute-start.14 = (bf16[64,4224]{1,0:T(8,128)(2,1)}, bf16[64,4224]{1,0:T(8,128)(2,1)S(1)}, u32[]{:S(2)}, u32[]{:S(2)}) collective-permute-start(bf16[64,4224]{1,0:T(8,128)(2,1)} %collective-permute-done.13.b_ref), channel_id=1, source_target_pairs={{0,2},{1,3},{4,0},{5,1},{8,4},{9,5},{12,8},{13,9},{14,12},{15,13},... | collective-permute-start | bytes 1622024 | tf_op jit(solution)/shard_map/ppermute | solution.py:138
  23.7 18.4 %collective-permute-start.7 = (bf16[64,4224]{1,0:T(8,128)(2,1)}, bf16[64,4224]{1,0:T(8,128)(2,1)S(1)}, u32[]{:S(2)}, u32[]{:S(2)}) collective-permute-start(bf16[64,4224]{1,0:T(8,128)(2,1)} %collective-permute-done.6.a_ref), channel_id=1, source_target_pairs={{0,4},{1,5},{4,8},{5,9},{8,12},{9,13},{12,14},{13,15},{14,10},{15,... | collective-permute-start | bytes 1622024 | tf_op jit(solution)/shard_map/ppermute | solution.py:138
  38.4 14.2 %collective-permute-start.20 = (bf16[64,2048]{1,0:T(8,128)(2,1)S(1)}, bf16[64,2048]{1,0:T(8,128)(2,1)S(1)}, u32[]{:S(2)}, u32[]{:S(2)}) collective-permute-start(bf16[64,2048]{1,0:T(8,128)(2,1)S(1)} %get-tuple-element.22), channel_id=1, source_target_pairs={{0,4},{1,5},{4,8},{5,9},{8,12},{9,13},{12,14},{13,15},{14,10},{15,... | collective-permute-start | bytes 786440 | tf_op jit(solution)/shard_map/ppermute | solution.py:138
  40.5 20.6 %collective-permute-start.15 = (bf16[64,4224]{1,0:T(8,128)(2,1)S(1)}, bf16[64,4224]{1,0:T(8,128)(2,1)S(1)}, u32[]{:S(2)}, u32[]{:S(2)}) collective-permute-start(bf16[64,4224]{1,0:T(8,128)(2,1)S(1)} %collective-permute-done.14.b_ref), channel_id=1, source_target_pairs={{0,2},{1,3},{4,0},{5,1},{8,4},{9,5},{12,8},{13,9},{14,12},{15,13},... | collective-permute-start | bytes 1622024 | tf_op jit(solution)/shard_map/ppermute | solution.py:138
  42.2 19.2 %collective-permute-start.8 = (bf16[64,4224]{1,0:T(8,128)(2,1)S(1)}, bf16[64,4224]{1,0:T(8,128)(2,1)S(1)}, u32[]{:S(2)}, u32[]{:S(2)}) collective-permute-start(bf16[64,4224]{1,0:T(8,128)(2,1)S(1)} %collective-permute-done.7.a_ref), channel_id=1, source_target_pairs={{0,4},{1,5},{4,8},{5,9},{8,12},{9,13},{12,14},{13,15},{14,10},{15,... | collective-permute-start | bytes 1622024 | tf_op jit(solution)/shard_map/ppermute | solution.py:138
  52.8 20.4 %collective-permute-start.21 = (bf16[64,2048]{1,0:T(8,128)(2,1)S(1)}, bf16[64,2048]{1,0:T(8,128)(2,1)S(1)}, u32[]{:S(2)}, u32[]{:S(2)}) collective-permute-start(bf16[64,2048]{1,0:T(8,128)(2,1)S(1)} %get-tuple-element.20), channel_id=1, source_target_pairs={{0,4},{1,5},{4,8},{5,9},{8,12},{9,13},{12,14},{13,15},{14,10},{15,... | collective-permute-start | bytes 786440 | tf_op jit(solution)/shard_map/ppermute | solution.py:138
  54.6 18.6 %collective-permute-start.28 = (bf16[64,2048]{1,0:T(8,128)(2,1)S(1)}, bf16[64,2048]{1,0:T(8,128)(2,1)S(1)}, u32[]{:S(2)}, u32[]{:S(2)}) collective-permute-start(bf16[64,2048]{1,0:T(8,128)(2,1)S(1)} %get-tuple-element.19), channel_id=1, source_target_pairs={{0,2},{1,3},{4,0},{5,1},{8,4},{9,5},{12,8},{13,9},{14,12},{15,13},... | collective-permute-start | bytes 786440 | tf_op jit(solution)/shard_map/ppermute | solution.py:138
  61.1 17.2 %collective-permute-start.16 = (bf16[64,4224]{1,0:T(8,128)(2,1)S(1)}, bf16[64,4224]{1,0:T(8,128)(2,1)S(1)}, u32[]{:S(2)}, u32[]{:S(2)}) collective-permute-start(bf16[64,4224]{1,0:T(8,128)(2,1)S(1)} %collective-permute-done.15.b_ref), channel_id=1, source_target_pairs={{0,2},{1,3},{4,0},{5,1},{8,4},{9,5},{12,8},{13,9},{14,12},{15,13},... | collective-permute-start | bytes 1622024 | tf_op jit(solution)/shard_map/ppermute | solution.py:138
  61.4 15.2 %collective-permute-start.9 = (bf16[64,4224]{1,0:T(8,128)(2,1)S(1)}, bf16[64,4224]{1,0:T(8,128)(2,1)S(1)}, u32[]{:S(2)}, u32[]{:S(2)}) collective-permute-start(bf16[64,4224]{1,0:T(8,128)(2,1)S(1)} %collective-permute-done.8.a_ref), channel_id=1, source_target_pairs={{0,4},{1,5},{4,8},{5,9},{8,12},{9,13},{12,14},{13,15},{14,10},{15,... | collective-permute-start | bytes 1622024 | tf_op jit(solution)/shard_map/ppermute | solution.py:138
  73.4 15.3 %collective-permute-start.22 = (bf16[64,2048]{1,0:T(8,128)(2,1)S(1)}, bf16[64,2048]{1,0:T(8,128)(2,1)S(1)}, u32[]{:S(2)}, u32[]{:S(2)}) collective-permute-start(bf16[64,2048]{1,0:T(8,128)(2,1)S(1)} %get-tuple-element.18), channel_id=1, source_target_pairs={{0,4},{1,5},{4,8},{5,9},{8,12},{9,13},{12,14},{13,15},{14,10},{15,... | collective-permute-start | bytes 786440 | tf_op jit(solution)/shard_map/ppermute | solution.py:138
  76.5 17.7 %collective-permute-start.10 = (bf16[64,4224]{1,0:T(8,128)(2,1)S(1)}, bf16[64,4224]{1,0:T(8,128)(2,1)S(1)}, u32[]{:S(2)}, u32[]{:S(2)}) collective-permute-start(bf16[64,4224]{1,0:T(8,128)(2,1)S(1)} %collective-permute-done.9.a_ref), channel_id=1, source_target_pairs={{0,4},{1,5},{4,8},{5,9},{8,12},{9,13},{12,14},{13,15},{14,10},{15,... | collective-permute-start | bytes 1622024 | tf_op jit(solution)/shard_map/ppermute | solution.py:138
  78.3 17.5 %collective-permute-start.17 = (bf16[64,4224]{1,0:T(8,128)(2,1)S(1)}, bf16[64,4224]{1,0:T(8,128)(2,1)S(1)}, u32[]{:S(2)}, u32[]{:S(2)}) collective-permute-start(bf16[64,4224]{1,0:T(8,128)(2,1)S(1)} %collective-permute-done.16.b_ref), channel_id=1, source_target_pairs={{0,2},{1,3},{4,0},{5,1},{8,4},{9,5},{12,8},{13,9},{14,12},{15,13},... | collective-permute-start | bytes 1622024 | tf_op jit(solution)/shard_map/ppermute | solution.py:138
  88.8 17.6 %collective-permute-start.23 = (bf16[64,2048]{1,0:T(8,128)(2,1)S(1)}, bf16[64,2048]{1,0:T(8,128)(2,1)S(1)}, u32[]{:S(2)}, u32[]{:S(2)}) collective-permute-start(bf16[64,2048]{1,0:T(8,128)(2,1)S(1)} %get-tuple-element.16), channel_id=1, source_target_pairs={{0,4},{1,5},{4,8},{5,9},{8,12},{9,13},{12,14},{13,15},{14,10},{15,... | collective-permute-start | bytes 786440 | tf_op jit(solution)/shard_map/ppermute | solution.py:138
  90.6 15.8 %collective-permute-start.30 = (bf16[64,2048]{1,0:T(8,128)(2,1)S(1)}, bf16[64,2048]{1,0:T(8,128)(2,1)S(1)}, u32[]{:S(2)}, u32[]{:S(2)}) collective-permute-start(bf16[64,2048]{1,0:T(8,128)(2,1)S(1)} %get-tuple-element.15), channel_id=1, source_target_pairs={{0,2},{1,3},{4,0},{5,1},{8,4},{9,5},{12,8},{13,9},{14,12},{15,13},... | collective-permute-start | bytes 786440 | tf_op jit(solution)/shard_map/ppermute | solution.py:138
  94.2 17.2 %collective-permute-start.11 = (bf16[64,4224]{1,0:T(8,128)(2,1)S(1)}, bf16[64,4224]{1,0:T(8,128)(2,1)S(1)}, u32[]{:S(2)}, u32[]{:S(2)}) collective-permute-start(bf16[64,4224]{1,0:T(8,128)(2,1)S(1)} %collective-permute-done.10.a_ref), channel_id=1, source_target_pairs={{0,4},{1,5},{4,8},{5,9},{8,12},{9,13},{12,14},{13,15},{14,10},{15,... | collective-permute-start | bytes 1622024 | tf_op jit(solution)/shard_map/ppermute | solution.py:138
  95.8 17.2 %collective-permute-start.18 = (bf16[64,4224]{1,0:T(8,128)(2,1)S(1)}, bf16[64,4224]{1,0:T(8,128)(2,1)S(1)}, u32[]{:S(2)}, u32[]{:S(2)}) collective-permute-start(bf16[64,4224]{1,0:T(8,128)(2,1)S(1)} %collective-permute-done.17.b_ref), channel_id=1, source_target_pairs={{0,2},{1,3},{4,0},{5,1},{8,4},{9,5},{12,8},{13,9},{14,12},{15,13},... | collective-permute-start | bytes 1622024 | tf_op jit(solution)/shard_map/ppermute | solution.py:138
  106.5 17.2 %collective-permute-start.24 = (bf16[64,2048]{1,0:T(8,128)(2,1)S(1)}, bf16[64,2048]{1,0:T(8,128)(2,1)S(1)}, u32[]{:S(2)}, u32[]{:S(2)}) collective-permute-start(bf16[64,2048]{1,0:T(8,128)(2,1)S(1)} %get-tuple-element.14), channel_id=1, source_target_pairs={{0,4},{1,5},{4,8},{5,9},{8,12},{9,13},{12,14},{13,15},{14,10},{15,... | collective-permute-start | bytes 786440 | tf_op jit(solution)/shard_map/ppermute | solution.py:138
  108.1 15.6 %collective-permute-start.31 = (bf16[64,2048]{1,0:T(8,128)(2,1)S(1)}, bf16[64,2048]{1,0:T(8,128)(2,1)S(1)}, u32[]{:S(2)}, u32[]{:S(2)}) collective-permute-start(bf16[64,2048]{1,0:T(8,128)(2,1)S(1)} %get-tuple-element.13), channel_id=1, source_target_pairs={{0,2},{1,3},{4,0},{5,1},{8,4},{9,5},{12,8},{13,9},{14,12},{15,13},... | collective-permute-start | bytes 786440 | tf_op jit(solution)/shard_map/ppermute | solution.py:138
  108.6 45.8 %collective-permute-start = (bf16[128,2048]{1,0:T(8,128)(2,1)S(1)}, bf16[128,2048]{1,0:T(8,128)(2,1)S(1)}, u32[]{:S(2)}, u32[]{:S(2)}) collective-permute-start(bf16[128,2048]{1,0:T(8,128)(2,1)S(1)} %bitcast.28), channel_id=1, source_target_pairs={{0,16},{16,0},{1,17},{17,1},{2,18},{18,2},{3,19},{19,3},{4,20},{20... | collective-permute-start | bytes 1572872 | tf_op jit(solution)/shard_map/ppermute | solution.py:154
  111.4 25.0 %collective-permute-start.12 = (bf16[64,4224]{1,0:T(8,128)(2,1)S(1)}, bf16[64,4224]{1,0:T(8,128)(2,1)S(1)}, u32[]{:S(2)}, u32[]{:S(2)}) collective-permute-start(bf16[64,4224]{1,0:T(8,128)(2,1)S(1)} %collective-permute-done.11.a_ref), channel_id=1, source_target_pairs={{0,4},{1,5},{4,8},{5,9},{8,12},{9,13},{12,14},{13,15},{14,10},{15,... | collective-permute-start | bytes 1622024 | tf_op jit(solution)/shard_map/ppermute | solution.py:138
  113.0 25.0 %collective-permute-start.19 = (bf16[64,4224]{1,0:T(8,128)(2,1)S(1)}, bf16[64,4224]{1,0:T(8,128)(2,1)S(1)}, u32[]{:S(2)}, u32[]{:S(2)}) collective-permute-start(bf16[64,4224]{1,0:T(8,128)(2,1)S(1)} %collective-permute-done.18.b_ref), channel_id=1, source_target_pairs={{0,2},{1,3},{4,0},{5,1},{8,4},{9,5},{12,8},{13,9},{14,12},{15,13},... | collective-permute-start | bytes 1622024 | tf_op jit(solution)/shard_map/ppermute | solution.py:138
  123.9 24.8 %collective-permute-start.25 = (bf16[64,2048]{1,0:T(8,128)(2,1)S(1)}, bf16[64,2048]{1,0:T(8,128)(2,1)S(1)}, u32[]{:S(2)}, u32[]{:S(2)}) collective-permute-start(bf16[64,2048]{1,0:T(8,128)(2,1)S(1)} %get-tuple-element.12), channel_id=1, source_target_pairs={{0,4},{1,5},{4,8},{5,9},{8,12},{9,13},{12,14},{13,15},{14,10},{15,... | collective-permute-start | bytes 786440 | tf_op jit(solution)/shard_map/ppermute | solution.py:138
  125.5 24.8 %collective-permute-start.32 = (bf16[64,2048]{1,0:T(8,128)(2,1)S(1)}, bf16[64,2048]{1,0:T(8,128)(2,1)S(1)}, u32[]{:S(2)}, u32[]{:S(2)}) collective-permute-start(bf16[64,2048]{1,0:T(8,128)(2,1)S(1)} %get-tuple-element.11), channel_id=1, source_target_pairs={{0,2},{1,3},{4,0},{5,1},{8,4},{9,5},{12,8},{13,9},{14,12},{15,13},... | collective-permute-start | bytes 786440 | tf_op jit(solution)/shard_map/ppermute | solution.py:138
  136.5 17.9 %collective-permute-start.1 = (bf16[128,2048]{1,0:T(8,128)(2,1)S(1)}, bf16[128,2048]{1,0:T(8,128)(2,1)S(1)}, u32[]{:S(2)}, u32[]{:S(2)}) collective-permute-start(bf16[128,2048]{1,0:T(8,128)(2,1)S(1)} %bitcast.30), channel_id=1, source_target_pairs={{0,16},{16,0},{1,17},{17,1},{2,18},{18,2},{3,19},{19,3},{4,20},{20... | collective-permute-start | bytes 1572872 | tf_op jit(solution)/shard_map/ppermute | solution.py:154
  138.0 14.6 %collective-permute-start.2 = (f32[1,2048]{1,0:T(1,128)S(1)}, f32[1,2048]{1,0:T(1,128)S(1)}, u32[]{:S(2)}, u32[]{:S(2)}) collective-permute-start(f32[1,2048]{1,0:T(1,128)S(1)} %copy-done.9), channel_id=1, source_target_pairs={{0,16},{16,0},{1,17},{17,1},{2,18},{18,2},{3,19},{19,3},{4,20},{20... | collective-permute-start | bytes 24584 | tf_op jit(solution)/shard_map/ppermute | solution.py:154
  148.7 19.6 %collective-permute-start.5 = (bf16[128,2048]{1,0:T(8,128)(2,1)S(1)}, bf16[128,2048]{1,0:T(8,128)(2,1)S(1)}, u32[]{:S(2)}, u32[]{:S(2)}) collective-permute-start(bf16[128,2048]{1,0:T(8,128)(2,1)S(1)} %convert_element_type.77), channel_id=1, source_target_pairs={{0,16},{16,0},{1,17},{17,1},{2,18},{18,2},{3,19},{19,3},{4,20},{20... | collective-permute-start | bytes 1572872 | tf_op jit(solution)/shard_map/ppermute | solution.py:154
  150.4 17.9 %collective-permute-start.26 = (bf16[64,2048]{1,0:T(8,128)(2,1)S(1)}, bf16[64,2048]{1,0:T(8,128)(2,1)S(1)}, u32[]{:S(2)}, u32[]{:S(2)}) collective-permute-start(bf16[64,2048]{1,0:T(8,128)(2,1)S(1)} %get-tuple-element.10), channel_id=1, source_target_pairs={{0,20},{1,21},{4,24},{5,25},{8,28},{9,29},{12,30},{13,31},{14,26},... | collective-permute-start | bytes 786440 | tf_op jit(solution)/shard_map/ppermute | solution.py:142
  152.7 15.6 %collective-permute-start.33 = (bf16[64,2048]{1,0:T(8,128)(2,1)S(1)}, bf16[64,2048]{1,0:T(8,128)(2,1)S(1)}, u32[]{:S(2)}, u32[]{:S(2)}) collective-permute-start(bf16[64,2048]{1,0:T(8,128)(2,1)S(1)} %get-tuple-element.9), channel_id=1, source_target_pairs={{0,18},{1,19},{4,16},{5,17},{8,20},{9,21},{12,24},{13,25},{14,28},... | collective-permute-start | bytes 786440 | tf_op jit(solution)/shard_map/ppermute | solution.py:142
  (12 other events, 99.2 us)

commit v2 on v1

--- a/solution.py
+++ b/solution.py
@@ -40,62 +40,39 @@
     )(x, grad, gain, routes, gates)
 
 
-def expert_kernel(me_ref, a_ref, b_ref, u0_ref, u1_ref, d0_ref, d1_ref, o_ref, n_s, g_s, w_s):
+def expert_kernel(me_ref, a_ref, b_ref, u0_ref, u1_ref, d0_ref, d1_ref, o_ref):
     width = u0_ref.shape[0]
-    half = a_ref.shape[0]
 
-    @pl.when(pl.program_id(0) == 0)
-    def _():
-        lane = lax.broadcasted_iota(jnp.int32, (half, a_ref.shape[1] - 2 * width), 1)
-        for ref, first in ((a_ref, 0), (b_ref, half)):
-            n_s[first : first + half, :] = ref[:, :width]
-            g_s[first : first + half, :] = ref[:, width : 2 * width]
-            dense = ref[:, 2 * width :].astype(jnp.float32)
-            for i in range(2):
-                w_s[first : first + half, i : i + 1] = jnp.sum(
-                    jnp.where(lane == me_ref[i], dense, 0.0), axis=-1, keepdims=True
-                )
+    def rows(first, last):
+        return jnp.concatenate([a_ref[:, first:last], b_ref[:, first:last]], axis=0)
 
-    total = None
+    normed, grad = rows(0, width), rows(width, 2 * width)
+    dense = rows(2 * width, a_ref.shape[1]).astype(jnp.float32)
+    lane = lax.broadcasted_iota(jnp.int32, dense.shape, 1)
     for i, (u_ref, d_ref) in enumerate(((u0_ref, d0_ref), (u1_ref, d1_ref))):
-        before = jnp.dot(n_s[...], u_ref[...], preferred_element_type=jnp.float32)
-        d_hidden = lax.dot_general(g_s[...], d_ref[...], NT, preferred_element_type=jnp.float32)
+        before = jnp.dot(normed, u_ref[...], preferred_element_type=jnp.float32)
+        d_hidden = lax.dot_general(grad, d_ref[...], NT, preferred_element_type=jnp.float32)
         sigmoid_of = jax.nn.sigmoid(before)
-        d_before = d_hidden * sigmoid_of * (1.0 + before * (1.0 - sigmoid_of))
-        d_before = (d_before * w_s[:, i : i + 1]).astype(jnp.bfloat16)
-        part = lax.dot_general(d_before, u_ref[...], NT, preferred_element_type=jnp.float32)
-        total = part if total is None else total + part
-
-    @pl.when(pl.program_id(0) == 0)
-    def _():
-        o_ref[...] = total
-
-    @pl.when(pl.program_id(0) > 0)
-    def _():
-        o_ref[...] += total
+        d_before = (d_hidden * sigmoid_of * (1.0 + before * (1.0 - sigmoid_of))).astype(jnp.bfloat16)
+        d_route = lax.dot_general(d_before, u_ref[...], NT, preferred_element_type=jnp.float32)
+        gate = jnp.sum(jnp.where(lane == me_ref[i], dense, 0.0), axis=-1, keepdims=True)
+        part = d_route.astype(jnp.bfloat16).astype(jnp.float32) * gate
+        if i == 0:
+            o_ref[...] = part
+        else:
+            o_ref[...] += part
 
 
 def expert_part(me, a, b, u0, u1, d0, d1):
-    half, wide = a.shape
+    half = a.shape[0]
     width, hidden = u0.shape
-    chunk = 256
-    up = pl.BlockSpec((width, chunk), lambda i: (0, i))
-    down = pl.BlockSpec((chunk, width), lambda i: (i, 0))
-    rows = pl.BlockSpec((half, wide), lambda i: (0, 0))
+    whole = pl.BlockSpec(memory_space=pltpu.VMEM)
     return pl.pallas_call(
         expert_kernel,
         out_shape=jax.ShapeDtypeStruct((2 * half, width), jnp.float32),
-        grid=(hidden // chunk,),
-        in_specs=[pl.BlockSpec(memory_space=pltpu.SMEM), rows, rows, up, up, down, down],
-        out_specs=pl.BlockSpec((2 * half, width), lambda i: (0, 0)),
-        scratch_shapes=[
-            pltpu.VMEM((2 * half, width), jnp.bfloat16),
-            pltpu.VMEM((2 * half, width), jnp.bfloat16),
-            pltpu.VMEM((2 * half, LANES), jnp.float32),
-        ],
-        compiler_params=pltpu.CompilerParams(
-            dimension_semantics=("arbitrary",), vmem_limit_bytes=40 << 20
-        ),
+        in_specs=[pl.BlockSpec(memory_space=pltpu.SMEM)] + [whole] * 6,
+        out_specs=whole,
+        compiler_params=pltpu.CompilerParams(vmem_limit_bytes=30 << 20),
         cost_estimate=pl.CostEstimate(
             flops=24 * half * width * hidden,
             transcendentals=4 * half * hidden,
@@ -161,15 +138,22 @@
     e = lax.axis_index("expert").astype(jnp.int32)
     me = jnp.stack([e, e ^ 1])
 
+    u1, d1 = swap(u0), swap(d0)
     a, b = pack(x, grad, norm_gain, bwd_routes[0], bwd_gates[0], experts)
+    half = a.shape[0]
     a1, b1 = hop(a, 1), hop(b, -1)
-    u1, d1 = swap(u0), swap(d0)
     x_out, grad_out, gain_out = to_previous(x), to_previous(grad), to_previous(norm_gain)
-    own = to_previous(expert_part(me, a, b, u0, u1, d0, d1).astype(jnp.bfloat16))
-    half = a.shape[0]
+    own = expert_part(me, a, b, u0, u1, d0, d1).astype(jnp.bfloat16)
+    own_out = to_previous(own)
     sum_a = sum_b = None
     for step in range(1, chips):
         a, b = a1, b1
+        if step == 1:
+            a, b, own = lax.optimization_barrier((a, b, own))
+        if step == 3:
+            a, b, x_out, grad_out, gain_out = lax.optimization_barrier((a, b, x_out, grad_out, gain_out))
+        if step == 5:
+            a, b, own_out = lax.optimization_barrier((a, b, own_out))
         if step < chips - 1:
             a1, b1 = hop(a, 1), hop(b, -1)
         part = expert_part(me, a, b, u0, u1, d0, d1)
@@ -180,7 +164,7 @@
         move = hop if step < chips - 1 else last_hop
         sum_a = move(part_a.astype(jnp.bfloat16), 1)
         sum_b = move(part_b.astype(jnp.bfloat16), -1)
-    return finish(x_out, grad_out, gain_out, own, sum_a, sum_b)[None]
+    return finish(x_out, grad_out, gain_out, own_out, sum_a, sum_b)[None]
 
 
 def solution(mesh):

time: 170 us -> 152 us (0.89)
  Pallas kernels: 84.6 us -> 60.1 us
  waiting for transfers between devices: 39.4 us -> 45.9 us
    pallas_call x8, Pallas kernels: 81.6 us -> 57.2 us  [expert_part(): pl.pallas_call(expert_kernel, out_shape=jax.ShapeDtypeStruct((2 * half, w...]
    ppermute x4, waiting for transfers between devices: 14.6 us -> 4.58 us  [to_previous(): lax.ppermute(value, 'pipe', [(s, (s - 1) % sections) for s in range(secti...]
    ppermute x26, waiting for transfers between devices: 24.8 us -> 32.9 us  [hop(): lax.ppermute(value, 'expert', [(2 * a + c, 2 * b + c) for a, b in moves f...]
    ppermute x2, waiting for transfers between devices: 0.01 us -> 7.15 us  [last_hop(): lax.ppermute(value, ('pipe', 'expert'), [(s * experts + 2 * a + c, (s - 1...]
  transfers between devices with their start and end apart: 34 -> 34, of which waited for: 7 -> 13; matrix products, arithmetic and copies ran while one was open for 1% -> 2% of each run, Pallas kernels for 49% -> 39%
where the time goes in v2:
time: 152 us
  Pallas kernels  60.1 us (40%)
  waiting for transfers between devices  45.9 us (30%)
  starting transfers between devices  36.4 us (24%)
  local copies, waits for them, and re-layouts  8.2 us (5%)
    pallas_call x8, Pallas kernels, expert_part(): pl.pallas_call(expert_kernel, out_shape=jax.ShapeDtypeStruct((2 * half, w...  57.2 us
    ppermute x26, waiting for transfers between devices, hop(): lax.ppermute(value, 'expert', [(2 * a + c, 2 * b + c) for a, b in moves f...  32.9 us
    ppermute x26, starting transfers between devices, hop(): lax.ppermute(value, 'expert', [(2 * a + c, 2 * b + c) for a, b in moves f...  27.7 us
    unnamed x22, local copies, waits for them, and re-layouts  8.17 us
    ppermute x2, waiting for transfers between devices, last_hop(): lax.ppermute(value, ('pipe', 'expert'), [(s * experts + 2 * a + c, (s - 1...  7.15 us
    ppermute x4, starting transfers between devices, to_previous(): lax.ppermute(value, 'pipe', [(s, (s - 1) % sections) for s in range(secti...  5.24 us
    ppermute x4, waiting for transfers between devices, to_previous(): lax.ppermute(value, 'pipe', [(s, (s - 1) % sections) for s in range(secti...  4.58 us
  transfers between devices with their start and end apart: 34, of which 13 were waited for; matrix products, arithmetic and copies ran while one was open for 2% of the time, Pallas kernels for 39%

profile of v2, /device:TPU:0, one launch (start us, length us, event | category | flops | bytes accessed | tf_op | source)
XLA Modules:
  0.0 151.7 jit_solution(12069069623066080796)
XLA Ops:
  6.3 3.0 %collective-permute-start = (bf16[64,4224]{1,0:T(8,128)(2,1)}, bf16[64,4224]{1,0:T(8,128)(2,1)}, u32[]{:S(2)}, u32[]{:S(2)}) collective-permute-start(bf16[64,4224]{1,0:T(8,128)(2,1)} %get-tuple-element.17.a_ref), channel_id=1, source_target_pairs={{0,4},{1,5},{4,8},{5,9},{8,12},{9,13},{12,14},{13,15},{14,10},{15,... | collective-permute-start | bytes 1622024 | tf_op jit(solution)/shard_map/ppermute | solution.py:115
  10.6 1.9 %copy-done = bf16[1,1,2048,768]{3,2,1,0:T(8,128)(2,1)S(1)} copy-done((bf16[1,1,2048,768]{3,2,1,0:T(8,128)(2,1)S(1)}, bf16[1,1,2048,768]{3,2,1,0:T(8,128)(2,1)}, u32[]{:S(2)}) %copy-start) | copy-done | bytes 3145752
  12.5 1.9 %copy-done.2 = bf16[1,1,768,2048]{3,2,1,0:T(8,128)(2,1)S(1)} copy-done((bf16[1,1,768,2048]{3,2,1,0:T(8,128)(2,1)S(1)}, bf16[1,1,768,2048]{3,2,1,0:T(8,128)(2,1)}, u32[]{:S(2)}) %copy-start.2) | copy-done | bytes 3145752
  14.4 7.5 %expert_part.8 = f32[128,2048]{1,0:T(8,128)S(1)} custom-call(s32[2]{0:T(128)S(1)} %pad_add_fusion.me_ref, bf16[64,4224]{1,0:T(8,128)(2,1)} %get-tuple-element.17.a_ref, bf16[64,4224]{1,0:T(8,128)(2,1)} %get-tuple-element.18.b_ref, bf16[2048,768]{1,0:T(8,128)(2,1)S(1)} %bitcast.10, bf16[2048,768]{1,0:T(8,128)(2,1)S(1)} %collective-permute-done.2.u1_ref, ...), custom_call_target="tpu_custom_call" | custom-call | flops 2415919104 | bytes 14155776 | tf_op jit(solution)/shard_map/expert_part/pallas_call | solution.py:70
  25.6 7.4 %expert_part.15 = f32[128,2048]{1,0:T(8,128)S(1)} custom-call(s32[2]{0:T(128)S(1)} %pad_add_fusion.me_ref, bf16[64,4224]{1,0:T(8,128)(2,1)} %collective-permute-done.a_ref, bf16[64,4224]{1,0:T(8,128)(2,1)} %collective-permute-done.1.b_ref, bf16[2048,768]{1,0:T(8,128)(2,1)S(1)} %bitcast.11, bf16[2048,768]{1,0:T(8,128)(2,1)S(1)} %collective-permute-done.2.u1_ref, ...), custom_call_target="tpu_custom_call" | custom-call | flops 2415919104 | bytes 14155776 | tf_op jit(solution)/shard_map/expert_part/pallas_call | solution.py:70
  33.1 1.6 %collective-permute-start.20 = (bf16[64,2048]{1,0:T(8,128)(2,1)S(1)}, bf16[64,2048]{1,0:T(8,128)(2,1)S(1)}, u32[]{:S(2)}, u32[]{:S(2)}) collective-permute-start(bf16[64,2048]{1,0:T(8,128)(2,1)S(1)} %get-tuple-element.42), channel_id=1, source_target_pairs={{0,4},{1,5},{4,8},{5,9},{8,12},{9,13},{12,14},{13,15},{14,10},{15,... | collective-permute-start | bytes 786440 | tf_op jit(solution)/shard_map/ppermute | solution.py:115
  36.7 6.6 %collective-permute-done.20 = bf16[64,2048]{1,0:T(8,128)(2,1)S(1)} collective-permute-done((bf16[64,2048]{1,0:T(8,128)(2,1)S(1)}, bf16[64,2048]{1,0:T(8,128)(2,1)S(1)}, u32[]{:S(2)}, u32[]{:S(2)}) %collective-permute-start.20) | collective-permute-done | bytes 262176 | tf_op jit(solution)/shard_map/ppermute | solution.py:115
  43.3 1.8 %collective-permute-start.9 = (bf16[128,2048]{1,0:T(8,128)(2,1)S(1)}, bf16[128,2048]{1,0:T(8,128)(2,1)S(1)}, u32[]{:S(2)}, u32[]{:S(2)}) collective-permute-start(bf16[128,2048]{1,0:T(8,128)(2,1)S(1)} %bitcast.30), channel_id=1, source_target_pairs={{0,16},{16,0},{1,17},{17,1},{2,18},{18,2},{3,19},{19,3},{4,20},{20... | collective-permute-start | bytes 1572872 | tf_op jit(solution)/shard_map/ppermute | solution.py:131
  47.1 7.0 %expert_part.14 = f32[128,2048]{1,0:T(8,128)S(1)} custom-call(s32[2]{0:T(128)S(1)} %pad_add_fusion.me_ref, bf16[64,4224]{1,0:T(8,128)(2,1)S(1)} %collective-permute-done.4.a_ref, bf16[64,4224]{1,0:T(8,128)(2,1)S(1)} %collective-permute-done.6.b_ref, bf16[2048,768]{1,0:T(8,128)(2,1)S(1)} %bitcast.12, bf16[2048,768]{1,0:T(8,128)(2,1)S(1)} %collective-permute-done.2.u1_ref, ...), custom_call_target="tpu_custom_call" | custom-call | flops 2415919104 | bytes 14155776 | tf_op jit(solution)/shard_map/expert_part/pallas_call | solution.py:70
  54.6 4.6 %collective-permute-done.10.gain_ref = f32[1,2048]{1,0:T(1,128)S(1)} collective-permute-done((f32[1,2048]{1,0:T(1,128)S(1)}, f32[1,2048]{1,0:T(1,128)S(1)}, u32[]{:S(2)}, u32[]{:S(2)}) %collective-permute-start.10) | collective-permute-done | bytes 8224 | tf_op jit(solution)/shard_map/ppermute | solution.py:131
  59.2 1.7 %collective-permute-start.21 = (bf16[64,2048]{1,0:T(8,128)(2,1)S(1)}, bf16[64,2048]{1,0:T(8,128)(2,1)S(1)}, u32[]{:S(2)}, u32[]{:S(2)}) collective-permute-start(bf16[64,2048]{1,0:T(8,128)(2,1)S(1)} %get-tuple-element.40), channel_id=1, source_target_pairs={{0,4},{1,5},{4,8},{5,9},{8,12},{9,13},{12,14},{13,15},{14,10},{15,... | collective-permute-start | bytes 786440 | tf_op jit(solution)/shard_map/ppermute | solution.py:115
  61.3 1.7 %collective-permute-start.11 = (bf16[64,4224]{1,0:T(8,128)(2,1)S(1)}, bf16[64,4224]{1,0:T(8,128)(2,1)S(1)}, u32[]{:S(2)}, u32[]{:S(2)}) collective-permute-start(bf16[64,4224]{1,0:T(8,128)(2,1)S(1)} %collective-permute-done.5.a_ref), channel_id=1, source_target_pairs={{0,4},{1,5},{4,8},{5,9},{8,12},{9,13},{12,14},{13,15},{14,10},{15,... | collective-permute-start | bytes 1622024 | tf_op jit(solution)/shard_map/ppermute | solution.py:115
  63.3 7.0 %expert_part.13 = f32[128,2048]{1,0:T(8,128)S(1)} custom-call(s32[2]{0:T(128)S(1)} %pad_add_fusion.me_ref, bf16[64,4224]{1,0:T(8,128)(2,1)S(1)} %collective-permute-done.5.a_ref, bf16[64,4224]{1,0:T(8,128)(2,1)S(1)} %collective-permute-done.7.b_ref, bf16[2048,768]{1,0:T(8,128)(2,1)S(1)} %bitcast.13, bf16[2048,768]{1,0:T(8,128)(2,1)S(1)} %collective-permute-done.2.u1_ref, ...), custom_call_target="tpu_custom_call" | custom-call | flops 2415919104 | bytes 14155776 | tf_op jit(solution)/shard_map/expert_part/pallas_call | solution.py:70
  70.5 1.7 %collective-permute-start.22 = (bf16[64,2048]{1,0:T(8,128)(2,1)S(1)}, bf16[64,2048]{1,0:T(8,128)(2,1)S(1)}, u32[]{:S(2)}, u32[]{:S(2)}) collective-permute-start(bf16[64,2048]{1,0:T(8,128)(2,1)S(1)} %get-tuple-element.38), channel_id=1, source_target_pairs={{0,4},{1,5},{4,8},{5,9},{8,12},{9,13},{12,14},{13,15},{14,10},{15,... | collective-permute-start | bytes 786440 | tf_op jit(solution)/shard_map/ppermute | solution.py:115
  72.6 1.6 %collective-permute-start.15 = (bf16[128,2048]{1,0:T(8,128)(2,1)S(1)}, bf16[128,2048]{1,0:T(8,128)(2,1)S(1)}, u32[]{:S(2)}, u32[]{:S(2)}) collective-permute-start(bf16[128,2048]{1,0:T(8,128)(2,1)S(1)} %convert_element_type.77), channel_id=1, source_target_pairs={{0,16},{16,0},{1,17},{17,1},{2,18},{18,2},{3,19},{19,3},{4,20},{20... | collective-permute-start | bytes 1572872 | tf_op jit(solution)/shard_map/ppermute | solution.py:131
  74.2 5.8 %collective-permute-done.11.a_ref = bf16[64,4224]{1,0:T(8,128)(2,1)S(1)} collective-permute-done((bf16[64,4224]{1,0:T(8,128)(2,1)S(1)}, bf16[64,4224]{1,0:T(8,128)(2,1)S(1)}, u32[]{:S(2)}, u32[]{:S(2)}) %collective-permute-start.11) | collective-permute-done | bytes 540704 | tf_op jit(solution)/shard_map/ppermute | solution.py:115
  80.0 1.7 %collective-permute-start.12 = (bf16[64,4224]{1,0:T(8,128)(2,1)S(1)}, bf16[64,4224]{1,0:T(8,128)(2,1)S(1)}, u32[]{:S(2)}, u32[]{:S(2)}) collective-permute-start(bf16[64,4224]{1,0:T(8,128)(2,1)S(1)} %collective-permute-done.11.a_ref), channel_id=1, source_target_pairs={{0,4},{1,5},{4,8},{5,9},{8,12},{9,13},{12,14},{13,15},{14,10},{15,... | collective-permute-start | bytes 1622024 | tf_op jit(solution)/shard_map/ppermute | solution.py:115
  82.1 7.0 %expert_part.12 = f32[128,2048]{1,0:T(8,128)S(1)} custom-call(s32[2]{0:T(128)S(1)} %pad_add_fusion.me_ref, bf16[64,4224]{1,0:T(8,128)(2,1)S(1)} %collective-permute-done.11.a_ref, bf16[64,4224]{1,0:T(8,128)(2,1)S(1)} %collective-permute-done.13.b_ref, bf16[2048,768]{1,0:T(8,128)(2,1)S(1)} %bitcast.14, bf16[2048,768]{1,0:T(8,128)(2,1)S(1)} %collective-permute-done.2.u1_ref, ...), custom_call_target="tpu_custom_call" | custom-call | flops 2415919104 | bytes 14155776 | tf_op jit(solution)/shard_map/expert_part/pallas_call | solution.py:70
  89.2 1.7 %collective-permute-start.23 = (bf16[64,2048]{1,0:T(8,128)(2,1)S(1)}, bf16[64,2048]{1,0:T(8,128)(2,1)S(1)}, u32[]{:S(2)}, u32[]{:S(2)}) collective-permute-start(bf16[64,2048]{1,0:T(8,128)(2,1)S(1)} %get-tuple-element.36), channel_id=1, source_target_pairs={{0,4},{1,5},{4,8},{5,9},{8,12},{9,13},{12,14},{13,15},{14,10},{15,... | collective-permute-start | bytes 786440 | tf_op jit(solution)/shard_map/ppermute | solution.py:115
  91.3 5.9 %collective-permute-done.12.a_ref = bf16[64,4224]{1,0:T(8,128)(2,1)S(1)} collective-permute-done((bf16[64,4224]{1,0:T(8,128)(2,1)S(1)}, bf16[64,4224]{1,0:T(8,128)(2,1)S(1)}, u32[]{:S(2)}, u32[]{:S(2)}) %collective-permute-start.12) | collective-permute-done | bytes 540704 | tf_op jit(solution)/shard_map/ppermute | solution.py:115
  97.2 1.7 %collective-permute-done.14.b_ref = bf16[64,4224]{1,0:T(8,128)(2,1)S(1)} collective-permute-done((bf16[64,4224]{1,0:T(8,128)(2,1)S(1)}, bf16[64,4224]{1,0:T(8,128)(2,1)S(1)}, u32[]{:S(2)}, u32[]{:S(2)}) %collective-permute-start.14) | collective-permute-done | bytes 540704 | tf_op jit(solution)/shard_map/ppermute | solution.py:115
  101.0 7.0 %expert_part.11 = f32[128,2048]{1,0:T(8,128)S(1)} custom-call(s32[2]{0:T(128)S(1)} %pad_add_fusion.me_ref, bf16[64,4224]{1,0:T(8,128)(2,1)S(1)} %collective-permute-done.12.a_ref, bf16[64,4224]{1,0:T(8,128)(2,1)S(1)} %collective-permute-done.14.b_ref, bf16[2048,768]{1,0:T(8,128)(2,1)S(1)} %bitcast.15, bf16[2048,768]{1,0:T(8,128)(2,1)S(1)} %collective-permute-done.2.u1_ref, ...), custom_call_target="tpu_custom_call" | custom-call | flops 2415919104 | bytes 14155776 | tf_op jit(solution)/shard_map/expert_part/pallas_call | solution.py:70
  108.1 1.6 %collective-permute-start.24 = (bf16[64,2048]{1,0:T(8,128)(2,1)S(1)}, bf16[64,2048]{1,0:T(8,128)(2,1)S(1)}, u32[]{:S(2)}, u32[]{:S(2)}) collective-permute-start(bf16[64,2048]{1,0:T(8,128)(2,1)S(1)} %get-tuple-element.34), channel_id=1, source_target_pairs={{0,4},{1,5},{4,8},{5,9},{8,12},{9,13},{12,14},{13,15},{14,10},{15,... | collective-permute-start | bytes 786440 | tf_op jit(solution)/shard_map/ppermute | solution.py:115
  110.2 4.2 %collective-permute-done.16.a_ref = bf16[64,4224]{1,0:T(8,128)(2,1)S(1)} collective-permute-done((bf16[64,4224]{1,0:T(8,128)(2,1)S(1)}, bf16[64,4224]{1,0:T(8,128)(2,1)S(1)}, u32[]{:S(2)}, u32[]{:S(2)}) %collective-permute-start.16) | collective-permute-done | bytes 540704 | tf_op jit(solution)/shard_map/ppermute | solution.py:115
  114.4 1.7 %collective-permute-start.17 = (bf16[64,4224]{1,0:T(8,128)(2,1)S(1)}, bf16[64,4224]{1,0:T(8,128)(2,1)S(1)}, u32[]{:S(2)}, u32[]{:S(2)}) collective-permute-start(bf16[64,4224]{1,0:T(8,128)(2,1)S(1)} %collective-permute-done.16.a_ref), channel_id=1, source_target_pairs={{0,4},{1,5},{4,8},{5,9},{8,12},{9,13},{12,14},{13,15},{14,10},{15,... | collective-permute-start | bytes 1622024 | tf_op jit(solution)/shard_map/ppermute | solution.py:115
  116.5 7.0 %expert_part.10 = f32[128,2048]{1,0:T(8,128)S(1)} custom-call(s32[2]{0:T(128)S(1)} %pad_add_fusion.me_ref, bf16[64,4224]{1,0:T(8,128)(2,1)S(1)} %collective-permute-done.16.a_ref, bf16[64,4224]{1,0:T(8,128)(2,1)S(1)} %collective-permute-done.18.b_ref, bf16[2048,768]{1,0:T(8,128)(2,1)S(1)} %bitcast.16, bf16[2048,768]{1,0:T(8,128)(2,1)S(1)} %collective-permute-done.2.u1_ref, ...), custom_call_target="tpu_custom_call" | custom-call | flops 2415919104 | bytes 14155776 | tf_op jit(solution)/shard_map/expert_part/pallas_call | solution.py:70
  123.7 1.7 %collective-permute-start.25 = (bf16[64,2048]{1,0:T(8,128)(2,1)S(1)}, bf16[64,2048]{1,0:T(8,128)(2,1)S(1)}, u32[]{:S(2)}, u32[]{:S(2)}) collective-permute-start(bf16[64,2048]{1,0:T(8,128)(2,1)S(1)} %get-tuple-element.32), channel_id=1, source_target_pairs={{0,4},{1,5},{4,8},{5,9},{8,12},{9,13},{12,14},{13,15},{14,10},{15,... | collective-permute-start | bytes 786440 | tf_op jit(solution)/shard_map/ppermute | solution.py:115
  125.7 5.6 %collective-permute-done.17.a_ref = bf16[64,4224]{1,0:T(8,128)(2,1)S(1)} collective-permute-done((bf16[64,4224]{1,0:T(8,128)(2,1)S(1)}, bf16[64,4224]{1,0:T(8,128)(2,1)S(1)}, u32[]{:S(2)}, u32[]{:S(2)}) %collective-permute-start.17) | collective-permute-done | bytes 540704 | tf_op jit(solution)/shard_map/ppermute | solution.py:115
  132.8 7.0 %expert_part.9 = f32[128,2048]{1,0:T(8,128)S(1)} custom-call(s32[2]{0:T(128)S(1)} %pad_add_fusion.me_ref, bf16[64,4224]{1,0:T(8,128)(2,1)S(1)} %collective-permute-done.17.a_ref, bf16[64,4224]{1,0:T(8,128)(2,1)S(1)} %collective-permute-done.19.b_ref, bf16[2048,768]{1,0:T(8,128)(2,1)S(1)} %bitcast.17, bf16[2048,768]{1,0:T(8,128)(2,1)S(1)} %collective-permute-done.2.u1_ref, ...), custom_call_target="tpu_custom_call" | custom-call | flops 2415919104 | bytes 14155776 | tf_op jit(solution)/shard_map/expert_part/pallas_call | solution.py:70
  140.0 2.6 %collective-permute-start.26 = (bf16[64,2048]{1,0:T(8,128)(2,1)S(1)}, bf16[64,2048]{1,0:T(8,128)(2,1)S(1)}, u32[]{:S(2)}, u32[]{:S(2)}) collective-permute-start(bf16[64,2048]{1,0:T(8,128)(2,1)S(1)} %get-tuple-element.30), channel_id=1, source_target_pairs={{0,20},{1,21},{4,24},{5,25},{8,28},{9,29},{12,30},{13,31},{14,26},... | collective-permute-start | bytes 786440 | tf_op jit(solution)/shard_map/ppermute | solution.py:119
  143.0 4.6 %collective-permute-done.26.a_ref = bf16[64,2048]{1,0:T(8,128)(2,1)S(1)} collective-permute-done((bf16[64,2048]{1,0:T(8,128)(2,1)S(1)}, bf16[64,2048]{1,0:T(8,128)(2,1)S(1)}, u32[]{:S(2)}, u32[]{:S(2)}) %collective-permute-start.26) | collective-permute-done | bytes 262176 | tf_op jit(solution)/shard_map/ppermute | solution.py:119
  147.6 2.5 %collective-permute-done.33.b_ref = bf16[64,2048]{1,0:T(8,128)(2,1)S(1)} collective-permute-done((bf16[64,2048]{1,0:T(8,128)(2,1)S(1)}, bf16[64,2048]{1,0:T(8,128)(2,1)S(1)}, u32[]{:S(2)}, u32[]{:S(2)}) %collective-permute-start.33) | collective-permute-done | bytes 262176 | tf_op jit(solution)/shard_map/ppermute | solution.py:119
  (78 shorter events, 24.5 us)
Async XLA Ops:
  0.0 9.9 %collective-permute-start.2 = (bf16[2048,768]{1,0:T(8,128)(2,1)}, bf16[2048,768]{1,0:T(8,128)(2,1)S(1)}, u32[]{:S(2)}, u32[]{:S(2)}) collective-permute-start(bf16[2048,768]{1,0:T(8,128)(2,1)} %bitcast.9), channel_id=1, source_target_pairs={{0,1},{1,0},{2,3},{3,2},{4,5},{5,4},{6,7},{7,6},{8,9},{9,8},{10,11... | collective-permute-start | bytes 9437192 | tf_op jit(solution)/shard_map/ppermute | solution.py:134
  0.5 10.1 %collective-permute-start.3 = (bf16[768,2048]{1,0:T(8,128)(2,1)}, bf16[768,2048]{1,0:T(8,128)(2,1)}, u32[]{:S(2)}, u32[]{:S(2)}) collective-permute-start(bf16[768,2048]{1,0:T(8,128)(2,1)} %bitcast.18), channel_id=1, source_target_pairs={{0,1},{1,0},{2,3},{3,2},{4,5},{5,4},{6,7},{7,6},{8,9},{9,8},{10,11... | collective-permute-start | bytes 9437192 | tf_op jit(solution)/shard_map/ppermute | solution.py:134
  6.3 15.7 %collective-permute-start = (bf16[64,4224]{1,0:T(8,128)(2,1)}, bf16[64,4224]{1,0:T(8,128)(2,1)}, u32[]{:S(2)}, u32[]{:S(2)}) collective-permute-start(bf16[64,4224]{1,0:T(8,128)(2,1)} %get-tuple-element.17.a_ref), channel_id=1, source_target_pairs={{0,4},{1,5},{4,8},{5,9},{8,12},{9,13},{12,14},{13,15},{14,10},{15,... | collective-permute-start | bytes 1622024 | tf_op jit(solution)/shard_map/ppermute | solution.py:115
  9.3 14.2 %collective-permute-start.1 = (bf16[64,4224]{1,0:T(8,128)(2,1)}, bf16[64,4224]{1,0:T(8,128)(2,1)}, u32[]{:S(2)}, u32[]{:S(2)}) collective-permute-start(bf16[64,4224]{1,0:T(8,128)(2,1)} %get-tuple-element.18.b_ref), channel_id=1, source_target_pairs={{0,2},{1,3},{4,0},{5,1},{8,4},{9,5},{12,8},{13,9},{14,12},{15,13},... | collective-permute-start | bytes 1622024 | tf_op jit(solution)/shard_map/ppermute | solution.py:115
  23.5 21.6 %collective-permute-start.4 = (bf16[64,4224]{1,0:T(8,128)(2,1)}, bf16[64,4224]{1,0:T(8,128)(2,1)S(1)}, u32[]{:S(2)}, u32[]{:S(2)}) collective-permute-start(bf16[64,4224]{1,0:T(8,128)(2,1)} %collective-permute-done.a_ref), channel_id=1, source_target_pairs={{0,4},{1,5},{4,8},{5,9},{8,12},{9,13},{12,14},{13,15},{14,10},{15,... | collective-permute-start | bytes 1622024 | tf_op jit(solution)/shard_map/ppermute | solution.py:115
  25.1 21.6 %collective-permute-start.6 = (bf16[64,4224]{1,0:T(8,128)(2,1)}, bf16[64,4224]{1,0:T(8,128)(2,1)S(1)}, u32[]{:S(2)}, u32[]{:S(2)}) collective-permute-start(bf16[64,4224]{1,0:T(8,128)(2,1)} %collective-permute-done.1.b_ref), channel_id=1, source_target_pairs={{0,2},{1,3},{4,0},{5,1},{8,4},{9,5},{12,8},{13,9},{14,12},{15,13},... | collective-permute-start | bytes 1622024 | tf_op jit(solution)/shard_map/ppermute | solution.py:115
  33.1 10.2 %collective-permute-start.20 = (bf16[64,2048]{1,0:T(8,128)(2,1)S(1)}, bf16[64,2048]{1,0:T(8,128)(2,1)S(1)}, u32[]{:S(2)}, u32[]{:S(2)}) collective-permute-start(bf16[64,2048]{1,0:T(8,128)(2,1)S(1)} %get-tuple-element.42), channel_id=1, source_target_pairs={{0,4},{1,5},{4,8},{5,9},{8,12},{9,13},{12,14},{13,15},{14,10},{15,... | collective-permute-start | bytes 786440 | tf_op jit(solution)/shard_map/ppermute | solution.py:115
  34.7 19.5 %collective-permute-start.27 = (bf16[64,2048]{1,0:T(8,128)(2,1)S(1)}, bf16[64,2048]{1,0:T(8,128)(2,1)S(1)}, u32[]{:S(2)}, u32[]{:S(2)}) collective-permute-start(bf16[64,2048]{1,0:T(8,128)(2,1)S(1)} %get-tuple-element.41), channel_id=1, source_target_pairs={{0,2},{1,3},{4,0},{5,1},{8,4},{9,5},{12,8},{13,9},{14,12},{15,13},... | collective-permute-start | bytes 786440 | tf_op jit(solution)/shard_map/ppermute | solution.py:115
  35.2 25.7 %collective-permute-start.8 = (bf16[128,2048]{1,0:T(8,128)(2,1)S(1)}, bf16[128,2048]{1,0:T(8,128)(2,1)S(1)}, u32[]{:S(2)}, u32[]{:S(2)}) collective-permute-start(bf16[128,2048]{1,0:T(8,128)(2,1)S(1)} %bitcast.28), channel_id=1, source_target_pairs={{0,16},{16,0},{1,17},{17,1},{2,18},{18,2},{3,19},{19,3},{4,20},{20... | collective-permute-start | bytes 1572872 | tf_op jit(solution)/shard_map/ppermute | solution.py:131
  43.3 17.9 %collective-permute-start.9 = (bf16[128,2048]{1,0:T(8,128)(2,1)S(1)}, bf16[128,2048]{1,0:T(8,128)(2,1)S(1)}, u32[]{:S(2)}, u32[]{:S(2)}) collective-permute-start(bf16[128,2048]{1,0:T(8,128)(2,1)S(1)} %bitcast.30), channel_id=1, source_target_pairs={{0,16},{16,0},{1,17},{17,1},{2,18},{18,2},{3,19},{19,3},{4,20},{20... | collective-permute-start | bytes 1572872 | tf_op jit(solution)/shard_map/ppermute | solution.py:131
  45.1 16.1 %collective-permute-start.5 = (bf16[64,4224]{1,0:T(8,128)(2,1)S(1)}, bf16[64,4224]{1,0:T(8,128)(2,1)S(1)}, u32[]{:S(2)}, u32[]{:S(2)}) collective-permute-start(bf16[64,4224]{1,0:T(8,128)(2,1)S(1)} %collective-permute-done.4.a_ref), channel_id=1, source_target_pairs={{0,4},{1,5},{4,8},{5,9},{8,12},{9,13},{12,14},{13,15},{14,10},{15,... | collective-permute-start | bytes 1622024 | tf_op jit(solution)/shard_map/ppermute | solution.py:115
  46.7 14.6 %collective-permute-start.7 = (bf16[64,4224]{1,0:T(8,128)(2,1)S(1)}, bf16[64,4224]{1,0:T(8,128)(2,1)S(1)}, u32[]{:S(2)}, u32[]{:S(2)}) collective-permute-start(bf16[64,4224]{1,0:T(8,128)(2,1)S(1)} %collective-permute-done.6.b_ref), channel_id=1, source_target_pairs={{0,2},{1,3},{4,0},{5,1},{8,4},{9,5},{12,8},{13,9},{14,12},{15,13},... | collective-permute-start | bytes 1622024 | tf_op jit(solution)/shard_map/ppermute | solution.py:115
  59.2 11.2 %collective-permute-start.21 = (bf16[64,2048]{1,0:T(8,128)(2,1)S(1)}, bf16[64,2048]{1,0:T(8,128)(2,1)S(1)}, u32[]{:S(2)}, u32[]{:S(2)}) collective-permute-start(bf16[64,2048]{1,0:T(8,128)(2,1)S(1)} %get-tuple-element.40), channel_id=1, source_target_pairs={{0,4},{1,5},{4,8},{5,9},{8,12},{9,13},{12,14},{13,15},{14,10},{15,... | collective-permute-start | bytes 786440 | tf_op jit(solution)/shard_map/ppermute | solution.py:115
  60.9 9.5 %collective-permute-start.28 = (bf16[64,2048]{1,0:T(8,128)(2,1)S(1)}, bf16[64,2048]{1,0:T(8,128)(2,1)S(1)}, u32[]{:S(2)}, u32[]{:S(2)}) collective-permute-start(bf16[64,2048]{1,0:T(8,128)(2,1)S(1)} %get-tuple-element.39), channel_id=1, source_target_pairs={{0,2},{1,3},{4,0},{5,1},{8,4},{9,5},{12,8},{13,9},{14,12},{15,13},... | collective-permute-start | bytes 786440 | tf_op jit(solution)/shard_map/ppermute | solution.py:115
  61.3 18.8 %collective-permute-start.11 = (bf16[64,4224]{1,0:T(8,128)(2,1)S(1)}, bf16[64,4224]{1,0:T(8,128)(2,1)S(1)}, u32[]{:S(2)}, u32[]{:S(2)}) collective-permute-start(bf16[64,4224]{1,0:T(8,128)(2,1)S(1)} %collective-permute-done.5.a_ref), channel_id=1, source_target_pairs={{0,4},{1,5},{4,8},{5,9},{8,12},{9,13},{12,14},{13,15},{14,10},{15,... | collective-permute-start | bytes 1622024 | tf_op jit(solution)/shard_map/ppermute | solution.py:115
  63.0 18.7 %collective-permute-start.13 = (bf16[64,4224]{1,0:T(8,128)(2,1)S(1)}, bf16[64,4224]{1,0:T(8,128)(2,1)S(1)}, u32[]{:S(2)}, u32[]{:S(2)}) collective-permute-start(bf16[64,4224]{1,0:T(8,128)(2,1)S(1)} %collective-permute-done.7.b_ref), channel_id=1, source_target_pairs={{0,2},{1,3},{4,0},{5,1},{8,4},{9,5},{12,8},{13,9},{14,12},{15,13},... | collective-permute-start | bytes 1622024 | tf_op jit(solution)/shard_map/ppermute | solution.py:115
  70.5 18.6 %collective-permute-start.22 = (bf16[64,2048]{1,0:T(8,128)(2,1)S(1)}, bf16[64,2048]{1,0:T(8,128)(2,1)S(1)}, u32[]{:S(2)}, u32[]{:S(2)}) collective-permute-start(bf16[64,2048]{1,0:T(8,128)(2,1)S(1)} %get-tuple-element.38), channel_id=1, source_target_pairs={{0,4},{1,5},{4,8},{5,9},{8,12},{9,13},{12,14},{13,15},{14,10},{15,... | collective-permute-start | bytes 786440 | tf_op jit(solution)/shard_map/ppermute | solution.py:115
  72.3 16.9 %collective-permute-start.29 = (bf16[64,2048]{1,0:T(8,128)(2,1)S(1)}, bf16[64,2048]{1,0:T(8,128)(2,1)S(1)}, u32[]{:S(2)}, u32[]{:S(2)}) collective-permute-start(bf16[64,2048]{1,0:T(8,128)(2,1)S(1)} %get-tuple-element.37), channel_id=1, source_target_pairs={{0,2},{1,3},{4,0},{5,1},{8,4},{9,5},{12,8},{13,9},{14,12},{15,13},... | collective-permute-start | bytes 786440 | tf_op jit(solution)/shard_map/ppermute | solution.py:115
  72.6 18.7 %collective-permute-start.15 = (bf16[128,2048]{1,0:T(8,128)(2,1)S(1)}, bf16[128,2048]{1,0:T(8,128)(2,1)S(1)}, u32[]{:S(2)}, u32[]{:S(2)}) collective-permute-start(bf16[128,2048]{1,0:T(8,128)(2,1)S(1)} %convert_element_type.77), channel_id=1, source_target_pairs={{0,16},{16,0},{1,17},{17,1},{2,18},{18,2},{3,19},{19,3},{4,20},{20... | collective-permute-start | bytes 1572872 | tf_op jit(solution)/shard_map/ppermute | solution.py:131
  80.0 17.2 %collective-permute-start.12 = (bf16[64,4224]{1,0:T(8,128)(2,1)S(1)}, bf16[64,4224]{1,0:T(8,128)(2,1)S(1)}, u32[]{:S(2)}, u32[]{:S(2)}) collective-permute-start(bf16[64,4224]{1,0:T(8,128)(2,1)S(1)} %collective-permute-done.11.a_ref), channel_id=1, source_target_pairs={{0,4},{1,5},{4,8},{5,9},{8,12},{9,13},{12,14},{13,15},{14,10},{15,... | collective-permute-start | bytes 1622024 | tf_op jit(solution)/shard_map/ppermute | solution.py:115
  81.7 17.2 %collective-permute-start.14 = (bf16[64,4224]{1,0:T(8,128)(2,1)S(1)}, bf16[64,4224]{1,0:T(8,128)(2,1)S(1)}, u32[]{:S(2)}, u32[]{:S(2)}) collective-permute-start(bf16[64,4224]{1,0:T(8,128)(2,1)S(1)} %collective-permute-done.13.b_ref), channel_id=1, source_target_pairs={{0,2},{1,3},{4,0},{5,1},{8,4},{9,5},{12,8},{13,9},{14,12},{15,13},... | collective-permute-start | bytes 1622024 | tf_op jit(solution)/shard_map/ppermute | solution.py:115
  89.2 18.8 %collective-permute-start.23 = (bf16[64,2048]{1,0:T(8,128)(2,1)S(1)}, bf16[64,2048]{1,0:T(8,128)(2,1)S(1)}, u32[]{:S(2)}, u32[]{:S(2)}) collective-permute-start(bf16[64,2048]{1,0:T(8,128)(2,1)S(1)} %get-tuple-element.36), channel_id=1, source_target_pairs={{0,4},{1,5},{4,8},{5,9},{8,12},{9,13},{12,14},{13,15},{14,10},{15,... | collective-permute-start | bytes 786440 | tf_op jit(solution)/shard_map/ppermute | solution.py:115
  91.0 17.0 %collective-permute-start.30 = (bf16[64,2048]{1,0:T(8,128)(2,1)S(1)}, bf16[64,2048]{1,0:T(8,128)(2,1)S(1)}, u32[]{:S(2)}, u32[]{:S(2)}) collective-permute-start(bf16[64,2048]{1,0:T(8,128)(2,1)S(1)} %get-tuple-element.35), channel_id=1, source_target_pairs={{0,2},{1,3},{4,0},{5,1},{8,4},{9,5},{12,8},{13,9},{14,12},{15,13},... | collective-permute-start | bytes 786440 | tf_op jit(solution)/shard_map/ppermute | solution.py:115
  98.9 15.5 %collective-permute-start.16 = (bf16[64,4224]{1,0:T(8,128)(2,1)S(1)}, bf16[64,4224]{1,0:T(8,128)(2,1)S(1)}, u32[]{:S(2)}, u32[]{:S(2)}) collective-permute-start(bf16[64,4224]{1,0:T(8,128)(2,1)S(1)} %collective-permute-done.12.a_ref), channel_id=1, source_target_pairs={{0,4},{1,5},{4,8},{5,9},{8,12},{9,13},{12,14},{13,15},{14,10},{15,... | collective-permute-start | bytes 1622024 | tf_op jit(solution)/shard_map/ppermute | solution.py:115
  100.5 15.6 %collective-permute-start.18 = (bf16[64,4224]{1,0:T(8,128)(2,1)S(1)}, bf16[64,4224]{1,0:T(8,128)(2,1)S(1)}, u32[]{:S(2)}, u32[]{:S(2)}) collective-permute-start(bf16[64,4224]{1,0:T(8,128)(2,1)S(1)} %collective-permute-done.14.b_ref), channel_id=1, source_target_pairs={{0,2},{1,3},{4,0},{5,1},{8,4},{9,5},{12,8},{13,9},{14,12},{15,13},... | collective-permute-start | bytes 1622024 | tf_op jit(solution)/shard_map/ppermute | solution.py:115
  108.1 15.4 %collective-permute-start.24 = (bf16[64,2048]{1,0:T(8,128)(2,1)S(1)}, bf16[64,2048]{1,0:T(8,128)(2,1)S(1)}, u32[]{:S(2)}, u32[]{:S(2)}) collective-permute-start(bf16[64,2048]{1,0:T(8,128)(2,1)S(1)} %get-tuple-element.34), channel_id=1, source_target_pairs={{0,4},{1,5},{4,8},{5,9},{8,12},{9,13},{12,14},{13,15},{14,10},{15,... | collective-permute-start | bytes 786440 | tf_op jit(solution)/shard_map/ppermute | solution.py:115
  109.8 13.8 %collective-permute-start.31 = (bf16[64,2048]{1,0:T(8,128)(2,1)S(1)}, bf16[64,2048]{1,0:T(8,128)(2,1)S(1)}, u32[]{:S(2)}, u32[]{:S(2)}) collective-permute-start(bf16[64,2048]{1,0:T(8,128)(2,1)S(1)} %get-tuple-element.33), channel_id=1, source_target_pairs={{0,2},{1,3},{4,0},{5,1},{8,4},{9,5},{12,8},{13,9},{14,12},{15,13},... | collective-permute-start | bytes 786440 | tf_op jit(solution)/shard_map/ppermute | solution.py:115
  114.4 16.9 %collective-permute-start.17 = (bf16[64,4224]{1,0:T(8,128)(2,1)S(1)}, bf16[64,4224]{1,0:T(8,128)(2,1)S(1)}, u32[]{:S(2)}, u32[]{:S(2)}) collective-permute-start(bf16[64,4224]{1,0:T(8,128)(2,1)S(1)} %collective-permute-done.16.a_ref), channel_id=1, source_target_pairs={{0,4},{1,5},{4,8},{5,9},{8,12},{9,13},{12,14},{13,15},{14,10},{15,... | collective-permute-start | bytes 1622024 | tf_op jit(solution)/shard_map/ppermute | solution.py:115
  116.1 16.7 %collective-permute-start.19 = (bf16[64,4224]{1,0:T(8,128)(2,1)S(1)}, bf16[64,4224]{1,0:T(8,128)(2,1)S(1)}, u32[]{:S(2)}, u32[]{:S(2)}) collective-permute-start(bf16[64,4224]{1,0:T(8,128)(2,1)S(1)} %collective-permute-done.18.b_ref), channel_id=1, source_target_pairs={{0,2},{1,3},{4,0},{5,1},{8,4},{9,5},{12,8},{13,9},{14,12},{15,13},... | collective-permute-start | bytes 1622024 | tf_op jit(solution)/shard_map/ppermute | solution.py:115
  123.7 16.2 %collective-permute-start.25 = (bf16[64,2048]{1,0:T(8,128)(2,1)S(1)}, bf16[64,2048]{1,0:T(8,128)(2,1)S(1)}, u32[]{:S(2)}, u32[]{:S(2)}) collective-permute-start(bf16[64,2048]{1,0:T(8,128)(2,1)S(1)} %get-tuple-element.32), channel_id=1, source_target_pairs={{0,4},{1,5},{4,8},{5,9},{8,12},{9,13},{12,14},{13,15},{14,10},{15,... | collective-permute-start | bytes 786440 | tf_op jit(solution)/shard_map/ppermute | solution.py:115
  125.4 14.5 %collective-permute-start.32 = (bf16[64,2048]{1,0:T(8,128)(2,1)S(1)}, bf16[64,2048]{1,0:T(8,128)(2,1)S(1)}, u32[]{:S(2)}, u32[]{:S(2)}) collective-permute-start(bf16[64,2048]{1,0:T(8,128)(2,1)S(1)} %get-tuple-element.31), channel_id=1, source_target_pairs={{0,2},{1,3},{4,0},{5,1},{8,4},{9,5},{12,8},{13,9},{14,12},{15,13},... | collective-permute-start | bytes 786440 | tf_op jit(solution)/shard_map/ppermute | solution.py:115
  140.0 7.6 %collective-permute-start.26 = (bf16[64,2048]{1,0:T(8,128)(2,1)S(1)}, bf16[64,2048]{1,0:T(8,128)(2,1)S(1)}, u32[]{:S(2)}, u32[]{:S(2)}) collective-permute-start(bf16[64,2048]{1,0:T(8,128)(2,1)S(1)} %get-tuple-element.30), channel_id=1, source_target_pairs={{0,20},{1,21},{4,24},{5,25},{8,28},{9,29},{12,30},{13,31},{14,26},... | collective-permute-start | bytes 786440 | tf_op jit(solution)/shard_map/ppermute | solution.py:119
  (12 other events, 95.6 us)

commit v3 on v2

--- a/solution.py
+++ b/solution.py
@@ -1,3 +1,5 @@
+import functools
+
 import jax
 import jax.numpy as jnp
 from jax import lax
@@ -7,50 +9,58 @@
 
 epsilon = 1e-06
 LANES = 128
+VMEM = 24 << 20
 NT = (((1,), (1,)), ((), ()))
 
 
-def pack_kernel(x_ref, g_ref, gain_ref, routes_ref, gates_ref, up_ref, down_ref):
-    half, width = up_ref.shape[0], x_ref.shape[1]
+def pack_kernel(x_ref, gain_ref, routes_ref, gates_ref, up_ref, down_ref):
+    half = up_ref.shape[0]
+    rows, width = x_ref.shape
     values = x_ref[...].astype(jnp.float32)
     scaling = lax.rsqrt(jnp.mean(values * values, axis=-1, keepdims=True) + epsilon)
     normed = (values * scaling * gain_ref[...]).astype(jnp.bfloat16)
-    lanes = up_ref.shape[1] - 2 * width
-    lane = lax.broadcasted_iota(jnp.int32, (x_ref.shape[0], lanes), 1)
-    dense = jnp.zeros((x_ref.shape[0], lanes), jnp.float32)
+    expert = lax.broadcasted_iota(jnp.int32, (up_ref.shape[1] - width, rows), 0)
+    dense = jnp.zeros(expert.shape, jnp.float32)
     routes, gates = routes_ref[...], gates_ref[...].astype(jnp.float32)
-    for k in range(routes.shape[1]):
-        dense = dense + jnp.where(lane == routes[:, k : k + 1], gates[:, k : k + 1], 0.0)
-    dense = dense.astype(jnp.bfloat16)
+    for k in range(routes.shape[0]):
+        dense = dense + jnp.where(expert == routes[k : k + 1, :], gates[k : k + 1, :], 0.0)
+    dense = dense.T.astype(jnp.bfloat16)
     for ref, first in ((up_ref, 0), (down_ref, half)):
         ref[:, :width] = normed[first : first + half]
-        ref[:, width : 2 * width] = g_ref[first : first + half, :]
-        ref[:, 2 * width :] = dense[first : first + half]
-
-
-def pack(x, grad, gain, routes, gates, experts):
+        ref[:, width:] = dense[first : first + half]
+
+
+def pack(x, gain, routes, gates, experts):
     rows, width = x.shape
     lanes = -(-experts // LANES) * LANES
-    shape = jax.ShapeDtypeStruct((rows // 2, 2 * width + lanes), jnp.bfloat16)
+    shape = jax.ShapeDtypeStruct((rows // 2, width + lanes), jnp.bfloat16)
     return pl.pallas_call(
         pack_kernel,
         out_shape=(shape, shape),
-        compiler_params=pltpu.CompilerParams(vmem_limit_bytes=40 << 20),
+        compiler_params=pltpu.CompilerParams(vmem_limit_bytes=VMEM),
         name="pack",
-    )(x, grad, gain, routes, gates)
-
-
-def expert_kernel(me_ref, a_ref, b_ref, u0_ref, u1_ref, d0_ref, d1_ref, o_ref):
+    )(x, gain, routes.T, gates.T)
+
+
+def expert_kernel(pieces, me_ref, *refs):
+    rows, (u0_ref, u1_ref, d0_hbm, d1_hbm, o_ref, d0_ref, d1_ref, sems) = refs[: 2 * pieces], refs[2 * pieces :]
+    copies = [
+        pltpu.make_async_copy(hbm, vmem, sems.at[i])
+        for i, (hbm, vmem) in enumerate(((d0_hbm, d0_ref), (d1_hbm, d1_ref)))
+    ]
+    for copy in copies:
+        copy.start()
     width = u0_ref.shape[0]
-
-    def rows(first, last):
-        return jnp.concatenate([a_ref[:, first:last], b_ref[:, first:last]], axis=0)
-
-    normed, grad = rows(0, width), rows(width, 2 * width)
-    dense = rows(2 * width, a_ref.shape[1]).astype(jnp.float32)
+    split = rows[0].shape[1] - (width if pieces == 1 else 0)
+    heads = rows[:2]
+    normed = jnp.concatenate([ref[:, :width] for ref in heads], axis=0)
+    dense = jnp.concatenate([ref[:, width:split] for ref in heads], axis=0).astype(jnp.float32)
+    tails = [ref[:, split:] for ref in heads] if pieces == 1 else [ref[...] for ref in rows[2:]]
+    grad = jnp.concatenate(tails, axis=0)
     lane = lax.broadcasted_iota(jnp.int32, dense.shape, 1)
     for i, (u_ref, d_ref) in enumerate(((u0_ref, d0_ref), (u1_ref, d1_ref))):
         before = jnp.dot(normed, u_ref[...], preferred_element_type=jnp.float32)
+        copies[i].wait()
         d_hidden = lax.dot_general(grad, d_ref[...], NT, preferred_element_type=jnp.float32)
         sigmoid_of = jax.nn.sigmoid(before)
         d_before = (d_hidden * sigmoid_of * (1.0 + before * (1.0 - sigmoid_of))).astype(jnp.bfloat16)
@@ -63,23 +73,28 @@
             o_ref[...] += part
 
 
-def expert_part(me, a, b, u0, u1, d0, d1):
-    half = a.shape[0]
-    width, hidden = u0.shape
-    whole = pl.BlockSpec(memory_space=pltpu.VMEM)
+def expert_part(me, rows, weights):
+    half = rows[0].shape[0]
+    width, hidden = weights[0].shape
+    whole, stay = pl.BlockSpec(memory_space=pltpu.VMEM), pl.BlockSpec(memory_space=pl.ANY)
     return pl.pallas_call(
-        expert_kernel,
+        functools.partial(expert_kernel, len(rows) // 2),
         out_shape=jax.ShapeDtypeStruct((2 * half, width), jnp.float32),
-        in_specs=[pl.BlockSpec(memory_space=pltpu.SMEM)] + [whole] * 6,
+        in_specs=[pl.BlockSpec(memory_space=pltpu.SMEM)] + [whole] * (len(rows) + 2) + [stay] * 2,
         out_specs=whole,
-        compiler_params=pltpu.CompilerParams(vmem_limit_bytes=30 << 20),
+        scratch_shapes=[
+            pltpu.VMEM((hidden, width), jnp.bfloat16),
+            pltpu.VMEM((hidden, width), jnp.bfloat16),
+            pltpu.SemaphoreType.DMA((2,)),
+        ],
+        compiler_params=pltpu.CompilerParams(vmem_limit_bytes=VMEM),
         cost_estimate=pl.CostEstimate(
             flops=24 * half * width * hidden,
             transcendentals=4 * half * hidden,
             bytes_accessed=8 * width * hidden + 12 * half * width,
         ),
         name="expert_part",
-    )(me, a, b, u0, u1, d0, d1)
+    )(me, *rows, *weights)
 
 
 def finish_kernel(x_ref, g_ref, gain_ref, own_ref, a_ref, b_ref, o_ref):
@@ -99,7 +114,7 @@
     return pl.pallas_call(
         finish_kernel,
         out_shape=jax.ShapeDtypeStruct(x.shape, jnp.bfloat16),
-        compiler_params=pltpu.CompilerParams(vmem_limit_bytes=40 << 20),
+        compiler_params=pltpu.CompilerParams(vmem_limit_bytes=VMEM),
         name="finish",
     )(x, grad, gain, own, a, b)
 
@@ -138,32 +153,34 @@
     e = lax.axis_index("expert").astype(jnp.int32)
     me = jnp.stack([e, e ^ 1])
 
-    u1, d1 = swap(u0), swap(d0)
-    a, b = pack(x, grad, norm_gain, bwd_routes[0], bwd_gates[0], experts)
-    half = a.shape[0]
-    a1, b1 = hop(a, 1), hop(b, -1)
+    half = grad.shape[0] // 2
+    ga, gb = grad[:half], grad[half:]
+    ga1, gb1 = hop(ga, 1), hop(gb, -1)
+    weights = (u0, swap(u0), d0, swap(d0))
+    na, nb = pack(x, norm_gain, bwd_routes[0], bwd_gates[0], experts)
+    na1, nb1 = hop(na, 1), hop(nb, -1)
+    a1, b1 = jnp.concatenate([na1, ga1], axis=1), jnp.concatenate([nb1, gb1], axis=1)
     x_out, grad_out, gain_out = to_previous(x), to_previous(grad), to_previous(norm_gain)
-    own = expert_part(me, a, b, u0, u1, d0, d1).astype(jnp.bfloat16)
+    own = expert_part(me, (na, nb, ga, gb), weights).astype(jnp.bfloat16)
     own_out = to_previous(own)
+    early = {2: gain_out, 3: x_out, 4: grad_out, 5: own, 7: own_out}
     sum_a = sum_b = None
     for step in range(1, chips):
         a, b = a1, b1
-        if step == 1:
-            a, b, own = lax.optimization_barrier((a, b, own))
-        if step == 3:
-            a, b, x_out, grad_out, gain_out = lax.optimization_barrier((a, b, x_out, grad_out, gain_out))
-        if step == 5:
-            a, b, own_out = lax.optimization_barrier((a, b, own_out))
+        if step in early:
+            a, b, early[step] = lax.optimization_barrier((a, b, early[step]))
         if step < chips - 1:
             a1, b1 = hop(a, 1), hop(b, -1)
-        part = expert_part(me, a, b, u0, u1, d0, d1)
+        part = expert_part(me, (a, b), weights)
         part_a, part_b = part[:half], part[half:]
         if step > 1:
             part_a = part_a + sum_a.astype(jnp.float32)
             part_b = part_b + sum_b.astype(jnp.float32)
+        send_a, send_b = part_a.astype(jnp.bfloat16), part_b.astype(jnp.bfloat16)
+        if step == chips - 2:
+            a1, b1, send_a, send_b = lax.optimization_barrier((a1, b1, send_a, send_b))
         move = hop if step < chips - 1 else last_hop
-        sum_a = move(part_a.astype(jnp.bfloat16), 1)
-        sum_b = move(part_b.astype(jnp.bfloat16), -1)
+        sum_a, sum_b = move(send_a, 1), move(send_b, -1)
     return finish(x_out, grad_out, gain_out, own_out, sum_a, sum_b)[None]
 
 

time: 152 us -> 148 us (0.974)
  waiting for transfers between devices: 45.9 us -> 29.4 us
  Pallas kernels: 60.1 us -> 66.3 us
  starting transfers between devices: 36.4 us -> 40.4 us
  local copies, waits for them, and re-layouts: 8.2 us -> 10 us
    ppermute x26 -> x28, waiting for transfers between devices: 32.9 us -> 20 us  [hop(): lax.ppermute(value, 'expert', [(2 * a + c, 2 * b + c) for a, b in moves f...]
    pallas_call x8, Pallas kernels: 57.2 us -> 63.7 us  [expert_part(): pl.pallas_call(functools.partial(expert_kernel, len(rows) // 2), out_shap...]
    ppermute x26 -> x28, starting transfers between devices: 27.7 us -> 31.8 us  [hop(): lax.ppermute(value, 'expert', [(2 * a + c, 2 * b + c) for a, b in moves f...]
    ppermute x4, waiting for transfers between devices: 4.58 us -> 2.16 us  [to_previous(): lax.ppermute(value, 'pipe', [(s, (s - 1) % sections) for s in range(secti...]
    slice x0 -> x1, local copies, waits for them, and re-layouts: none -> 1.77 us  [shards(): ga, gb = (grad[:half], grad[half:])]
    unnamed x22 -> x24, local copies, waits for them, and re-layouts: 8.17 us -> 7.22 us
  transfers between devices with their start and end apart: 34 -> 36, of which waited for: 13 -> 10; matrix products, arithmetic and copies ran while one was open for 2% -> 4% of each run, Pallas kernels for 39% -> 44%
where the time goes in v3:
time: 148 us; the launch traced here: 147 us
  Pallas kernels  66.3 us (45%)
  starting transfers between devices  40.4 us (27%)
  waiting for transfers between devices  29.4 us (20%)
  local copies, waits for them, and re-layouts  10 us (7%)
    pallas_call x8, Pallas kernels, expert_part(): pl.pallas_call(functools.partial(expert_kernel, len(rows) // 2), out_shap...  63.7 us
    ppermute x28, starting transfers between devices, hop(): lax.ppermute(value, 'expert', [(2 * a + c, 2 * b + c) for a, b in moves f...  31.8 us
    ppermute x28, waiting for transfers between devices, hop(): lax.ppermute(value, 'expert', [(2 * a + c, 2 * b + c) for a, b in moves f...  20 us
    unnamed x24, local copies, waits for them, and re-layouts  7.22 us
    ppermute x2, waiting for transfers between devices, last_hop(): lax.ppermute(value, ('pipe', 'expert'), [(s * experts + 2 * a + c, (s - 1...  7.15 us
    ppermute x4, starting transfers between devices, to_previous(): lax.ppermute(value, 'pipe', [(s, (s - 1) % sections) for s in range(secti...  5.04 us
    ppermute x2, starting transfers between devices, last_hop(): lax.ppermute(value, ('pipe', 'expert'), [(s * experts + 2 * a + c, (s - 1...  2.98 us
  transfers between devices with their start and end apart: 36, of which 10 were waited for; matrix products, arithmetic and copies ran while one was open for 4% of the time, Pallas kernels for 44%

profile of v3, /device:TPU:0, one launch (start us, length us, event | category | flops | bytes accessed | tf_op | source)
XLA Modules:
  0.0 147.3 jit_solution(11112566555635069993)
XLA Ops:
  5.0 2.9 %collective-permute-start.9 = (bf16[64,2176]{1,0:T(8,128)(2,1)}, bf16[64,2176]{1,0:T(8,128)(2,1)}, u32[]{:S(2)}, u32[]{:S(2)}) collective-permute-start(bf16[64,2176]{1,0:T(8,128)(2,1)} %get-tuple-element.22.refs_1_), channel_id=1, source_target_pairs={{0,2},{1,3},{4,0},{5,1},{8,4},{9,5},{12,8},{13,9},{14,12},{15,13},... | collective-permute-start | bytes 835592 | tf_op jit(solution)/shard_map/ppermute | solution.py:130
  7.9 1.8 %slice_bitcast_fusion = (bf16[64,2048]{1,0:T(8,128)(2,1)S(1)}, bf16[64,2048]{1,0:T(8,128)(2,1)}) fusion(bf16[1,128,2048]{2,1,0:T(8,128)(2,1)} %param.8), kind=kLoop, calls=%fused_computation.24 | loop fusion | bytes 1048576 | tf_op jit(solution)/shard_map/slice | solution.py:157
  9.7 1.6 %collective-permute-start.10 = (bf16[64,2048]{1,0:T(8,128)(2,1)S(1)}, bf16[64,2048]{1,0:T(8,128)(2,1)}, u32[]{:S(2)}, u32[]{:S(2)}) collective-permute-start(bf16[64,2048]{1,0:T(8,128)(2,1)S(1)} %get-tuple-element.51.refs_3_), channel_id=1, source_target_pairs={{0,2},{1,3},{4,0},{5,1},{8,4},{9,5},{12,8},{13,9},{14,12},{15,13},... | collective-permute-start | bytes 786440 | tf_op jit(solution)/shard_map/ppermute | solution.py:130
  11.8 4.0 %collective-permute-done.9 = bf16[64,2176]{1,0:T(8,128)(2,1)} collective-permute-done((bf16[64,2176]{1,0:T(8,128)(2,1)}, bf16[64,2176]{1,0:T(8,128)(2,1)}, u32[]{:S(2)}, u32[]{:S(2)}) %collective-permute-start.9) | collective-permute-done | bytes 278560 | tf_op jit(solution)/shard_map/ppermute | solution.py:130
  15.7 2.1 %collective-permute-start.7 = (bf16[64,2048]{1,0:T(8,128)(2,1)}, bf16[64,2048]{1,0:T(8,128)(2,1)S(1)}, u32[]{:S(2)}, u32[]{:S(2)}) collective-permute-start(bf16[64,2048]{1,0:T(8,128)(2,1)} %get-tuple-element.52.refs_2_), channel_id=1, source_target_pairs={{0,4},{1,5},{4,8},{5,9},{8,12},{9,13},{12,14},{13,15},{14,10},{15,... | collective-permute-start | bytes 786440 | tf_op jit(solution)/shard_map/ppermute | solution.py:130
  18.8 2.0 %collective-permute-done.10 = bf16[64,2048]{1,0:T(8,128)(2,1)} collective-permute-done((bf16[64,2048]{1,0:T(8,128)(2,1)S(1)}, bf16[64,2048]{1,0:T(8,128)(2,1)}, u32[]{:S(2)}, u32[]{:S(2)}) %collective-permute-start.10) | collective-permute-done | bytes 262176 | tf_op jit(solution)/shard_map/ppermute | solution.py:130
  21.7 1.7 %collective-permute-start.11 = (bf16[64,4224]{1,0:T(8,128)(2,1)S(1)}, bf16[64,4224]{1,0:T(8,128)(2,1)S(1)}, u32[]{:S(2)}, u32[]{:S(2)}) collective-permute-start(bf16[64,4224]{1,0:T(8,128)(2,1)S(1)} %constant_dynamic-update-slice_fusion.2.refs_1_), channel_id=1, source_target_pairs={{0,2},{1,3},{4,0},{5,1},{8,4},{9,5},{12,8},{13,9},{14,12},{15,13},... | collective-permute-start | bytes 1622024 | tf_op jit(solution)/shard_map/ppermute | solution.py:130
  25.6 1.9 %copy-done.1 = bf16[1,1,768,2048]{3,2,1,0:T(8,128)(2,1)S(1)} copy-done((bf16[1,1,768,2048]{3,2,1,0:T(8,128)(2,1)S(1)}, bf16[1,1,768,2048]{3,2,1,0:T(8,128)(2,1)}, u32[]{:S(2)}) %copy-start.1) | copy-done | bytes 3145752
  27.5 7.9 %expert_part.14 = f32[128,2048]{1,0:T(8,128)S(1)} custom-call(s32[2]{0:T(128)S(1)} %pad_add_fusion.me_ref, bf16[64,4224]{1,0:T(8,128)(2,1)S(1)} %constant_dynamic-update-slice_fusion.refs_0_, bf16[64,4224]{1,0:T(8,128)(2,1)S(1)} %constant_dynamic-update-slice_fusion.2.refs_1_, bf16[2048,768]{1,0:T(8,128)(2,1)S(1)} %bitcast.18, ...), custom_call_target="tpu_custom_call" | custom-call | flops 2415919104 | bytes 14155776 | tf_op jit(solution)/shard_map/expert_part/pallas_call | solution.py:80
  37.6 1.5 %collective-permute-start.2 = (f32[1,2048]{1,0:T(1,128)S(1)}, f32[1,2048]{1,0:T(1,128)S(1)}, u32[]{:S(2)}, u32[]{:S(2)}) collective-permute-start(f32[1,2048]{1,0:T(1,128)S(1)} %copy-done.7), channel_id=1, source_target_pairs={{0,16},{16,0},{1,17},{17,1},{2,18},{18,2},{3,19},{19,3},{4,20},{20... | collective-permute-start | bytes 24584 | tf_op jit(solution)/shard_map/ppermute | solution.py:146
  39.2 2.1 %collective-permute-done.2.gain_ref = f32[1,2048]{1,0:T(1,128)S(1)} collective-permute-done((f32[1,2048]{1,0:T(1,128)S(1)}, f32[1,2048]{1,0:T(1,128)S(1)}, u32[]{:S(2)}, u32[]{:S(2)}) %collective-permute-start.2) | collective-permute-done | bytes 8224 | tf_op jit(solution)/shard_map/ppermute | solution.py:146
  41.3 1.5 %collective-permute-start = (bf16[128,2048]{1,0:T(8,128)(2,1)S(1)}, bf16[128,2048]{1,0:T(8,128)(2,1)S(1)}, u32[]{:S(2)}, u32[]{:S(2)}) collective-permute-start(bf16[128,2048]{1,0:T(8,128)(2,1)S(1)} %bitcast.36), channel_id=1, source_target_pairs={{0,16},{16,0},{1,17},{17,1},{2,18},{18,2},{3,19},{19,3},{4,20},{20... | collective-permute-start | bytes 1572872 | tf_op jit(solution)/shard_map/ppermute | solution.py:146
  44.9 7.9 %expert_part.13 = f32[128,2048]{1,0:T(8,128)S(1)} custom-call(s32[2]{0:T(128)S(1)} %pad_add_fusion.me_ref, bf16[64,4224]{1,0:T(8,128)(2,1)S(1)} %collective-permute-done.8.refs_0_, bf16[64,4224]{1,0:T(8,128)(2,1)S(1)} %collective-permute-done.11.refs_1_, bf16[2048,768]{1,0:T(8,128)(2,1)S(1)} %bitcast.19, ...), custom_call_target="tpu_custom_call" | custom-call | flops 2415919104 | bytes 14155776 | tf_op jit(solution)/shard_map/expert_part/pallas_call | solution.py:80
  55.5 2.5 %collective-permute-done.12.refs_0_ = bf16[64,4224]{1,0:T(8,128)(2,1)S(1)} collective-permute-done((bf16[64,4224]{1,0:T(8,128)(2,1)S(1)}, bf16[64,4224]{1,0:T(8,128)(2,1)S(1)}, u32[]{:S(2)}, u32[]{:S(2)}) %collective-permute-start.12) | collective-permute-done | bytes 540704 | tf_op jit(solution)/shard_map/ppermute | solution.py:130
  58.6 1.5 collective-permute-start.15
  60.1 7.9 %expert_part.12 = f32[128,2048]{1,0:T(8,128)S(1)} custom-call(s32[2]{0:T(128)S(1)} %pad_add_fusion.me_ref, bf16[64,4224]{1,0:T(8,128)(2,1)S(1)} %collective-permute-done.12.refs_0_, bf16[64,4224]{1,0:T(8,128)(2,1)S(1)} %collective-permute-done.13.refs_1_, bf16[2048,768]{1,0:T(8,128)(2,1)S(1)} %bitcast.20, ...), custom_call_target="tpu_custom_call" | custom-call | flops 2415919104 | bytes 14155776 | tf_op jit(solution)/shard_map/expert_part/pallas_call | solution.py:80
  68.8 1.5 collective-permute-start.29
  70.3 5.0 %collective-permute-done.14.refs_0_ = bf16[64,4224]{1,0:T(8,128)(2,1)S(1)} collective-permute-done((bf16[64,4224]{1,0:T(8,128)(2,1)S(1)}, bf16[64,4224]{1,0:T(8,128)(2,1)S(1)}, u32[]{:S(2)}, u32[]{:S(2)}) %collective-permute-start.14) | collective-permute-done | bytes 540704 | tf_op jit(solution)/shard_map/ppermute | solution.py:130
  77.3 8.1 %expert_part.11 = f32[128,2048]{1,0:T(8,128)S(1)} custom-call(s32[2]{0:T(128)S(1)} %pad_add_fusion.me_ref, bf16[64,4224]{1,0:T(8,128)(2,1)S(1)} %collective-permute-done.14.refs_0_, bf16[64,4224]{1,0:T(8,128)(2,1)S(1)} %collective-permute-done.15.refs_1_, bf16[2048,768]{1,0:T(8,128)(2,1)S(1)} %bitcast.21, ...), custom_call_target="tpu_custom_call" | custom-call | flops 2415919104 | bytes 14155776 | tf_op jit(solution)/shard_map/expert_part/pallas_call | solution.py:80
  87.6 8.1 %expert_part.8 = f32[128,2048]{1,0:T(8,128)S(1)} custom-call(s32[2]{0:T(128)S(1)} %pad_add_fusion.me_ref, bf16[64,2176]{1,0:T(8,128)(2,1)} %get-tuple-element.21.refs_0_, bf16[64,2176]{1,0:T(8,128)(2,1)} %get-tuple-element.22.refs_1_, bf16[64,2048]{1,0:T(8,128)(2,1)S(1)} %copy-done.3, bf16[64,2048]{1,0:T(8,128)(2,1)S(1)} %get-tuple-element.51.refs_3_, ...), custom_call_target="tpu_custom_call" | custom-call | flops 2415919104 | bytes 14155776 | tf_op jit(solution)/shard_map/expert_part/pallas_call | solution.py:80
  97.9 7.9 %expert_part.10 = f32[128,2048]{1,0:T(8,128)S(1)} custom-call(s32[2]{0:T(128)S(1)} %pad_add_fusion.me_ref, bf16[64,4224]{1,0:T(8,128)(2,1)S(1)} %collective-permute-done.16.refs_0_, bf16[64,4224]{1,0:T(8,128)(2,1)S(1)} %collective-permute-done.17.refs_1_, bf16[2048,768]{1,0:T(8,128)(2,1)S(1)} %bitcast.23, ...), custom_call_target="tpu_custom_call" | custom-call | flops 2415919104 | bytes 14155776 | tf_op jit(solution)/shard_map/expert_part/pallas_call | solution.py:80
  108.0 1.5 %collective-permute-start.5 = (bf16[128,2048]{1,0:T(8,128)(2,1)S(1)}, bf16[128,2048]{1,0:T(8,128)(2,1)S(1)}, u32[]{:S(2)}, u32[]{:S(2)}) collective-permute-start(bf16[128,2048]{1,0:T(8,128)(2,1)S(1)} %convert_element_type.77), channel_id=1, source_target_pairs={{0,16},{16,0},{1,17},{17,1},{2,18},{18,2},{3,19},{19,3},{4,20},{20... | collective-permute-start | bytes 1572872 | tf_op jit(solution)/shard_map/ppermute | solution.py:146
  109.5 1.5 %collective-permute-done.18.refs_0_ = bf16[64,4224]{1,0:T(8,128)(2,1)S(1)} collective-permute-done((bf16[64,4224]{1,0:T(8,128)(2,1)S(1)}, bf16[64,4224]{1,0:T(8,128)(2,1)S(1)}, u32[]{:S(2)}, u32[]{:S(2)}) %collective-permute-start.18) | collective-permute-done | bytes 540704 | tf_op jit(solution)/shard_map/ppermute | solution.py:130
  111.7 1.4 collective-permute-start.21
  113.1 7.9 %expert_part.9 = f32[128,2048]{1,0:T(8,128)S(1)} custom-call(s32[2]{0:T(128)S(1)} %pad_add_fusion.me_ref, bf16[64,4224]{1,0:T(8,128)(2,1)S(1)} %collective-permute-done.18.refs_0_, bf16[64,4224]{1,0:T(8,128)(2,1)S(1)} %collective-permute-done.20.refs_1_, bf16[2048,768]{1,0:T(8,128)(2,1)S(1)} %bitcast.24, ...), custom_call_target="tpu_custom_call" | custom-call | flops 2415919104 | bytes 14155776 | tf_op jit(solution)/shard_map/expert_part/pallas_call | solution.py:80
  121.2 4.3 %collective-permute-done.19.refs_0_ = bf16[64,4224]{1,0:T(8,128)(2,1)S(1)} collective-permute-done((bf16[64,4224]{1,0:T(8,128)(2,1)S(1)}, bf16[64,4224]{1,0:T(8,128)(2,1)S(1)}, u32[]{:S(2)}, u32[]{:S(2)}) %collective-permute-start.19) | collective-permute-done | bytes 540704 | tf_op jit(solution)/shard_map/ppermute | solution.py:130
  125.5 2.0 %collective-permute-start.34 = (bf16[64,2048]{1,0:T(8,128)(2,1)S(1)}, bf16[64,2048]{1,0:T(8,128)(2,1)S(1)}, u32[]{:S(2)}, u32[]{:S(2)}) collective-permute-start(bf16[64,2048]{1,0:T(8,128)(2,1)S(1)} %get-tuple-element.36), channel_id=1, source_target_pairs={{0,2},{1,3},{4,0},{5,1},{8,4},{9,5},{12,8},{13,9},{14,12},{15,13},... | collective-permute-start | bytes 786440 | tf_op jit(solution)/shard_map/ppermute | solution.py:130
  127.5 7.9 %expert_part.15 = f32[128,2048]{1,0:T(8,128)S(1)} custom-call(s32[2]{0:T(128)S(1)} %pad_add_fusion.me_ref, bf16[64,4224]{1,0:T(8,128)(2,1)S(1)} %collective-permute-done.19.refs_0_, bf16[64,4224]{1,0:T(8,128)(2,1)S(1)} %collective-permute-done.21.refs_1_, bf16[2048,768]{1,0:T(8,128)(2,1)S(1)} %bitcast.25, ...), custom_call_target="tpu_custom_call" | custom-call | flops 2415919104 | bytes 14155776 | tf_op jit(solution)/shard_map/expert_part/pallas_call | solution.py:80
  135.6 2.2 %collective-permute-start.33 = (bf16[64,2048]{1,0:T(8,128)(2,1)S(1)}, bf16[64,2048]{1,0:T(8,128)(2,1)S(1)}, u32[]{:S(2)}, u32[]{:S(2)}) collective-permute-start(bf16[64,2048]{1,0:T(8,128)(2,1)S(1)} %get-tuple-element.38), channel_id=1, source_target_pairs={{0,20},{1,21},{4,24},{5,25},{8,28},{9,29},{12,30},{13,31},{14,26},... | collective-permute-start | bytes 786440 | tf_op jit(solution)/shard_map/ppermute | solution.py:134
  138.6 5.0 %collective-permute-done.33.a_ref = bf16[64,2048]{1,0:T(8,128)(2,1)S(1)} collective-permute-done((bf16[64,2048]{1,0:T(8,128)(2,1)S(1)}, bf16[64,2048]{1,0:T(8,128)(2,1)S(1)}, u32[]{:S(2)}, u32[]{:S(2)}) %collective-permute-start.33) | collective-permute-done | bytes 262176 | tf_op jit(solution)/shard_map/ppermute | solution.py:134
  143.6 2.1 %collective-permute-done.35.b_ref = bf16[64,2048]{1,0:T(8,128)(2,1)S(1)} collective-permute-done((bf16[64,2048]{1,0:T(8,128)(2,1)S(1)}, bf16[64,2048]{1,0:T(8,128)(2,1)S(1)}, u32[]{:S(2)}, u32[]{:S(2)}) %collective-permute-start.35) | collective-permute-done | bytes 262176 | tf_op jit(solution)/shard_map/ppermute | solution.py:134
  145.7 1.6 %finish.1 = bf16[128,2048]{1,0:T(8,128)(2,1)} custom-call(bf16[128,2048]{1,0:T(8,128)(2,1)S(1)} %collective-permute-done.x_ref, bf16[128,2048]{1,0:T(8,128)(2,1)S(1)} %collective-permute-done.1.g_ref, f32[1,2048]{1,0:T(1,128)S(1)} %collective-permute-done.2.gain_ref, bf16[128,2048]{1,0:T(8,128)(2,1)S(1)} %collective-permute-done.5.own_ref, ...), custom_call_target="tpu_custom_call" | custom-call | tf_op jit(solution)/shard_map/finish/pallas_call | solution.py:114
  (87 shorter events, 28.1 us)
Async XLA Ops:
  0.0 25.6 %collective-permute-start.3 = (bf16[2048,768]{1,0:T(8,128)(2,1)}, bf16[2048,768]{1,0:T(8,128)(2,1)}, u32[]{:S(2)}, u32[]{:S(2)}) collective-permute-start(bf16[2048,768]{1,0:T(8,128)(2,1)} %bitcast.17), channel_id=1, source_target_pairs={{0,1},{1,0},{2,3},{3,2},{4,5},{5,4},{6,7},{7,6},{8,9},{9,8},{10,11... | collective-permute-start | bytes 9437192 | tf_op jit(solution)/shard_map/ppermute | solution.py:149
  0.5 25.1 %collective-permute-start.4 = (bf16[768,2048]{1,0:T(8,128)(2,1)}, bf16[768,2048]{1,0:T(8,128)(2,1)}, u32[]{:S(2)}, u32[]{:S(2)}) collective-permute-start(bf16[768,2048]{1,0:T(8,128)(2,1)} %bitcast.26), channel_id=1, source_target_pairs={{0,1},{1,0},{2,3},{3,2},{4,5},{5,4},{6,7},{7,6},{8,9},{9,8},{10,11... | collective-permute-start | bytes 9437192 | tf_op jit(solution)/shard_map/ppermute | solution.py:149
  5.0 10.8 %collective-permute-start.9 = (bf16[64,2176]{1,0:T(8,128)(2,1)}, bf16[64,2176]{1,0:T(8,128)(2,1)}, u32[]{:S(2)}, u32[]{:S(2)}) collective-permute-start(bf16[64,2176]{1,0:T(8,128)(2,1)} %get-tuple-element.22.refs_1_), channel_id=1, source_target_pairs={{0,2},{1,3},{4,0},{5,1},{8,4},{9,5},{12,8},{13,9},{14,12},{15,13},... | collective-permute-start | bytes 835592 | tf_op jit(solution)/shard_map/ppermute | solution.py:130
  9.7 11.1 %collective-permute-start.10 = (bf16[64,2048]{1,0:T(8,128)(2,1)S(1)}, bf16[64,2048]{1,0:T(8,128)(2,1)}, u32[]{:S(2)}, u32[]{:S(2)}) collective-permute-start(bf16[64,2048]{1,0:T(8,128)(2,1)S(1)} %get-tuple-element.51.refs_3_), channel_id=1, source_target_pairs={{0,2},{1,3},{4,0},{5,1},{8,4},{9,5},{12,8},{13,9},{14,12},{15,13},... | collective-permute-start | bytes 786440 | tf_op jit(solution)/shard_map/ppermute | solution.py:130
  11.2 12.2 %collective-permute-start.6 = (bf16[64,2176]{1,0:T(8,128)(2,1)}, bf16[64,2176]{1,0:T(8,128)(2,1)}, u32[]{:S(2)}, u32[]{:S(2)}) collective-permute-start(bf16[64,2176]{1,0:T(8,128)(2,1)} %get-tuple-element.21.refs_0_), channel_id=1, source_target_pairs={{0,4},{1,5},{4,8},{5,9},{8,12},{9,13},{12,14},{13,15},{14,10},{15,... | collective-permute-start | bytes 835592 | tf_op jit(solution)/shard_map/ppermute | solution.py:130
  21.7 21.1 %collective-permute-start.11 = (bf16[64,4224]{1,0:T(8,128)(2,1)S(1)}, bf16[64,4224]{1,0:T(8,128)(2,1)S(1)}, u32[]{:S(2)}, u32[]{:S(2)}) collective-permute-start(bf16[64,4224]{1,0:T(8,128)(2,1)S(1)} %constant_dynamic-update-slice_fusion.2.refs_1_), channel_id=1, source_target_pairs={{0,2},{1,3},{4,0},{5,1},{8,4},{9,5},{12,8},{13,9},{14,12},{15,13},... | collective-permute-start | bytes 1622024 | tf_op jit(solution)/shard_map/ppermute | solution.py:130
  25.1 17.7 %collective-permute-start.8 = (bf16[64,4224]{1,0:T(8,128)(2,1)S(1)}, bf16[64,4224]{1,0:T(8,128)(2,1)S(1)}, u32[]{:S(2)}, u32[]{:S(2)}) collective-permute-start(bf16[64,4224]{1,0:T(8,128)(2,1)S(1)} %constant_dynamic-update-slice_fusion.refs_0_), channel_id=1, source_target_pairs={{0,4},{1,5},{4,8},{5,9},{8,12},{9,13},{12,14},{13,15},{14,10},{15,... | collective-permute-start | bytes 1622024 | tf_op jit(solution)/shard_map/ppermute | solution.py:130
  35.6 17.3 %collective-permute-start.22 = (bf16[64,2048]{1,0:T(8,128)(2,1)S(1)}, bf16[64,2048]{1,0:T(8,128)(2,1)S(1)}, u32[]{:S(2)}, u32[]{:S(2)}) collective-permute-start(bf16[64,2048]{1,0:T(8,128)(2,1)S(1)} %get-tuple-element.50), channel_id=1, source_target_pairs={{0,4},{1,5},{4,8},{5,9},{8,12},{9,13},{12,14},{13,15},{14,10},{15,... | collective-permute-start | bytes 786440 | tf_op jit(solution)/shard_map/ppermute | solution.py:130
  36.6 16.2 %collective-permute-start.27 = (bf16[64,2048]{1,0:T(8,128)(2,1)S(1)}, bf16[64,2048]{1,0:T(8,128)(2,1)S(1)}, u32[]{:S(2)}, u32[]{:S(2)}) collective-permute-start(bf16[64,2048]{1,0:T(8,128)(2,1)S(1)} %get-tuple-element.49), channel_id=1, source_target_pairs={{0,2},{1,3},{4,0},{5,1},{8,4},{9,5},{12,8},{13,9},{14,12},{15,13},... | collective-permute-start | bytes 786440 | tf_op jit(solution)/shard_map/ppermute | solution.py:130
  41.3 13.7 %collective-permute-start = (bf16[128,2048]{1,0:T(8,128)(2,1)S(1)}, bf16[128,2048]{1,0:T(8,128)(2,1)S(1)}, u32[]{:S(2)}, u32[]{:S(2)}) collective-permute-start(bf16[128,2048]{1,0:T(8,128)(2,1)S(1)} %bitcast.36), channel_id=1, source_target_pairs={{0,16},{16,0},{1,17},{17,1},{2,18},{18,2},{3,19},{19,3},{4,20},{20... | collective-permute-start | bytes 1572872 | tf_op jit(solution)/shard_map/ppermute | solution.py:146
  42.8 15.2 %collective-permute-start.12 = (bf16[64,4224]{1,0:T(8,128)(2,1)S(1)}, bf16[64,4224]{1,0:T(8,128)(2,1)S(1)}, u32[]{:S(2)}, u32[]{:S(2)}) collective-permute-start(bf16[64,4224]{1,0:T(8,128)(2,1)S(1)} %collective-permute-done.8.refs_0_), channel_id=1, source_target_pairs={{0,4},{1,5},{4,8},{5,9},{8,12},{9,13},{12,14},{13,15},{14,10},{15,... | collective-permute-start | bytes 1622024 | tf_op jit(solution)/shard_map/ppermute | solution.py:130
  43.8 14.2 %collective-permute-start.13 = (bf16[64,4224]{1,0:T(8,128)(2,1)S(1)}, bf16[64,4224]{1,0:T(8,128)(2,1)S(1)}, u32[]{:S(2)}, u32[]{:S(2)}) collective-permute-start(bf16[64,4224]{1,0:T(8,128)(2,1)S(1)} %collective-permute-done.11.refs_1_), channel_id=1, source_target_pairs={{0,2},{1,3},{4,0},{5,1},{8,4},{9,5},{12,8},{13,9},{14,12},{15,13},... | collective-permute-start | bytes 1622024 | tf_op jit(solution)/shard_map/ppermute | solution.py:130
  53.0 15.1 %collective-permute-start.23 = (bf16[64,2048]{1,0:T(8,128)(2,1)S(1)}, bf16[64,2048]{1,0:T(8,128)(2,1)S(1)}, u32[]{:S(2)}, u32[]{:S(2)}) collective-permute-start(bf16[64,2048]{1,0:T(8,128)(2,1)S(1)} %get-tuple-element.48), channel_id=1, source_target_pairs={{0,4},{1,5},{4,8},{5,9},{8,12},{9,13},{12,14},{13,15},{14,10},{15,... | collective-permute-start | bytes 786440 | tf_op jit(solution)/shard_map/ppermute | solution.py:130
  54.0 14.0 %collective-permute-start.28 = (bf16[64,2048]{1,0:T(8,128)(2,1)S(1)}, bf16[64,2048]{1,0:T(8,128)(2,1)S(1)}, u32[]{:S(2)}, u32[]{:S(2)}) collective-permute-start(bf16[64,2048]{1,0:T(8,128)(2,1)S(1)} %get-tuple-element.47), channel_id=1, source_target_pairs={{0,2},{1,3},{4,0},{5,1},{8,4},{9,5},{12,8},{13,9},{14,12},{15,13},... | collective-permute-start | bytes 786440 | tf_op jit(solution)/shard_map/ppermute | solution.py:130
  55.0 15.2 %collective-permute-start.1 = (bf16[128,2048]{1,0:T(8,128)(2,1)S(1)}, bf16[128,2048]{1,0:T(8,128)(2,1)S(1)}, u32[]{:S(2)}, u32[]{:S(2)}) collective-permute-start(bf16[128,2048]{1,0:T(8,128)(2,1)S(1)} %bitcast.39), channel_id=1, source_target_pairs={{0,16},{16,0},{1,17},{17,1},{2,18},{18,2},{3,19},{19,3},{4,20},{20... | collective-permute-start | bytes 1572872 | tf_op jit(solution)/shard_map/ppermute | solution.py:146
  58.1 17.2 %collective-permute-start.14 = (bf16[64,4224]{1,0:T(8,128)(2,1)S(1)}, bf16[64,4224]{1,0:T(8,128)(2,1)S(1)}, u32[]{:S(2)}, u32[]{:S(2)}) collective-permute-start(bf16[64,4224]{1,0:T(8,128)(2,1)S(1)} %collective-permute-done.12.refs_0_), channel_id=1, source_target_pairs={{0,4},{1,5},{4,8},{5,9},{8,12},{9,13},{12,14},{13,15},{14,10},{15,... | collective-permute-start | bytes 1622024 | tf_op jit(solution)/shard_map/ppermute | solution.py:130
  58.6 16.6 %collective-permute-start.15 = (bf16[64,4224]{1,0:T(8,128)(2,1)S(1)}, bf16[64,4224]{1,0:T(8,128)(2,1)S(1)}, u32[]{:S(2)}, u32[]{:S(2)}) collective-permute-start(bf16[64,4224]{1,0:T(8,128)(2,1)S(1)} %collective-permute-done.13.refs_1_), channel_id=1, source_target_pairs={{0,2},{1,3},{4,0},{5,1},{8,4},{9,5},{12,8},{13,9},{14,12},{15,13},... | collective-permute-start | bytes 1622024 | tf_op jit(solution)/shard_map/ppermute | solution.py:130
  68.2 17.2 %collective-permute-start.24 = (bf16[64,2048]{1,0:T(8,128)(2,1)S(1)}, bf16[64,2048]{1,0:T(8,128)(2,1)S(1)}, u32[]{:S(2)}, u32[]{:S(2)}) collective-permute-start(bf16[64,2048]{1,0:T(8,128)(2,1)S(1)} %get-tuple-element.46), channel_id=1, source_target_pairs={{0,4},{1,5},{4,8},{5,9},{8,12},{9,13},{12,14},{13,15},{14,10},{15,... | collective-permute-start | bytes 786440 | tf_op jit(solution)/shard_map/ppermute | solution.py:130
  68.8 16.6 %collective-permute-start.29 = (bf16[64,2048]{1,0:T(8,128)(2,1)S(1)}, bf16[64,2048]{1,0:T(8,128)(2,1)S(1)}, u32[]{:S(2)}, u32[]{:S(2)}) collective-permute-start(bf16[64,2048]{1,0:T(8,128)(2,1)S(1)} %get-tuple-element.45), channel_id=1, source_target_pairs={{0,2},{1,3},{4,0},{5,1},{8,4},{9,5},{12,8},{13,9},{14,12},{15,13},... | collective-permute-start | bytes 786440 | tf_op jit(solution)/shard_map/ppermute | solution.py:130
  75.3 20.5 %collective-permute-start.16 = (bf16[64,4224]{1,0:T(8,128)(2,1)S(1)}, bf16[64,4224]{1,0:T(8,128)(2,1)S(1)}, u32[]{:S(2)}, u32[]{:S(2)}) collective-permute-start(bf16[64,4224]{1,0:T(8,128)(2,1)S(1)} %collective-permute-done.14.refs_0_), channel_id=1, source_target_pairs={{0,4},{1,5},{4,8},{5,9},{8,12},{9,13},{12,14},{13,15},{14,10},{15,... | collective-permute-start | bytes 1622024 | tf_op jit(solution)/shard_map/ppermute | solution.py:130
  76.4 19.4 %collective-permute-start.17 = (bf16[64,4224]{1,0:T(8,128)(2,1)S(1)}, bf16[64,4224]{1,0:T(8,128)(2,1)S(1)}, u32[]{:S(2)}, u32[]{:S(2)}) collective-permute-start(bf16[64,4224]{1,0:T(8,128)(2,1)S(1)} %collective-permute-done.15.refs_1_), channel_id=1, source_target_pairs={{0,2},{1,3},{4,0},{5,1},{8,4},{9,5},{12,8},{13,9},{14,12},{15,13},... | collective-permute-start | bytes 1622024 | tf_op jit(solution)/shard_map/ppermute | solution.py:130
  85.5 20.3 %collective-permute-start.25 = (bf16[64,2048]{1,0:T(8,128)(2,1)S(1)}, bf16[64,2048]{1,0:T(8,128)(2,1)S(1)}, u32[]{:S(2)}, u32[]{:S(2)}) collective-permute-start(bf16[64,2048]{1,0:T(8,128)(2,1)S(1)} %get-tuple-element.44), channel_id=1, source_target_pairs={{0,4},{1,5},{4,8},{5,9},{8,12},{9,13},{12,14},{13,15},{14,10},{15,... | collective-permute-start | bytes 786440 | tf_op jit(solution)/shard_map/ppermute | solution.py:130
  86.7 19.1 %collective-permute-start.30 = (bf16[64,2048]{1,0:T(8,128)(2,1)S(1)}, bf16[64,2048]{1,0:T(8,128)(2,1)S(1)}, u32[]{:S(2)}, u32[]{:S(2)}) collective-permute-start(bf16[64,2048]{1,0:T(8,128)(2,1)S(1)} %get-tuple-element.43), channel_id=1, source_target_pairs={{0,2},{1,3},{4,0},{5,1},{8,4},{9,5},{12,8},{13,9},{14,12},{15,13},... | collective-permute-start | bytes 786440 | tf_op jit(solution)/shard_map/ppermute | solution.py:130
  95.8 15.3 %collective-permute-start.18 = (bf16[64,4224]{1,0:T(8,128)(2,1)S(1)}, bf16[64,4224]{1,0:T(8,128)(2,1)S(1)}, u32[]{:S(2)}, u32[]{:S(2)}) collective-permute-start(bf16[64,4224]{1,0:T(8,128)(2,1)S(1)} %collective-permute-done.16.refs_0_), channel_id=1, source_target_pairs={{0,4},{1,5},{4,8},{5,9},{8,12},{9,13},{12,14},{13,15},{14,10},{15,... | collective-permute-start | bytes 1622024 | tf_op jit(solution)/shard_map/ppermute | solution.py:130
  97.0 14.7 %collective-permute-start.20 = (bf16[64,4224]{1,0:T(8,128)(2,1)S(1)}, bf16[64,4224]{1,0:T(8,128)(2,1)S(1)}, u32[]{:S(2)}, u32[]{:S(2)}) collective-permute-start(bf16[64,4224]{1,0:T(8,128)(2,1)S(1)} %collective-permute-done.17.refs_1_), channel_id=1, source_target_pairs={{0,2},{1,3},{4,0},{5,1},{8,4},{9,5},{12,8},{13,9},{14,12},{15,13},... | collective-permute-start | bytes 1622024 | tf_op jit(solution)/shard_map/ppermute | solution.py:130
  105.9 15.1 %collective-permute-start.26 = (bf16[64,2048]{1,0:T(8,128)(2,1)S(1)}, bf16[64,2048]{1,0:T(8,128)(2,1)S(1)}, u32[]{:S(2)}, u32[]{:S(2)}) collective-permute-start(bf16[64,2048]{1,0:T(8,128)(2,1)S(1)} %get-tuple-element.42), channel_id=1, source_target_pairs={{0,4},{1,5},{4,8},{5,9},{8,12},{9,13},{12,14},{13,15},{14,10},{15,... | collective-permute-start | bytes 786440 | tf_op jit(solution)/shard_map/ppermute | solution.py:130
  107.2 13.9 %collective-permute-start.31 = (bf16[64,2048]{1,0:T(8,128)(2,1)S(1)}, bf16[64,2048]{1,0:T(8,128)(2,1)S(1)}, u32[]{:S(2)}, u32[]{:S(2)}) collective-permute-start(bf16[64,2048]{1,0:T(8,128)(2,1)S(1)} %get-tuple-element.41), channel_id=1, source_target_pairs={{0,2},{1,3},{4,0},{5,1},{8,4},{9,5},{12,8},{13,9},{14,12},{15,13},... | collective-permute-start | bytes 786440 | tf_op jit(solution)/shard_map/ppermute | solution.py:130
  108.0 19.5 %collective-permute-start.5 = (bf16[128,2048]{1,0:T(8,128)(2,1)S(1)}, bf16[128,2048]{1,0:T(8,128)(2,1)S(1)}, u32[]{:S(2)}, u32[]{:S(2)}) collective-permute-start(bf16[128,2048]{1,0:T(8,128)(2,1)S(1)} %convert_element_type.77), channel_id=1, source_target_pairs={{0,16},{16,0},{1,17},{17,1},{2,18},{18,2},{3,19},{19,3},{4,20},{20... | collective-permute-start | bytes 1572872 | tf_op jit(solution)/shard_map/ppermute | solution.py:146
  111.1 14.4 %collective-permute-start.19 = (bf16[64,4224]{1,0:T(8,128)(2,1)S(1)}, bf16[64,4224]{1,0:T(8,128)(2,1)S(1)}, u32[]{:S(2)}, u32[]{:S(2)}) collective-permute-start(bf16[64,4224]{1,0:T(8,128)(2,1)S(1)} %collective-permute-done.18.refs_0_), channel_id=1, source_target_pairs={{0,4},{1,5},{4,8},{5,9},{8,12},{9,13},{12,14},{13,15},{14,10},{15,... | collective-permute-start | bytes 1622024 | tf_op jit(solution)/shard_map/ppermute | solution.py:130
  111.7 13.8 %collective-permute-start.21 = (bf16[64,4224]{1,0:T(8,128)(2,1)S(1)}, bf16[64,4224]{1,0:T(8,128)(2,1)S(1)}, u32[]{:S(2)}, u32[]{:S(2)}) collective-permute-start(bf16[64,4224]{1,0:T(8,128)(2,1)S(1)} %collective-permute-done.20.refs_1_), channel_id=1, source_target_pairs={{0,2},{1,3},{4,0},{5,1},{8,4},{9,5},{12,8},{13,9},{14,12},{15,13},... | collective-permute-start | bytes 1622024 | tf_op jit(solution)/shard_map/ppermute | solution.py:130
  125.5 10.0 %collective-permute-start.32 = (bf16[64,2048]{1,0:T(8,128)(2,1)S(1)}, bf16[64,2048]{1,0:T(8,128)(2,1)S(1)}, u32[]{:S(2)}, u32[]{:S(2)}) collective-permute-start(bf16[64,2048]{1,0:T(8,128)(2,1)S(1)} %get-tuple-element.35), channel_id=1, source_target_pairs={{0,4},{1,5},{4,8},{5,9},{8,12},{9,13},{12,14},{13,15},{14,10},{15,... | collective-permute-start | bytes 786440 | tf_op jit(solution)/shard_map/ppermute | solution.py:130
  125.5 10.0 %collective-permute-start.34 = (bf16[64,2048]{1,0:T(8,128)(2,1)S(1)}, bf16[64,2048]{1,0:T(8,128)(2,1)S(1)}, u32[]{:S(2)}, u32[]{:S(2)}) collective-permute-start(bf16[64,2048]{1,0:T(8,128)(2,1)S(1)} %get-tuple-element.36), channel_id=1, source_target_pairs={{0,2},{1,3},{4,0},{5,1},{8,4},{9,5},{12,8},{13,9},{14,12},{15,13},... | collective-permute-start | bytes 786440 | tf_op jit(solution)/shard_map/ppermute | solution.py:130
  (15 other events, 133.8 us)

commit v4 on v2

v4 whole, which is shorter than its diff:
```python
import jax
import jax.numpy as jnp
from jax import lax
from jax.experimental import pallas as pl
from jax.experimental.pallas import tpu as pltpu
from jax.sharding import PartitionSpec as P

epsilon = 1e-06
LANES = 128
VMEM = 16 << 20
NT = (((1,), (1,)), ((), ()))


def pack_kernel(x_hbm, grad_hbm, gain_hbm, routes_hbm, gates_hbm, a_ref, b_ref, keep_hbm, keep_ref, grad_s, gain_s, routes_s, gates_s, sems):
    half = a_ref.shape[0]
    rows, width = x_hbm.shape
    x_ref = keep_ref.at[pl.ds(0, rows)]
    copies = [
        pltpu.make_async_copy(hbm, vmem, sems.at[i])
        for i, (hbm, vmem) in enumerate(
            ((x_hbm, x_ref), (gain_hbm, gain_s), (routes_hbm, routes_s), (gates_hbm, gates_s), (grad_hbm, grad_s))
        )
    ]
    for copy in copies:
        copy.start()
    for copy in copies[:4]:
        copy.wait()
    gain = gain_s[...]
    values = x_ref[...].astype(jnp.float32)
    scaling = lax.rsqrt(jnp.mean(values * values, axis=-1, keepdims=True) + epsilon)
    normed = (values * scaling * gain).astype(jnp.bfloat16)
    expert = lax.broadcasted_iota(jnp.int32, (a_ref.shape[1] - 2 * width, rows), 0)
    dense = jnp.zeros(expert.shape, jnp.float32)
    routes, gates = routes_s[...], gates_s[...].astype(jnp.float32)
    for k in range(routes.shape[0]):
        dense = dense + jnp.where(expert == routes[k : k + 1, :], gates[k : k + 1, :], 0.0)
    dense = dense.T.astype(jnp.bfloat16)
    high = gain.astype(jnp.bfloat16).astype(jnp.float32)
    middle = (gain - high).astype(jnp.bfloat16).astype(jnp.float32)
    low = gain - high - middle
    row = lax.broadcasted_iota(jnp.int32, (keep_ref.shape[0] - rows, width), 0)
    pieces = jnp.where(row == 0, high, jnp.where(row == 1, middle, jnp.where(row == 2, low, 0.0)))
    keep_ref[rows:, :] = pieces.astype(jnp.bfloat16)
    kept = pltpu.make_async_copy(keep_ref, keep_hbm, sems.at[5])
    kept.start()
    copies[4].wait()
    for ref, first in ((a_ref, 0), (b_ref, half)):
        ref[:, :width] = normed[first : first + half]
        ref[:, width:-width] = dense[first : first + half]
        ref[:, -width:] = grad_s[first : first + half, :]
    kept.wait()


def pack(x, grad, gain, routes, gates, experts):
    rows, width = x.shape
    top = routes.shape[1]
    lanes = -(-experts // LANES) * LANES
    shape = pltpu.VMEM((rows // 2, 2 * width + lanes), jnp.bfloat16)
    args = (x, grad, gain, routes.T, gates.T)
    return pl.pallas_call(
        pack_kernel,
        out_shape=(shape, shape, pltpu.HBM((rows + 16, width), jnp.bfloat16)),
        in_specs=[pl.BlockSpec(memory_space=pltpu.HBM)] * 5,
        out_specs=(pl.BlockSpec(memory_space=pltpu.VMEM),) * 2 + (pl.BlockSpec(memory_space=pltpu.HBM),),
        scratch_shapes=[
            pltpu.VMEM((rows + 16, width), jnp.bfloat16),
            pltpu.VMEM((rows, width), jnp.bfloat16),
            pltpu.VMEM((1, width), jnp.float32),
            pltpu.VMEM((top, rows), jnp.int32),
            pltpu.VMEM((top, rows), jnp.bfloat16),
            pltpu.SemaphoreType.DMA((6,)),
        ],
        compiler_params=pltpu.CompilerParams(vmem_limit_bytes=VMEM),
        name="pack",
    )(*(pltpu.with_memory_space_constraint(value, pltpu.HBM) for value in args))


def hold_kernel(up_hbm, down_hbm, up_ref, down_ref, sems):
    copies = [pltpu.make_async_copy(up_hbm, up_ref, sems.at[0]), pltpu.make_async_copy(down_hbm, down_ref, sems.at[1])]
    for copy in copies:
        copy.start()
    for copy in copies:
        copy.wait()


def hold(up, down):
    return pl.pallas_call(
        hold_kernel,
        out_shape=(pltpu.VMEM(up.shape, up.dtype), pltpu.VMEM(down.shape, down.dtype)),
        in_specs=[pl.BlockSpec(memory_space=pltpu.HBM)] * 2,
        out_specs=(pl.BlockSpec(memory_space=pltpu.VMEM),) * 2,
        scratch_shapes=[pltpu.SemaphoreType.DMA((2,))],
        compiler_params=pltpu.CompilerParams(vmem_limit_bytes=1 << 20),
        name="hold",
    )(*(pltpu.with_memory_space_constraint(value, pltpu.HBM) for value in (up, down)))


def expert_kernel(me_ref, a_ref, b_ref, u0_ref, d0_ref, u1_ref, d1_ref, o_ref):
    width = u0_ref.shape[0]

    def rows(first, last):
        return jnp.concatenate([a_ref[:, first:last], b_ref[:, first:last]], axis=0)

    last = a_ref.shape[1]
    normed, dense, grad = rows(0, width), rows(width, last - width).astype(jnp.float32), rows(last - width, last)
    lane = lax.broadcasted_iota(jnp.int32, dense.shape, 1)
    for i, (u_ref, d_ref) in enumerate(((u0_ref, d0_ref), (u1_ref, d1_ref))):
        before = jnp.dot(normed, u_ref[...], preferred_element_type=jnp.float32)
        d_hidden = lax.dot_general(grad, d_ref[...], NT, preferred_element_type=jnp.float32)
        sigmoid_of = jax.nn.sigmoid(before)
        d_before = (d_hidden * sigmoid_of * (1.0 + before * (1.0 - sigmoid_of))).astype(jnp.bfloat16)
        d_route = lax.dot_general(d_before, u_ref[...], NT, preferred_element_type=jnp.float32)
        gate = jnp.sum(jnp.where(lane == me_ref[i], dense, 0.0), axis=-1, keepdims=True)
        part = d_route.astype(jnp.bfloat16).astype(jnp.float32) * gate
        if i == 0:
            o_ref[...] = part
        else:
            o_ref[...] += part


def expert_part(me, a, b, weights):
    half = a.shape[0]
    width, hidden = weights[0].shape
    whole = pl.BlockSpec(memory_space=pltpu.VMEM)
    return pl.pallas_call(
        expert_kernel,
        out_shape=jax.ShapeDtypeStruct((2 * half, width), jnp.float32),
        in_specs=[pl.BlockSpec(memory_space=pltpu.SMEM)] + [whole] * 6,
        out_specs=whole,
        compiler_params=pltpu.CompilerParams(vmem_limit_bytes=VMEM),
        cost_estimate=pl.CostEstimate(
            flops=24 * half * width * hidden,
            transcendentals=4 * half * hidden,
            bytes_accessed=8 * width * hidden + 12 * half * width,
        ),
        name="expert_part",
    )(me, a, b, *weights)


def finish_kernel(keep_ref, g_ref, own_ref, a_ref, b_ref, o_ref):
    half = a_ref.shape[0]
    rows = 2 * half
    pieces = keep_ref[rows : rows + 16, :].astype(jnp.float32)
    gain = (pieces[0:1, :] + pieces[1:2, :]) + pieces[2:3, :]
    for ref, first in ((a_ref, 0), (b_ref, half)):
        part = slice(first, first + half)
        values = keep_ref[part, :].astype(jnp.float32)
        scaling = lax.rsqrt(jnp.mean(values * values, axis=-1, keepdims=True) + epsilon)
        d_normed = own_ref[part, :].astype(jnp.float32) + ref[...].astype(jnp.float32)
        weighted = gain * d_normed
        inner_mean = jnp.mean(values * weighted, axis=-1, keepdims=True)
        back = scaling * weighted - values * (scaling * scaling * scaling) * inner_mean
        o_ref[part, :] = (g_ref[part, :].astype(jnp.float32) + back).astype(jnp.bfloat16)


def finish(keep, grad, own, a, b):
    return pl.pallas_call(
        finish_kernel,
        out_shape=jax.ShapeDtypeStruct(grad.shape, jnp.bfloat16),
        compiler_params=pltpu.CompilerParams(vmem_limit_bytes=VMEM),
        name="finish",
    )(keep, grad, own, a, b)


def shards(bwd_input, out_grad, norm_gain, up_weight, down_weight, bwd_routes, bwd_gates):
    experts = lax.axis_size("expert")
    sections = lax.axis_size("pipe")
    chips = experts // 2
    ring = list(range(0, chips, 2)) + list(range(1, chips, 2))[::-1]

    def hop(value, by):
        moves = [(ring[i], ring[(i + by) % chips]) for i in range(chips)]
        return lax.ppermute(value, "expert", [(2 * a + c, 2 * b + c) for a, b in moves for c in (0, 1)])

    def last_hop(value, by):
        moves = [(ring[i], ring[(i + by) % chips]) for i in range(chips)]
        return lax.ppermute(
            value,
            ("pipe", "expert"),
            [
                (s * experts + 2 * a + c, (s - 1) % sections * experts + 2 * b + c)
                for s in range(sections)
                for a, b in moves
                for c in (0, 1)
            ],
        )

    def to_previous(value):
        return lax.ppermute(value, "pipe", [(s, (s - 1) % sections) for s in range(sections)])

    def swap(value):
        return lax.ppermute(value, "expert", [(e, e ^ 1) for e in range(experts)])

    x, grad = bwd_input[0], out_grad[0]
    u0, d0 = up_weight[0, 0], down_weight[0, 0]
    e = lax.axis_index("expert").astype(jnp.int32)
    me = jnp.stack([e, e ^ 1])

    half = grad.shape[0] // 2
    u1, d1 = swap(u0), swap(d0)
    a, b, keep = pack(x, grad, norm_gain, bwd_routes[0], bwd_gates[0], experts)
    a1, b1 = hop(a, 1), hop(b, -1)
    weights = (*hold(u0, d0), *hold(u1, d1))
    own = expert_part(me, a, b, weights).astype(jnp.bfloat16)
    own_out, keep_out, grad_out = to_previous(own), to_previous(keep), to_previous(grad)
    early = {3: own, 2: keep_out, 4: grad_out, 6: own_out}
    sum_a = sum_b = None
    for step in range(1, chips):
        a, b = a1, b1
        if step in early:
            a, b, early[step] = lax.optimization_barrier((a, b, early[step]))
        if step < chips - 1:
            a1, b1 = hop(a, 1), hop(b, -1)
        part = expert_part(me, a, b, weights)
        part_a, part_b = part[:half], part[half:]
        if step > 1:
            part_a = part_a + sum_a.astype(jnp.float32)
            part_b = part_b + sum_b.astype(jnp.float32)
        send_a, send_b = part_a.astype(jnp.bfloat16), part_b.astype(jnp.bfloat16)
        if step == chips - 2:
            a1, b1, send_a, send_b = lax.optimization_barrier((a1, b1, send_a, send_b))
        move = hop if step < chips - 1 else last_hop
        sum_a, sum_b = move(send_a, 1), move(send_b, -1)
    return finish(keep_out, grad_out, own_out, sum_a, sum_b)[None]


def solution(mesh):
    return jax.shard_map(
        shards,
        mesh=mesh,
        in_specs=(
            P("pipe", "expert", None),
            P("pipe", "expert", None),
            P("pipe", None),
            P("pipe", "expert", None, None),
            P("pipe", "expert", None, None),
            P("pipe", "expert", None),
            P("pipe", "expert", None),
        ),
        out_specs=P("pipe", "expert", None),
        check_vma=False,
    )
```

time: 152 us -> 144 us (0.947)
  local copies, waits for them, and re-layouts: 8.2 us -> 1.74 us
  Pallas kernels: 60.1 us -> 58.4 us
    pallas_call x8, Pallas kernels: 57.2 us -> 46.8 us  [expert_part(): pl.pallas_call(expert_kernel, out_shape=jax.ShapeDtypeStruct((2 * half, w...]
    pallas_call x2 -> x4, Pallas kernels: 2.98 us -> 11.6 us  [the longest x2 5.72 us: hold(): pl.pallas_call(hold_kernel, out_shape=(pltpu.VMEM(up.shape, up.dtype), pl...]
    unnamed x22 -> x6, local copies, waits for them, and re-layouts: 8.17 us -> 1.7 us
    ppermute x4 -> x3, waiting for transfers between devices: 4.58 us -> 0.01 us  [to_previous(): lax.ppermute(value, 'pipe', [(s, (s - 1) % sections) for s in range(secti...]
    ppermute x26, waiting for transfers between devices: 32.9 us -> 36.6 us  [hop(): lax.ppermute(value, 'expert', [(2 * a + c, 2 * b + c) for a, b in moves f...]
    ppermute x2, waiting for transfers between devices: 7.15 us -> 9.23 us  [last_hop(): lax.ppermute(value, ('pipe', 'expert'), [(s * experts + 2 * a + c, (s - 1...]
    ppermute x4 -> x3, starting transfers between devices: 5.24 us -> 5.26 us  [to_previous(): lax.ppermute(value, 'pipe', [(s, (s - 1) % sections) for s in range(secti...]
  transfers between devices with their start and end apart: 34 -> 33, of which waited for: 13 -> 13; matrix products, arithmetic and copies ran while one was open for 2% -> 1% of each run, Pallas kernels for 39% -> 39%
where the time goes in v4:
time: 144 us
  Pallas kernels  58.4 us (41%)
  waiting for transfers between devices  45.8 us (32%)
  starting transfers between devices  36.4 us (25%)
  local copies, waits for them, and re-layouts  1.74 us (1%)
    pallas_call x8, Pallas kernels, expert_part(): pl.pallas_call(expert_kernel, out_shape=jax.ShapeDtypeStruct((2 * half, w...  46.8 us
    ppermute x26, waiting for transfers between devices, hop(): lax.ppermute(value, 'expert', [(2 * a + c, 2 * b + c) for a, b in moves f...  36.6 us
    ppermute x26, starting transfers between devices, hop(): lax.ppermute(value, 'expert', [(2 * a + c, 2 * b + c) for a, b in moves f...  27.7 us
    ppermute x2, waiting for transfers between devices, last_hop(): lax.ppermute(value, ('pipe', 'expert'), [(s * experts + 2 * a + c, (s - 1...  9.23 us
    pallas_call x2, Pallas kernels, hold(): pl.pallas_call(hold_kernel, out_shape=(pltpu.VMEM(up.shape, up.dtype), pl...  5.72 us
    ppermute x3, starting transfers between devices, to_previous(): lax.ppermute(value, 'pipe', [(s, (s - 1) % sections) for s in range(secti...  5.26 us
    pallas_call x1, Pallas kernels, pack(): pl.pallas_call(pack_kernel, out_shape=(shape, shape, pltpu.HBM((rows + 16...  3.25 us
    ppermute x2, starting transfers between devices, last_hop(): lax.ppermute(value, ('pipe', 'expert'), [(s * experts + 2 * a + c, (s - 1...  2.98 us
  transfers between devices with their start and end apart: 33, of which 13 were waited for; matrix products, arithmetic and copies ran while one was open for 1% of the time, Pallas kernels for 39%

profile of v4, /device:TPU:0, one launch (start us, length us, event | category | flops | bytes accessed | tf_op | source)
XLA Modules:
  0.0 143.5 jit_solution(10019274636409852744)
XLA Ops:
  0.5 3.2 %pack.1 = (bf16[64,4224]{1,0:T(8,128)(2,1)}, bf16[64,4224]{1,0:T(8,128)(2,1)}, bf16[144,2048]{1,0:T(8,128)(2,1)}) custom-call(bf16[128,2048]{1,0:T(8,128)(2,1)} %bitcast.17, bf16[128,2048]{1,0:T(8,128)(2,1)} %bitcast.18, f32[1,2048]{1,0:T(1,128)} %gain_hbm.1, s32[8,128]{1,0:T(8,128)} %bitcast.20, bf16[8,128]{1,0:T(8,128)(2,1)} %bitcast.21), custom_call_target="tpu_custom_call" | custom-call | tf_op jit(solution)/shard_map/pack/pallas_call | solution.py:60
  3.8 3.1 %collective-permute-start.5 = (bf16[64,4224]{1,0:T(8,128)(2,1)}, bf16[64,4224]{1,0:T(8,128)(2,1)}, u32[]{:S(2)}, u32[]{:S(2)}) collective-permute-start(bf16[64,4224]{1,0:T(8,128)(2,1)} %get-tuple-element.25.a_ref), channel_id=1, source_target_pairs={{0,4},{1,5},{4,8},{5,9},{8,12},{9,13},{12,14},{13,15},{14,10},{15,... | collective-permute-start | bytes 1622024 | tf_op jit(solution)/shard_map/ppermute | solution.py:173
  6.8 2.0 %collective-permute-start = (bf16[144,2048]{1,0:T(8,128)(2,1)}, bf16[144,2048]{1,0:T(8,128)(2,1)}, u32[]{:S(2)}, u32[]{:S(2)}) collective-permute-start(bf16[144,2048]{1,0:T(8,128)(2,1)} %get-tuple-element.24), channel_id=1, source_target_pairs={{0,16},{16,0},{1,17},{17,1},{2,18},{18,2},{3,19},{19,3},{4,20},{20... | collective-permute-start | bytes 1769480 | tf_op jit(solution)/shard_map/ppermute | solution.py:189
  8.8 2.9 %hold.2 = (bf16[2048,768]{1,0:T(8,128)(2,1)S(1)}, bf16[768,2048]{1,0:T(8,128)(2,1)S(1)}) custom-call(bf16[2048,768]{1,0:T(8,128)(2,1)} %bitcast.14, bf16[768,2048]{1,0:T(8,128)(2,1)} %bitcast.16), custom_call_target="tpu_custom_call" | custom-call | tf_op jit(solution)/shard_map/hold/pallas_call | solution.py:87
  11.7 1.7 %copy-done = bf16[768,2048]{1,0:T(8,128)(2,1)} copy-done((bf16[768,2048]{1,0:T(8,128)(2,1)}, bf16[768,2048]{1,0:T(8,128)(2,1)S(1)}, u32[]{:S(2)}) %copy-start) | copy-done | bytes 3145752
  13.5 6.1 %collective-permute-done.5.a_ref = bf16[64,4224]{1,0:T(8,128)(2,1)} collective-permute-done((bf16[64,4224]{1,0:T(8,128)(2,1)}, bf16[64,4224]{1,0:T(8,128)(2,1)}, u32[]{:S(2)}, u32[]{:S(2)}) %collective-permute-start.5) | collective-permute-done | bytes 540704 | tf_op jit(solution)/shard_map/ppermute | solution.py:173
  19.5 1.8 %collective-permute-start.6 = (bf16[64,4224]{1,0:T(8,128)(2,1)}, bf16[64,4224]{1,0:T(8,128)(2,1)S(1)}, u32[]{:S(2)}, u32[]{:S(2)}) collective-permute-start(bf16[64,4224]{1,0:T(8,128)(2,1)} %collective-permute-done.5.a_ref), channel_id=1, source_target_pairs={{0,4},{1,5},{4,8},{5,9},{8,12},{9,13},{12,14},{13,15},{14,10},{15,... | collective-permute-start | bytes 1622024 | tf_op jit(solution)/shard_map/ppermute | solution.py:173
  21.6 2.9 %hold.3 = (bf16[2048,768]{1,0:T(8,128)(2,1)S(1)}, bf16[768,2048]{1,0:T(8,128)(2,1)S(1)}) custom-call(bf16[2048,768]{1,0:T(8,128)(2,1)} %collective-permute-done.2.up_hbm, bf16[768,2048]{1,0:T(8,128)(2,1)} %collective-permute-done.3.down_hbm), custom_call_target="tpu_custom_call" | custom-call | tf_op jit(solution)/shard_map/hold/pallas_call | solution.py:87
  24.4 6.4 %expert_part.14 = f32[128,2048]{1,0:T(8,128)S(1)} custom-call(s32[2]{0:T(128)S(1)} %pad_add_fusion.me_ref, bf16[64,4224]{1,0:T(8,128)(2,1)} %collective-permute-done.5.a_ref, bf16[64,4224]{1,0:T(8,128)(2,1)} %collective-permute-done.7.b_ref, bf16[2048,768]{1,0:T(8,128)(2,1)S(1)} %get-tuple-element.27.u0_ref, bf16[768,2048]{1,0:T(8,128)(2,1)S(1)} %copy-done.1, ...), custom_call_target="tpu_custom_call" | custom-call | flops 2415919104 | bytes 14155776 | tf_op jit(solution)/shard_map/expert_part/pallas_call | solution.py:125
  31.0 1.9 %collective-permute-start.19 = (bf16[64,2048]{1,0:T(8,128)(2,1)S(1)}, bf16[64,2048]{1,0:T(8,128)(2,1)S(1)}, u32[]{:S(2)}, u32[]{:S(2)}) collective-permute-start(bf16[64,2048]{1,0:T(8,128)(2,1)S(1)} %get-tuple-element.56), channel_id=1, source_target_pairs={{0,4},{1,5},{4,8},{5,9},{8,12},{9,13},{12,14},{13,15},{14,10},{15,... | collective-permute-start | bytes 786440 | tf_op jit(solution)/shard_map/ppermute | solution.py:173
  33.1 1.8 %collective-permute-start.1 = (bf16[128,2048]{1,0:T(8,128)(2,1)S(1)}, bf16[128,2048]{1,0:T(8,128)(2,1)S(1)}, u32[]{:S(2)}, u32[]{:S(2)}) collective-permute-start(bf16[128,2048]{1,0:T(8,128)(2,1)S(1)} %bitcast.19), channel_id=1, source_target_pairs={{0,16},{16,0},{1,17},{17,1},{2,18},{18,2},{3,19},{19,3},{4,20},{20... | collective-permute-start | bytes 1572872 | tf_op jit(solution)/shard_map/ppermute | solution.py:189
  37.4 5.7 %expert_part.13 = f32[128,2048]{1,0:T(8,128)S(1)} custom-call(s32[2]{0:T(128)S(1)} %pad_add_fusion.me_ref, bf16[64,4224]{1,0:T(8,128)(2,1)S(1)} %collective-permute-done.6.a_ref, bf16[64,4224]{1,0:T(8,128)(2,1)S(1)} %collective-permute-done.8.b_ref, bf16[2048,768]{1,0:T(8,128)(2,1)S(1)} %get-tuple-element.27.u0_ref, bf16[768,2048]{1,0:T(8,128)(2,1)S(1)} %copy-done.1, ...), custom_call_target="tpu_custom_call" | custom-call | flops 2415919104 | bytes 14155776 | tf_op jit(solution)/shard_map/expert_part/pallas_call | solution.py:125
  43.2 1.6 %collective-permute-start.20 = (bf16[64,2048]{1,0:T(8,128)(2,1)S(1)}, bf16[64,2048]{1,0:T(8,128)(2,1)S(1)}, u32[]{:S(2)}, u32[]{:S(2)}) collective-permute-start(bf16[64,2048]{1,0:T(8,128)(2,1)S(1)} %get-tuple-element.54), channel_id=1, source_target_pairs={{0,4},{1,5},{4,8},{5,9},{8,12},{9,13},{12,14},{13,15},{14,10},{15,... | collective-permute-start | bytes 786440 | tf_op jit(solution)/shard_map/ppermute | solution.py:173
  45.3 6.4 %expert_part.8 = f32[128,2048]{1,0:T(8,128)S(1)} custom-call(s32[2]{0:T(128)S(1)} %pad_add_fusion.me_ref, bf16[64,4224]{1,0:T(8,128)(2,1)} %get-tuple-element.25.a_ref, bf16[64,4224]{1,0:T(8,128)(2,1)} %get-tuple-element.26.b_ref, bf16[2048,768]{1,0:T(8,128)(2,1)S(1)} %get-tuple-element.27.u0_ref, bf16[768,2048]{1,0:T(8,128)(2,1)S(1)} %copy-done.1, ...), custom_call_target="tpu_custom_call" | custom-call | flops 2415919104 | bytes 14155776 | tf_op jit(solution)/shard_map/expert_part/pallas_call | solution.py:125
  51.7 2.0 %collective-permute-done.10.b_ref = bf16[64,4224]{1,0:T(8,128)(2,1)S(1)} collective-permute-done((bf16[64,4224]{1,0:T(8,128)(2,1)S(1)}, bf16[64,4224]{1,0:T(8,128)(2,1)S(1)}, u32[]{:S(2)}, u32[]{:S(2)}) %collective-permute-start.10) | collective-permute-done | bytes 540704 | tf_op jit(solution)/shard_map/ppermute | solution.py:173
  55.7 5.7 %expert_part.12 = f32[128,2048]{1,0:T(8,128)S(1)} custom-call(s32[2]{0:T(128)S(1)} %pad_add_fusion.me_ref, bf16[64,4224]{1,0:T(8,128)(2,1)S(1)} %collective-permute-done.9.a_ref, bf16[64,4224]{1,0:T(8,128)(2,1)S(1)} %collective-permute-done.10.b_ref, bf16[2048,768]{1,0:T(8,128)(2,1)S(1)} %get-tuple-element.27.u0_ref, bf16[768,2048]{1,0:T(8,128)(2,1)S(1)} %copy-done.1, ...), custom_call_target="tpu_custom_call" | custom-call | flops 2415919104 | bytes 14155776 | tf_op jit(solution)/shard_map/expert_part/pallas_call | solution.py:125
  63.6 5.4 %collective-permute-done.11.a_ref = bf16[64,4224]{1,0:T(8,128)(2,1)S(1)} collective-permute-done((bf16[64,4224]{1,0:T(8,128)(2,1)S(1)}, bf16[64,4224]{1,0:T(8,128)(2,1)S(1)}, u32[]{:S(2)}, u32[]{:S(2)}) %collective-permute-start.11) | collective-permute-done | bytes 540704 | tf_op jit(solution)/shard_map/ppermute | solution.py:173
  69.1 1.8 %collective-permute-done.12.b_ref = bf16[64,4224]{1,0:T(8,128)(2,1)S(1)} collective-permute-done((bf16[64,4224]{1,0:T(8,128)(2,1)S(1)}, bf16[64,4224]{1,0:T(8,128)(2,1)S(1)}, u32[]{:S(2)}, u32[]{:S(2)}) %collective-permute-start.12) | collective-permute-done | bytes 540704 | tf_op jit(solution)/shard_map/ppermute | solution.py:173
  72.9 5.7 %expert_part.11 = f32[128,2048]{1,0:T(8,128)S(1)} custom-call(s32[2]{0:T(128)S(1)} %pad_add_fusion.me_ref, bf16[64,4224]{1,0:T(8,128)(2,1)S(1)} %collective-permute-done.11.a_ref, bf16[64,4224]{1,0:T(8,128)(2,1)S(1)} %collective-permute-done.12.b_ref, bf16[2048,768]{1,0:T(8,128)(2,1)S(1)} %get-tuple-element.27.u0_ref, bf16[768,2048]{1,0:T(8,128)(2,1)S(1)} %copy-done.1, ...), custom_call_target="tpu_custom_call" | custom-call | flops 2415919104 | bytes 14155776 | tf_op jit(solution)/shard_map/expert_part/pallas_call | solution.py:125
  82.3 3.9 %collective-permute-done.13.a_ref = bf16[64,4224]{1,0:T(8,128)(2,1)S(1)} collective-permute-done((bf16[64,4224]{1,0:T(8,128)(2,1)S(1)}, bf16[64,4224]{1,0:T(8,128)(2,1)S(1)}, u32[]{:S(2)}, u32[]{:S(2)}) %collective-permute-start.13) | collective-permute-done | bytes 540704 | tf_op jit(solution)/shard_map/ppermute | solution.py:173
  86.3 1.8 %collective-permute-start.14 = (bf16[64,4224]{1,0:T(8,128)(2,1)S(1)}, bf16[64,4224]{1,0:T(8,128)(2,1)S(1)}, u32[]{:S(2)}, u32[]{:S(2)}) collective-permute-start(bf16[64,4224]{1,0:T(8,128)(2,1)S(1)} %collective-permute-done.13.a_ref), channel_id=1, source_target_pairs={{0,4},{1,5},{4,8},{5,9},{8,12},{9,13},{12,14},{13,15},{14,10},{15,... | collective-permute-start | bytes 1622024 | tf_op jit(solution)/shard_map/ppermute | solution.py:173
  88.3 5.7 %expert_part.10 = f32[128,2048]{1,0:T(8,128)S(1)} custom-call(s32[2]{0:T(128)S(1)} %pad_add_fusion.me_ref, bf16[64,4224]{1,0:T(8,128)(2,1)S(1)} %collective-permute-done.13.a_ref, bf16[64,4224]{1,0:T(8,128)(2,1)S(1)} %collective-permute-done.15.b_ref, bf16[2048,768]{1,0:T(8,128)(2,1)S(1)} %get-tuple-element.27.u0_ref, bf16[768,2048]{1,0:T(8,128)(2,1)S(1)} %copy-done.1, ...), custom_call_target="tpu_custom_call" | custom-call | flops 2415919104 | bytes 14155776 | tf_op jit(solution)/shard_map/expert_part/pallas_call | solution.py:125
  94.1 1.9 %collective-permute-start.23 = (bf16[64,2048]{1,0:T(8,128)(2,1)S(1)}, bf16[64,2048]{1,0:T(8,128)(2,1)S(1)}, u32[]{:S(2)}, u32[]{:S(2)}) collective-permute-start(bf16[64,2048]{1,0:T(8,128)(2,1)S(1)} %get-tuple-element.48), channel_id=1, source_target_pairs={{0,4},{1,5},{4,8},{5,9},{8,12},{9,13},{12,14},{13,15},{14,10},{15,... | collective-permute-start | bytes 786440 | tf_op jit(solution)/shard_map/ppermute | solution.py:173
  96.2 7.3 %collective-permute-done.14.a_ref = bf16[64,4224]{1,0:T(8,128)(2,1)S(1)} collective-permute-done((bf16[64,4224]{1,0:T(8,128)(2,1)S(1)}, bf16[64,4224]{1,0:T(8,128)(2,1)S(1)}, u32[]{:S(2)}, u32[]{:S(2)}) %collective-permute-start.14) | collective-permute-done | bytes 540704 | tf_op jit(solution)/shard_map/ppermute | solution.py:173
  103.5 1.8 %collective-permute-done.16.b_ref = bf16[64,4224]{1,0:T(8,128)(2,1)S(1)} collective-permute-done((bf16[64,4224]{1,0:T(8,128)(2,1)S(1)}, bf16[64,4224]{1,0:T(8,128)(2,1)S(1)}, u32[]{:S(2)}, u32[]{:S(2)}) %collective-permute-start.16) | collective-permute-done | bytes 540704 | tf_op jit(solution)/shard_map/ppermute | solution.py:173
  107.3 5.7 %expert_part.9 = f32[128,2048]{1,0:T(8,128)S(1)} custom-call(s32[2]{0:T(128)S(1)} %pad_add_fusion.me_ref, bf16[64,4224]{1,0:T(8,128)(2,1)S(1)} %collective-permute-done.14.a_ref, bf16[64,4224]{1,0:T(8,128)(2,1)S(1)} %collective-permute-done.16.b_ref, bf16[2048,768]{1,0:T(8,128)(2,1)S(1)} %get-tuple-element.27.u0_ref, bf16[768,2048]{1,0:T(8,128)(2,1)S(1)} %copy-done.1, ...), custom_call_target="tpu_custom_call" | custom-call | flops 2415919104 | bytes 14155776 | tf_op jit(solution)/shard_map/expert_part/pallas_call | solution.py:125
  113.2 6.2 %collective-permute-done.17.a_ref = bf16[64,4224]{1,0:T(8,128)(2,1)S(1)} collective-permute-done((bf16[64,4224]{1,0:T(8,128)(2,1)S(1)}, bf16[64,4224]{1,0:T(8,128)(2,1)S(1)}, u32[]{:S(2)}, u32[]{:S(2)}) %collective-permute-start.17) | collective-permute-done | bytes 540704 | tf_op jit(solution)/shard_map/ppermute | solution.py:173
  122.7 5.7 %expert_part.15 = f32[128,2048]{1,0:T(8,128)S(1)} custom-call(s32[2]{0:T(128)S(1)} %pad_add_fusion.me_ref, bf16[64,4224]{1,0:T(8,128)(2,1)S(1)} %collective-permute-done.17.a_ref, bf16[64,4224]{1,0:T(8,128)(2,1)S(1)} %collective-permute-done.18.b_ref, bf16[2048,768]{1,0:T(8,128)(2,1)S(1)} %get-tuple-element.27.u0_ref, bf16[768,2048]{1,0:T(8,128)(2,1)S(1)} %copy-done.1, ...), custom_call_target="tpu_custom_call" | custom-call | flops 2415919104 | bytes 14155776 | tf_op jit(solution)/shard_map/expert_part/pallas_call | solution.py:125
  128.7 2.6 %collective-permute-start.30 = (bf16[64,2048]{1,0:T(8,128)(2,1)S(1)}, bf16[64,2048]{1,0:T(8,128)(2,1)S(1)}, u32[]{:S(2)}, u32[]{:S(2)}) collective-permute-start(bf16[64,2048]{1,0:T(8,128)(2,1)S(1)} %get-tuple-element.44), channel_id=1, source_target_pairs={{0,20},{1,21},{4,24},{5,25},{8,28},{9,29},{12,30},{13,31},{14,26},... | collective-permute-start | bytes 786440 | tf_op jit(solution)/shard_map/ppermute | solution.py:177
  131.7 7.2 %collective-permute-done.30.a_ref = bf16[64,2048]{1,0:T(8,128)(2,1)S(1)} collective-permute-done((bf16[64,2048]{1,0:T(8,128)(2,1)S(1)}, bf16[64,2048]{1,0:T(8,128)(2,1)S(1)}, u32[]{:S(2)}, u32[]{:S(2)}) %collective-permute-start.30) | collective-permute-done | bytes 262176 | tf_op jit(solution)/shard_map/ppermute | solution.py:177
  138.9 2.0 %collective-permute-done.32.b_ref = bf16[64,2048]{1,0:T(8,128)(2,1)S(1)} collective-permute-done((bf16[64,2048]{1,0:T(8,128)(2,1)S(1)}, bf16[64,2048]{1,0:T(8,128)(2,1)S(1)}, u32[]{:S(2)}, u32[]{:S(2)}) %collective-permute-start.32) | collective-permute-done | bytes 262176 | tf_op jit(solution)/shard_map/ppermute | solution.py:177
  140.9 2.6 %finish.1 = bf16[128,2048]{1,0:T(8,128)(2,1)} custom-call(bf16[144,2048]{1,0:T(8,128)(2,1)} %collective-permute-done.keep_ref, bf16[128,2048]{1,0:T(8,128)(2,1)S(1)} %collective-permute-done.1.g_ref, bf16[128,2048]{1,0:T(8,128)(2,1)S(1)} %collective-permute-done.4.own_ref, bf16[64,2048]{1,0:T(8,128)(2,1)S(1)} %collective-permute-done.30.a_ref, ...), custom_call_target="tpu_custom_call" | custom-call | tf_op jit(solution)/shard_map/finish/pallas_call | solution.py:157
  (62 shorter events, 20.9 us)
Async XLA Ops:
  0.0 21.5 %collective-permute-start.2 = (bf16[2048,768]{1,0:T(8,128)(2,1)}, bf16[2048,768]{1,0:T(8,128)(2,1)}, u32[]{:S(2)}, u32[]{:S(2)}) collective-permute-start(bf16[2048,768]{1,0:T(8,128)(2,1)} %bitcast.13), channel_id=1, source_target_pairs={{0,1},{1,0},{2,3},{3,2},{4,5},{5,4},{6,7},{7,6},{8,9},{9,8},{10,11... | collective-permute-start | bytes 9437192 | tf_op jit(solution)/shard_map/ppermute | solution.py:192
  0.5 21.1 %collective-permute-start.3 = (bf16[768,2048]{1,0:T(8,128)(2,1)}, bf16[768,2048]{1,0:T(8,128)(2,1)}, u32[]{:S(2)}, u32[]{:S(2)}) collective-permute-start(bf16[768,2048]{1,0:T(8,128)(2,1)} %bitcast.15), channel_id=1, source_target_pairs={{0,1},{1,0},{2,3},{3,2},{4,5},{5,4},{6,7},{7,6},{8,9},{9,8},{10,11... | collective-permute-start | bytes 9437192 | tf_op jit(solution)/shard_map/ppermute | solution.py:192
  3.8 15.8 %collective-permute-start.5 = (bf16[64,4224]{1,0:T(8,128)(2,1)}, bf16[64,4224]{1,0:T(8,128)(2,1)}, u32[]{:S(2)}, u32[]{:S(2)}) collective-permute-start(bf16[64,4224]{1,0:T(8,128)(2,1)} %get-tuple-element.25.a_ref), channel_id=1, source_target_pairs={{0,4},{1,5},{4,8},{5,9},{8,12},{9,13},{12,14},{13,15},{14,10},{15,... | collective-permute-start | bytes 1622024 | tf_op jit(solution)/shard_map/ppermute | solution.py:173
  6.8 14.5 %collective-permute-start.7 = (bf16[64,4224]{1,0:T(8,128)(2,1)}, bf16[64,4224]{1,0:T(8,128)(2,1)}, u32[]{:S(2)}, u32[]{:S(2)}) collective-permute-start(bf16[64,4224]{1,0:T(8,128)(2,1)} %get-tuple-element.26.b_ref), channel_id=1, source_target_pairs={{0,2},{1,3},{4,0},{5,1},{8,4},{9,5},{12,8},{13,9},{14,12},{15,13},... | collective-permute-start | bytes 1622024 | tf_op jit(solution)/shard_map/ppermute | solution.py:173
  6.8 26.2 %collective-permute-start = (bf16[144,2048]{1,0:T(8,128)(2,1)}, bf16[144,2048]{1,0:T(8,128)(2,1)}, u32[]{:S(2)}, u32[]{:S(2)}) collective-permute-start(bf16[144,2048]{1,0:T(8,128)(2,1)} %get-tuple-element.24), channel_id=1, source_target_pairs={{0,16},{16,0},{1,17},{17,1},{2,18},{18,2},{3,19},{19,3},{4,20},{20... | collective-permute-start | bytes 1769480 | tf_op jit(solution)/shard_map/ppermute | solution.py:189
  19.5 15.3 %collective-permute-start.6 = (bf16[64,4224]{1,0:T(8,128)(2,1)}, bf16[64,4224]{1,0:T(8,128)(2,1)S(1)}, u32[]{:S(2)}, u32[]{:S(2)}) collective-permute-start(bf16[64,4224]{1,0:T(8,128)(2,1)} %collective-permute-done.5.a_ref), channel_id=1, source_target_pairs={{0,4},{1,5},{4,8},{5,9},{8,12},{9,13},{12,14},{13,15},{14,10},{15,... | collective-permute-start | bytes 1622024 | tf_op jit(solution)/shard_map/ppermute | solution.py:173
  21.3 14.0 %collective-permute-start.8 = (bf16[64,4224]{1,0:T(8,128)(2,1)}, bf16[64,4224]{1,0:T(8,128)(2,1)S(1)}, u32[]{:S(2)}, u32[]{:S(2)}) collective-permute-start(bf16[64,4224]{1,0:T(8,128)(2,1)} %collective-permute-done.7.b_ref), channel_id=1, source_target_pairs={{0,2},{1,3},{4,0},{5,1},{8,4},{9,5},{12,8},{13,9},{14,12},{15,13},... | collective-permute-start | bytes 1622024 | tf_op jit(solution)/shard_map/ppermute | solution.py:173
  31.0 12.1 %collective-permute-start.19 = (bf16[64,2048]{1,0:T(8,128)(2,1)S(1)}, bf16[64,2048]{1,0:T(8,128)(2,1)S(1)}, u32[]{:S(2)}, u32[]{:S(2)}) collective-permute-start(bf16[64,2048]{1,0:T(8,128)(2,1)S(1)} %get-tuple-element.56), channel_id=1, source_target_pairs={{0,4},{1,5},{4,8},{5,9},{8,12},{9,13},{12,14},{13,15},{14,10},{15,... | collective-permute-start | bytes 786440 | tf_op jit(solution)/shard_map/ppermute | solution.py:173
  32.9 10.2 %collective-permute-start.24 = (bf16[64,2048]{1,0:T(8,128)(2,1)S(1)}, bf16[64,2048]{1,0:T(8,128)(2,1)S(1)}, u32[]{:S(2)}, u32[]{:S(2)}) collective-permute-start(bf16[64,2048]{1,0:T(8,128)(2,1)S(1)} %get-tuple-element.55), channel_id=1, source_target_pairs={{0,2},{1,3},{4,0},{5,1},{8,4},{9,5},{12,8},{13,9},{14,12},{15,13},... | collective-permute-start | bytes 786440 | tf_op jit(solution)/shard_map/ppermute | solution.py:173
  33.1 30.6 %collective-permute-start.1 = (bf16[128,2048]{1,0:T(8,128)(2,1)S(1)}, bf16[128,2048]{1,0:T(8,128)(2,1)S(1)}, u32[]{:S(2)}, u32[]{:S(2)}) collective-permute-start(bf16[128,2048]{1,0:T(8,128)(2,1)S(1)} %bitcast.19), channel_id=1, source_target_pairs={{0,16},{16,0},{1,17},{17,1},{2,18},{18,2},{3,19},{19,3},{4,20},{20... | collective-permute-start | bytes 1572872 | tf_op jit(solution)/shard_map/ppermute | solution.py:189
  35.4 18.3 %collective-permute-start.10 = (bf16[64,4224]{1,0:T(8,128)(2,1)S(1)}, bf16[64,4224]{1,0:T(8,128)(2,1)S(1)}, u32[]{:S(2)}, u32[]{:S(2)}) collective-permute-start(bf16[64,4224]{1,0:T(8,128)(2,1)S(1)} %collective-permute-done.8.b_ref), channel_id=1, source_target_pairs={{0,2},{1,3},{4,0},{5,1},{8,4},{9,5},{12,8},{13,9},{14,12},{15,13},... | collective-permute-start | bytes 1622024 | tf_op jit(solution)/shard_map/ppermute | solution.py:173
  36.3 17.4 %collective-permute-start.9 = (bf16[64,4224]{1,0:T(8,128)(2,1)S(1)}, bf16[64,4224]{1,0:T(8,128)(2,1)S(1)}, u32[]{:S(2)}, u32[]{:S(2)}) collective-permute-start(bf16[64,4224]{1,0:T(8,128)(2,1)S(1)} %collective-permute-done.6.a_ref), channel_id=1, source_target_pairs={{0,4},{1,5},{4,8},{5,9},{8,12},{9,13},{12,14},{13,15},{14,10},{15,... | collective-permute-start | bytes 1622024 | tf_op jit(solution)/shard_map/ppermute | solution.py:173
  43.2 18.2 %collective-permute-start.20 = (bf16[64,2048]{1,0:T(8,128)(2,1)S(1)}, bf16[64,2048]{1,0:T(8,128)(2,1)S(1)}, u32[]{:S(2)}, u32[]{:S(2)}) collective-permute-start(bf16[64,2048]{1,0:T(8,128)(2,1)S(1)} %get-tuple-element.54), channel_id=1, source_target_pairs={{0,4},{1,5},{4,8},{5,9},{8,12},{9,13},{12,14},{13,15},{14,10},{15,... | collective-permute-start | bytes 786440 | tf_op jit(solution)/shard_map/ppermute | solution.py:173
  44.8 16.6 %collective-permute-start.25 = (bf16[64,2048]{1,0:T(8,128)(2,1)S(1)}, bf16[64,2048]{1,0:T(8,128)(2,1)S(1)}, u32[]{:S(2)}, u32[]{:S(2)}) collective-permute-start(bf16[64,2048]{1,0:T(8,128)(2,1)S(1)} %get-tuple-element.53), channel_id=1, source_target_pairs={{0,2},{1,3},{4,0},{5,1},{8,4},{9,5},{12,8},{13,9},{14,12},{15,13},... | collective-permute-start | bytes 786440 | tf_op jit(solution)/shard_map/ppermute | solution.py:173
  53.7 15.4 %collective-permute-start.11 = (bf16[64,4224]{1,0:T(8,128)(2,1)S(1)}, bf16[64,4224]{1,0:T(8,128)(2,1)S(1)}, u32[]{:S(2)}, u32[]{:S(2)}) collective-permute-start(bf16[64,4224]{1,0:T(8,128)(2,1)S(1)} %collective-permute-done.9.a_ref), channel_id=1, source_target_pairs={{0,4},{1,5},{4,8},{5,9},{8,12},{9,13},{12,14},{13,15},{14,10},{15,... | collective-permute-start | bytes 1622024 | tf_op jit(solution)/shard_map/ppermute | solution.py:173
  55.3 15.6 %collective-permute-start.12 = (bf16[64,4224]{1,0:T(8,128)(2,1)S(1)}, bf16[64,4224]{1,0:T(8,128)(2,1)S(1)}, u32[]{:S(2)}, u32[]{:S(2)}) collective-permute-start(bf16[64,4224]{1,0:T(8,128)(2,1)S(1)} %collective-permute-done.10.b_ref), channel_id=1, source_target_pairs={{0,2},{1,3},{4,0},{5,1},{8,4},{9,5},{12,8},{13,9},{14,12},{15,13},... | collective-permute-start | bytes 1622024 | tf_op jit(solution)/shard_map/ppermute | solution.py:173
  61.5 17.1 %collective-permute-start.21 = (bf16[64,2048]{1,0:T(8,128)(2,1)S(1)}, bf16[64,2048]{1,0:T(8,128)(2,1)S(1)}, u32[]{:S(2)}, u32[]{:S(2)}) collective-permute-start(bf16[64,2048]{1,0:T(8,128)(2,1)S(1)} %get-tuple-element.52), channel_id=1, source_target_pairs={{0,4},{1,5},{4,8},{5,9},{8,12},{9,13},{12,14},{13,15},{14,10},{15,... | collective-permute-start | bytes 786440 | tf_op jit(solution)/shard_map/ppermute | solution.py:173
  63.2 15.4 %collective-permute-start.26 = (bf16[64,2048]{1,0:T(8,128)(2,1)S(1)}, bf16[64,2048]{1,0:T(8,128)(2,1)S(1)}, u32[]{:S(2)}, u32[]{:S(2)}) collective-permute-start(bf16[64,2048]{1,0:T(8,128)(2,1)S(1)} %get-tuple-element.51), channel_id=1, source_target_pairs={{0,2},{1,3},{4,0},{5,1},{8,4},{9,5},{12,8},{13,9},{14,12},{15,13},... | collective-permute-start | bytes 786440 | tf_op jit(solution)/shard_map/ppermute | solution.py:173
  70.9 15.4 %collective-permute-start.13 = (bf16[64,4224]{1,0:T(8,128)(2,1)S(1)}, bf16[64,4224]{1,0:T(8,128)(2,1)S(1)}, u32[]{:S(2)}, u32[]{:S(2)}) collective-permute-start(bf16[64,4224]{1,0:T(8,128)(2,1)S(1)} %collective-permute-done.11.a_ref), channel_id=1, source_target_pairs={{0,4},{1,5},{4,8},{5,9},{8,12},{9,13},{12,14},{13,15},{14,10},{15,... | collective-permute-start | bytes 1622024 | tf_op jit(solution)/shard_map/ppermute | solution.py:173
  72.5 15.6 %collective-permute-start.15 = (bf16[64,4224]{1,0:T(8,128)(2,1)S(1)}, bf16[64,4224]{1,0:T(8,128)(2,1)S(1)}, u32[]{:S(2)}, u32[]{:S(2)}) collective-permute-start(bf16[64,4224]{1,0:T(8,128)(2,1)S(1)} %collective-permute-done.12.b_ref), channel_id=1, source_target_pairs={{0,2},{1,3},{4,0},{5,1},{8,4},{9,5},{12,8},{13,9},{14,12},{15,13},... | collective-permute-start | bytes 1622024 | tf_op jit(solution)/shard_map/ppermute | solution.py:173
  78.7 15.2 %collective-permute-start.22 = (bf16[64,2048]{1,0:T(8,128)(2,1)S(1)}, bf16[64,2048]{1,0:T(8,128)(2,1)S(1)}, u32[]{:S(2)}, u32[]{:S(2)}) collective-permute-start(bf16[64,2048]{1,0:T(8,128)(2,1)S(1)} %get-tuple-element.50), channel_id=1, source_target_pairs={{0,4},{1,5},{4,8},{5,9},{8,12},{9,13},{12,14},{13,15},{14,10},{15,... | collective-permute-start | bytes 786440 | tf_op jit(solution)/shard_map/ppermute | solution.py:173
  80.4 13.6 %collective-permute-start.27 = (bf16[64,2048]{1,0:T(8,128)(2,1)S(1)}, bf16[64,2048]{1,0:T(8,128)(2,1)S(1)}, u32[]{:S(2)}, u32[]{:S(2)}) collective-permute-start(bf16[64,2048]{1,0:T(8,128)(2,1)S(1)} %get-tuple-element.49), channel_id=1, source_target_pairs={{0,2},{1,3},{4,0},{5,1},{8,4},{9,5},{12,8},{13,9},{14,12},{15,13},... | collective-permute-start | bytes 786440 | tf_op jit(solution)/shard_map/ppermute | solution.py:173
  80.8 15.4 %collective-permute-start.4 = (bf16[128,2048]{1,0:T(8,128)(2,1)S(1)}, bf16[128,2048]{1,0:T(8,128)(2,1)S(1)}, u32[]{:S(2)}, u32[]{:S(2)}) collective-permute-start(bf16[128,2048]{1,0:T(8,128)(2,1)S(1)} %convert_element_type.77), channel_id=1, source_target_pairs={{0,16},{16,0},{1,17},{17,1},{2,18},{18,2},{3,19},{19,3},{4,20},{20... | collective-permute-start | bytes 1572872 | tf_op jit(solution)/shard_map/ppermute | solution.py:189
  86.3 17.2 %collective-permute-start.14 = (bf16[64,4224]{1,0:T(8,128)(2,1)S(1)}, bf16[64,4224]{1,0:T(8,128)(2,1)S(1)}, u32[]{:S(2)}, u32[]{:S(2)}) collective-permute-start(bf16[64,4224]{1,0:T(8,128)(2,1)S(1)} %collective-permute-done.13.a_ref), channel_id=1, source_target_pairs={{0,4},{1,5},{4,8},{5,9},{8,12},{9,13},{12,14},{13,15},{14,10},{15,... | collective-permute-start | bytes 1622024 | tf_op jit(solution)/shard_map/ppermute | solution.py:173
  88.1 17.2 %collective-permute-start.16 = (bf16[64,4224]{1,0:T(8,128)(2,1)S(1)}, bf16[64,4224]{1,0:T(8,128)(2,1)S(1)}, u32[]{:S(2)}, u32[]{:S(2)}) collective-permute-start(bf16[64,4224]{1,0:T(8,128)(2,1)S(1)} %collective-permute-done.15.b_ref), channel_id=1, source_target_pairs={{0,2},{1,3},{4,0},{5,1},{8,4},{9,5},{12,8},{13,9},{14,12},{15,13},... | collective-permute-start | bytes 1622024 | tf_op jit(solution)/shard_map/ppermute | solution.py:173
  94.1 18.9 %collective-permute-start.23 = (bf16[64,2048]{1,0:T(8,128)(2,1)S(1)}, bf16[64,2048]{1,0:T(8,128)(2,1)S(1)}, u32[]{:S(2)}, u32[]{:S(2)}) collective-permute-start(bf16[64,2048]{1,0:T(8,128)(2,1)S(1)} %get-tuple-element.48), channel_id=1, source_target_pairs={{0,4},{1,5},{4,8},{5,9},{8,12},{9,13},{12,14},{13,15},{14,10},{15,... | collective-permute-start | bytes 786440 | tf_op jit(solution)/shard_map/ppermute | solution.py:173
  96.0 17.0 %collective-permute-start.28 = (bf16[64,2048]{1,0:T(8,128)(2,1)S(1)}, bf16[64,2048]{1,0:T(8,128)(2,1)S(1)}, u32[]{:S(2)}, u32[]{:S(2)}) collective-permute-start(bf16[64,2048]{1,0:T(8,128)(2,1)S(1)} %get-tuple-element.47), channel_id=1, source_target_pairs={{0,2},{1,3},{4,0},{5,1},{8,4},{9,5},{12,8},{13,9},{14,12},{15,13},... | collective-permute-start | bytes 786440 | tf_op jit(solution)/shard_map/ppermute | solution.py:173
  105.3 14.1 %collective-permute-start.17 = (bf16[64,4224]{1,0:T(8,128)(2,1)S(1)}, bf16[64,4224]{1,0:T(8,128)(2,1)S(1)}, u32[]{:S(2)}, u32[]{:S(2)}) collective-permute-start(bf16[64,4224]{1,0:T(8,128)(2,1)S(1)} %collective-permute-done.14.a_ref), channel_id=1, source_target_pairs={{0,4},{1,5},{4,8},{5,9},{8,12},{9,13},{12,14},{13,15},{14,10},{15,... | collective-permute-start | bytes 1622024 | tf_op jit(solution)/shard_map/ppermute | solution.py:173
  106.9 13.7 %collective-permute-start.18 = (bf16[64,4224]{1,0:T(8,128)(2,1)S(1)}, bf16[64,4224]{1,0:T(8,128)(2,1)S(1)}, u32[]{:S(2)}, u32[]{:S(2)}) collective-permute-start(bf16[64,4224]{1,0:T(8,128)(2,1)S(1)} %collective-permute-done.16.b_ref), channel_id=1, source_target_pairs={{0,2},{1,3},{4,0},{5,1},{8,4},{9,5},{12,8},{13,9},{14,12},{15,13},... | collective-permute-start | bytes 1622024 | tf_op jit(solution)/shard_map/ppermute | solution.py:173
  120.6 7.7 %collective-permute-start.29 = (bf16[64,2048]{1,0:T(8,128)(2,1)S(1)}, bf16[64,2048]{1,0:T(8,128)(2,1)S(1)}, u32[]{:S(2)}, u32[]{:S(2)}) collective-permute-start(bf16[64,2048]{1,0:T(8,128)(2,1)S(1)} %get-tuple-element.41), channel_id=1, source_target_pairs={{0,4},{1,5},{4,8},{5,9},{8,12},{9,13},{12,14},{13,15},{14,10},{15,... | collective-permute-start | bytes 786440 | tf_op jit(solution)/shard_map/ppermute | solution.py:173
  128.7 10.2 %collective-permute-start.30 = (bf16[64,2048]{1,0:T(8,128)(2,1)S(1)}, bf16[64,2048]{1,0:T(8,128)(2,1)S(1)}, u32[]{:S(2)}, u32[]{:S(2)}) collective-permute-start(bf16[64,2048]{1,0:T(8,128)(2,1)S(1)} %get-tuple-element.44), channel_id=1, source_target_pairs={{0,20},{1,21},{4,24},{5,25},{8,28},{9,29},{12,30},{13,31},{14,26},... | collective-permute-start | bytes 786440 | tf_op jit(solution)/shard_map/ppermute | solution.py:177
  131.3 9.6 %collective-permute-start.32 = (bf16[64,2048]{1,0:T(8,128)(2,1)S(1)}, bf16[64,2048]{1,0:T(8,128)(2,1)S(1)}, u32[]{:S(2)}, u32[]{:S(2)}) collective-permute-start(bf16[64,2048]{1,0:T(8,128)(2,1)S(1)} %get-tuple-element.43), channel_id=1, source_target_pairs={{0,18},{1,19},{4,16},{5,17},{8,20},{9,21},{12,24},{13,25},{14,28},... | collective-permute-start | bytes 786440 | tf_op jit(solution)/shard_map/ppermute | solution.py:177
  (4 other events, 27.7 us)

commit v5 on v4

--- a/solution.py
+++ b/solution.py
@@ -11,9 +11,9 @@
 NT = (((1,), (1,)), ((), ()))
 
 
-def pack_kernel(x_hbm, grad_hbm, gain_hbm, routes_hbm, gates_hbm, a_ref, b_ref, keep_hbm, keep_ref, grad_s, gain_s, routes_s, gates_s, sems):
-    half = a_ref.shape[0]
+def pack_kernel(x_hbm, grad_hbm, gain_hbm, routes_hbm, gates_hbm, a_ref, b_ref, keep_ref, grad_s, gain_s, routes_s, gates_s, sems):
     rows, width = x_hbm.shape
+    half, slabs = rows // 2, width // LANES
     x_ref = keep_ref.at[pl.ds(0, rows)]
     copies = [
         pltpu.make_async_copy(hbm, vmem, sems.at[i])
@@ -29,88 +29,98 @@
     values = x_ref[...].astype(jnp.float32)
     scaling = lax.rsqrt(jnp.mean(values * values, axis=-1, keepdims=True) + epsilon)
     normed = (values * scaling * gain).astype(jnp.bfloat16)
-    expert = lax.broadcasted_iota(jnp.int32, (a_ref.shape[1] - 2 * width, rows), 0)
-    dense = jnp.zeros(expert.shape, jnp.float32)
+    shape = (a_ref.shape[0] - 2 * slabs * half, rows)
+    expert = lax.broadcasted_iota(jnp.int32, shape, 0)
+    dense = jnp.zeros(shape, jnp.float32)
     routes, gates = routes_s[...], gates_s[...].astype(jnp.float32)
     for k in range(routes.shape[0]):
         dense = dense + jnp.where(expert == routes[k : k + 1, :], gates[k : k + 1, :], 0.0)
-    dense = dense.T.astype(jnp.bfloat16)
+    token = lax.broadcasted_iota(jnp.int32, shape, 1)
     high = gain.astype(jnp.bfloat16).astype(jnp.float32)
     middle = (gain - high).astype(jnp.bfloat16).astype(jnp.float32)
     low = gain - high - middle
     row = lax.broadcasted_iota(jnp.int32, (keep_ref.shape[0] - rows, width), 0)
     pieces = jnp.where(row == 0, high, jnp.where(row == 1, middle, jnp.where(row == 2, low, 0.0)))
     keep_ref[rows:, :] = pieces.astype(jnp.bfloat16)
-    kept = pltpu.make_async_copy(keep_ref, keep_hbm, sems.at[5])
-    kept.start()
     copies[4].wait()
     for ref, first in ((a_ref, 0), (b_ref, half)):
-        ref[:, :width] = normed[first : first + half]
-        ref[:, width:-width] = dense[first : first + half]
-        ref[:, -width:] = grad_s[first : first + half, :]
-    kept.wait()
+        for k in range(slabs):
+            part, lanes = slice(first, first + half), slice(k * LANES, (k + 1) * LANES)
+            ref[k * half : (k + 1) * half, :] = normed[part, lanes]
+            ref[(slabs + k) * half : (slabs + k + 1) * half, :] = grad_s[part, lanes]
+        here = (token >= first) & (token < first + half)
+        ref[2 * slabs * half :, :] = jnp.where(here, dense, 0.0).astype(jnp.bfloat16)
 
 
 def pack(x, grad, gain, routes, gates, experts):
     rows, width = x.shape
     top = routes.shape[1]
-    lanes = -(-experts // LANES) * LANES
-    shape = pltpu.VMEM((rows // 2, 2 * width + lanes), jnp.bfloat16)
+    shape = pltpu.VMEM((width // LANES * rows + -(-experts // 16) * 16, LANES), jnp.bfloat16)
     args = (x, grad, gain, routes.T, gates.T)
     return pl.pallas_call(
         pack_kernel,
-        out_shape=(shape, shape, pltpu.HBM((rows + 16, width), jnp.bfloat16)),
+        out_shape=(shape, shape, pltpu.VMEM((rows + 16, width), jnp.bfloat16)),
         in_specs=[pl.BlockSpec(memory_space=pltpu.HBM)] * 5,
-        out_specs=(pl.BlockSpec(memory_space=pltpu.VMEM),) * 2 + (pl.BlockSpec(memory_space=pltpu.HBM),),
+        out_specs=(pl.BlockSpec(memory_space=pltpu.VMEM),) * 3,
         scratch_shapes=[
-            pltpu.VMEM((rows + 16, width), jnp.bfloat16),
             pltpu.VMEM((rows, width), jnp.bfloat16),
             pltpu.VMEM((1, width), jnp.float32),
             pltpu.VMEM((top, rows), jnp.int32),
             pltpu.VMEM((top, rows), jnp.bfloat16),
-            pltpu.SemaphoreType.DMA((6,)),
+            pltpu.SemaphoreType.DMA((5,)),
         ],
         compiler_params=pltpu.CompilerParams(vmem_limit_bytes=VMEM),
         name="pack",
     )(*(pltpu.with_memory_space_constraint(value, pltpu.HBM) for value in args))
 
 
-def hold_kernel(up_hbm, down_hbm, up_ref, down_ref, sems):
-    copies = [pltpu.make_async_copy(up_hbm, up_ref, sems.at[0]), pltpu.make_async_copy(down_hbm, down_ref, sems.at[1])]
+def hold_kernel(*refs):
+    count = len(refs) // 2
+    copies = [pltpu.make_async_copy(refs[i], refs[count + i], refs[-1].at[i]) for i in range(count)]
     for copy in copies:
         copy.start()
     for copy in copies:
         copy.wait()
 
 
-def hold(up, down):
+def hold(*values):
     return pl.pallas_call(
         hold_kernel,
-        out_shape=(pltpu.VMEM(up.shape, up.dtype), pltpu.VMEM(down.shape, down.dtype)),
-        in_specs=[pl.BlockSpec(memory_space=pltpu.HBM)] * 2,
-        out_specs=(pl.BlockSpec(memory_space=pltpu.VMEM),) * 2,
-        scratch_shapes=[pltpu.SemaphoreType.DMA((2,))],
+        out_shape=[pltpu.VMEM(value.shape, value.dtype) for value in values],
+        in_specs=[pl.BlockSpec(memory_space=pltpu.HBM)] * len(values),
+        out_specs=[pl.BlockSpec(memory_space=pltpu.VMEM)] * len(values),
+        scratch_shapes=[pltpu.SemaphoreType.DMA((len(values),))],
         compiler_params=pltpu.CompilerParams(vmem_limit_bytes=1 << 20),
         name="hold",
-    )(*(pltpu.with_memory_space_constraint(value, pltpu.HBM) for value in (up, down)))
+    )(*(pltpu.with_memory_space_constraint(value, pltpu.HBM) for value in values))
 
 
 def expert_kernel(me_ref, a_ref, b_ref, u0_ref, d0_ref, u1_ref, d1_ref, o_ref):
-    width = u0_ref.shape[0]
-
-    def rows(first, last):
-        return jnp.concatenate([a_ref[:, first:last], b_ref[:, first:last]], axis=0)
-
-    last = a_ref.shape[1]
-    normed, dense, grad = rows(0, width), rows(width, last - width).astype(jnp.float32), rows(last - width, last)
-    lane = lax.broadcasted_iota(jnp.int32, dense.shape, 1)
+    rows, width = o_ref.shape
+    half, slabs = rows // 2, width // LANES
+
+    def features(first):
+        return jnp.concatenate(
+            [
+                jnp.concatenate([ref[k * half : (k + 1) * half, :] for k in range(first, first + slabs)], axis=1)
+                for ref in (a_ref, b_ref)
+            ],
+            axis=0,
+        )
+
+    normed, grad = features(0), features(slabs)
+    dense = sum(ref[2 * slabs * half :, :].astype(jnp.float32) for ref in (a_ref, b_ref))
+    expert = lax.broadcasted_iota(jnp.int32, dense.shape, 0)
+    square = (rows, rows)
+    on_line = lax.broadcasted_iota(jnp.int32, square, 0) == lax.broadcasted_iota(jnp.int32, square, 1)
     for i, (u_ref, d_ref) in enumerate(((u0_ref, d0_ref), (u1_ref, d1_ref))):
         before = jnp.dot(normed, u_ref[...], preferred_element_type=jnp.float32)
         d_hidden = lax.dot_general(grad, d_ref[...], NT, preferred_element_type=jnp.float32)
         sigmoid_of = jax.nn.sigmoid(before)
         d_before = (d_hidden * sigmoid_of * (1.0 + before * (1.0 - sigmoid_of))).astype(jnp.bfloat16)
         d_route = lax.dot_general(d_before, u_ref[...], NT, preferred_element_type=jnp.float32)
-        gate = jnp.sum(jnp.where(lane == me_ref[i], dense, 0.0), axis=-1, keepdims=True)
+        named = jnp.sum(jnp.where(expert == me_ref[i], dense, 0.0), axis=0, keepdims=True)
+        gate = jnp.sum(jnp.where(on_line, jnp.broadcast_to(named, square), 0.0), axis=-1, keepdims=True)
         part = d_route.astype(jnp.bfloat16).astype(jnp.float32) * gate
         if i == 0:
             o_ref[...] = part
@@ -118,20 +128,19 @@
             o_ref[...] += part
 
 
-def expert_part(me, a, b, weights):
-    half = a.shape[0]
+def expert_part(me, a, b, rows, weights):
     width, hidden = weights[0].shape
     whole = pl.BlockSpec(memory_space=pltpu.VMEM)
     return pl.pallas_call(
         expert_kernel,
-        out_shape=jax.ShapeDtypeStruct((2 * half, width), jnp.float32),
+        out_shape=jax.ShapeDtypeStruct((rows, width), jnp.float32),
         in_specs=[pl.BlockSpec(memory_space=pltpu.SMEM)] + [whole] * 6,
         out_specs=whole,
         compiler_params=pltpu.CompilerParams(vmem_limit_bytes=VMEM),
         cost_estimate=pl.CostEstimate(
-            flops=24 * half * width * hidden,
-            transcendentals=4 * half * hidden,
-            bytes_accessed=8 * width * hidden + 12 * half * width,
+            flops=12 * rows * width * hidden,
+            transcendentals=2 * rows * hidden,
+            bytes_accessed=8 * width * hidden + 8 * rows * width,
         ),
         name="expert_part",
     )(me, a, b, *weights)
@@ -201,9 +210,9 @@
     a, b, keep = pack(x, grad, norm_gain, bwd_routes[0], bwd_gates[0], experts)
     a1, b1 = hop(a, 1), hop(b, -1)
     weights = (*hold(u0, d0), *hold(u1, d1))
-    own = expert_part(me, a, b, weights).astype(jnp.bfloat16)
+    own = expert_part(me, a, b, 2 * half, weights).astype(jnp.bfloat16)
     own_out, keep_out, grad_out = to_previous(own), to_previous(keep), to_previous(grad)
-    early = {3: own, 2: keep_out, 4: grad_out, 6: own_out}
+    early = {3: own, 2: keep_out, 5: grad_out, 6: own_out}
     sum_a = sum_b = None
     for step in range(1, chips):
         a, b = a1, b1
@@ -211,17 +220,19 @@
             a, b, early[step] = lax.optimization_barrier((a, b, early[step]))
         if step < chips - 1:
             a1, b1 = hop(a, 1), hop(b, -1)
-        part = expert_part(me, a, b, weights)
+        part = expert_part(me, a, b, 2 * half, weights)
         part_a, part_b = part[:half], part[half:]
         if step > 1:
             part_a = part_a + sum_a.astype(jnp.float32)
             part_b = part_b + sum_b.astype(jnp.float32)
         send_a, send_b = part_a.astype(jnp.bfloat16), part_b.astype(jnp.bfloat16)
         if step == chips - 2:
-            a1, b1, send_a, send_b = lax.optimization_barrier((a1, b1, send_a, send_b))
+            a1, send_a = lax.optimization_barrier((a1, send_a))
+            b1, send_b = lax.optimization_barrier((b1, send_b))
         move = hop if step < chips - 1 else last_hop
         sum_a, sum_b = move(send_a, 1), move(send_b, -1)
-    return finish(keep_out, grad_out, own_out, sum_a, sum_b)[None]
+    held = hold(keep_out, grad_out, own_out)
+    return finish(*held, sum_a, sum_b)[None]
 
 
 def solution(mesh):

time: 144 us -> 140 us (0.972)
  waiting for transfers between devices: 45.8 us -> 42.2 us
    ppermute x26, waiting for transfers between devices: 36.6 us -> 34.3 us  [hop(): lax.ppermute(value, 'expert', [(2 * a + c, 2 * b + c) for a, b in moves f...]
    pallas_call x11 -> x12, Pallas kernels: 55.8 us -> 56.9 us  [the longest x8 47.1 us: expert_part(): pl.pallas_call(expert_kernel, out_shape=jax.ShapeDtypeStruct((rows, width...]
  transfers between devices with their start and end apart: 33 -> 33, of which waited for: 13 -> 12; matrix products, arithmetic and copies ran while one was open for 1% -> 1% of each run, Pallas kernels for 39% -> 41%
where the time goes in v5:
time: 140 us
  Pallas kernels  58.4 us (42%)
  waiting for transfers between devices  42.2 us (30%)
  starting transfers between devices  36.4 us (26%)
  local copies, waits for them, and re-layouts  1.74 us (1%)
    pallas_call x8, Pallas kernels, expert_part(): pl.pallas_call(expert_kernel, out_shape=jax.ShapeDtypeStruct((rows, width...  47.1 us
    ppermute x26, waiting for transfers between devices, hop(): lax.ppermute(value, 'expert', [(2 * a + c, 2 * b + c) for a, b in moves f...  34.3 us
    ppermute x26, starting transfers between devices, hop(): lax.ppermute(value, 'expert', [(2 * a + c, 2 * b + c) for a, b in moves f...  27.7 us
    ppermute x2, waiting for transfers between devices, last_hop(): lax.ppermute(value, ('pipe', 'expert'), [(s * experts + 2 * a + c, (s - 1...  7.85 us
    pallas_call x3, Pallas kernels, hold(): pl.pallas_call(hold_kernel, out_shape=[pltpu.VMEM(value.shape, value.dtyp...  7.13 us
    ppermute x3, starting transfers between devices, to_previous(): lax.ppermute(value, 'pipe', [(s, (s - 1) % sections) for s in range(secti...  5.24 us
    ppermute x2, starting transfers between devices, last_hop(): lax.ppermute(value, ('pipe', 'expert'), [(s * experts + 2 * a + c, (s - 1...  2.98 us
  transfers between devices with their start and end apart: 33, of which 12 were waited for; matrix products, arithmetic and copies ran while one was open for 1% of the time, Pallas kernels for 41%

profile of v5, /device:TPU:0, one launch (start us, length us, event | category | flops | bytes accessed | tf_op | source)
XLA Modules:
  0.0 139.9 jit_solution(3984022419210324960)
XLA Ops:
  0.5 2.7 %pack.1 = (bf16[2064,128]{1,0:T(8,128)(2,1)}, bf16[2064,128]{1,0:T(8,128)(2,1)}, bf16[144,2048]{1,0:T(8,128)(2,1)}) custom-call(bf16[128,2048]{1,0:T(8,128)(2,1)} %bitcast.17, bf16[128,2048]{1,0:T(8,128)(2,1)} %bitcast.18, f32[1,2048]{1,0:T(1,128)} %gain_hbm.1, s32[8,128]{1,0:T(8,128)} %bitcast.20, bf16[8,128]{1,0:T(8,128)(2,1)} %bitcast.21), custom_call_target="tpu_custom_call" | custom-call | tf_op jit(solution)/shard_map/pack/pallas_call | solution.py:60
  3.2 3.1 %collective-permute-start.5 = (bf16[2064,128]{1,0:T(8,128)(2,1)}, bf16[2064,128]{1,0:T(8,128)(2,1)}, u32[]{:S(2)}, u32[]{:S(2)}) collective-permute-start(bf16[2064,128]{1,0:T(8,128)(2,1)} %get-tuple-element.28.a_ref), channel_id=1, source_target_pairs={{0,4},{1,5},{4,8},{5,9},{8,12},{9,13},{12,14},{13,15},{14,10},{15,... | collective-permute-start | bytes 1585160 | tf_op jit(solution)/shard_map/ppermute | solution.py:182
  6.3 2.0 %collective-permute-start = (bf16[144,2048]{1,0:T(8,128)(2,1)}, bf16[144,2048]{1,0:T(8,128)(2,1)}, u32[]{:S(2)}, u32[]{:S(2)}) collective-permute-start(bf16[144,2048]{1,0:T(8,128)(2,1)} %get-tuple-element.27), channel_id=1, source_target_pairs={{0,16},{16,0},{1,17},{17,1},{2,18},{18,2},{3,19},{19,3},{4,20},{20... | collective-permute-start | bytes 1769480 | tf_op jit(solution)/shard_map/ppermute | solution.py:198
  8.2 2.9 %hold.3 = (bf16[2048,768]{1,0:T(8,128)(2,1)S(1)}, bf16[768,2048]{1,0:T(8,128)(2,1)S(1)}) custom-call(bf16[2048,768]{1,0:T(8,128)(2,1)} %bitcast.14, bf16[768,2048]{1,0:T(8,128)(2,1)} %bitcast.16), custom_call_target="tpu_custom_call" | custom-call | tf_op jit(solution)/shard_map/hold/pallas_call | solution.py:87
  11.1 1.7 %copy-done = bf16[768,2048]{1,0:T(8,128)(2,1)} copy-done((bf16[768,2048]{1,0:T(8,128)(2,1)}, bf16[768,2048]{1,0:T(8,128)(2,1)S(1)}, u32[]{:S(2)}) %copy-start) | copy-done | bytes 3145752
  12.9 5.8 %collective-permute-done.5.a_ref = bf16[2064,128]{1,0:T(8,128)(2,1)} collective-permute-done((bf16[2064,128]{1,0:T(8,128)(2,1)}, bf16[2064,128]{1,0:T(8,128)(2,1)}, u32[]{:S(2)}, u32[]{:S(2)}) %collective-permute-start.5) | collective-permute-done | bytes 528416 | tf_op jit(solution)/shard_map/ppermute | solution.py:182
  18.7 1.8 %collective-permute-start.6 = (bf16[2064,128]{1,0:T(8,128)(2,1)}, bf16[2064,128]{1,0:T(8,128)(2,1)S(1)}, u32[]{:S(2)}, u32[]{:S(2)}) collective-permute-start(bf16[2064,128]{1,0:T(8,128)(2,1)} %collective-permute-done.5.a_ref), channel_id=1, source_target_pairs={{0,4},{1,5},{4,8},{5,9},{8,12},{9,13},{12,14},{13,15},{14,10},{15,... | collective-permute-start | bytes 1585160 | tf_op jit(solution)/shard_map/ppermute | solution.py:182
  20.7 2.9 %hold.4 = (bf16[2048,768]{1,0:T(8,128)(2,1)S(1)}, bf16[768,2048]{1,0:T(8,128)(2,1)S(1)}) custom-call(bf16[2048,768]{1,0:T(8,128)(2,1)} %collective-permute-done.2.refs_0_, bf16[768,2048]{1,0:T(8,128)(2,1)} %collective-permute-done.3.refs_1_), custom_call_target="tpu_custom_call" | custom-call | tf_op jit(solution)/shard_map/hold/pallas_call | solution.py:87
  23.6 6.4 %expert_part.14 = f32[128,2048]{1,0:T(8,128)S(1)} custom-call(s32[2]{0:T(128)S(1)} %pad_add_fusion.me_ref, bf16[2064,128]{1,0:T(8,128)(2,1)} %collective-permute-done.5.a_ref, bf16[2064,128]{1,0:T(8,128)(2,1)} %collective-permute-done.7.b_ref, bf16[2048,768]{1,0:T(8,128)(2,1)S(1)} %get-tuple-element.30.u0_ref, bf16[768,2048]{1,0:T(8,128)(2,1)S(1)} %copy-done.1, ...), custom_call_target="tpu_custom_call" | custom-call | flops 2415919104 | bytes 14680064 | tf_op jit(solution)/shard_map/expert_part/pallas_call | solution.py:134
  30.1 1.9 %collective-permute-start.18 = (bf16[64,2048]{1,0:T(8,128)(2,1)S(1)}, bf16[64,2048]{1,0:T(8,128)(2,1)S(1)}, u32[]{:S(2)}, u32[]{:S(2)}) collective-permute-start(bf16[64,2048]{1,0:T(8,128)(2,1)S(1)} %get-tuple-element.62), channel_id=1, source_target_pairs={{0,4},{1,5},{4,8},{5,9},{8,12},{9,13},{12,14},{13,15},{14,10},{15,... | collective-permute-start | bytes 786440 | tf_op jit(solution)/shard_map/ppermute | solution.py:182
  36.1 5.7 %expert_part.13 = f32[128,2048]{1,0:T(8,128)S(1)} custom-call(s32[2]{0:T(128)S(1)} %pad_add_fusion.me_ref, bf16[2064,128]{1,0:T(8,128)(2,1)S(1)} %collective-permute-done.6.a_ref, bf16[2064,128]{1,0:T(8,128)(2,1)S(1)} %collective-permute-done.8.b_ref, bf16[2048,768]{1,0:T(8,128)(2,1)S(1)} %get-tuple-element.30.u0_ref, bf16[768,2048]{1,0:T(8,128)(2,1)S(1)} %copy-done.1, ...), custom_call_target="tpu_custom_call" | custom-call | flops 2415919104 | bytes 14680064 | tf_op jit(solution)/shard_map/expert_part/pallas_call | solution.py:134
  44.0 6.4 %expert_part.8 = f32[128,2048]{1,0:T(8,128)S(1)} custom-call(s32[2]{0:T(128)S(1)} %pad_add_fusion.me_ref, bf16[2064,128]{1,0:T(8,128)(2,1)} %get-tuple-element.28.a_ref, bf16[2064,128]{1,0:T(8,128)(2,1)} %get-tuple-element.29.b_ref, bf16[2048,768]{1,0:T(8,128)(2,1)S(1)} %get-tuple-element.30.u0_ref, bf16[768,2048]{1,0:T(8,128)(2,1)S(1)} %copy-done.1, ...), custom_call_target="tpu_custom_call" | custom-call | flops 2415919104 | bytes 14680064 | tf_op jit(solution)/shard_map/expert_part/pallas_call | solution.py:134
  50.5 2.0 %collective-permute-done.10.b_ref = bf16[2064,128]{1,0:T(8,128)(2,1)S(1)} collective-permute-done((bf16[2064,128]{1,0:T(8,128)(2,1)S(1)}, bf16[2064,128]{1,0:T(8,128)(2,1)S(1)}, u32[]{:S(2)}, u32[]{:S(2)}) %collective-permute-start.10) | collective-permute-done | bytes 528416 | tf_op jit(solution)/shard_map/ppermute | solution.py:182
  54.5 5.7 %expert_part.12 = f32[128,2048]{1,0:T(8,128)S(1)} custom-call(s32[2]{0:T(128)S(1)} %pad_add_fusion.me_ref, bf16[2064,128]{1,0:T(8,128)(2,1)S(1)} %collective-permute-done.9.a_ref, bf16[2064,128]{1,0:T(8,128)(2,1)S(1)} %collective-permute-done.10.b_ref, bf16[2048,768]{1,0:T(8,128)(2,1)S(1)} %get-tuple-element.30.u0_ref, bf16[768,2048]{1,0:T(8,128)(2,1)S(1)} %copy-done.1, ...), custom_call_target="tpu_custom_call" | custom-call | flops 2415919104 | bytes 14680064 | tf_op jit(solution)/shard_map/expert_part/pallas_call | solution.py:134
  60.4 1.6 %collective-permute-start.20 = (bf16[64,2048]{1,0:T(8,128)(2,1)S(1)}, bf16[64,2048]{1,0:T(8,128)(2,1)S(1)}, u32[]{:S(2)}, u32[]{:S(2)}) collective-permute-start(bf16[64,2048]{1,0:T(8,128)(2,1)S(1)} %get-tuple-element.58), channel_id=1, source_target_pairs={{0,4},{1,5},{4,8},{5,9},{8,12},{9,13},{12,14},{13,15},{14,10},{15,... | collective-permute-start | bytes 786440 | tf_op jit(solution)/shard_map/ppermute | solution.py:182
  64.0 3.6 %collective-permute-done.11.a_ref = bf16[2064,128]{1,0:T(8,128)(2,1)S(1)} collective-permute-done((bf16[2064,128]{1,0:T(8,128)(2,1)S(1)}, bf16[2064,128]{1,0:T(8,128)(2,1)S(1)}, u32[]{:S(2)}, u32[]{:S(2)}) %collective-permute-start.11) | collective-permute-done | bytes 528416 | tf_op jit(solution)/shard_map/ppermute | solution.py:182
  67.6 1.8 %collective-permute-start.12 = (bf16[2064,128]{1,0:T(8,128)(2,1)S(1)}, bf16[2064,128]{1,0:T(8,128)(2,1)S(1)}, u32[]{:S(2)}, u32[]{:S(2)}) collective-permute-start(bf16[2064,128]{1,0:T(8,128)(2,1)S(1)} %collective-permute-done.11.a_ref), channel_id=1, source_target_pairs={{0,4},{1,5},{4,8},{5,9},{8,12},{9,13},{12,14},{13,15},{14,10},{15,... | collective-permute-start | bytes 1585160 | tf_op jit(solution)/shard_map/ppermute | solution.py:182
  69.7 5.7 %expert_part.11 = f32[128,2048]{1,0:T(8,128)S(1)} custom-call(s32[2]{0:T(128)S(1)} %pad_add_fusion.me_ref, bf16[2064,128]{1,0:T(8,128)(2,1)S(1)} %collective-permute-done.11.a_ref, bf16[2064,128]{1,0:T(8,128)(2,1)S(1)} %collective-permute-done.13.b_ref, bf16[2048,768]{1,0:T(8,128)(2,1)S(1)} %get-tuple-element.30.u0_ref, bf16[768,2048]{1,0:T(8,128)(2,1)S(1)} %copy-done.1, ...), custom_call_target="tpu_custom_call" | custom-call | flops 2415919104 | bytes 14680064 | tf_op jit(solution)/shard_map/expert_part/pallas_call | solution.py:134
  75.5 1.9 %collective-permute-start.21 = (bf16[64,2048]{1,0:T(8,128)(2,1)S(1)}, bf16[64,2048]{1,0:T(8,128)(2,1)S(1)}, u32[]{:S(2)}, u32[]{:S(2)}) collective-permute-start(bf16[64,2048]{1,0:T(8,128)(2,1)S(1)} %get-tuple-element.56), channel_id=1, source_target_pairs={{0,4},{1,5},{4,8},{5,9},{8,12},{9,13},{12,14},{13,15},{14,10},{15,... | collective-permute-start | bytes 786440 | tf_op jit(solution)/shard_map/ppermute | solution.py:182
  77.6 1.8 %collective-permute-start.4 = (bf16[128,2048]{1,0:T(8,128)(2,1)S(1)}, bf16[128,2048]{1,0:T(8,128)(2,1)S(1)}, u32[]{:S(2)}, u32[]{:S(2)}) collective-permute-start(bf16[128,2048]{1,0:T(8,128)(2,1)S(1)} %convert_element_type.77), channel_id=1, source_target_pairs={{0,16},{16,0},{1,17},{17,1},{2,18},{18,2},{3,19},{19,3},{4,20},{20... | collective-permute-start | bytes 1572872 | tf_op jit(solution)/shard_map/ppermute | solution.py:198
  79.4 5.2 %collective-permute-done.12.a_ref = bf16[2064,128]{1,0:T(8,128)(2,1)S(1)} collective-permute-done((bf16[2064,128]{1,0:T(8,128)(2,1)S(1)}, bf16[2064,128]{1,0:T(8,128)(2,1)S(1)}, u32[]{:S(2)}, u32[]{:S(2)}) %collective-permute-start.12) | collective-permute-done | bytes 528416 | tf_op jit(solution)/shard_map/ppermute | solution.py:182
  84.6 1.8 %collective-permute-done.14.b_ref = bf16[2064,128]{1,0:T(8,128)(2,1)S(1)} collective-permute-done((bf16[2064,128]{1,0:T(8,128)(2,1)S(1)}, bf16[2064,128]{1,0:T(8,128)(2,1)S(1)}, u32[]{:S(2)}, u32[]{:S(2)}) %collective-permute-start.14) | collective-permute-done | bytes 528416 | tf_op jit(solution)/shard_map/ppermute | solution.py:182
  88.4 5.7 %expert_part.10 = f32[128,2048]{1,0:T(8,128)S(1)} custom-call(s32[2]{0:T(128)S(1)} %pad_add_fusion.me_ref, bf16[2064,128]{1,0:T(8,128)(2,1)S(1)} %collective-permute-done.12.a_ref, bf16[2064,128]{1,0:T(8,128)(2,1)S(1)} %collective-permute-done.14.b_ref, bf16[2048,768]{1,0:T(8,128)(2,1)S(1)} %get-tuple-element.30.u0_ref, bf16[768,2048]{1,0:T(8,128)(2,1)S(1)} %copy-done.1, ...), custom_call_target="tpu_custom_call" | custom-call | flops 2415919104 | bytes 14680064 | tf_op jit(solution)/shard_map/expert_part/pallas_call | solution.py:134
  96.4 5.1 %collective-permute-done.15.a_ref = bf16[2064,128]{1,0:T(8,128)(2,1)S(1)} collective-permute-done((bf16[2064,128]{1,0:T(8,128)(2,1)S(1)}, bf16[2064,128]{1,0:T(8,128)(2,1)S(1)}, u32[]{:S(2)}, u32[]{:S(2)}) %collective-permute-start.15) | collective-permute-done | bytes 528416 | tf_op jit(solution)/shard_map/ppermute | solution.py:182
  101.5 1.8 %collective-permute-done.16.b_ref = bf16[2064,128]{1,0:T(8,128)(2,1)S(1)} collective-permute-done((bf16[2064,128]{1,0:T(8,128)(2,1)S(1)}, bf16[2064,128]{1,0:T(8,128)(2,1)S(1)}, u32[]{:S(2)}, u32[]{:S(2)}) %collective-permute-start.16) | collective-permute-done | bytes 528416 | tf_op jit(solution)/shard_map/ppermute | solution.py:182
  103.5 1.8 %collective-permute-start.17 = (bf16[2064,128]{1,0:T(8,128)(2,1)S(1)}, bf16[2064,128]{1,0:T(8,128)(2,1)S(1)}, u32[]{:S(2)}, u32[]{:S(2)}) collective-permute-start(bf16[2064,128]{1,0:T(8,128)(2,1)S(1)} %collective-permute-done.15.a_ref), channel_id=1, source_target_pairs={{0,4},{1,5},{4,8},{5,9},{8,12},{9,13},{12,14},{13,15},{14,10},{15,... | collective-permute-start | bytes 1585160 | tf_op jit(solution)/shard_map/ppermute | solution.py:182
  105.4 5.7 %expert_part.9 = f32[128,2048]{1,0:T(8,128)S(1)} custom-call(s32[2]{0:T(128)S(1)} %pad_add_fusion.me_ref, bf16[2064,128]{1,0:T(8,128)(2,1)S(1)} %collective-permute-done.15.a_ref, bf16[2064,128]{1,0:T(8,128)(2,1)S(1)} %collective-permute-done.16.b_ref, bf16[2048,768]{1,0:T(8,128)(2,1)S(1)} %get-tuple-element.30.u0_ref, bf16[768,2048]{1,0:T(8,128)(2,1)S(1)} %copy-done.1, ...), custom_call_target="tpu_custom_call" | custom-call | flops 2415919104 | bytes 14680064 | tf_op jit(solution)/shard_map/expert_part/pallas_call | solution.py:134
  111.2 7.0 %collective-permute-done.23.b_ref = bf16[2064,128]{1,0:T(8,128)(2,1)S(1)} collective-permute-done((bf16[2064,128]{1,0:T(8,128)(2,1)S(1)}, bf16[2064,128]{1,0:T(8,128)(2,1)S(1)}, u32[]{:S(2)}, u32[]{:S(2)}) %collective-permute-start.23) | collective-permute-done | bytes 528416 | tf_op jit(solution)/shard_map/ppermute | solution.py:182
  120.2 5.7 %expert_part.15 = f32[128,2048]{1,0:T(8,128)S(1)} custom-call(s32[2]{0:T(128)S(1)} %pad_add_fusion.me_ref, bf16[2064,128]{1,0:T(8,128)(2,1)S(1)} %collective-permute-done.17.a_ref, bf16[2064,128]{1,0:T(8,128)(2,1)S(1)} %collective-permute-done.23.b_ref, bf16[2048,768]{1,0:T(8,128)(2,1)S(1)} %get-tuple-element.30.u0_ref, bf16[768,2048]{1,0:T(8,128)(2,1)S(1)} %copy-done.1, ...), custom_call_target="tpu_custom_call" | custom-call | flops 2415919104 | bytes 14680064 | tf_op jit(solution)/shard_map/expert_part/pallas_call | solution.py:134
  126.1 2.6 %collective-permute-start.30 = (bf16[64,2048]{1,0:T(8,128)(2,1)S(1)}, bf16[64,2048]{1,0:T(8,128)(2,1)S(1)}, u32[]{:S(2)}, u32[]{:S(2)}) collective-permute-start(bf16[64,2048]{1,0:T(8,128)(2,1)S(1)} %get-tuple-element.50), channel_id=1, source_target_pairs={{0,20},{1,21},{4,24},{5,25},{8,28},{9,29},{12,30},{13,31},{14,26},... | collective-permute-start | bytes 786440 | tf_op jit(solution)/shard_map/ppermute | solution.py:186
  130.5 5.8 %collective-permute-done.30.a_ref = bf16[64,2048]{1,0:T(8,128)(2,1)S(1)} collective-permute-done((bf16[64,2048]{1,0:T(8,128)(2,1)S(1)}, bf16[64,2048]{1,0:T(8,128)(2,1)S(1)}, u32[]{:S(2)}, u32[]{:S(2)}) %collective-permute-start.30) | collective-permute-done | bytes 262176 | tf_op jit(solution)/shard_map/ppermute | solution.py:186
  136.3 2.1 %collective-permute-done.32.b_ref = bf16[64,2048]{1,0:T(8,128)(2,1)S(1)} collective-permute-done((bf16[64,2048]{1,0:T(8,128)(2,1)S(1)}, bf16[64,2048]{1,0:T(8,128)(2,1)S(1)}, u32[]{:S(2)}, u32[]{:S(2)}) %collective-permute-start.32) | collective-permute-done | bytes 262176 | tf_op jit(solution)/shard_map/ppermute | solution.py:186
  (67 shorter events, 21.9 us)
Async XLA Ops:
  0.0 20.7 %collective-permute-start.2 = (bf16[2048,768]{1,0:T(8,128)(2,1)}, bf16[2048,768]{1,0:T(8,128)(2,1)}, u32[]{:S(2)}, u32[]{:S(2)}) collective-permute-start(bf16[2048,768]{1,0:T(8,128)(2,1)} %bitcast.13), channel_id=1, source_target_pairs={{0,1},{1,0},{2,3},{3,2},{4,5},{5,4},{6,7},{7,6},{8,9},{9,8},{10,11... | collective-permute-start | bytes 9437192 | tf_op jit(solution)/shard_map/ppermute | solution.py:201
  0.5 20.2 %collective-permute-start.3 = (bf16[768,2048]{1,0:T(8,128)(2,1)}, bf16[768,2048]{1,0:T(8,128)(2,1)}, u32[]{:S(2)}, u32[]{:S(2)}) collective-permute-start(bf16[768,2048]{1,0:T(8,128)(2,1)} %bitcast.15), channel_id=1, source_target_pairs={{0,1},{1,0},{2,3},{3,2},{4,5},{5,4},{6,7},{7,6},{8,9},{9,8},{10,11... | collective-permute-start | bytes 9437192 | tf_op jit(solution)/shard_map/ppermute | solution.py:201
  3.2 15.5 %collective-permute-start.5 = (bf16[2064,128]{1,0:T(8,128)(2,1)}, bf16[2064,128]{1,0:T(8,128)(2,1)}, u32[]{:S(2)}, u32[]{:S(2)}) collective-permute-start(bf16[2064,128]{1,0:T(8,128)(2,1)} %get-tuple-element.28.a_ref), channel_id=1, source_target_pairs={{0,4},{1,5},{4,8},{5,9},{8,12},{9,13},{12,14},{13,15},{14,10},{15,... | collective-permute-start | bytes 1585160 | tf_op jit(solution)/shard_map/ppermute | solution.py:182
  6.2 14.2 %collective-permute-start.7 = (bf16[2064,128]{1,0:T(8,128)(2,1)}, bf16[2064,128]{1,0:T(8,128)(2,1)}, u32[]{:S(2)}, u32[]{:S(2)}) collective-permute-start(bf16[2064,128]{1,0:T(8,128)(2,1)} %get-tuple-element.29.b_ref), channel_id=1, source_target_pairs={{0,2},{1,3},{4,0},{5,1},{8,4},{9,5},{12,8},{13,9},{14,12},{15,13},... | collective-permute-start | bytes 1585160 | tf_op jit(solution)/shard_map/ppermute | solution.py:182
  6.3 25.9 %collective-permute-start = (bf16[144,2048]{1,0:T(8,128)(2,1)}, bf16[144,2048]{1,0:T(8,128)(2,1)}, u32[]{:S(2)}, u32[]{:S(2)}) collective-permute-start(bf16[144,2048]{1,0:T(8,128)(2,1)} %get-tuple-element.27), channel_id=1, source_target_pairs={{0,16},{16,0},{1,17},{17,1},{2,18},{18,2},{3,19},{19,3},{4,20},{20... | collective-permute-start | bytes 1769480 | tf_op jit(solution)/shard_map/ppermute | solution.py:198
  18.7 14.2 %collective-permute-start.6 = (bf16[2064,128]{1,0:T(8,128)(2,1)}, bf16[2064,128]{1,0:T(8,128)(2,1)S(1)}, u32[]{:S(2)}, u32[]{:S(2)}) collective-permute-start(bf16[2064,128]{1,0:T(8,128)(2,1)} %collective-permute-done.5.a_ref), channel_id=1, source_target_pairs={{0,4},{1,5},{4,8},{5,9},{8,12},{9,13},{12,14},{13,15},{14,10},{15,... | collective-permute-start | bytes 1585160 | tf_op jit(solution)/shard_map/ppermute | solution.py:182
  20.5 13.6 %collective-permute-start.8 = (bf16[2064,128]{1,0:T(8,128)(2,1)}, bf16[2064,128]{1,0:T(8,128)(2,1)S(1)}, u32[]{:S(2)}, u32[]{:S(2)}) collective-permute-start(bf16[2064,128]{1,0:T(8,128)(2,1)} %collective-permute-done.7.b_ref), channel_id=1, source_target_pairs={{0,2},{1,3},{4,0},{5,1},{8,4},{9,5},{12,8},{13,9},{14,12},{15,13},... | collective-permute-start | bytes 1585160 | tf_op jit(solution)/shard_map/ppermute | solution.py:182
  30.1 11.7 %collective-permute-start.18 = (bf16[64,2048]{1,0:T(8,128)(2,1)S(1)}, bf16[64,2048]{1,0:T(8,128)(2,1)S(1)}, u32[]{:S(2)}, u32[]{:S(2)}) collective-permute-start(bf16[64,2048]{1,0:T(8,128)(2,1)S(1)} %get-tuple-element.62), channel_id=1, source_target_pairs={{0,4},{1,5},{4,8},{5,9},{8,12},{9,13},{12,14},{13,15},{14,10},{15,... | collective-permute-start | bytes 786440 | tf_op jit(solution)/shard_map/ppermute | solution.py:182
  31.9 9.9 %collective-permute-start.24 = (bf16[64,2048]{1,0:T(8,128)(2,1)S(1)}, bf16[64,2048]{1,0:T(8,128)(2,1)S(1)}, u32[]{:S(2)}, u32[]{:S(2)}) collective-permute-start(bf16[64,2048]{1,0:T(8,128)(2,1)S(1)} %get-tuple-element.61), channel_id=1, source_target_pairs={{0,2},{1,3},{4,0},{5,1},{8,4},{9,5},{12,8},{13,9},{14,12},{15,13},... | collective-permute-start | bytes 786440 | tf_op jit(solution)/shard_map/ppermute | solution.py:182
  34.1 18.5 %collective-permute-start.10 = (bf16[2064,128]{1,0:T(8,128)(2,1)S(1)}, bf16[2064,128]{1,0:T(8,128)(2,1)S(1)}, u32[]{:S(2)}, u32[]{:S(2)}) collective-permute-start(bf16[2064,128]{1,0:T(8,128)(2,1)S(1)} %collective-permute-done.8.b_ref), channel_id=1, source_target_pairs={{0,2},{1,3},{4,0},{5,1},{8,4},{9,5},{12,8},{13,9},{14,12},{15,13},... | collective-permute-start | bytes 1585160 | tf_op jit(solution)/shard_map/ppermute | solution.py:182
  34.6 17.9 %collective-permute-start.9 = (bf16[2064,128]{1,0:T(8,128)(2,1)S(1)}, bf16[2064,128]{1,0:T(8,128)(2,1)S(1)}, u32[]{:S(2)}, u32[]{:S(2)}) collective-permute-start(bf16[2064,128]{1,0:T(8,128)(2,1)S(1)} %collective-permute-done.6.a_ref), channel_id=1, source_target_pairs={{0,4},{1,5},{4,8},{5,9},{8,12},{9,13},{12,14},{13,15},{14,10},{15,... | collective-permute-start | bytes 1585160 | tf_op jit(solution)/shard_map/ppermute | solution.py:182
  41.9 18.3 %collective-permute-start.19 = (bf16[64,2048]{1,0:T(8,128)(2,1)S(1)}, bf16[64,2048]{1,0:T(8,128)(2,1)S(1)}, u32[]{:S(2)}, u32[]{:S(2)}) collective-permute-start(bf16[64,2048]{1,0:T(8,128)(2,1)S(1)} %get-tuple-element.60), channel_id=1, source_target_pairs={{0,4},{1,5},{4,8},{5,9},{8,12},{9,13},{12,14},{13,15},{14,10},{15,... | collective-permute-start | bytes 786440 | tf_op jit(solution)/shard_map/ppermute | solution.py:182
  43.6 16.7 %collective-permute-start.25 = (bf16[64,2048]{1,0:T(8,128)(2,1)S(1)}, bf16[64,2048]{1,0:T(8,128)(2,1)S(1)}, u32[]{:S(2)}, u32[]{:S(2)}) collective-permute-start(bf16[64,2048]{1,0:T(8,128)(2,1)S(1)} %get-tuple-element.59), channel_id=1, source_target_pairs={{0,2},{1,3},{4,0},{5,1},{8,4},{9,5},{12,8},{13,9},{14,12},{15,13},... | collective-permute-start | bytes 786440 | tf_op jit(solution)/shard_map/ppermute | solution.py:182
  52.5 15.1 %collective-permute-start.11 = (bf16[2064,128]{1,0:T(8,128)(2,1)S(1)}, bf16[2064,128]{1,0:T(8,128)(2,1)S(1)}, u32[]{:S(2)}, u32[]{:S(2)}) collective-permute-start(bf16[2064,128]{1,0:T(8,128)(2,1)S(1)} %collective-permute-done.9.a_ref), channel_id=1, source_target_pairs={{0,4},{1,5},{4,8},{5,9},{8,12},{9,13},{12,14},{13,15},{14,10},{15,... | collective-permute-start | bytes 1585160 | tf_op jit(solution)/shard_map/ppermute | solution.py:182
  54.1 15.4 %collective-permute-start.13 = (bf16[2064,128]{1,0:T(8,128)(2,1)S(1)}, bf16[2064,128]{1,0:T(8,128)(2,1)S(1)}, u32[]{:S(2)}, u32[]{:S(2)}) collective-permute-start(bf16[2064,128]{1,0:T(8,128)(2,1)S(1)} %collective-permute-done.10.b_ref), channel_id=1, source_target_pairs={{0,2},{1,3},{4,0},{5,1},{8,4},{9,5},{12,8},{13,9},{14,12},{15,13},... | collective-permute-start | bytes 1585160 | tf_op jit(solution)/shard_map/ppermute | solution.py:182
  60.4 15.0 %collective-permute-start.20 = (bf16[64,2048]{1,0:T(8,128)(2,1)S(1)}, bf16[64,2048]{1,0:T(8,128)(2,1)S(1)}, u32[]{:S(2)}, u32[]{:S(2)}) collective-permute-start(bf16[64,2048]{1,0:T(8,128)(2,1)S(1)} %get-tuple-element.58), channel_id=1, source_target_pairs={{0,4},{1,5},{4,8},{5,9},{8,12},{9,13},{12,14},{13,15},{14,10},{15,... | collective-permute-start | bytes 786440 | tf_op jit(solution)/shard_map/ppermute | solution.py:182
  62.0 13.4 %collective-permute-start.26 = (bf16[64,2048]{1,0:T(8,128)(2,1)S(1)}, bf16[64,2048]{1,0:T(8,128)(2,1)S(1)}, u32[]{:S(2)}, u32[]{:S(2)}) collective-permute-start(bf16[64,2048]{1,0:T(8,128)(2,1)S(1)} %get-tuple-element.57), channel_id=1, source_target_pairs={{0,2},{1,3},{4,0},{5,1},{8,4},{9,5},{12,8},{13,9},{14,12},{15,13},... | collective-permute-start | bytes 786440 | tf_op jit(solution)/shard_map/ppermute | solution.py:182
  62.5 15.1 %collective-permute-start.1 = (bf16[128,2048]{1,0:T(8,128)(2,1)S(1)}, bf16[128,2048]{1,0:T(8,128)(2,1)S(1)}, u32[]{:S(2)}, u32[]{:S(2)}) collective-permute-start(bf16[128,2048]{1,0:T(8,128)(2,1)S(1)} %bitcast.19), channel_id=1, source_target_pairs={{0,16},{16,0},{1,17},{17,1},{2,18},{18,2},{3,19},{19,3},{4,20},{20... | collective-permute-start | bytes 1572872 | tf_op jit(solution)/shard_map/ppermute | solution.py:198
  67.6 16.9 %collective-permute-start.12 = (bf16[2064,128]{1,0:T(8,128)(2,1)S(1)}, bf16[2064,128]{1,0:T(8,128)(2,1)S(1)}, u32[]{:S(2)}, u32[]{:S(2)}) collective-permute-start(bf16[2064,128]{1,0:T(8,128)(2,1)S(1)} %collective-permute-done.11.a_ref), channel_id=1, source_target_pairs={{0,4},{1,5},{4,8},{5,9},{8,12},{9,13},{12,14},{13,15},{14,10},{15,... | collective-permute-start | bytes 1585160 | tf_op jit(solution)/shard_map/ppermute | solution.py:182
  69.5 16.9 %collective-permute-start.14 = (bf16[2064,128]{1,0:T(8,128)(2,1)S(1)}, bf16[2064,128]{1,0:T(8,128)(2,1)S(1)}, u32[]{:S(2)}, u32[]{:S(2)}) collective-permute-start(bf16[2064,128]{1,0:T(8,128)(2,1)S(1)} %collective-permute-done.13.b_ref), channel_id=1, source_target_pairs={{0,2},{1,3},{4,0},{5,1},{8,4},{9,5},{12,8},{13,9},{14,12},{15,13},... | collective-permute-start | bytes 1585160 | tf_op jit(solution)/shard_map/ppermute | solution.py:182
  75.5 18.6 %collective-permute-start.21 = (bf16[64,2048]{1,0:T(8,128)(2,1)S(1)}, bf16[64,2048]{1,0:T(8,128)(2,1)S(1)}, u32[]{:S(2)}, u32[]{:S(2)}) collective-permute-start(bf16[64,2048]{1,0:T(8,128)(2,1)S(1)} %get-tuple-element.56), channel_id=1, source_target_pairs={{0,4},{1,5},{4,8},{5,9},{8,12},{9,13},{12,14},{13,15},{14,10},{15,... | collective-permute-start | bytes 786440 | tf_op jit(solution)/shard_map/ppermute | solution.py:182
  77.4 16.8 %collective-permute-start.27 = (bf16[64,2048]{1,0:T(8,128)(2,1)S(1)}, bf16[64,2048]{1,0:T(8,128)(2,1)S(1)}, u32[]{:S(2)}, u32[]{:S(2)}) collective-permute-start(bf16[64,2048]{1,0:T(8,128)(2,1)S(1)} %get-tuple-element.55), channel_id=1, source_target_pairs={{0,2},{1,3},{4,0},{5,1},{8,4},{9,5},{12,8},{13,9},{14,12},{15,13},... | collective-permute-start | bytes 786440 | tf_op jit(solution)/shard_map/ppermute | solution.py:182
  77.6 18.8 %collective-permute-start.4 = (bf16[128,2048]{1,0:T(8,128)(2,1)S(1)}, bf16[128,2048]{1,0:T(8,128)(2,1)S(1)}, u32[]{:S(2)}, u32[]{:S(2)}) collective-permute-start(bf16[128,2048]{1,0:T(8,128)(2,1)S(1)} %convert_element_type.77), channel_id=1, source_target_pairs={{0,16},{16,0},{1,17},{17,1},{2,18},{18,2},{3,19},{19,3},{4,20},{20... | collective-permute-start | bytes 1572872 | tf_op jit(solution)/shard_map/ppermute | solution.py:198
  86.4 15.1 %collective-permute-start.15 = (bf16[2064,128]{1,0:T(8,128)(2,1)S(1)}, bf16[2064,128]{1,0:T(8,128)(2,1)S(1)}, u32[]{:S(2)}, u32[]{:S(2)}) collective-permute-start(bf16[2064,128]{1,0:T(8,128)(2,1)S(1)} %collective-permute-done.12.a_ref), channel_id=1, source_target_pairs={{0,4},{1,5},{4,8},{5,9},{8,12},{9,13},{12,14},{13,15},{14,10},{15,... | collective-permute-start | bytes 1585160 | tf_op jit(solution)/shard_map/ppermute | solution.py:182
  88.0 15.4 %collective-permute-start.16 = (bf16[2064,128]{1,0:T(8,128)(2,1)S(1)}, bf16[2064,128]{1,0:T(8,128)(2,1)S(1)}, u32[]{:S(2)}, u32[]{:S(2)}) collective-permute-start(bf16[2064,128]{1,0:T(8,128)(2,1)S(1)} %collective-permute-done.14.b_ref), channel_id=1, source_target_pairs={{0,2},{1,3},{4,0},{5,1},{8,4},{9,5},{12,8},{13,9},{14,12},{15,13},... | collective-permute-start | bytes 1585160 | tf_op jit(solution)/shard_map/ppermute | solution.py:182
  94.3 16.8 %collective-permute-start.22 = (bf16[64,2048]{1,0:T(8,128)(2,1)S(1)}, bf16[64,2048]{1,0:T(8,128)(2,1)S(1)}, u32[]{:S(2)}, u32[]{:S(2)}) collective-permute-start(bf16[64,2048]{1,0:T(8,128)(2,1)S(1)} %get-tuple-element.54), channel_id=1, source_target_pairs={{0,4},{1,5},{4,8},{5,9},{8,12},{9,13},{12,14},{13,15},{14,10},{15,... | collective-permute-start | bytes 786440 | tf_op jit(solution)/shard_map/ppermute | solution.py:182
  95.9 15.2 %collective-permute-start.28 = (bf16[64,2048]{1,0:T(8,128)(2,1)S(1)}, bf16[64,2048]{1,0:T(8,128)(2,1)S(1)}, u32[]{:S(2)}, u32[]{:S(2)}) collective-permute-start(bf16[64,2048]{1,0:T(8,128)(2,1)S(1)} %get-tuple-element.53), channel_id=1, source_target_pairs={{0,2},{1,3},{4,0},{5,1},{8,4},{9,5},{12,8},{13,9},{14,12},{15,13},... | collective-permute-start | bytes 786440 | tf_op jit(solution)/shard_map/ppermute | solution.py:182
  103.3 14.9 %collective-permute-start.23 = (bf16[2064,128]{1,0:T(8,128)(2,1)S(1)}, bf16[2064,128]{1,0:T(8,128)(2,1)S(1)}, u32[]{:S(2)}, u32[]{:S(2)}) collective-permute-start(bf16[2064,128]{1,0:T(8,128)(2,1)S(1)} %collective-permute-done.16.b_ref), channel_id=1, source_target_pairs={{0,2},{1,3},{4,0},{5,1},{8,4},{9,5},{12,8},{13,9},{14,12},{15,13},... | collective-permute-start | bytes 1585160 | tf_op jit(solution)/shard_map/ppermute | solution.py:182
  103.5 14.7 %collective-permute-start.17 = (bf16[2064,128]{1,0:T(8,128)(2,1)S(1)}, bf16[2064,128]{1,0:T(8,128)(2,1)S(1)}, u32[]{:S(2)}, u32[]{:S(2)}) collective-permute-start(bf16[2064,128]{1,0:T(8,128)(2,1)S(1)} %collective-permute-done.15.a_ref), channel_id=1, source_target_pairs={{0,4},{1,5},{4,8},{5,9},{8,12},{9,13},{12,14},{13,15},{14,10},{15,... | collective-permute-start | bytes 1585160 | tf_op jit(solution)/shard_map/ppermute | solution.py:182
  118.2 7.8 %collective-permute-start.31 = (bf16[64,2048]{1,0:T(8,128)(2,1)S(1)}, bf16[64,2048]{1,0:T(8,128)(2,1)S(1)}, u32[]{:S(2)}, u32[]{:S(2)}) collective-permute-start(bf16[64,2048]{1,0:T(8,128)(2,1)S(1)} %get-tuple-element.48), channel_id=1, source_target_pairs={{0,2},{1,3},{4,0},{5,1},{8,4},{9,5},{12,8},{13,9},{14,12},{15,13},... | collective-permute-start | bytes 786440 | tf_op jit(solution)/shard_map/ppermute | solution.py:182
  126.1 10.2 %collective-permute-start.30 = (bf16[64,2048]{1,0:T(8,128)(2,1)S(1)}, bf16[64,2048]{1,0:T(8,128)(2,1)S(1)}, u32[]{:S(2)}, u32[]{:S(2)}) collective-permute-start(bf16[64,2048]{1,0:T(8,128)(2,1)S(1)} %get-tuple-element.50), channel_id=1, source_target_pairs={{0,20},{1,21},{4,24},{5,25},{8,28},{9,29},{12,30},{13,31},{14,26},... | collective-permute-start | bytes 786440 | tf_op jit(solution)/shard_map/ppermute | solution.py:186
  128.7 9.7 %collective-permute-start.32 = (bf16[64,2048]{1,0:T(8,128)(2,1)S(1)}, bf16[64,2048]{1,0:T(8,128)(2,1)S(1)}, u32[]{:S(2)}, u32[]{:S(2)}) collective-permute-start(bf16[64,2048]{1,0:T(8,128)(2,1)S(1)} %get-tuple-element.49), channel_id=1, source_target_pairs={{0,18},{1,19},{4,16},{5,17},{8,20},{9,21},{12,24},{13,25},{14,28},... | collective-permute-start | bytes 786440 | tf_op jit(solution)/shard_map/ppermute | solution.py:186
  (6 other events, 62.9 us)

commit v6 on v5

--- a/solution.py
+++ b/solution.py
@@ -8,7 +8,6 @@
 epsilon = 1e-06
 LANES = 128
 VMEM = 16 << 20
-NT = (((1,), (1,)), ((), ()))
 
 
 def pack_kernel(x_hbm, grad_hbm, gain_hbm, routes_hbm, gates_hbm, a_ref, b_ref, keep_ref, grad_s, gain_s, routes_s, gates_s, sems):
@@ -95,7 +94,34 @@
     )(*(pltpu.with_memory_space_constraint(value, pltpu.HBM) for value in values))
 
 
-def expert_kernel(me_ref, a_ref, b_ref, u0_ref, d0_ref, u1_ref, d1_ref, o_ref):
+def turn_kernel(up_hbm, down_hbm, up_ref, up_t_ref, down_t_ref, down_ref, sems):
+    copies = [
+        pltpu.make_async_copy(up_hbm, up_ref, sems.at[0]),
+        pltpu.make_async_copy(down_hbm, down_ref, sems.at[1]),
+    ]
+    for copy in copies:
+        copy.start()
+    for copy, value, turned in zip(copies, (up_ref, down_ref), (up_t_ref, down_t_ref)):
+        copy.wait()
+        for first in range(0, value.shape[0], 256):
+            turned[:, first : first + 256] = value[first : first + 256, :].T
+
+
+def turn(up, down):
+    whole = pl.BlockSpec(memory_space=pltpu.VMEM)
+    return pl.pallas_call(
+        turn_kernel,
+        out_shape=[pltpu.VMEM(shape, up.dtype) for shape in (up.shape, up.shape[::-1], down.shape[::-1])],
+        in_specs=[pl.BlockSpec(memory_space=pltpu.HBM)] * 2,
+        out_specs=[whole] * 3,
+        scratch_shapes=[pltpu.VMEM(down.shape, down.dtype), pltpu.SemaphoreType.DMA((2,))],
+        compiler_params=pltpu.CompilerParams(vmem_limit_bytes=VMEM),
+        name="turn",
+    )(*(pltpu.with_memory_space_constraint(value, pltpu.HBM) for value in (up, down)))
+
+
+def expert_kernel(me_ref, a_ref, b_ref, *refs):
+    o_ref = refs[-1]
     rows, width = o_ref.shape
     half, slabs = rows // 2, width // LANES
 
@@ -113,12 +139,12 @@
     expert = lax.broadcasted_iota(jnp.int32, dense.shape, 0)
     square = (rows, rows)
     on_line = lax.broadcasted_iota(jnp.int32, square, 0) == lax.broadcasted_iota(jnp.int32, square, 1)
-    for i, (u_ref, d_ref) in enumerate(((u0_ref, d0_ref), (u1_ref, d1_ref))):
-        before = jnp.dot(normed, u_ref[...], preferred_element_type=jnp.float32)
-        d_hidden = lax.dot_general(grad, d_ref[...], NT, preferred_element_type=jnp.float32)
+    for i, (up_ref, up_t_ref, down_t_ref) in enumerate((refs[:3], refs[3:6])):
+        before = jnp.dot(normed, up_ref[...], preferred_element_type=jnp.float32)
+        d_hidden = jnp.dot(grad, down_t_ref[...], preferred_element_type=jnp.float32)
         sigmoid_of = jax.nn.sigmoid(before)
         d_before = (d_hidden * sigmoid_of * (1.0 + before * (1.0 - sigmoid_of))).astype(jnp.bfloat16)
-        d_route = lax.dot_general(d_before, u_ref[...], NT, preferred_element_type=jnp.float32)
+        d_route = jnp.dot(d_before, up_t_ref[...], preferred_element_type=jnp.float32)
         named = jnp.sum(jnp.where(expert == me_ref[i], dense, 0.0), axis=0, keepdims=True)
         gate = jnp.sum(jnp.where(on_line, jnp.broadcast_to(named, square), 0.0), axis=-1, keepdims=True)
         part = d_route.astype(jnp.bfloat16).astype(jnp.float32) * gate
@@ -134,7 +160,7 @@
     return pl.pallas_call(
         expert_kernel,
         out_shape=jax.ShapeDtypeStruct((rows, width), jnp.float32),
-        in_specs=[pl.BlockSpec(memory_space=pltpu.SMEM)] + [whole] * 6,
+        in_specs=[pl.BlockSpec(memory_space=pltpu.SMEM)] + [whole] * 8,
         out_specs=whole,
         compiler_params=pltpu.CompilerParams(vmem_limit_bytes=VMEM),
         cost_estimate=pl.CostEstimate(
@@ -209,7 +235,7 @@
     u1, d1 = swap(u0), swap(d0)
     a, b, keep = pack(x, grad, norm_gain, bwd_routes[0], bwd_gates[0], experts)
     a1, b1 = hop(a, 1), hop(b, -1)
-    weights = (*hold(u0, d0), *hold(u1, d1))
+    weights = (*turn(u0, d0), *turn(u1, d1))
     own = expert_part(me, a, b, 2 * half, weights).astype(jnp.bfloat16)
     own_out, keep_out, grad_out = to_previous(own), to_previous(keep), to_previous(grad)
     early = {3: own, 2: keep_out, 5: grad_out, 6: own_out}

time: 140 us -> 139 us (level)
  Pallas kernels: 58.4 us -> 42.6 us
  waiting for transfers between devices: 42.2 us -> 55.3 us
  local copies, waits for them, and re-layouts: 1.74 us -> 3.51 us
    pallas_call x8, Pallas kernels: 47.1 us -> 29.5 us  [expert_part(): pl.pallas_call(expert_kernel, out_shape=jax.ShapeDtypeStruct((rows, width...]
    ppermute x26, waiting for transfers between devices: 34.3 us -> 47.7 us  [hop(): lax.ppermute(value, 'expert', [(2 * a + c, 2 * b + c) for a, b in moves f...]
    pallas_call x0 -> x2, Pallas kernels: none -> 7.45 us  [turn(): pl.pallas_call(turn_kernel, out_shape=[pltpu.VMEM(shape, up.dtype) for sh...]
    pallas_call x3 -> x1, Pallas kernels: 7.13 us -> 1.4 us  [hold(): pl.pallas_call(hold_kernel, out_shape=[pltpu.VMEM(value.shape, value.dtyp...]
    unnamed x10 -> x14, local copies, waits for them, and re-layouts: 1.71 us -> 3.47 us
  transfers between devices with their start and end apart: 33 -> 33, of which waited for: 12 -> 15; matrix products, arithmetic and copies ran while one was open for 1% -> 1% of each run, Pallas kernels for 41% -> 30%
where the time goes in v6:
time: 139 us
  waiting for transfers between devices  55.3 us (40%)
  Pallas kernels  42.6 us (31%)
  starting transfers between devices  36.1 us (26%)
  local copies, waits for them, and re-layouts  3.51 us (3%)
    ppermute x26, waiting for transfers between devices, hop(): lax.ppermute(value, 'expert', [(2 * a + c, 2 * b + c) for a, b in moves f...  47.7 us
    pallas_call x8, Pallas kernels, expert_part(): pl.pallas_call(expert_kernel, out_shape=jax.ShapeDtypeStruct((rows, width...  29.5 us
    ppermute x26, starting transfers between devices, hop(): lax.ppermute(value, 'expert', [(2 * a + c, 2 * b + c) for a, b in moves f...  27.7 us
    ppermute x2, waiting for transfers between devices, last_hop(): lax.ppermute(value, ('pipe', 'expert'), [(s * experts + 2 * a + c, (s - 1...  7.61 us
    pallas_call x2, Pallas kernels, turn(): pl.pallas_call(turn_kernel, out_shape=[pltpu.VMEM(shape, up.dtype) for sh...  7.45 us
    ppermute x3, starting transfers between devices, to_previous(): lax.ppermute(value, 'pipe', [(s, (s - 1) % sections) for s in range(secti...  5.01 us
    unnamed x14, local copies, waits for them, and re-layouts  3.47 us
    ppermute x2, starting transfers between devices, last_hop(): lax.ppermute(value, ('pipe', 'expert'), [(s * experts + 2 * a + c, (s - 1...  2.98 us
  transfers between devices with their start and end apart: 33, of which 15 were waited for; matrix products, arithmetic and copies ran while one was open for 1% of the time, Pallas kernels for 30%

profile of v6, /device:TPU:0, one launch (start us, length us, event | category | flops | bytes accessed | tf_op | source)
XLA Modules:
  0.0 138.7 jit_solution(1025211889540248572)
XLA Ops:
  0.5 2.6 %pack.1 = (bf16[2064,128]{1,0:T(8,128)(2,1)}, bf16[2064,128]{1,0:T(8,128)(2,1)}, bf16[144,2048]{1,0:T(8,128)(2,1)}) custom-call(bf16[128,2048]{1,0:T(8,128)(2,1)} %bitcast.17, bf16[128,2048]{1,0:T(8,128)(2,1)} %bitcast.18, f32[1,2048]{1,0:T(1,128)} %gain_hbm.1, s32[8,128]{1,0:T(8,128)} %bitcast.20, bf16[8,128]{1,0:T(8,128)(2,1)} %bitcast.21), custom_call_target="tpu_custom_call" | custom-call | tf_op jit(solution)/shard_map/pack/pallas_call | solution.py:59
  3.2 3.1 %collective-permute-start.5 = (bf16[2064,128]{1,0:T(8,128)(2,1)}, bf16[2064,128]{1,0:T(8,128)(2,1)}, u32[]{:S(2)}, u32[]{:S(2)}) collective-permute-start(bf16[2064,128]{1,0:T(8,128)(2,1)} %get-tuple-element.30.a_ref), channel_id=1, source_target_pairs={{0,4},{1,5},{4,8},{5,9},{8,12},{9,13},{12,14},{13,15},{14,10},{15,... | collective-permute-start | bytes 1585160 | tf_op jit(solution)/shard_map/ppermute | solution.py:208
  6.2 2.0 %collective-permute-start = (bf16[144,2048]{1,0:T(8,128)(2,1)}, bf16[144,2048]{1,0:T(8,128)(2,1)}, u32[]{:S(2)}, u32[]{:S(2)}) collective-permute-start(bf16[144,2048]{1,0:T(8,128)(2,1)} %get-tuple-element.29), channel_id=1, source_target_pairs={{0,16},{16,0},{1,17},{17,1},{2,18},{18,2},{3,19},{19,3},{4,20},{20... | collective-permute-start | bytes 1769480 | tf_op jit(solution)/shard_map/ppermute | solution.py:224
  8.2 3.7 %turn.2 = (bf16[2048,768]{1,0:T(8,128)(2,1)S(1)}, bf16[768,2048]{1,0:T(8,128)(2,1)S(1)}, bf16[2048,768]{1,0:T(8,128)(2,1)S(1)}) custom-call(bf16[2048,768]{1,0:T(8,128)(2,1)} %bitcast.14, bf16[768,2048]{1,0:T(8,128)(2,1)} %bitcast.16), custom_call_target="tpu_custom_call" | custom-call | tf_op jit(solution)/shard_map/turn/pallas_call | solution.py:112
  11.9 1.7 %copy-done = bf16[768,2048]{1,0:T(8,128)(2,1)} copy-done((bf16[768,2048]{1,0:T(8,128)(2,1)}, bf16[768,2048]{1,0:T(8,128)(2,1)S(1)}, u32[]{:S(2)}) %copy-start) | copy-done | bytes 3145752
  13.7 1.7 %copy-done.2 = bf16[2048,768]{1,0:T(8,128)(2,1)} copy-done((bf16[2048,768]{1,0:T(8,128)(2,1)}, bf16[2048,768]{1,0:T(8,128)(2,1)S(1)}, u32[]{:S(2)}) %copy-start.2) | copy-done | bytes 3145752
  15.5 3.2 %collective-permute-done.5.a_ref = bf16[2064,128]{1,0:T(8,128)(2,1)} collective-permute-done((bf16[2064,128]{1,0:T(8,128)(2,1)}, bf16[2064,128]{1,0:T(8,128)(2,1)}, u32[]{:S(2)}, u32[]{:S(2)}) %collective-permute-start.5) | collective-permute-done | bytes 528416 | tf_op jit(solution)/shard_map/ppermute | solution.py:208
  18.6 1.8 %collective-permute-start.6 = (bf16[2064,128]{1,0:T(8,128)(2,1)}, bf16[2064,128]{1,0:T(8,128)(2,1)S(1)}, u32[]{:S(2)}, u32[]{:S(2)}) collective-permute-start(bf16[2064,128]{1,0:T(8,128)(2,1)} %collective-permute-done.5.a_ref), channel_id=1, source_target_pairs={{0,4},{1,5},{4,8},{5,9},{8,12},{9,13},{12,14},{13,15},{14,10},{15,... | collective-permute-start | bytes 1585160 | tf_op jit(solution)/shard_map/ppermute | solution.py:208
  20.7 3.7 %turn.3 = (bf16[2048,768]{1,0:T(8,128)(2,1)S(1)}, bf16[768,2048]{1,0:T(8,128)(2,1)S(1)}, bf16[2048,768]{1,0:T(8,128)(2,1)S(1)}) custom-call(bf16[2048,768]{1,0:T(8,128)(2,1)} %collective-permute-done.2.up_hbm, bf16[768,2048]{1,0:T(8,128)(2,1)} %collective-permute-done.3.down_hbm), custom_call_target="tpu_custom_call" | custom-call | tf_op jit(solution)/shard_map/turn/pallas_call | solution.py:112
  24.4 4.1 %expert_part.14 = f32[128,2048]{1,0:T(8,128)S(1)} custom-call(s32[2]{0:T(128)S(1)} %pad_add_fusion.me_ref, bf16[2064,128]{1,0:T(8,128)(2,1)} %collective-permute-done.5.a_ref, bf16[2064,128]{1,0:T(8,128)(2,1)} %collective-permute-done.7.b_ref, bf16[2048,768]{1,0:T(8,128)(2,1)S(1)} %get-tuple-element.32.refs_0_, bf16[768,2048]{1,0:T(8,128)(2,1)S(1)} %copy-done.1, ...), custom_call_target="tpu_custom_call" | custom-call | flops 2415919104 | bytes 14680064 | tf_op jit(solution)/shard_map/expert_part/pallas_call | solution.py:160
  28.7 1.9 %collective-permute-start.18 = (bf16[64,2048]{1,0:T(8,128)(2,1)S(1)}, bf16[64,2048]{1,0:T(8,128)(2,1)S(1)}, u32[]{:S(2)}, u32[]{:S(2)}) collective-permute-start(bf16[64,2048]{1,0:T(8,128)(2,1)S(1)} %get-tuple-element.66), channel_id=1, source_target_pairs={{0,4},{1,5},{4,8},{5,9},{8,12},{9,13},{12,14},{13,15},{14,10},{15,... | collective-permute-start | bytes 786440 | tf_op jit(solution)/shard_map/ppermute | solution.py:208
  30.8 3.0 %collective-permute-done.6.a_ref = bf16[2064,128]{1,0:T(8,128)(2,1)S(1)} collective-permute-done((bf16[2064,128]{1,0:T(8,128)(2,1)}, bf16[2064,128]{1,0:T(8,128)(2,1)S(1)}, u32[]{:S(2)}, u32[]{:S(2)}) %collective-permute-start.6) | collective-permute-done | bytes 528416 | tf_op jit(solution)/shard_map/ppermute | solution.py:208
  37.4 3.5 %expert_part.13 = f32[128,2048]{1,0:T(8,128)S(1)} custom-call(s32[2]{0:T(128)S(1)} %pad_add_fusion.me_ref, bf16[2064,128]{1,0:T(8,128)(2,1)S(1)} %collective-permute-done.6.a_ref, bf16[2064,128]{1,0:T(8,128)(2,1)S(1)} %collective-permute-done.8.b_ref, bf16[2048,768]{1,0:T(8,128)(2,1)S(1)} %get-tuple-element.32.refs_0_, bf16[768,2048]{1,0:T(8,128)(2,1)S(1)} %copy-done.1, ...), custom_call_target="tpu_custom_call" | custom-call | flops 2415919104 | bytes 14680064 | tf_op jit(solution)/shard_map/expert_part/pallas_call | solution.py:160
  41.1 1.6 %collective-permute-start.19 = (bf16[64,2048]{1,0:T(8,128)(2,1)S(1)}, bf16[64,2048]{1,0:T(8,128)(2,1)S(1)}, u32[]{:S(2)}, u32[]{:S(2)}) collective-permute-start(bf16[64,2048]{1,0:T(8,128)(2,1)S(1)} %get-tuple-element.64), channel_id=1, source_target_pairs={{0,4},{1,5},{4,8},{5,9},{8,12},{9,13},{12,14},{13,15},{14,10},{15,... | collective-permute-start | bytes 786440 | tf_op jit(solution)/shard_map/ppermute | solution.py:208
  43.2 4.1 %expert_part.8 = f32[128,2048]{1,0:T(8,128)S(1)} custom-call(s32[2]{0:T(128)S(1)} %pad_add_fusion.me_ref, bf16[2064,128]{1,0:T(8,128)(2,1)} %get-tuple-element.30.a_ref, bf16[2064,128]{1,0:T(8,128)(2,1)} %get-tuple-element.31.b_ref, bf16[2048,768]{1,0:T(8,128)(2,1)S(1)} %get-tuple-element.32.refs_0_, bf16[768,2048]{1,0:T(8,128)(2,1)S(1)} %copy-done.1, ...), custom_call_target="tpu_custom_call" | custom-call | flops 2415919104 | bytes 14680064 | tf_op jit(solution)/shard_map/expert_part/pallas_call | solution.py:160
  47.4 4.9 %collective-permute-done.10.b_ref = bf16[2064,128]{1,0:T(8,128)(2,1)S(1)} collective-permute-done((bf16[2064,128]{1,0:T(8,128)(2,1)S(1)}, bf16[2064,128]{1,0:T(8,128)(2,1)S(1)}, u32[]{:S(2)}, u32[]{:S(2)}) %collective-permute-start.10) | collective-permute-done | bytes 528416 | tf_op jit(solution)/shard_map/ppermute | solution.py:208
  54.3 3.5 %expert_part.12 = f32[128,2048]{1,0:T(8,128)S(1)} custom-call(s32[2]{0:T(128)S(1)} %pad_add_fusion.me_ref, bf16[2064,128]{1,0:T(8,128)(2,1)S(1)} %collective-permute-done.9.a_ref, bf16[2064,128]{1,0:T(8,128)(2,1)S(1)} %collective-permute-done.10.b_ref, bf16[2048,768]{1,0:T(8,128)(2,1)S(1)} %get-tuple-element.32.refs_0_, bf16[768,2048]{1,0:T(8,128)(2,1)S(1)} %copy-done.1, ...), custom_call_target="tpu_custom_call" | custom-call | flops 2415919104 | bytes 14680064 | tf_op jit(solution)/shard_map/expert_part/pallas_call | solution.py:160
  58.1 1.6 %collective-permute-start.20 = (bf16[64,2048]{1,0:T(8,128)(2,1)S(1)}, bf16[64,2048]{1,0:T(8,128)(2,1)S(1)}, u32[]{:S(2)}, u32[]{:S(2)}) collective-permute-start(bf16[64,2048]{1,0:T(8,128)(2,1)S(1)} %get-tuple-element.62), channel_id=1, source_target_pairs={{0,4},{1,5},{4,8},{5,9},{8,12},{9,13},{12,14},{13,15},{14,10},{15,... | collective-permute-start | bytes 786440 | tf_op jit(solution)/shard_map/ppermute | solution.py:208
  61.7 6.0 %collective-permute-done.11.a_ref = bf16[2064,128]{1,0:T(8,128)(2,1)S(1)} collective-permute-done((bf16[2064,128]{1,0:T(8,128)(2,1)S(1)}, bf16[2064,128]{1,0:T(8,128)(2,1)S(1)}, u32[]{:S(2)}, u32[]{:S(2)}) %collective-permute-start.11) | collective-permute-done | bytes 528416 | tf_op jit(solution)/shard_map/ppermute | solution.py:208
  67.7 1.8 %collective-permute-start.12 = (bf16[2064,128]{1,0:T(8,128)(2,1)S(1)}, bf16[2064,128]{1,0:T(8,128)(2,1)S(1)}, u32[]{:S(2)}, u32[]{:S(2)}) collective-permute-start(bf16[2064,128]{1,0:T(8,128)(2,1)S(1)} %collective-permute-done.11.a_ref), channel_id=1, source_target_pairs={{0,4},{1,5},{4,8},{5,9},{8,12},{9,13},{12,14},{13,15},{14,10},{15,... | collective-permute-start | bytes 1585160 | tf_op jit(solution)/shard_map/ppermute | solution.py:208
  69.7 3.5 %expert_part.11 = f32[128,2048]{1,0:T(8,128)S(1)} custom-call(s32[2]{0:T(128)S(1)} %pad_add_fusion.me_ref, bf16[2064,128]{1,0:T(8,128)(2,1)S(1)} %collective-permute-done.11.a_ref, bf16[2064,128]{1,0:T(8,128)(2,1)S(1)} %collective-permute-done.13.b_ref, bf16[2048,768]{1,0:T(8,128)(2,1)S(1)} %get-tuple-element.32.refs_0_, bf16[768,2048]{1,0:T(8,128)(2,1)S(1)} %copy-done.1, ...), custom_call_target="tpu_custom_call" | custom-call | flops 2415919104 | bytes 14680064 | tf_op jit(solution)/shard_map/expert_part/pallas_call | solution.py:160
  75.0 1.6 %collective-permute-start.21 = (bf16[64,2048]{1,0:T(8,128)(2,1)S(1)}, bf16[64,2048]{1,0:T(8,128)(2,1)S(1)}, u32[]{:S(2)}, u32[]{:S(2)}) collective-permute-start(bf16[64,2048]{1,0:T(8,128)(2,1)S(1)} %get-tuple-element.60), channel_id=1, source_target_pairs={{0,4},{1,5},{4,8},{5,9},{8,12},{9,13},{12,14},{13,15},{14,10},{15,... | collective-permute-start | bytes 786440 | tf_op jit(solution)/shard_map/ppermute | solution.py:208
  78.6 6.0 %collective-permute-done.12.a_ref = bf16[2064,128]{1,0:T(8,128)(2,1)S(1)} collective-permute-done((bf16[2064,128]{1,0:T(8,128)(2,1)S(1)}, bf16[2064,128]{1,0:T(8,128)(2,1)S(1)}, u32[]{:S(2)}, u32[]{:S(2)}) %collective-permute-start.12) | collective-permute-done | bytes 528416 | tf_op jit(solution)/shard_map/ppermute | solution.py:208
  88.2 3.5 %expert_part.10 = f32[128,2048]{1,0:T(8,128)S(1)} custom-call(s32[2]{0:T(128)S(1)} %pad_add_fusion.me_ref, bf16[2064,128]{1,0:T(8,128)(2,1)S(1)} %collective-permute-done.12.a_ref, bf16[2064,128]{1,0:T(8,128)(2,1)S(1)} %collective-permute-done.14.b_ref, bf16[2048,768]{1,0:T(8,128)(2,1)S(1)} %get-tuple-element.32.refs_0_, bf16[768,2048]{1,0:T(8,128)(2,1)S(1)} %copy-done.1, ...), custom_call_target="tpu_custom_call" | custom-call | flops 2415919104 | bytes 14680064 | tf_op jit(solution)/shard_map/expert_part/pallas_call | solution.py:160
  91.9 1.6 %collective-permute-start.22 = (bf16[64,2048]{1,0:T(8,128)(2,1)S(1)}, bf16[64,2048]{1,0:T(8,128)(2,1)S(1)}, u32[]{:S(2)}, u32[]{:S(2)}) collective-permute-start(bf16[64,2048]{1,0:T(8,128)(2,1)S(1)} %get-tuple-element.58), channel_id=1, source_target_pairs={{0,4},{1,5},{4,8},{5,9},{8,12},{9,13},{12,14},{13,15},{14,10},{15,... | collective-permute-start | bytes 786440 | tf_op jit(solution)/shard_map/ppermute | solution.py:208
  94.0 7.5 %collective-permute-done.15.a_ref = bf16[2064,128]{1,0:T(8,128)(2,1)S(1)} collective-permute-done((bf16[2064,128]{1,0:T(8,128)(2,1)S(1)}, bf16[2064,128]{1,0:T(8,128)(2,1)S(1)}, u32[]{:S(2)}, u32[]{:S(2)}) %collective-permute-start.15) | collective-permute-done | bytes 528416 | tf_op jit(solution)/shard_map/ppermute | solution.py:208
  105.2 3.6 %expert_part.9 = f32[128,2048]{1,0:T(8,128)S(1)} custom-call(s32[2]{0:T(128)S(1)} %pad_add_fusion.me_ref, bf16[2064,128]{1,0:T(8,128)(2,1)S(1)} %collective-permute-done.15.a_ref, bf16[2064,128]{1,0:T(8,128)(2,1)S(1)} %collective-permute-done.16.b_ref, bf16[2048,768]{1,0:T(8,128)(2,1)S(1)} %get-tuple-element.32.refs_0_, bf16[768,2048]{1,0:T(8,128)(2,1)S(1)} %copy-done.1, ...), custom_call_target="tpu_custom_call" | custom-call | flops 2415919104 | bytes 14680064 | tf_op jit(solution)/shard_map/expert_part/pallas_call | solution.py:160
  108.9 9.3 %collective-permute-done.23.b_ref = bf16[2064,128]{1,0:T(8,128)(2,1)S(1)} collective-permute-done((bf16[2064,128]{1,0:T(8,128)(2,1)S(1)}, bf16[2064,128]{1,0:T(8,128)(2,1)S(1)}, u32[]{:S(2)}, u32[]{:S(2)}) %collective-permute-start.23) | collective-permute-done | bytes 528416 | tf_op jit(solution)/shard_map/ppermute | solution.py:208
  120.2 3.5 %expert_part.15 = f32[128,2048]{1,0:T(8,128)S(1)} custom-call(s32[2]{0:T(128)S(1)} %pad_add_fusion.me_ref, bf16[2064,128]{1,0:T(8,128)(2,1)S(1)} %collective-permute-done.17.a_ref, bf16[2064,128]{1,0:T(8,128)(2,1)S(1)} %collective-permute-done.23.b_ref, bf16[2048,768]{1,0:T(8,128)(2,1)S(1)} %get-tuple-element.32.refs_0_, bf16[768,2048]{1,0:T(8,128)(2,1)S(1)} %copy-done.1, ...), custom_call_target="tpu_custom_call" | custom-call | flops 2415919104 | bytes 14680064 | tf_op jit(solution)/shard_map/expert_part/pallas_call | solution.py:160
  125.2 2.7 %collective-permute-start.30 = (bf16[64,2048]{1,0:T(8,128)(2,1)S(1)}, bf16[64,2048]{1,0:T(8,128)(2,1)S(1)}, u32[]{:S(2)}, u32[]{:S(2)}) collective-permute-start(bf16[64,2048]{1,0:T(8,128)(2,1)S(1)} %get-tuple-element.54), channel_id=1, source_target_pairs={{0,20},{1,21},{4,24},{5,25},{8,28},{9,29},{12,30},{13,31},{14,26},... | collective-permute-start | bytes 786440 | tf_op jit(solution)/shard_map/ppermute | solution.py:212
  129.6 5.8 %collective-permute-done.30.a_ref = bf16[64,2048]{1,0:T(8,128)(2,1)S(1)} collective-permute-done((bf16[64,2048]{1,0:T(8,128)(2,1)S(1)}, bf16[64,2048]{1,0:T(8,128)(2,1)S(1)}, u32[]{:S(2)}, u32[]{:S(2)}) %collective-permute-start.30) | collective-permute-done | bytes 262176 | tf_op jit(solution)/shard_map/ppermute | solution.py:212
  135.4 1.8 %collective-permute-done.32.b_ref = bf16[64,2048]{1,0:T(8,128)(2,1)S(1)} collective-permute-done((bf16[64,2048]{1,0:T(8,128)(2,1)S(1)}, bf16[64,2048]{1,0:T(8,128)(2,1)S(1)}, u32[]{:S(2)}, u32[]{:S(2)}) %collective-permute-start.32) | collective-permute-done | bytes 262176 | tf_op jit(solution)/shard_map/ppermute | solution.py:212
  (71 shorter events, 28.1 us)
Async XLA Ops:
  0.0 20.7 %collective-permute-start.2 = (bf16[2048,768]{1,0:T(8,128)(2,1)}, bf16[2048,768]{1,0:T(8,128)(2,1)}, u32[]{:S(2)}, u32[]{:S(2)}) collective-permute-start(bf16[2048,768]{1,0:T(8,128)(2,1)} %bitcast.13), channel_id=1, source_target_pairs={{0,1},{1,0},{2,3},{3,2},{4,5},{5,4},{6,7},{7,6},{8,9},{9,8},{10,11... | collective-permute-start | bytes 9437192 | tf_op jit(solution)/shard_map/ppermute | solution.py:227
  0.5 20.2 %collective-permute-start.3 = (bf16[768,2048]{1,0:T(8,128)(2,1)}, bf16[768,2048]{1,0:T(8,128)(2,1)}, u32[]{:S(2)}, u32[]{:S(2)}) collective-permute-start(bf16[768,2048]{1,0:T(8,128)(2,1)} %bitcast.15), channel_id=1, source_target_pairs={{0,1},{1,0},{2,3},{3,2},{4,5},{5,4},{6,7},{7,6},{8,9},{9,8},{10,11... | collective-permute-start | bytes 9437192 | tf_op jit(solution)/shard_map/ppermute | solution.py:227
  3.2 15.5 %collective-permute-start.5 = (bf16[2064,128]{1,0:T(8,128)(2,1)}, bf16[2064,128]{1,0:T(8,128)(2,1)}, u32[]{:S(2)}, u32[]{:S(2)}) collective-permute-start(bf16[2064,128]{1,0:T(8,128)(2,1)} %get-tuple-element.30.a_ref), channel_id=1, source_target_pairs={{0,4},{1,5},{4,8},{5,9},{8,12},{9,13},{12,14},{13,15},{14,10},{15,... | collective-permute-start | bytes 1585160 | tf_op jit(solution)/shard_map/ppermute | solution.py:208
  6.2 14.2 %collective-permute-start.7 = (bf16[2064,128]{1,0:T(8,128)(2,1)}, bf16[2064,128]{1,0:T(8,128)(2,1)}, u32[]{:S(2)}, u32[]{:S(2)}) collective-permute-start(bf16[2064,128]{1,0:T(8,128)(2,1)} %get-tuple-element.31.b_ref), channel_id=1, source_target_pairs={{0,2},{1,3},{4,0},{5,1},{8,4},{9,5},{12,8},{13,9},{14,12},{15,13},... | collective-permute-start | bytes 1585160 | tf_op jit(solution)/shard_map/ppermute | solution.py:208
  6.2 24.6 %collective-permute-start = (bf16[144,2048]{1,0:T(8,128)(2,1)}, bf16[144,2048]{1,0:T(8,128)(2,1)}, u32[]{:S(2)}, u32[]{:S(2)}) collective-permute-start(bf16[144,2048]{1,0:T(8,128)(2,1)} %get-tuple-element.29), channel_id=1, source_target_pairs={{0,16},{16,0},{1,17},{17,1},{2,18},{18,2},{3,19},{19,3},{4,20},{20... | collective-permute-start | bytes 1769480 | tf_op jit(solution)/shard_map/ppermute | solution.py:224
  18.6 15.2 %collective-permute-start.6 = (bf16[2064,128]{1,0:T(8,128)(2,1)}, bf16[2064,128]{1,0:T(8,128)(2,1)S(1)}, u32[]{:S(2)}, u32[]{:S(2)}) collective-permute-start(bf16[2064,128]{1,0:T(8,128)(2,1)} %collective-permute-done.5.a_ref), channel_id=1, source_target_pairs={{0,4},{1,5},{4,8},{5,9},{8,12},{9,13},{12,14},{13,15},{14,10},{15,... | collective-permute-start | bytes 1585160 | tf_op jit(solution)/shard_map/ppermute | solution.py:208
  20.5 14.9 %collective-permute-start.8 = (bf16[2064,128]{1,0:T(8,128)(2,1)}, bf16[2064,128]{1,0:T(8,128)(2,1)S(1)}, u32[]{:S(2)}, u32[]{:S(2)}) collective-permute-start(bf16[2064,128]{1,0:T(8,128)(2,1)} %collective-permute-done.7.b_ref), channel_id=1, source_target_pairs={{0,2},{1,3},{4,0},{5,1},{8,4},{9,5},{12,8},{13,9},{14,12},{15,13},... | collective-permute-start | bytes 1585160 | tf_op jit(solution)/shard_map/ppermute | solution.py:208
  28.7 12.2 %collective-permute-start.18 = (bf16[64,2048]{1,0:T(8,128)(2,1)S(1)}, bf16[64,2048]{1,0:T(8,128)(2,1)S(1)}, u32[]{:S(2)}, u32[]{:S(2)}) collective-permute-start(bf16[64,2048]{1,0:T(8,128)(2,1)S(1)} %get-tuple-element.66), channel_id=1, source_target_pairs={{0,4},{1,5},{4,8},{5,9},{8,12},{9,13},{12,14},{13,15},{14,10},{15,... | collective-permute-start | bytes 786440 | tf_op jit(solution)/shard_map/ppermute | solution.py:208
  30.6 10.4 %collective-permute-start.24 = (bf16[64,2048]{1,0:T(8,128)(2,1)S(1)}, bf16[64,2048]{1,0:T(8,128)(2,1)S(1)}, u32[]{:S(2)}, u32[]{:S(2)}) collective-permute-start(bf16[64,2048]{1,0:T(8,128)(2,1)S(1)} %get-tuple-element.65), channel_id=1, source_target_pairs={{0,2},{1,3},{4,0},{5,1},{8,4},{9,5},{12,8},{13,9},{14,12},{15,13},... | collective-permute-start | bytes 786440 | tf_op jit(solution)/shard_map/ppermute | solution.py:208
  35.4 16.9 %collective-permute-start.10 = (bf16[2064,128]{1,0:T(8,128)(2,1)S(1)}, bf16[2064,128]{1,0:T(8,128)(2,1)S(1)}, u32[]{:S(2)}, u32[]{:S(2)}) collective-permute-start(bf16[2064,128]{1,0:T(8,128)(2,1)S(1)} %collective-permute-done.8.b_ref), channel_id=1, source_target_pairs={{0,2},{1,3},{4,0},{5,1},{8,4},{9,5},{12,8},{13,9},{14,12},{15,13},... | collective-permute-start | bytes 1585160 | tf_op jit(solution)/shard_map/ppermute | solution.py:208
  35.8 16.5 %collective-permute-start.9 = (bf16[2064,128]{1,0:T(8,128)(2,1)S(1)}, bf16[2064,128]{1,0:T(8,128)(2,1)S(1)}, u32[]{:S(2)}, u32[]{:S(2)}) collective-permute-start(bf16[2064,128]{1,0:T(8,128)(2,1)S(1)} %collective-permute-done.6.a_ref), channel_id=1, source_target_pairs={{0,4},{1,5},{4,8},{5,9},{8,12},{9,13},{12,14},{13,15},{14,10},{15,... | collective-permute-start | bytes 1585160 | tf_op jit(solution)/shard_map/ppermute | solution.py:208
  41.1 16.8 %collective-permute-start.19 = (bf16[64,2048]{1,0:T(8,128)(2,1)S(1)}, bf16[64,2048]{1,0:T(8,128)(2,1)S(1)}, u32[]{:S(2)}, u32[]{:S(2)}) collective-permute-start(bf16[64,2048]{1,0:T(8,128)(2,1)S(1)} %get-tuple-element.64), channel_id=1, source_target_pairs={{0,4},{1,5},{4,8},{5,9},{8,12},{9,13},{12,14},{13,15},{14,10},{15,... | collective-permute-start | bytes 786440 | tf_op jit(solution)/shard_map/ppermute | solution.py:208
  42.8 15.2 %collective-permute-start.25 = (bf16[64,2048]{1,0:T(8,128)(2,1)S(1)}, bf16[64,2048]{1,0:T(8,128)(2,1)S(1)}, u32[]{:S(2)}, u32[]{:S(2)}) collective-permute-start(bf16[64,2048]{1,0:T(8,128)(2,1)S(1)} %get-tuple-element.63), channel_id=1, source_target_pairs={{0,2},{1,3},{4,0},{5,1},{8,4},{9,5},{12,8},{13,9},{14,12},{15,13},... | collective-permute-start | bytes 786440 | tf_op jit(solution)/shard_map/ppermute | solution.py:208
  52.3 15.4 %collective-permute-start.11 = (bf16[2064,128]{1,0:T(8,128)(2,1)S(1)}, bf16[2064,128]{1,0:T(8,128)(2,1)S(1)}, u32[]{:S(2)}, u32[]{:S(2)}) collective-permute-start(bf16[2064,128]{1,0:T(8,128)(2,1)S(1)} %collective-permute-done.9.a_ref), channel_id=1, source_target_pairs={{0,4},{1,5},{4,8},{5,9},{8,12},{9,13},{12,14},{13,15},{14,10},{15,... | collective-permute-start | bytes 1585160 | tf_op jit(solution)/shard_map/ppermute | solution.py:208
  53.9 15.6 %collective-permute-start.13 = (bf16[2064,128]{1,0:T(8,128)(2,1)S(1)}, bf16[2064,128]{1,0:T(8,128)(2,1)S(1)}, u32[]{:S(2)}, u32[]{:S(2)}) collective-permute-start(bf16[2064,128]{1,0:T(8,128)(2,1)S(1)} %collective-permute-done.10.b_ref), channel_id=1, source_target_pairs={{0,2},{1,3},{4,0},{5,1},{8,4},{9,5},{12,8},{13,9},{14,12},{15,13},... | collective-permute-start | bytes 1585160 | tf_op jit(solution)/shard_map/ppermute | solution.py:208
  58.1 15.2 %collective-permute-start.20 = (bf16[64,2048]{1,0:T(8,128)(2,1)S(1)}, bf16[64,2048]{1,0:T(8,128)(2,1)S(1)}, u32[]{:S(2)}, u32[]{:S(2)}) collective-permute-start(bf16[64,2048]{1,0:T(8,128)(2,1)S(1)} %get-tuple-element.62), channel_id=1, source_target_pairs={{0,4},{1,5},{4,8},{5,9},{8,12},{9,13},{12,14},{13,15},{14,10},{15,... | collective-permute-start | bytes 786440 | tf_op jit(solution)/shard_map/ppermute | solution.py:208
  59.7 15.2 %collective-permute-start.26 = (bf16[64,2048]{1,0:T(8,128)(2,1)S(1)}, bf16[64,2048]{1,0:T(8,128)(2,1)S(1)}, u32[]{:S(2)}, u32[]{:S(2)}) collective-permute-start(bf16[64,2048]{1,0:T(8,128)(2,1)S(1)} %get-tuple-element.61), channel_id=1, source_target_pairs={{0,2},{1,3},{4,0},{5,1},{8,4},{9,5},{12,8},{13,9},{14,12},{15,13},... | collective-permute-start | bytes 786440 | tf_op jit(solution)/shard_map/ppermute | solution.py:208
  60.1 16.9 %collective-permute-start.1 = (bf16[128,2048]{1,0:T(8,128)(2,1)S(1)}, bf16[128,2048]{1,0:T(8,128)(2,1)S(1)}, u32[]{:S(2)}, u32[]{:S(2)}) collective-permute-start(bf16[128,2048]{1,0:T(8,128)(2,1)S(1)} %bitcast.19), channel_id=1, source_target_pairs={{0,16},{16,0},{1,17},{17,1},{2,18},{18,2},{3,19},{19,3},{4,20},{20... | collective-permute-start | bytes 1572872 | tf_op jit(solution)/shard_map/ppermute | solution.py:224
  67.7 16.9 %collective-permute-start.12 = (bf16[2064,128]{1,0:T(8,128)(2,1)S(1)}, bf16[2064,128]{1,0:T(8,128)(2,1)S(1)}, u32[]{:S(2)}, u32[]{:S(2)}) collective-permute-start(bf16[2064,128]{1,0:T(8,128)(2,1)S(1)} %collective-permute-done.11.a_ref), channel_id=1, source_target_pairs={{0,4},{1,5},{4,8},{5,9},{8,12},{9,13},{12,14},{13,15},{14,10},{15,... | collective-permute-start | bytes 1585160 | tf_op jit(solution)/shard_map/ppermute | solution.py:208
  69.5 16.7 %collective-permute-start.14 = (bf16[2064,128]{1,0:T(8,128)(2,1)S(1)}, bf16[2064,128]{1,0:T(8,128)(2,1)S(1)}, u32[]{:S(2)}, u32[]{:S(2)}) collective-permute-start(bf16[2064,128]{1,0:T(8,128)(2,1)S(1)} %collective-permute-done.13.b_ref), channel_id=1, source_target_pairs={{0,2},{1,3},{4,0},{5,1},{8,4},{9,5},{12,8},{13,9},{14,12},{15,13},... | collective-permute-start | bytes 1585160 | tf_op jit(solution)/shard_map/ppermute | solution.py:208
  75.0 16.8 %collective-permute-start.21 = (bf16[64,2048]{1,0:T(8,128)(2,1)S(1)}, bf16[64,2048]{1,0:T(8,128)(2,1)S(1)}, u32[]{:S(2)}, u32[]{:S(2)}) collective-permute-start(bf16[64,2048]{1,0:T(8,128)(2,1)S(1)} %get-tuple-element.60), channel_id=1, source_target_pairs={{0,4},{1,5},{4,8},{5,9},{8,12},{9,13},{12,14},{13,15},{14,10},{15,... | collective-permute-start | bytes 786440 | tf_op jit(solution)/shard_map/ppermute | solution.py:208
  76.6 15.2 %collective-permute-start.27 = (bf16[64,2048]{1,0:T(8,128)(2,1)S(1)}, bf16[64,2048]{1,0:T(8,128)(2,1)S(1)}, u32[]{:S(2)}, u32[]{:S(2)}) collective-permute-start(bf16[64,2048]{1,0:T(8,128)(2,1)S(1)} %get-tuple-element.59), channel_id=1, source_target_pairs={{0,2},{1,3},{4,0},{5,1},{8,4},{9,5},{12,8},{13,9},{14,12},{15,13},... | collective-permute-start | bytes 786440 | tf_op jit(solution)/shard_map/ppermute | solution.py:208
  77.1 16.9 %collective-permute-start.4 = (bf16[128,2048]{1,0:T(8,128)(2,1)S(1)}, bf16[128,2048]{1,0:T(8,128)(2,1)S(1)}, u32[]{:S(2)}, u32[]{:S(2)}) collective-permute-start(bf16[128,2048]{1,0:T(8,128)(2,1)S(1)} %convert_element_type.77), channel_id=1, source_target_pairs={{0,16},{16,0},{1,17},{17,1},{2,18},{18,2},{3,19},{19,3},{4,20},{20... | collective-permute-start | bytes 1572872 | tf_op jit(solution)/shard_map/ppermute | solution.py:224
  86.2 15.4 %collective-permute-start.15 = (bf16[2064,128]{1,0:T(8,128)(2,1)S(1)}, bf16[2064,128]{1,0:T(8,128)(2,1)S(1)}, u32[]{:S(2)}, u32[]{:S(2)}) collective-permute-start(bf16[2064,128]{1,0:T(8,128)(2,1)S(1)} %collective-permute-done.12.a_ref), channel_id=1, source_target_pairs={{0,4},{1,5},{4,8},{5,9},{8,12},{9,13},{12,14},{13,15},{14,10},{15,... | collective-permute-start | bytes 1585160 | tf_op jit(solution)/shard_map/ppermute | solution.py:208
  87.8 15.4 %collective-permute-start.16 = (bf16[2064,128]{1,0:T(8,128)(2,1)S(1)}, bf16[2064,128]{1,0:T(8,128)(2,1)S(1)}, u32[]{:S(2)}, u32[]{:S(2)}) collective-permute-start(bf16[2064,128]{1,0:T(8,128)(2,1)S(1)} %collective-permute-done.14.b_ref), channel_id=1, source_target_pairs={{0,2},{1,3},{4,0},{5,1},{8,4},{9,5},{12,8},{13,9},{14,12},{15,13},... | collective-permute-start | bytes 1585160 | tf_op jit(solution)/shard_map/ppermute | solution.py:208
  91.9 16.8 %collective-permute-start.22 = (bf16[64,2048]{1,0:T(8,128)(2,1)S(1)}, bf16[64,2048]{1,0:T(8,128)(2,1)S(1)}, u32[]{:S(2)}, u32[]{:S(2)}) collective-permute-start(bf16[64,2048]{1,0:T(8,128)(2,1)S(1)} %get-tuple-element.58), channel_id=1, source_target_pairs={{0,4},{1,5},{4,8},{5,9},{8,12},{9,13},{12,14},{13,15},{14,10},{15,... | collective-permute-start | bytes 786440 | tf_op jit(solution)/shard_map/ppermute | solution.py:208
  93.6 15.2 %collective-permute-start.28 = (bf16[64,2048]{1,0:T(8,128)(2,1)S(1)}, bf16[64,2048]{1,0:T(8,128)(2,1)S(1)}, u32[]{:S(2)}, u32[]{:S(2)}) collective-permute-start(bf16[64,2048]{1,0:T(8,128)(2,1)S(1)} %get-tuple-element.57), channel_id=1, source_target_pairs={{0,2},{1,3},{4,0},{5,1},{8,4},{9,5},{12,8},{13,9},{14,12},{15,13},... | collective-permute-start | bytes 786440 | tf_op jit(solution)/shard_map/ppermute | solution.py:208
  103.1 15.0 %collective-permute-start.23 = (bf16[2064,128]{1,0:T(8,128)(2,1)S(1)}, bf16[2064,128]{1,0:T(8,128)(2,1)S(1)}, u32[]{:S(2)}, u32[]{:S(2)}) collective-permute-start(bf16[2064,128]{1,0:T(8,128)(2,1)S(1)} %collective-permute-done.16.b_ref), channel_id=1, source_target_pairs={{0,2},{1,3},{4,0},{5,1},{8,4},{9,5},{12,8},{13,9},{14,12},{15,13},... | collective-permute-start | bytes 1585160 | tf_op jit(solution)/shard_map/ppermute | solution.py:208
  103.6 14.6 %collective-permute-start.17 = (bf16[2064,128]{1,0:T(8,128)(2,1)S(1)}, bf16[2064,128]{1,0:T(8,128)(2,1)S(1)}, u32[]{:S(2)}, u32[]{:S(2)}) collective-permute-start(bf16[2064,128]{1,0:T(8,128)(2,1)S(1)} %collective-permute-done.15.a_ref), channel_id=1, source_target_pairs={{0,4},{1,5},{4,8},{5,9},{8,12},{9,13},{12,14},{13,15},{14,10},{15,... | collective-permute-start | bytes 1585160 | tf_op jit(solution)/shard_map/ppermute | solution.py:208
  118.2 6.4 %collective-permute-start.31 = (bf16[64,2048]{1,0:T(8,128)(2,1)S(1)}, bf16[64,2048]{1,0:T(8,128)(2,1)S(1)}, u32[]{:S(2)}, u32[]{:S(2)}) collective-permute-start(bf16[64,2048]{1,0:T(8,128)(2,1)S(1)} %get-tuple-element.52), channel_id=1, source_target_pairs={{0,2},{1,3},{4,0},{5,1},{8,4},{9,5},{12,8},{13,9},{14,12},{15,13},... | collective-permute-start | bytes 786440 | tf_op jit(solution)/shard_map/ppermute | solution.py:208
  125.2 10.2 %collective-permute-start.30 = (bf16[64,2048]{1,0:T(8,128)(2,1)S(1)}, bf16[64,2048]{1,0:T(8,128)(2,1)S(1)}, u32[]{:S(2)}, u32[]{:S(2)}) collective-permute-start(bf16[64,2048]{1,0:T(8,128)(2,1)S(1)} %get-tuple-element.54), channel_id=1, source_target_pairs={{0,20},{1,21},{4,24},{5,25},{8,28},{9,29},{12,30},{13,31},{14,26},... | collective-permute-start | bytes 786440 | tf_op jit(solution)/shard_map/ppermute | solution.py:212
  127.9 9.3 %collective-permute-start.32 = (bf16[64,2048]{1,0:T(8,128)(2,1)S(1)}, bf16[64,2048]{1,0:T(8,128)(2,1)S(1)}, u32[]{:S(2)}, u32[]{:S(2)}) collective-permute-start(bf16[64,2048]{1,0:T(8,128)(2,1)S(1)} %get-tuple-element.53), channel_id=1, source_target_pairs={{0,18},{1,19},{4,16},{5,17},{8,20},{9,21},{12,24},{13,25},{14,28},... | collective-permute-start | bytes 786440 | tf_op jit(solution)/shard_map/ppermute | solution.py:212
  (8 other events, 69.9 us)

commit v7 on v6

--- a/solution.py
+++ b/solution.py
@@ -13,41 +13,43 @@
 def pack_kernel(x_hbm, grad_hbm, gain_hbm, routes_hbm, gates_hbm, a_ref, b_ref, keep_ref, grad_s, gain_s, routes_s, gates_s, sems):
     rows, width = x_hbm.shape
     half, slabs = rows // 2, width // LANES
-    x_ref = keep_ref.at[pl.ds(0, rows)]
-    copies = [
-        pltpu.make_async_copy(hbm, vmem, sems.at[i])
-        for i, (hbm, vmem) in enumerate(
-            ((x_hbm, x_ref), (gain_hbm, gain_s), (routes_hbm, routes_s), (gates_hbm, gates_s), (grad_hbm, grad_s))
-        )
-    ]
+    parts = (slice(0, half), slice(half, rows))
+    pairs = [(gain_hbm, gain_s)]
+    pairs += [(x_hbm.at[part], keep_ref.at[part]) for part in parts]
+    pairs += [(routes_hbm, routes_s), (gates_hbm, gates_s)]
+    pairs += [(grad_hbm.at[part], grad_s.at[part]) for part in parts]
+    copies = [pltpu.make_async_copy(hbm, vmem, sems.at[i]) for i, (hbm, vmem) in enumerate(pairs)]
     for copy in copies:
         copy.start()
-    for copy in copies[:4]:
-        copy.wait()
+    copies[0].wait()
     gain = gain_s[...]
-    values = x_ref[...].astype(jnp.float32)
-    scaling = lax.rsqrt(jnp.mean(values * values, axis=-1, keepdims=True) + epsilon)
-    normed = (values * scaling * gain).astype(jnp.bfloat16)
-    shape = (a_ref.shape[0] - 2 * slabs * half, rows)
-    expert = lax.broadcasted_iota(jnp.int32, shape, 0)
-    dense = jnp.zeros(shape, jnp.float32)
-    routes, gates = routes_s[...], gates_s[...].astype(jnp.float32)
-    for k in range(routes.shape[0]):
-        dense = dense + jnp.where(expert == routes[k : k + 1, :], gates[k : k + 1, :], 0.0)
-    token = lax.broadcasted_iota(jnp.int32, shape, 1)
     high = gain.astype(jnp.bfloat16).astype(jnp.float32)
     middle = (gain - high).astype(jnp.bfloat16).astype(jnp.float32)
     low = gain - high - middle
     row = lax.broadcasted_iota(jnp.int32, (keep_ref.shape[0] - rows, width), 0)
     pieces = jnp.where(row == 0, high, jnp.where(row == 1, middle, jnp.where(row == 2, low, 0.0)))
     keep_ref[rows:, :] = pieces.astype(jnp.bfloat16)
+    for ref, part, copy in zip((a_ref, b_ref), parts, copies[1:3]):
+        copy.wait()
+        values = keep_ref[part, :].astype(jnp.float32)
+        scaling = lax.rsqrt(jnp.mean(values * values, axis=-1, keepdims=True) + epsilon)
+        normed = (values * scaling * gain).astype(jnp.bfloat16)
+        for k in range(slabs):
+            ref[k * half : (k + 1) * half, :] = normed[:, k * LANES : (k + 1) * LANES]
+    copies[3].wait()
     copies[4].wait()
-    for ref, first in ((a_ref, 0), (b_ref, half)):
+    shape = (a_ref.shape[0] - 2 * slabs * half, rows)
+    expert = lax.broadcasted_iota(jnp.int32, shape, 0)
+    token = lax.broadcasted_iota(jnp.int32, shape, 1)
+    dense = jnp.zeros(shape, jnp.float32)
+    routes, gates = routes_s[...], gates_s[...].astype(jnp.float32)
+    for k in range(routes.shape[0]):
+        dense = dense + jnp.where(expert == routes[k : k + 1, :], gates[k : k + 1, :], 0.0)
+    for ref, part, copy in zip((a_ref, b_ref), parts, copies[5:]):
+        copy.wait()
         for k in range(slabs):
-            part, lanes = slice(first, first + half), slice(k * LANES, (k + 1) * LANES)
-            ref[k * half : (k + 1) * half, :] = normed[part, lanes]
-            ref[(slabs + k) * half : (slabs + k + 1) * half, :] = grad_s[part, lanes]
-        here = (token >= first) & (token < first + half)
+            ref[(slabs + k) * half : (slabs + k + 1) * half, :] = grad_s[part, k * LANES : (k + 1) * LANES]
+        here = (token >= part.start) & (token < part.stop)
         ref[2 * slabs * half :, :] = jnp.where(here, dense, 0.0).astype(jnp.bfloat16)
 
 
@@ -66,7 +68,7 @@
             pltpu.VMEM((1, width), jnp.float32),
             pltpu.VMEM((top, rows), jnp.int32),
             pltpu.VMEM((top, rows), jnp.bfloat16),
-            pltpu.SemaphoreType.DMA((5,)),
+            pltpu.SemaphoreType.DMA((7,)),
         ],
         compiler_params=pltpu.CompilerParams(vmem_limit_bytes=VMEM),
         name="pack",
@@ -172,29 +174,65 @@
     )(me, a, b, *weights)
 
 
-def finish_kernel(keep_ref, g_ref, own_ref, a_ref, b_ref, o_ref):
+def settle_kernel(keep_hbm, g_hbm, own_hbm, base_ref, x_ref, rows_ref, keep_s, g_s, own_s, sems):
+    copies = [
+        pltpu.make_async_copy(hbm, vmem, sems.at[i])
+        for i, (hbm, vmem) in enumerate(((keep_hbm, keep_s), (own_hbm, own_s), (g_hbm, g_s)))
+    ]
+    for copy in copies:
+        copy.start()
+    for copy in copies:
+        copy.wait()
+    rows = g_s.shape[0]
+    pieces = keep_s[rows:, :].astype(jnp.float32)
+    gain = (pieces[0:1, :] + pieces[1:2, :]) + pieces[2:3, :]
+    values = keep_s[:rows, :].astype(jnp.float32)
+    scaling = lax.rsqrt(jnp.mean(values * values, axis=-1, keepdims=True) + epsilon)
+    weighted = gain * own_s[...].astype(jnp.float32)
+    inner_mean = jnp.mean(values * weighted, axis=-1, keepdims=True)
+    back = scaling * weighted - values * (scaling * scaling * scaling) * inner_mean
+    base_ref[...] = g_s[...].astype(jnp.float32) + back
+    x_ref[...] = values
+    rows_ref[0:8, :] = jnp.broadcast_to(gain, (8, gain.shape[1]))
+    rows_ref[8:, :LANES] = jnp.broadcast_to(scaling, (rows, LANES))
+
+
+def settle(keep, grad, own):
+    rows, width = grad.shape
+    whole = pl.BlockSpec(memory_space=pltpu.VMEM)
+    full = pltpu.VMEM((rows, width), jnp.float32)
+    return pl.pallas_call(
+        settle_kernel,
+        out_shape=[full, full, pltpu.VMEM((rows + 8, width), jnp.float32)],
+        in_specs=[pl.BlockSpec(memory_space=pltpu.HBM)] * 3,
+        out_specs=[whole] * 3,
+        scratch_shapes=[pltpu.VMEM(value.shape, value.dtype) for value in (keep, grad, own)]
+        + [pltpu.SemaphoreType.DMA((3,))],
+        compiler_params=pltpu.CompilerParams(vmem_limit_bytes=VMEM),
+        name="settle",
+    )(*(pltpu.with_memory_space_constraint(value, pltpu.HBM) for value in (keep, grad, own)))
+
+
+def finish_kernel(base_ref, x_ref, rows_ref, a_ref, b_ref, o_ref):
     half = a_ref.shape[0]
-    rows = 2 * half
-    pieces = keep_ref[rows : rows + 16, :].astype(jnp.float32)
-    gain = (pieces[0:1, :] + pieces[1:2, :]) + pieces[2:3, :]
+    gain = rows_ref[0:1, :]
     for ref, first in ((a_ref, 0), (b_ref, half)):
         part = slice(first, first + half)
-        values = keep_ref[part, :].astype(jnp.float32)
-        scaling = lax.rsqrt(jnp.mean(values * values, axis=-1, keepdims=True) + epsilon)
-        d_normed = own_ref[part, :].astype(jnp.float32) + ref[...].astype(jnp.float32)
-        weighted = gain * d_normed
+        scaling = rows_ref[8 + first : 8 + first + half, 0:1]
+        weighted = gain * ref[...].astype(jnp.float32)
+        values = x_ref[part, :]
         inner_mean = jnp.mean(values * weighted, axis=-1, keepdims=True)
-        back = scaling * weighted - values * (scaling * scaling * scaling) * inner_mean
-        o_ref[part, :] = (g_ref[part, :].astype(jnp.float32) + back).astype(jnp.bfloat16)
-
-
-def finish(keep, grad, own, a, b):
+        back = scaling * weighted - values * ((scaling * scaling * scaling) * inner_mean)
+        o_ref[part, :] = (base_ref[part, :] + back).astype(jnp.bfloat16)
+
+
+def finish(base, x, rows, a, b):
     return pl.pallas_call(
         finish_kernel,
-        out_shape=jax.ShapeDtypeStruct(grad.shape, jnp.bfloat16),
+        out_shape=jax.ShapeDtypeStruct(x.shape, jnp.bfloat16),
         compiler_params=pltpu.CompilerParams(vmem_limit_bytes=VMEM),
         name="finish",
-    )(keep, grad, own, a, b)
+    )(base, x, rows, a, b)
 
 
 def shards(bwd_input, out_grad, norm_gain, up_weight, down_weight, bwd_routes, bwd_gates):
@@ -257,7 +295,7 @@
             b1, send_b = lax.optimization_barrier((b1, send_b))
         move = hop if step < chips - 1 else last_hop
         sum_a, sum_b = move(send_a, 1), move(send_b, -1)
-    held = hold(keep_out, grad_out, own_out)
+    held = settle(keep_out, grad_out, own_out)
     return finish(*held, sum_a, sum_b)[None]
 
 

time: 139 us -> 139 us (level)
  no operation moved by 1% of the time
where the time goes in v7:
time: 139 us; the launch traced here: 138 us
  waiting for transfers between devices  54.6 us (39%)
  Pallas kernels  42.9 us (31%)
  starting transfers between devices  36.1 us (26%)
  local copies, waits for them, and re-layouts  3.51 us (3%)
    ppermute x26, waiting for transfers between devices, hop(): lax.ppermute(value, 'expert', [(2 * a + c, 2 * b + c) for a, b in moves f...  47.7 us
    pallas_call x8, Pallas kernels, expert_part(): pl.pallas_call(expert_kernel, out_shape=jax.ShapeDtypeStruct((rows, width...  29.5 us
    ppermute x26, starting transfers between devices, hop(): lax.ppermute(value, 'expert', [(2 * a + c, 2 * b + c) for a, b in moves f...  27.7 us
    pallas_call x2, Pallas kernels, turn(): pl.pallas_call(turn_kernel, out_shape=[pltpu.VMEM(shape, up.dtype) for sh...  7.45 us
    ppermute x2, waiting for transfers between devices, last_hop(): lax.ppermute(value, ('pipe', 'expert'), [(s * experts + 2 * a + c, (s - 1...  6.9 us
    ppermute x3, starting transfers between devices, to_previous(): lax.ppermute(value, 'pipe', [(s, (s - 1) % sections) for s in range(secti...  5.01 us
    unnamed x14, local copies, waits for them, and re-layouts  3.47 us
    ppermute x2, starting transfers between devices, last_hop(): lax.ppermute(value, ('pipe', 'expert'), [(s * experts + 2 * a + c, (s - 1...  2.98 us
  transfers between devices with their start and end apart: 33, of which 15 were waited for; matrix products, arithmetic and copies ran while one was open for 1% of the time, Pallas kernels for 30%

profile of v7, /device:TPU:0, one launch (start us, length us, event | category | flops | bytes accessed | tf_op | source)
XLA Modules:
  0.0 138.4 jit_solution(2816050948333610405)
XLA Ops:
  0.5 2.6 %pack.1 = (bf16[2064,128]{1,0:T(8,128)(2,1)}, bf16[2064,128]{1,0:T(8,128)(2,1)}, bf16[144,2048]{1,0:T(8,128)(2,1)}) custom-call(bf16[128,2048]{1,0:T(8,128)(2,1)} %bitcast.17, bf16[128,2048]{1,0:T(8,128)(2,1)} %bitcast.18, f32[1,2048]{1,0:T(1,128)} %gain_hbm.1, s32[8,128]{1,0:T(8,128)} %bitcast.20, bf16[8,128]{1,0:T(8,128)(2,1)} %bitcast.21), custom_call_target="tpu_custom_call" | custom-call | tf_op jit(solution)/shard_map/pack/pallas_call | solution.py:61
  3.1 3.1 %collective-permute-start.5 = (bf16[2064,128]{1,0:T(8,128)(2,1)}, bf16[2064,128]{1,0:T(8,128)(2,1)}, u32[]{:S(2)}, u32[]{:S(2)}) collective-permute-start(bf16[2064,128]{1,0:T(8,128)(2,1)} %get-tuple-element.30.a_ref), channel_id=1, source_target_pairs={{0,4},{1,5},{4,8},{5,9},{8,12},{9,13},{12,14},{13,15},{14,10},{15,... | collective-permute-start | bytes 1585160 | tf_op jit(solution)/shard_map/ppermute | solution.py:246
  6.2 2.0 %collective-permute-start = (bf16[144,2048]{1,0:T(8,128)(2,1)}, bf16[144,2048]{1,0:T(8,128)(2,1)}, u32[]{:S(2)}, u32[]{:S(2)}) collective-permute-start(bf16[144,2048]{1,0:T(8,128)(2,1)} %get-tuple-element.29), channel_id=1, source_target_pairs={{0,16},{16,0},{1,17},{17,1},{2,18},{18,2},{3,19},{19,3},{4,20},{20... | collective-permute-start | bytes 1769480 | tf_op jit(solution)/shard_map/ppermute | solution.py:262
  8.2 3.7 %turn.2 = (bf16[2048,768]{1,0:T(8,128)(2,1)S(1)}, bf16[768,2048]{1,0:T(8,128)(2,1)S(1)}, bf16[2048,768]{1,0:T(8,128)(2,1)S(1)}) custom-call(bf16[2048,768]{1,0:T(8,128)(2,1)} %bitcast.14, bf16[768,2048]{1,0:T(8,128)(2,1)} %bitcast.16), custom_call_target="tpu_custom_call" | custom-call | tf_op jit(solution)/shard_map/turn/pallas_call | solution.py:114
  11.9 1.7 %copy-done = bf16[768,2048]{1,0:T(8,128)(2,1)} copy-done((bf16[768,2048]{1,0:T(8,128)(2,1)}, bf16[768,2048]{1,0:T(8,128)(2,1)S(1)}, u32[]{:S(2)}) %copy-start) | copy-done | bytes 3145752
  13.6 1.7 %copy-done.2 = bf16[2048,768]{1,0:T(8,128)(2,1)} copy-done((bf16[2048,768]{1,0:T(8,128)(2,1)}, bf16[2048,768]{1,0:T(8,128)(2,1)S(1)}, u32[]{:S(2)}) %copy-start.2) | copy-done | bytes 3145752
  15.4 3.2 %collective-permute-done.5.a_ref = bf16[2064,128]{1,0:T(8,128)(2,1)} collective-permute-done((bf16[2064,128]{1,0:T(8,128)(2,1)}, bf16[2064,128]{1,0:T(8,128)(2,1)}, u32[]{:S(2)}, u32[]{:S(2)}) %collective-permute-start.5) | collective-permute-done | bytes 528416 | tf_op jit(solution)/shard_map/ppermute | solution.py:246
  18.6 1.8 %collective-permute-start.6 = (bf16[2064,128]{1,0:T(8,128)(2,1)}, bf16[2064,128]{1,0:T(8,128)(2,1)S(1)}, u32[]{:S(2)}, u32[]{:S(2)}) collective-permute-start(bf16[2064,128]{1,0:T(8,128)(2,1)} %collective-permute-done.5.a_ref), channel_id=1, source_target_pairs={{0,4},{1,5},{4,8},{5,9},{8,12},{9,13},{12,14},{13,15},{14,10},{15,... | collective-permute-start | bytes 1585160 | tf_op jit(solution)/shard_map/ppermute | solution.py:246
  20.6 3.7 %turn.3 = (bf16[2048,768]{1,0:T(8,128)(2,1)S(1)}, bf16[768,2048]{1,0:T(8,128)(2,1)S(1)}, bf16[2048,768]{1,0:T(8,128)(2,1)S(1)}) custom-call(bf16[2048,768]{1,0:T(8,128)(2,1)} %collective-permute-done.2.up_hbm, bf16[768,2048]{1,0:T(8,128)(2,1)} %collective-permute-done.3.down_hbm), custom_call_target="tpu_custom_call" | custom-call | tf_op jit(solution)/shard_map/turn/pallas_call | solution.py:114
  24.4 4.2 %expert_part.14 = f32[128,2048]{1,0:T(8,128)S(1)} custom-call(s32[2]{0:T(128)S(1)} %pad_add_fusion.me_ref, bf16[2064,128]{1,0:T(8,128)(2,1)} %collective-permute-done.5.a_ref, bf16[2064,128]{1,0:T(8,128)(2,1)} %collective-permute-done.7.b_ref, bf16[2048,768]{1,0:T(8,128)(2,1)S(1)} %get-tuple-element.32.refs_0_, bf16[768,2048]{1,0:T(8,128)(2,1)S(1)} %copy-done.1, ...), custom_call_target="tpu_custom_call" | custom-call | flops 2415919104 | bytes 14680064 | tf_op jit(solution)/shard_map/expert_part/pallas_call | solution.py:162
  28.7 1.9 %collective-permute-start.18 = (bf16[64,2048]{1,0:T(8,128)(2,1)S(1)}, bf16[64,2048]{1,0:T(8,128)(2,1)S(1)}, u32[]{:S(2)}, u32[]{:S(2)}) collective-permute-start(bf16[64,2048]{1,0:T(8,128)(2,1)S(1)} %get-tuple-element.66), channel_id=1, source_target_pairs={{0,4},{1,5},{4,8},{5,9},{8,12},{9,13},{12,14},{13,15},{14,10},{15,... | collective-permute-start | bytes 786440 | tf_op jit(solution)/shard_map/ppermute | solution.py:246
  30.7 3.0 %collective-permute-done.6.a_ref = bf16[2064,128]{1,0:T(8,128)(2,1)S(1)} collective-permute-done((bf16[2064,128]{1,0:T(8,128)(2,1)}, bf16[2064,128]{1,0:T(8,128)(2,1)S(1)}, u32[]{:S(2)}, u32[]{:S(2)}) %collective-permute-start.6) | collective-permute-done | bytes 528416 | tf_op jit(solution)/shard_map/ppermute | solution.py:246
  37.4 3.5 %expert_part.13 = f32[128,2048]{1,0:T(8,128)S(1)} custom-call(s32[2]{0:T(128)S(1)} %pad_add_fusion.me_ref, bf16[2064,128]{1,0:T(8,128)(2,1)S(1)} %collective-permute-done.6.a_ref, bf16[2064,128]{1,0:T(8,128)(2,1)S(1)} %collective-permute-done.8.b_ref, bf16[2048,768]{1,0:T(8,128)(2,1)S(1)} %get-tuple-element.32.refs_0_, bf16[768,2048]{1,0:T(8,128)(2,1)S(1)} %copy-done.1, ...), custom_call_target="tpu_custom_call" | custom-call | flops 2415919104 | bytes 14680064 | tf_op jit(solution)/shard_map/expert_part/pallas_call | solution.py:162
  41.1 1.6 %collective-permute-start.19 = (bf16[64,2048]{1,0:T(8,128)(2,1)S(1)}, bf16[64,2048]{1,0:T(8,128)(2,1)S(1)}, u32[]{:S(2)}, u32[]{:S(2)}) collective-permute-start(bf16[64,2048]{1,0:T(8,128)(2,1)S(1)} %get-tuple-element.64), channel_id=1, source_target_pairs={{0,4},{1,5},{4,8},{5,9},{8,12},{9,13},{12,14},{13,15},{14,10},{15,... | collective-permute-start | bytes 786440 | tf_op jit(solution)/shard_map/ppermute | solution.py:246
  43.2 4.1 %expert_part.8 = f32[128,2048]{1,0:T(8,128)S(1)} custom-call(s32[2]{0:T(128)S(1)} %pad_add_fusion.me_ref, bf16[2064,128]{1,0:T(8,128)(2,1)} %get-tuple-element.30.a_ref, bf16[2064,128]{1,0:T(8,128)(2,1)} %get-tuple-element.31.b_ref, bf16[2048,768]{1,0:T(8,128)(2,1)S(1)} %get-tuple-element.32.refs_0_, bf16[768,2048]{1,0:T(8,128)(2,1)S(1)} %copy-done.1, ...), custom_call_target="tpu_custom_call" | custom-call | flops 2415919104 | bytes 14680064 | tf_op jit(solution)/shard_map/expert_part/pallas_call | solution.py:162
  47.4 4.9 %collective-permute-done.10.b_ref = bf16[2064,128]{1,0:T(8,128)(2,1)S(1)} collective-permute-done((bf16[2064,128]{1,0:T(8,128)(2,1)S(1)}, bf16[2064,128]{1,0:T(8,128)(2,1)S(1)}, u32[]{:S(2)}, u32[]{:S(2)}) %collective-permute-start.10) | collective-permute-done | bytes 528416 | tf_op jit(solution)/shard_map/ppermute | solution.py:246
  54.3 3.5 %expert_part.12 = f32[128,2048]{1,0:T(8,128)S(1)} custom-call(s32[2]{0:T(128)S(1)} %pad_add_fusion.me_ref, bf16[2064,128]{1,0:T(8,128)(2,1)S(1)} %collective-permute-done.9.a_ref, bf16[2064,128]{1,0:T(8,128)(2,1)S(1)} %collective-permute-done.10.b_ref, bf16[2048,768]{1,0:T(8,128)(2,1)S(1)} %get-tuple-element.32.refs_0_, bf16[768,2048]{1,0:T(8,128)(2,1)S(1)} %copy-done.1, ...), custom_call_target="tpu_custom_call" | custom-call | flops 2415919104 | bytes 14680064 | tf_op jit(solution)/shard_map/expert_part/pallas_call | solution.py:162
  58.0 1.6 %collective-permute-start.20 = (bf16[64,2048]{1,0:T(8,128)(2,1)S(1)}, bf16[64,2048]{1,0:T(8,128)(2,1)S(1)}, u32[]{:S(2)}, u32[]{:S(2)}) collective-permute-start(bf16[64,2048]{1,0:T(8,128)(2,1)S(1)} %get-tuple-element.62), channel_id=1, source_target_pairs={{0,4},{1,5},{4,8},{5,9},{8,12},{9,13},{12,14},{13,15},{14,10},{15,... | collective-permute-start | bytes 786440 | tf_op jit(solution)/shard_map/ppermute | solution.py:246
  61.6 6.0 %collective-permute-done.11.a_ref = bf16[2064,128]{1,0:T(8,128)(2,1)S(1)} collective-permute-done((bf16[2064,128]{1,0:T(8,128)(2,1)S(1)}, bf16[2064,128]{1,0:T(8,128)(2,1)S(1)}, u32[]{:S(2)}, u32[]{:S(2)}) %collective-permute-start.11) | collective-permute-done | bytes 528416 | tf_op jit(solution)/shard_map/ppermute | solution.py:246
  67.6 1.8 %collective-permute-start.12 = (bf16[2064,128]{1,0:T(8,128)(2,1)S(1)}, bf16[2064,128]{1,0:T(8,128)(2,1)S(1)}, u32[]{:S(2)}, u32[]{:S(2)}) collective-permute-start(bf16[2064,128]{1,0:T(8,128)(2,1)S(1)} %collective-permute-done.11.a_ref), channel_id=1, source_target_pairs={{0,4},{1,5},{4,8},{5,9},{8,12},{9,13},{12,14},{13,15},{14,10},{15,... | collective-permute-start | bytes 1585160 | tf_op jit(solution)/shard_map/ppermute | solution.py:246
  69.7 3.5 %expert_part.11 = f32[128,2048]{1,0:T(8,128)S(1)} custom-call(s32[2]{0:T(128)S(1)} %pad_add_fusion.me_ref, bf16[2064,128]{1,0:T(8,128)(2,1)S(1)} %collective-permute-done.11.a_ref, bf16[2064,128]{1,0:T(8,128)(2,1)S(1)} %collective-permute-done.13.b_ref, bf16[2048,768]{1,0:T(8,128)(2,1)S(1)} %get-tuple-element.32.refs_0_, bf16[768,2048]{1,0:T(8,128)(2,1)S(1)} %copy-done.1, ...), custom_call_target="tpu_custom_call" | custom-call | flops 2415919104 | bytes 14680064 | tf_op jit(solution)/shard_map/expert_part/pallas_call | solution.py:162
  75.0 1.6 %collective-permute-start.21 = (bf16[64,2048]{1,0:T(8,128)(2,1)S(1)}, bf16[64,2048]{1,0:T(8,128)(2,1)S(1)}, u32[]{:S(2)}, u32[]{:S(2)}) collective-permute-start(bf16[64,2048]{1,0:T(8,128)(2,1)S(1)} %get-tuple-element.60), channel_id=1, source_target_pairs={{0,4},{1,5},{4,8},{5,9},{8,12},{9,13},{12,14},{13,15},{14,10},{15,... | collective-permute-start | bytes 786440 | tf_op jit(solution)/shard_map/ppermute | solution.py:246
  78.6 6.0 %collective-permute-done.12.a_ref = bf16[2064,128]{1,0:T(8,128)(2,1)S(1)} collective-permute-done((bf16[2064,128]{1,0:T(8,128)(2,1)S(1)}, bf16[2064,128]{1,0:T(8,128)(2,1)S(1)}, u32[]{:S(2)}, u32[]{:S(2)}) %collective-permute-start.12) | collective-permute-done | bytes 528416 | tf_op jit(solution)/shard_map/ppermute | solution.py:246
  88.2 3.5 %expert_part.10 = f32[128,2048]{1,0:T(8,128)S(1)} custom-call(s32[2]{0:T(128)S(1)} %pad_add_fusion.me_ref, bf16[2064,128]{1,0:T(8,128)(2,1)S(1)} %collective-permute-done.12.a_ref, bf16[2064,128]{1,0:T(8,128)(2,1)S(1)} %collective-permute-done.14.b_ref, bf16[2048,768]{1,0:T(8,128)(2,1)S(1)} %get-tuple-element.32.refs_0_, bf16[768,2048]{1,0:T(8,128)(2,1)S(1)} %copy-done.1, ...), custom_call_target="tpu_custom_call" | custom-call | flops 2415919104 | bytes 14680064 | tf_op jit(solution)/shard_map/expert_part/pallas_call | solution.py:162
  94.0 7.5 %collective-permute-done.15.a_ref = bf16[2064,128]{1,0:T(8,128)(2,1)S(1)} collective-permute-done((bf16[2064,128]{1,0:T(8,128)(2,1)S(1)}, bf16[2064,128]{1,0:T(8,128)(2,1)S(1)}, u32[]{:S(2)}, u32[]{:S(2)}) %collective-permute-start.15) | collective-permute-done | bytes 528416 | tf_op jit(solution)/shard_map/ppermute | solution.py:246
  105.1 3.6 %expert_part.9 = f32[128,2048]{1,0:T(8,128)S(1)} custom-call(s32[2]{0:T(128)S(1)} %pad_add_fusion.me_ref, bf16[2064,128]{1,0:T(8,128)(2,1)S(1)} %collective-permute-done.15.a_ref, bf16[2064,128]{1,0:T(8,128)(2,1)S(1)} %collective-permute-done.16.b_ref, bf16[2048,768]{1,0:T(8,128)(2,1)S(1)} %get-tuple-element.32.refs_0_, bf16[768,2048]{1,0:T(8,128)(2,1)S(1)} %copy-done.1, ...), custom_call_target="tpu_custom_call" | custom-call | flops 2415919104 | bytes 14680064 | tf_op jit(solution)/shard_map/expert_part/pallas_call | solution.py:162
  108.9 9.2 %collective-permute-done.23.b_ref = bf16[2064,128]{1,0:T(8,128)(2,1)S(1)} collective-permute-done((bf16[2064,128]{1,0:T(8,128)(2,1)S(1)}, bf16[2064,128]{1,0:T(8,128)(2,1)S(1)}, u32[]{:S(2)}, u32[]{:S(2)}) %collective-permute-start.23) | collective-permute-done | bytes 528416 | tf_op jit(solution)/shard_map/ppermute | solution.py:246
  120.2 3.5 %expert_part.15 = f32[128,2048]{1,0:T(8,128)S(1)} custom-call(s32[2]{0:T(128)S(1)} %pad_add_fusion.me_ref, bf16[2064,128]{1,0:T(8,128)(2,1)S(1)} %collective-permute-done.17.a_ref, bf16[2064,128]{1,0:T(8,128)(2,1)S(1)} %collective-permute-done.23.b_ref, bf16[2048,768]{1,0:T(8,128)(2,1)S(1)} %get-tuple-element.32.refs_0_, bf16[768,2048]{1,0:T(8,128)(2,1)S(1)} %copy-done.1, ...), custom_call_target="tpu_custom_call" | custom-call | flops 2415919104 | bytes 14680064 | tf_op jit(solution)/shard_map/expert_part/pallas_call | solution.py:162
  125.1 2.7 %collective-permute-start.30 = (bf16[64,2048]{1,0:T(8,128)(2,1)S(1)}, bf16[64,2048]{1,0:T(8,128)(2,1)S(1)}, u32[]{:S(2)}, u32[]{:S(2)}) collective-permute-start(bf16[64,2048]{1,0:T(8,128)(2,1)S(1)} %get-tuple-element.54), channel_id=1, source_target_pairs={{0,20},{1,21},{4,24},{5,25},{8,28},{9,29},{12,30},{13,31},{14,26},... | collective-permute-start | bytes 786440 | tf_op jit(solution)/shard_map/ppermute | solution.py:250
  128.1 2.1 %settle.1 = (f32[128,2048]{1,0:T(8,128)S(1)}, f32[128,2048]{1,0:T(8,128)S(1)}, f32[136,2048]{1,0:T(8,128)S(1)}) custom-call(bf16[144,2048]{1,0:T(8,128)(2,1)} %collective-permute-done.keep_hbm, bf16[128,2048]{1,0:T(8,128)(2,1)} %copy-done.4, bf16[128,2048]{1,0:T(8,128)(2,1)} %copy-done.5), custom_call_target="tpu_custom_call" | custom-call | tf_op jit(solution)/shard_map/settle/pallas_call | solution.py:204
  130.2 5.1 %collective-permute-done.30.a_ref = bf16[64,2048]{1,0:T(8,128)(2,1)S(1)} collective-permute-done((bf16[64,2048]{1,0:T(8,128)(2,1)S(1)}, bf16[64,2048]{1,0:T(8,128)(2,1)S(1)}, u32[]{:S(2)}, u32[]{:S(2)}) %collective-permute-start.30) | collective-permute-done | bytes 262176 | tf_op jit(solution)/shard_map/ppermute | solution.py:250
  135.3 1.8 %collective-permute-done.32.b_ref = bf16[64,2048]{1,0:T(8,128)(2,1)S(1)} collective-permute-done((bf16[64,2048]{1,0:T(8,128)(2,1)S(1)}, bf16[64,2048]{1,0:T(8,128)(2,1)S(1)}, u32[]{:S(2)}, u32[]{:S(2)}) %collective-permute-start.32) | collective-permute-done | bytes 262176 | tf_op jit(solution)/shard_map/ppermute | solution.py:250
  (71 shorter events, 28.1 us)
Async XLA Ops:
  0.0 20.6 %collective-permute-start.2 = (bf16[2048,768]{1,0:T(8,128)(2,1)}, bf16[2048,768]{1,0:T(8,128)(2,1)}, u32[]{:S(2)}, u32[]{:S(2)}) collective-permute-start(bf16[2048,768]{1,0:T(8,128)(2,1)} %bitcast.13), channel_id=1, source_target_pairs={{0,1},{1,0},{2,3},{3,2},{4,5},{5,4},{6,7},{7,6},{8,9},{9,8},{10,11... | collective-permute-start | bytes 9437192 | tf_op jit(solution)/shard_map/ppermute | solution.py:265
  0.5 20.2 %collective-permute-start.3 = (bf16[768,2048]{1,0:T(8,128)(2,1)}, bf16[768,2048]{1,0:T(8,128)(2,1)}, u32[]{:S(2)}, u32[]{:S(2)}) collective-permute-start(bf16[768,2048]{1,0:T(8,128)(2,1)} %bitcast.15), channel_id=1, source_target_pairs={{0,1},{1,0},{2,3},{3,2},{4,5},{5,4},{6,7},{7,6},{8,9},{9,8},{10,11... | collective-permute-start | bytes 9437192 | tf_op jit(solution)/shard_map/ppermute | solution.py:265
  3.1 15.5 %collective-permute-start.5 = (bf16[2064,128]{1,0:T(8,128)(2,1)}, bf16[2064,128]{1,0:T(8,128)(2,1)}, u32[]{:S(2)}, u32[]{:S(2)}) collective-permute-start(bf16[2064,128]{1,0:T(8,128)(2,1)} %get-tuple-element.30.a_ref), channel_id=1, source_target_pairs={{0,4},{1,5},{4,8},{5,9},{8,12},{9,13},{12,14},{13,15},{14,10},{15,... | collective-permute-start | bytes 1585160 | tf_op jit(solution)/shard_map/ppermute | solution.py:246
  6.2 14.2 %collective-permute-start.7 = (bf16[2064,128]{1,0:T(8,128)(2,1)}, bf16[2064,128]{1,0:T(8,128)(2,1)}, u32[]{:S(2)}, u32[]{:S(2)}) collective-permute-start(bf16[2064,128]{1,0:T(8,128)(2,1)} %get-tuple-element.31.b_ref), channel_id=1, source_target_pairs={{0,2},{1,3},{4,0},{5,1},{8,4},{9,5},{12,8},{13,9},{14,12},{15,13},... | collective-permute-start | bytes 1585160 | tf_op jit(solution)/shard_map/ppermute | solution.py:246
  6.2 24.6 %collective-permute-start = (bf16[144,2048]{1,0:T(8,128)(2,1)}, bf16[144,2048]{1,0:T(8,128)(2,1)}, u32[]{:S(2)}, u32[]{:S(2)}) collective-permute-start(bf16[144,2048]{1,0:T(8,128)(2,1)} %get-tuple-element.29), channel_id=1, source_target_pairs={{0,16},{16,0},{1,17},{17,1},{2,18},{18,2},{3,19},{19,3},{4,20},{20... | collective-permute-start | bytes 1769480 | tf_op jit(solution)/shard_map/ppermute | solution.py:262
  18.6 15.2 %collective-permute-start.6 = (bf16[2064,128]{1,0:T(8,128)(2,1)}, bf16[2064,128]{1,0:T(8,128)(2,1)S(1)}, u32[]{:S(2)}, u32[]{:S(2)}) collective-permute-start(bf16[2064,128]{1,0:T(8,128)(2,1)} %collective-permute-done.5.a_ref), channel_id=1, source_target_pairs={{0,4},{1,5},{4,8},{5,9},{8,12},{9,13},{12,14},{13,15},{14,10},{15,... | collective-permute-start | bytes 1585160 | tf_op jit(solution)/shard_map/ppermute | solution.py:246
  20.4 14.9 %collective-permute-start.8 = (bf16[2064,128]{1,0:T(8,128)(2,1)}, bf16[2064,128]{1,0:T(8,128)(2,1)S(1)}, u32[]{:S(2)}, u32[]{:S(2)}) collective-permute-start(bf16[2064,128]{1,0:T(8,128)(2,1)} %collective-permute-done.7.b_ref), channel_id=1, source_target_pairs={{0,2},{1,3},{4,0},{5,1},{8,4},{9,5},{12,8},{13,9},{14,12},{15,13},... | collective-permute-start | bytes 1585160 | tf_op jit(solution)/shard_map/ppermute | solution.py:246
  28.7 12.2 %collective-permute-start.18 = (bf16[64,2048]{1,0:T(8,128)(2,1)S(1)}, bf16[64,2048]{1,0:T(8,128)(2,1)S(1)}, u32[]{:S(2)}, u32[]{:S(2)}) collective-permute-start(bf16[64,2048]{1,0:T(8,128)(2,1)S(1)} %get-tuple-element.66), channel_id=1, source_target_pairs={{0,4},{1,5},{4,8},{5,9},{8,12},{9,13},{12,14},{13,15},{14,10},{15,... | collective-permute-start | bytes 786440 | tf_op jit(solution)/shard_map/ppermute | solution.py:246
  30.5 10.4 %collective-permute-start.24 = (bf16[64,2048]{1,0:T(8,128)(2,1)S(1)}, bf16[64,2048]{1,0:T(8,128)(2,1)S(1)}, u32[]{:S(2)}, u32[]{:S(2)}) collective-permute-start(bf16[64,2048]{1,0:T(8,128)(2,1)S(1)} %get-tuple-element.65), channel_id=1, source_target_pairs={{0,2},{1,3},{4,0},{5,1},{8,4},{9,5},{12,8},{13,9},{14,12},{15,13},... | collective-permute-start | bytes 786440 | tf_op jit(solution)/shard_map/ppermute | solution.py:246
  35.3 16.9 %collective-permute-start.10 = (bf16[2064,128]{1,0:T(8,128)(2,1)S(1)}, bf16[2064,128]{1,0:T(8,128)(2,1)S(1)}, u32[]{:S(2)}, u32[]{:S(2)}) collective-permute-start(bf16[2064,128]{1,0:T(8,128)(2,1)S(1)} %collective-permute-done.8.b_ref), channel_id=1, source_target_pairs={{0,2},{1,3},{4,0},{5,1},{8,4},{9,5},{12,8},{13,9},{14,12},{15,13},... | collective-permute-start | bytes 1585160 | tf_op jit(solution)/shard_map/ppermute | solution.py:246
  35.8 16.5 %collective-permute-start.9 = (bf16[2064,128]{1,0:T(8,128)(2,1)S(1)}, bf16[2064,128]{1,0:T(8,128)(2,1)S(1)}, u32[]{:S(2)}, u32[]{:S(2)}) collective-permute-start(bf16[2064,128]{1,0:T(8,128)(2,1)S(1)} %collective-permute-done.6.a_ref), channel_id=1, source_target_pairs={{0,4},{1,5},{4,8},{5,9},{8,12},{9,13},{12,14},{13,15},{14,10},{15,... | collective-permute-start | bytes 1585160 | tf_op jit(solution)/shard_map/ppermute | solution.py:246
  41.1 16.8 %collective-permute-start.19 = (bf16[64,2048]{1,0:T(8,128)(2,1)S(1)}, bf16[64,2048]{1,0:T(8,128)(2,1)S(1)}, u32[]{:S(2)}, u32[]{:S(2)}) collective-permute-start(bf16[64,2048]{1,0:T(8,128)(2,1)S(1)} %get-tuple-element.64), channel_id=1, source_target_pairs={{0,4},{1,5},{4,8},{5,9},{8,12},{9,13},{12,14},{13,15},{14,10},{15,... | collective-permute-start | bytes 786440 | tf_op jit(solution)/shard_map/ppermute | solution.py:246
  42.7 15.2 %collective-permute-start.25 = (bf16[64,2048]{1,0:T(8,128)(2,1)S(1)}, bf16[64,2048]{1,0:T(8,128)(2,1)S(1)}, u32[]{:S(2)}, u32[]{:S(2)}) collective-permute-start(bf16[64,2048]{1,0:T(8,128)(2,1)S(1)} %get-tuple-element.63), channel_id=1, source_target_pairs={{0,2},{1,3},{4,0},{5,1},{8,4},{9,5},{12,8},{13,9},{14,12},{15,13},... | collective-permute-start | bytes 786440 | tf_op jit(solution)/shard_map/ppermute | solution.py:246
  52.3 15.4 %collective-permute-start.11 = (bf16[2064,128]{1,0:T(8,128)(2,1)S(1)}, bf16[2064,128]{1,0:T(8,128)(2,1)S(1)}, u32[]{:S(2)}, u32[]{:S(2)}) collective-permute-start(bf16[2064,128]{1,0:T(8,128)(2,1)S(1)} %collective-permute-done.9.a_ref), channel_id=1, source_target_pairs={{0,4},{1,5},{4,8},{5,9},{8,12},{9,13},{12,14},{13,15},{14,10},{15,... | collective-permute-start | bytes 1585160 | tf_op jit(solution)/shard_map/ppermute | solution.py:246
  53.9 15.6 %collective-permute-start.13 = (bf16[2064,128]{1,0:T(8,128)(2,1)S(1)}, bf16[2064,128]{1,0:T(8,128)(2,1)S(1)}, u32[]{:S(2)}, u32[]{:S(2)}) collective-permute-start(bf16[2064,128]{1,0:T(8,128)(2,1)S(1)} %collective-permute-done.10.b_ref), channel_id=1, source_target_pairs={{0,2},{1,3},{4,0},{5,1},{8,4},{9,5},{12,8},{13,9},{14,12},{15,13},... | collective-permute-start | bytes 1585160 | tf_op jit(solution)/shard_map/ppermute | solution.py:246
  58.0 15.2 %collective-permute-start.20 = (bf16[64,2048]{1,0:T(8,128)(2,1)S(1)}, bf16[64,2048]{1,0:T(8,128)(2,1)S(1)}, u32[]{:S(2)}, u32[]{:S(2)}) collective-permute-start(bf16[64,2048]{1,0:T(8,128)(2,1)S(1)} %get-tuple-element.62), channel_id=1, source_target_pairs={{0,4},{1,5},{4,8},{5,9},{8,12},{9,13},{12,14},{13,15},{14,10},{15,... | collective-permute-start | bytes 786440 | tf_op jit(solution)/shard_map/ppermute | solution.py:246
  59.6 15.2 %collective-permute-start.26 = (bf16[64,2048]{1,0:T(8,128)(2,1)S(1)}, bf16[64,2048]{1,0:T(8,128)(2,1)S(1)}, u32[]{:S(2)}, u32[]{:S(2)}) collective-permute-start(bf16[64,2048]{1,0:T(8,128)(2,1)S(1)} %get-tuple-element.61), channel_id=1, source_target_pairs={{0,2},{1,3},{4,0},{5,1},{8,4},{9,5},{12,8},{13,9},{14,12},{15,13},... | collective-permute-start | bytes 786440 | tf_op jit(solution)/shard_map/ppermute | solution.py:246
  60.1 16.9 %collective-permute-start.1 = (bf16[128,2048]{1,0:T(8,128)(2,1)S(1)}, bf16[128,2048]{1,0:T(8,128)(2,1)S(1)}, u32[]{:S(2)}, u32[]{:S(2)}) collective-permute-start(bf16[128,2048]{1,0:T(8,128)(2,1)S(1)} %bitcast.19), channel_id=1, source_target_pairs={{0,16},{16,0},{1,17},{17,1},{2,18},{18,2},{3,19},{19,3},{4,20},{20... | collective-permute-start | bytes 1572872 | tf_op jit(solution)/shard_map/ppermute | solution.py:262
  67.6 16.9 %collective-permute-start.12 = (bf16[2064,128]{1,0:T(8,128)(2,1)S(1)}, bf16[2064,128]{1,0:T(8,128)(2,1)S(1)}, u32[]{:S(2)}, u32[]{:S(2)}) collective-permute-start(bf16[2064,128]{1,0:T(8,128)(2,1)S(1)} %collective-permute-done.11.a_ref), channel_id=1, source_target_pairs={{0,4},{1,5},{4,8},{5,9},{8,12},{9,13},{12,14},{13,15},{14,10},{15,... | collective-permute-start | bytes 1585160 | tf_op jit(solution)/shard_map/ppermute | solution.py:246
  69.5 16.7 %collective-permute-start.14 = (bf16[2064,128]{1,0:T(8,128)(2,1)S(1)}, bf16[2064,128]{1,0:T(8,128)(2,1)S(1)}, u32[]{:S(2)}, u32[]{:S(2)}) collective-permute-start(bf16[2064,128]{1,0:T(8,128)(2,1)S(1)} %collective-permute-done.13.b_ref), channel_id=1, source_target_pairs={{0,2},{1,3},{4,0},{5,1},{8,4},{9,5},{12,8},{13,9},{14,12},{15,13},... | collective-permute-start | bytes 1585160 | tf_op jit(solution)/shard_map/ppermute | solution.py:246
  75.0 16.8 %collective-permute-start.21 = (bf16[64,2048]{1,0:T(8,128)(2,1)S(1)}, bf16[64,2048]{1,0:T(8,128)(2,1)S(1)}, u32[]{:S(2)}, u32[]{:S(2)}) collective-permute-start(bf16[64,2048]{1,0:T(8,128)(2,1)S(1)} %get-tuple-element.60), channel_id=1, source_target_pairs={{0,4},{1,5},{4,8},{5,9},{8,12},{9,13},{12,14},{13,15},{14,10},{15,... | collective-permute-start | bytes 786440 | tf_op jit(solution)/shard_map/ppermute | solution.py:246
  76.6 15.2 %collective-permute-start.27 = (bf16[64,2048]{1,0:T(8,128)(2,1)S(1)}, bf16[64,2048]{1,0:T(8,128)(2,1)S(1)}, u32[]{:S(2)}, u32[]{:S(2)}) collective-permute-start(bf16[64,2048]{1,0:T(8,128)(2,1)S(1)} %get-tuple-element.59), channel_id=1, source_target_pairs={{0,2},{1,3},{4,0},{5,1},{8,4},{9,5},{12,8},{13,9},{14,12},{15,13},... | collective-permute-start | bytes 786440 | tf_op jit(solution)/shard_map/ppermute | solution.py:246
  77.0 16.9 %collective-permute-start.4 = (bf16[128,2048]{1,0:T(8,128)(2,1)S(1)}, bf16[128,2048]{1,0:T(8,128)(2,1)S(1)}, u32[]{:S(2)}, u32[]{:S(2)}) collective-permute-start(bf16[128,2048]{1,0:T(8,128)(2,1)S(1)} %convert_element_type.77), channel_id=1, source_target_pairs={{0,16},{16,0},{1,17},{17,1},{2,18},{18,2},{3,19},{19,3},{4,20},{20... | collective-permute-start | bytes 1572872 | tf_op jit(solution)/shard_map/ppermute | solution.py:262
  86.2 15.4 %collective-permute-start.15 = (bf16[2064,128]{1,0:T(8,128)(2,1)S(1)}, bf16[2064,128]{1,0:T(8,128)(2,1)S(1)}, u32[]{:S(2)}, u32[]{:S(2)}) collective-permute-start(bf16[2064,128]{1,0:T(8,128)(2,1)S(1)} %collective-permute-done.12.a_ref), channel_id=1, source_target_pairs={{0,4},{1,5},{4,8},{5,9},{8,12},{9,13},{12,14},{13,15},{14,10},{15,... | collective-permute-start | bytes 1585160 | tf_op jit(solution)/shard_map/ppermute | solution.py:246
  87.7 15.4 %collective-permute-start.16 = (bf16[2064,128]{1,0:T(8,128)(2,1)S(1)}, bf16[2064,128]{1,0:T(8,128)(2,1)S(1)}, u32[]{:S(2)}, u32[]{:S(2)}) collective-permute-start(bf16[2064,128]{1,0:T(8,128)(2,1)S(1)} %collective-permute-done.14.b_ref), channel_id=1, source_target_pairs={{0,2},{1,3},{4,0},{5,1},{8,4},{9,5},{12,8},{13,9},{14,12},{15,13},... | collective-permute-start | bytes 1585160 | tf_op jit(solution)/shard_map/ppermute | solution.py:246
  91.9 16.8 %collective-permute-start.22 = (bf16[64,2048]{1,0:T(8,128)(2,1)S(1)}, bf16[64,2048]{1,0:T(8,128)(2,1)S(1)}, u32[]{:S(2)}, u32[]{:S(2)}) collective-permute-start(bf16[64,2048]{1,0:T(8,128)(2,1)S(1)} %get-tuple-element.58), channel_id=1, source_target_pairs={{0,4},{1,5},{4,8},{5,9},{8,12},{9,13},{12,14},{13,15},{14,10},{15,... | collective-permute-start | bytes 786440 | tf_op jit(solution)/shard_map/ppermute | solution.py:246
  93.5 15.2 %collective-permute-start.28 = (bf16[64,2048]{1,0:T(8,128)(2,1)S(1)}, bf16[64,2048]{1,0:T(8,128)(2,1)S(1)}, u32[]{:S(2)}, u32[]{:S(2)}) collective-permute-start(bf16[64,2048]{1,0:T(8,128)(2,1)S(1)} %get-tuple-element.57), channel_id=1, source_target_pairs={{0,2},{1,3},{4,0},{5,1},{8,4},{9,5},{12,8},{13,9},{14,12},{15,13},... | collective-permute-start | bytes 786440 | tf_op jit(solution)/shard_map/ppermute | solution.py:246
  103.1 15.0 %collective-permute-start.23 = (bf16[2064,128]{1,0:T(8,128)(2,1)S(1)}, bf16[2064,128]{1,0:T(8,128)(2,1)S(1)}, u32[]{:S(2)}, u32[]{:S(2)}) collective-permute-start(bf16[2064,128]{1,0:T(8,128)(2,1)S(1)} %collective-permute-done.16.b_ref), channel_id=1, source_target_pairs={{0,2},{1,3},{4,0},{5,1},{8,4},{9,5},{12,8},{13,9},{14,12},{15,13},... | collective-permute-start | bytes 1585160 | tf_op jit(solution)/shard_map/ppermute | solution.py:246
  103.5 14.6 %collective-permute-start.17 = (bf16[2064,128]{1,0:T(8,128)(2,1)S(1)}, bf16[2064,128]{1,0:T(8,128)(2,1)S(1)}, u32[]{:S(2)}, u32[]{:S(2)}) collective-permute-start(bf16[2064,128]{1,0:T(8,128)(2,1)S(1)} %collective-permute-done.15.a_ref), channel_id=1, source_target_pairs={{0,4},{1,5},{4,8},{5,9},{8,12},{9,13},{12,14},{13,15},{14,10},{15,... | collective-permute-start | bytes 1585160 | tf_op jit(solution)/shard_map/ppermute | solution.py:246
  118.1 6.4 %collective-permute-start.31 = (bf16[64,2048]{1,0:T(8,128)(2,1)S(1)}, bf16[64,2048]{1,0:T(8,128)(2,1)S(1)}, u32[]{:S(2)}, u32[]{:S(2)}) collective-permute-start(bf16[64,2048]{1,0:T(8,128)(2,1)S(1)} %get-tuple-element.52), channel_id=1, source_target_pairs={{0,2},{1,3},{4,0},{5,1},{8,4},{9,5},{12,8},{13,9},{14,12},{15,13},... | collective-permute-start | bytes 786440 | tf_op jit(solution)/shard_map/ppermute | solution.py:246
  125.1 10.2 %collective-permute-start.30 = (bf16[64,2048]{1,0:T(8,128)(2,1)S(1)}, bf16[64,2048]{1,0:T(8,128)(2,1)S(1)}, u32[]{:S(2)}, u32[]{:S(2)}) collective-permute-start(bf16[64,2048]{1,0:T(8,128)(2,1)S(1)} %get-tuple-element.54), channel_id=1, source_target_pairs={{0,20},{1,21},{4,24},{5,25},{8,28},{9,29},{12,30},{13,31},{14,26},... | collective-permute-start | bytes 786440 | tf_op jit(solution)/shard_map/ppermute | solution.py:250
  127.8 9.3 %collective-permute-start.32 = (bf16[64,2048]{1,0:T(8,128)(2,1)S(1)}, bf16[64,2048]{1,0:T(8,128)(2,1)S(1)}, u32[]{:S(2)}, u32[]{:S(2)}) collective-permute-start(bf16[64,2048]{1,0:T(8,128)(2,1)S(1)} %get-tuple-element.53), channel_id=1, source_target_pairs={{0,18},{1,19},{4,16},{5,17},{8,20},{9,21},{12,24},{13,25},{14,28},... | collective-permute-start | bytes 786440 | tf_op jit(solution)/shard_map/ppermute | solution.py:250
  (8 other events, 69.9 us)

commit v8 on v7

--- a/solution.py
+++ b/solution.py
@@ -290,9 +290,6 @@
             part_a = part_a + sum_a.astype(jnp.float32)
             part_b = part_b + sum_b.astype(jnp.float32)
         send_a, send_b = part_a.astype(jnp.bfloat16), part_b.astype(jnp.bfloat16)
-        if step == chips - 2:
-            a1, send_a = lax.optimization_barrier((a1, send_a))
-            b1, send_b = lax.optimization_barrier((b1, send_b))
         move = hop if step < chips - 1 else last_hop
         sum_a, sum_b = move(send_a, 1), move(send_b, -1)
     held = settle(keep_out, grad_out, own_out)

time: 139 us -> 138 us (level)
  no operation moved by 1% of the time
where the time goes in v8:
time: 138 us
  waiting for transfers between devices  54.2 us (39%)
  Pallas kernels  42.9 us (31%)
  starting transfers between devices  36.2 us (26%)
  local copies, waits for them, and re-layouts  3.51 us (3%)
    ppermute x26, waiting for transfers between devices, hop(): lax.ppermute(value, 'expert', [(2 * a + c, 2 * b + c) for a, b in moves f...  46.3 us
    pallas_call x8, Pallas kernels, expert_part(): pl.pallas_call(expert_kernel, out_shape=jax.ShapeDtypeStruct((rows, width...  29.5 us
    ppermute x26, starting transfers between devices, hop(): lax.ppermute(value, 'expert', [(2 * a + c, 2 * b + c) for a, b in moves f...  27.7 us
    ppermute x2, waiting for transfers between devices, last_hop(): lax.ppermute(value, ('pipe', 'expert'), [(s * experts + 2 * a + c, (s - 1...  7.88 us
    pallas_call x2, Pallas kernels, turn(): pl.pallas_call(turn_kernel, out_shape=[pltpu.VMEM(shape, up.dtype) for sh...  7.45 us
    ppermute x3, starting transfers between devices, to_previous(): lax.ppermute(value, 'pipe', [(s, (s - 1) % sections) for s in range(secti...  5.01 us
    unnamed x14, local copies, waits for them, and re-layouts  3.47 us
    ppermute x2, starting transfers between devices, last_hop(): lax.ppermute(value, ('pipe', 'expert'), [(s * experts + 2 * a + c, (s - 1...  2.98 us
  transfers between devices with their start and end apart: 33, of which 15 were waited for; matrix products, arithmetic and copies ran while one was open for 1% of the time, Pallas kernels for 30%

profile of v8, /device:TPU:0, one launch (start us, length us, event | category | flops | bytes accessed | tf_op | source)
XLA Modules:
  0.0 138.1 jit_solution(14804469721108933024)
XLA Ops:
  0.5 2.6 %pack.1 = (bf16[2064,128]{1,0:T(8,128)(2,1)}, bf16[2064,128]{1,0:T(8,128)(2,1)}, bf16[144,2048]{1,0:T(8,128)(2,1)}) custom-call(bf16[128,2048]{1,0:T(8,128)(2,1)} %bitcast.17, bf16[128,2048]{1,0:T(8,128)(2,1)} %bitcast.18, f32[1,2048]{1,0:T(1,128)} %gain_hbm.1, s32[8,128]{1,0:T(8,128)} %bitcast.20, bf16[8,128]{1,0:T(8,128)(2,1)} %bitcast.21), custom_call_target="tpu_custom_call" | custom-call | tf_op jit(solution)/shard_map/pack/pallas_call | solution.py:61
  3.1 3.1 %collective-permute-start.5 = (bf16[2064,128]{1,0:T(8,128)(2,1)}, bf16[2064,128]{1,0:T(8,128)(2,1)}, u32[]{:S(2)}, u32[]{:S(2)}) collective-permute-start(bf16[2064,128]{1,0:T(8,128)(2,1)} %get-tuple-element.26.a_ref), channel_id=1, source_target_pairs={{0,4},{1,5},{4,8},{5,9},{8,12},{9,13},{12,14},{13,15},{14,10},{15,... | collective-permute-start | bytes 1585160 | tf_op jit(solution)/shard_map/ppermute | solution.py:246
  6.2 2.0 %collective-permute-start = (bf16[144,2048]{1,0:T(8,128)(2,1)}, bf16[144,2048]{1,0:T(8,128)(2,1)}, u32[]{:S(2)}, u32[]{:S(2)}) collective-permute-start(bf16[144,2048]{1,0:T(8,128)(2,1)} %get-tuple-element.25), channel_id=1, source_target_pairs={{0,16},{16,0},{1,17},{17,1},{2,18},{18,2},{3,19},{19,3},{4,20},{20... | collective-permute-start | bytes 1769480 | tf_op jit(solution)/shard_map/ppermute | solution.py:262
  8.2 3.7 %turn.2 = (bf16[2048,768]{1,0:T(8,128)(2,1)S(1)}, bf16[768,2048]{1,0:T(8,128)(2,1)S(1)}, bf16[2048,768]{1,0:T(8,128)(2,1)S(1)}) custom-call(bf16[2048,768]{1,0:T(8,128)(2,1)} %bitcast.14, bf16[768,2048]{1,0:T(8,128)(2,1)} %bitcast.16), custom_call_target="tpu_custom_call" | custom-call | tf_op jit(solution)/shard_map/turn/pallas_call | solution.py:114
  11.9 1.7 %copy-done = bf16[768,2048]{1,0:T(8,128)(2,1)} copy-done((bf16[768,2048]{1,0:T(8,128)(2,1)}, bf16[768,2048]{1,0:T(8,128)(2,1)S(1)}, u32[]{:S(2)}) %copy-start) | copy-done | bytes 3145752
  13.6 1.7 %copy-done.2 = bf16[2048,768]{1,0:T(8,128)(2,1)} copy-done((bf16[2048,768]{1,0:T(8,128)(2,1)}, bf16[2048,768]{1,0:T(8,128)(2,1)S(1)}, u32[]{:S(2)}) %copy-start.2) | copy-done | bytes 3145752
  15.4 3.2 %collective-permute-done.5.a_ref = bf16[2064,128]{1,0:T(8,128)(2,1)} collective-permute-done((bf16[2064,128]{1,0:T(8,128)(2,1)}, bf16[2064,128]{1,0:T(8,128)(2,1)}, u32[]{:S(2)}, u32[]{:S(2)}) %collective-permute-start.5) | collective-permute-done | bytes 528416 | tf_op jit(solution)/shard_map/ppermute | solution.py:246
  18.6 1.8 %collective-permute-start.6 = (bf16[2064,128]{1,0:T(8,128)(2,1)}, bf16[2064,128]{1,0:T(8,128)(2,1)S(1)}, u32[]{:S(2)}, u32[]{:S(2)}) collective-permute-start(bf16[2064,128]{1,0:T(8,128)(2,1)} %collective-permute-done.5.a_ref), channel_id=1, source_target_pairs={{0,4},{1,5},{4,8},{5,9},{8,12},{9,13},{12,14},{13,15},{14,10},{15,... | collective-permute-start | bytes 1585160 | tf_op jit(solution)/shard_map/ppermute | solution.py:246
  20.6 3.7 %turn.3 = (bf16[2048,768]{1,0:T(8,128)(2,1)S(1)}, bf16[768,2048]{1,0:T(8,128)(2,1)S(1)}, bf16[2048,768]{1,0:T(8,128)(2,1)S(1)}) custom-call(bf16[2048,768]{1,0:T(8,128)(2,1)} %collective-permute-done.2.up_hbm, bf16[768,2048]{1,0:T(8,128)(2,1)} %collective-permute-done.3.down_hbm), custom_call_target="tpu_custom_call" | custom-call | tf_op jit(solution)/shard_map/turn/pallas_call | solution.py:114
  24.4 4.2 %expert_part.15 = f32[128,2048]{1,0:T(8,128)S(1)} custom-call(s32[2]{0:T(128)S(1)} %pad_add_fusion.me_ref, bf16[2064,128]{1,0:T(8,128)(2,1)} %collective-permute-done.5.a_ref, bf16[2064,128]{1,0:T(8,128)(2,1)} %collective-permute-done.7.b_ref, bf16[2048,768]{1,0:T(8,128)(2,1)S(1)} %get-tuple-element.28.refs_0_, bf16[768,2048]{1,0:T(8,128)(2,1)S(1)} %copy-done.1, ...), custom_call_target="tpu_custom_call" | custom-call | flops 2415919104 | bytes 14680064 | tf_op jit(solution)/shard_map/expert_part/pallas_call | solution.py:162
  28.7 1.9 %collective-permute-start.19 = (bf16[64,2048]{1,0:T(8,128)(2,1)S(1)}, bf16[64,2048]{1,0:T(8,128)(2,1)S(1)}, u32[]{:S(2)}, u32[]{:S(2)}) collective-permute-start(bf16[64,2048]{1,0:T(8,128)(2,1)S(1)} %get-tuple-element.58), channel_id=1, source_target_pairs={{0,4},{1,5},{4,8},{5,9},{8,12},{9,13},{12,14},{13,15},{14,10},{15,... | collective-permute-start | bytes 786440 | tf_op jit(solution)/shard_map/ppermute | solution.py:246
  30.7 3.0 %collective-permute-done.6.a_ref = bf16[2064,128]{1,0:T(8,128)(2,1)S(1)} collective-permute-done((bf16[2064,128]{1,0:T(8,128)(2,1)}, bf16[2064,128]{1,0:T(8,128)(2,1)S(1)}, u32[]{:S(2)}, u32[]{:S(2)}) %collective-permute-start.6) | collective-permute-done | bytes 528416 | tf_op jit(solution)/shard_map/ppermute | solution.py:246
  37.4 3.5 %expert_part.14 = f32[128,2048]{1,0:T(8,128)S(1)} custom-call(s32[2]{0:T(128)S(1)} %pad_add_fusion.me_ref, bf16[2064,128]{1,0:T(8,128)(2,1)S(1)} %collective-permute-done.6.a_ref, bf16[2064,128]{1,0:T(8,128)(2,1)S(1)} %collective-permute-done.8.b_ref, bf16[2048,768]{1,0:T(8,128)(2,1)S(1)} %get-tuple-element.28.refs_0_, bf16[768,2048]{1,0:T(8,128)(2,1)S(1)} %copy-done.1, ...), custom_call_target="tpu_custom_call" | custom-call | flops 2415919104 | bytes 14680064 | tf_op jit(solution)/shard_map/expert_part/pallas_call | solution.py:162
  41.1 1.6 %collective-permute-start.20 = (bf16[64,2048]{1,0:T(8,128)(2,1)S(1)}, bf16[64,2048]{1,0:T(8,128)(2,1)S(1)}, u32[]{:S(2)}, u32[]{:S(2)}) collective-permute-start(bf16[64,2048]{1,0:T(8,128)(2,1)S(1)} %get-tuple-element.56), channel_id=1, source_target_pairs={{0,4},{1,5},{4,8},{5,9},{8,12},{9,13},{12,14},{13,15},{14,10},{15,... | collective-permute-start | bytes 786440 | tf_op jit(solution)/shard_map/ppermute | solution.py:246
  43.2 4.1 %expert_part.8 = f32[128,2048]{1,0:T(8,128)S(1)} custom-call(s32[2]{0:T(128)S(1)} %pad_add_fusion.me_ref, bf16[2064,128]{1,0:T(8,128)(2,1)} %get-tuple-element.26.a_ref, bf16[2064,128]{1,0:T(8,128)(2,1)} %get-tuple-element.27.b_ref, bf16[2048,768]{1,0:T(8,128)(2,1)S(1)} %get-tuple-element.28.refs_0_, bf16[768,2048]{1,0:T(8,128)(2,1)S(1)} %copy-done.1, ...), custom_call_target="tpu_custom_call" | custom-call | flops 2415919104 | bytes 14680064 | tf_op jit(solution)/shard_map/expert_part/pallas_call | solution.py:162
  47.4 4.9 %collective-permute-done.10.b_ref = bf16[2064,128]{1,0:T(8,128)(2,1)S(1)} collective-permute-done((bf16[2064,128]{1,0:T(8,128)(2,1)S(1)}, bf16[2064,128]{1,0:T(8,128)(2,1)S(1)}, u32[]{:S(2)}, u32[]{:S(2)}) %collective-permute-start.10) | collective-permute-done | bytes 528416 | tf_op jit(solution)/shard_map/ppermute | solution.py:246
  54.3 3.5 %expert_part.13 = f32[128,2048]{1,0:T(8,128)S(1)} custom-call(s32[2]{0:T(128)S(1)} %pad_add_fusion.me_ref, bf16[2064,128]{1,0:T(8,128)(2,1)S(1)} %collective-permute-done.9.a_ref, bf16[2064,128]{1,0:T(8,128)(2,1)S(1)} %collective-permute-done.10.b_ref, bf16[2048,768]{1,0:T(8,128)(2,1)S(1)} %get-tuple-element.28.refs_0_, bf16[768,2048]{1,0:T(8,128)(2,1)S(1)} %copy-done.1, ...), custom_call_target="tpu_custom_call" | custom-call | flops 2415919104 | bytes 14680064 | tf_op jit(solution)/shard_map/expert_part/pallas_call | solution.py:162
  58.0 1.6 %collective-permute-start.21 = (bf16[64,2048]{1,0:T(8,128)(2,1)S(1)}, bf16[64,2048]{1,0:T(8,128)(2,1)S(1)}, u32[]{:S(2)}, u32[]{:S(2)}) collective-permute-start(bf16[64,2048]{1,0:T(8,128)(2,1)S(1)} %get-tuple-element.54), channel_id=1, source_target_pairs={{0,4},{1,5},{4,8},{5,9},{8,12},{9,13},{12,14},{13,15},{14,10},{15,... | collective-permute-start | bytes 786440 | tf_op jit(solution)/shard_map/ppermute | solution.py:246
  61.6 6.0 %collective-permute-done.11.a_ref = bf16[2064,128]{1,0:T(8,128)(2,1)S(1)} collective-permute-done((bf16[2064,128]{1,0:T(8,128)(2,1)S(1)}, bf16[2064,128]{1,0:T(8,128)(2,1)S(1)}, u32[]{:S(2)}, u32[]{:S(2)}) %collective-permute-start.11) | collective-permute-done | bytes 528416 | tf_op jit(solution)/shard_map/ppermute | solution.py:246
  67.6 1.8 %collective-permute-start.12 = (bf16[2064,128]{1,0:T(8,128)(2,1)S(1)}, bf16[2064,128]{1,0:T(8,128)(2,1)S(1)}, u32[]{:S(2)}, u32[]{:S(2)}) collective-permute-start(bf16[2064,128]{1,0:T(8,128)(2,1)S(1)} %collective-permute-done.11.a_ref), channel_id=1, source_target_pairs={{0,4},{1,5},{4,8},{5,9},{8,12},{9,13},{12,14},{13,15},{14,10},{15,... | collective-permute-start | bytes 1585160 | tf_op jit(solution)/shard_map/ppermute | solution.py:246
  69.7 3.5 %expert_part.12 = f32[128,2048]{1,0:T(8,128)S(1)} custom-call(s32[2]{0:T(128)S(1)} %pad_add_fusion.me_ref, bf16[2064,128]{1,0:T(8,128)(2,1)S(1)} %collective-permute-done.11.a_ref, bf16[2064,128]{1,0:T(8,128)(2,1)S(1)} %collective-permute-done.13.b_ref, bf16[2048,768]{1,0:T(8,128)(2,1)S(1)} %get-tuple-element.28.refs_0_, bf16[768,2048]{1,0:T(8,128)(2,1)S(1)} %copy-done.1, ...), custom_call_target="tpu_custom_call" | custom-call | flops 2415919104 | bytes 14680064 | tf_op jit(solution)/shard_map/expert_part/pallas_call | solution.py:162
  75.0 1.6 %collective-permute-start.22 = (bf16[64,2048]{1,0:T(8,128)(2,1)S(1)}, bf16[64,2048]{1,0:T(8,128)(2,1)S(1)}, u32[]{:S(2)}, u32[]{:S(2)}) collective-permute-start(bf16[64,2048]{1,0:T(8,128)(2,1)S(1)} %get-tuple-element.52), channel_id=1, source_target_pairs={{0,4},{1,5},{4,8},{5,9},{8,12},{9,13},{12,14},{13,15},{14,10},{15,... | collective-permute-start | bytes 786440 | tf_op jit(solution)/shard_map/ppermute | solution.py:246
  78.6 6.0 %collective-permute-done.12.a_ref = bf16[2064,128]{1,0:T(8,128)(2,1)S(1)} collective-permute-done((bf16[2064,128]{1,0:T(8,128)(2,1)S(1)}, bf16[2064,128]{1,0:T(8,128)(2,1)S(1)}, u32[]{:S(2)}, u32[]{:S(2)}) %collective-permute-start.12) | collective-permute-done | bytes 528416 | tf_op jit(solution)/shard_map/ppermute | solution.py:246
  88.2 3.5 %expert_part.11 = f32[128,2048]{1,0:T(8,128)S(1)} custom-call(s32[2]{0:T(128)S(1)} %pad_add_fusion.me_ref, bf16[2064,128]{1,0:T(8,128)(2,1)S(1)} %collective-permute-done.12.a_ref, bf16[2064,128]{1,0:T(8,128)(2,1)S(1)} %collective-permute-done.14.b_ref, bf16[2048,768]{1,0:T(8,128)(2,1)S(1)} %get-tuple-element.28.refs_0_, bf16[768,2048]{1,0:T(8,128)(2,1)S(1)} %copy-done.1, ...), custom_call_target="tpu_custom_call" | custom-call | flops 2415919104 | bytes 14680064 | tf_op jit(solution)/shard_map/expert_part/pallas_call | solution.py:162
  94.0 7.5 %collective-permute-done.15.a_ref = bf16[2064,128]{1,0:T(8,128)(2,1)S(1)} collective-permute-done((bf16[2064,128]{1,0:T(8,128)(2,1)S(1)}, bf16[2064,128]{1,0:T(8,128)(2,1)S(1)}, u32[]{:S(2)}, u32[]{:S(2)}) %collective-permute-start.15) | collective-permute-done | bytes 528416 | tf_op jit(solution)/shard_map/ppermute | solution.py:246
  105.1 3.6 %expert_part.10 = f32[128,2048]{1,0:T(8,128)S(1)} custom-call(s32[2]{0:T(128)S(1)} %pad_add_fusion.me_ref, bf16[2064,128]{1,0:T(8,128)(2,1)S(1)} %collective-permute-done.15.a_ref, bf16[2064,128]{1,0:T(8,128)(2,1)S(1)} %collective-permute-done.16.b_ref, bf16[2048,768]{1,0:T(8,128)(2,1)S(1)} %get-tuple-element.28.refs_0_, bf16[768,2048]{1,0:T(8,128)(2,1)S(1)} %copy-done.1, ...), custom_call_target="tpu_custom_call" | custom-call | flops 2415919104 | bytes 14680064 | tf_op jit(solution)/shard_map/expert_part/pallas_call | solution.py:162
  111.0 7.5 %collective-permute-done.17.a_ref = bf16[2064,128]{1,0:T(8,128)(2,1)S(1)} collective-permute-done((bf16[2064,128]{1,0:T(8,128)(2,1)S(1)}, bf16[2064,128]{1,0:T(8,128)(2,1)S(1)}, u32[]{:S(2)}, u32[]{:S(2)}) %collective-permute-start.17) | collective-permute-done | bytes 528416 | tf_op jit(solution)/shard_map/ppermute | solution.py:246
  120.0 3.5 %expert_part.9 = f32[128,2048]{1,0:T(8,128)S(1)} custom-call(s32[2]{0:T(128)S(1)} %pad_add_fusion.me_ref, bf16[2064,128]{1,0:T(8,128)(2,1)S(1)} %collective-permute-done.17.a_ref, bf16[2064,128]{1,0:T(8,128)(2,1)S(1)} %collective-permute-done.18.b_ref, bf16[2048,768]{1,0:T(8,128)(2,1)S(1)} %get-tuple-element.28.refs_0_, bf16[768,2048]{1,0:T(8,128)(2,1)S(1)} %copy-done.1, ...), custom_call_target="tpu_custom_call" | custom-call | flops 2415919104 | bytes 14680064 | tf_op jit(solution)/shard_map/expert_part/pallas_call | solution.py:162
  123.9 2.6 %collective-permute-start.25 = (bf16[64,2048]{1,0:T(8,128)(2,1)S(1)}, bf16[64,2048]{1,0:T(8,128)(2,1)S(1)}, u32[]{:S(2)}, u32[]{:S(2)}) collective-permute-start(bf16[64,2048]{1,0:T(8,128)(2,1)S(1)} %get-tuple-element.46), channel_id=1, source_target_pairs={{0,20},{1,21},{4,24},{5,25},{8,28},{9,29},{12,30},{13,31},{14,26},... | collective-permute-start | bytes 786440 | tf_op jit(solution)/shard_map/ppermute | solution.py:250
  126.8 2.1 %settle.1 = (f32[128,2048]{1,0:T(8,128)S(1)}, f32[128,2048]{1,0:T(8,128)S(1)}, f32[136,2048]{1,0:T(8,128)S(1)}) custom-call(bf16[144,2048]{1,0:T(8,128)(2,1)} %collective-permute-done.keep_hbm, bf16[128,2048]{1,0:T(8,128)(2,1)} %copy-done.4, bf16[128,2048]{1,0:T(8,128)(2,1)} %copy-done.5), custom_call_target="tpu_custom_call" | custom-call | tf_op jit(solution)/shard_map/settle/pallas_call | solution.py:204
  129.0 5.6 %collective-permute-done.25.a_ref = bf16[64,2048]{1,0:T(8,128)(2,1)S(1)} collective-permute-done((bf16[64,2048]{1,0:T(8,128)(2,1)S(1)}, bf16[64,2048]{1,0:T(8,128)(2,1)S(1)}, u32[]{:S(2)}, u32[]{:S(2)}) %collective-permute-start.25) | collective-permute-done | bytes 262176 | tf_op jit(solution)/shard_map/ppermute | solution.py:250
  134.6 2.3 %collective-permute-done.32.b_ref = bf16[64,2048]{1,0:T(8,128)(2,1)S(1)} collective-permute-done((bf16[64,2048]{1,0:T(8,128)(2,1)S(1)}, bf16[64,2048]{1,0:T(8,128)(2,1)S(1)}, u32[]{:S(2)}, u32[]{:S(2)}) %collective-permute-start.32) | collective-permute-done | bytes 262176 | tf_op jit(solution)/shard_map/ppermute | solution.py:250
  (71 shorter events, 28.6 us)
Async XLA Ops:
  0.0 20.6 %collective-permute-start.2 = (bf16[2048,768]{1,0:T(8,128)(2,1)}, bf16[2048,768]{1,0:T(8,128)(2,1)}, u32[]{:S(2)}, u32[]{:S(2)}) collective-permute-start(bf16[2048,768]{1,0:T(8,128)(2,1)} %bitcast.13), channel_id=1, source_target_pairs={{0,1},{1,0},{2,3},{3,2},{4,5},{5,4},{6,7},{7,6},{8,9},{9,8},{10,11... | collective-permute-start | bytes 9437192 | tf_op jit(solution)/shard_map/ppermute | solution.py:265
  0.5 20.2 %collective-permute-start.3 = (bf16[768,2048]{1,0:T(8,128)(2,1)}, bf16[768,2048]{1,0:T(8,128)(2,1)}, u32[]{:S(2)}, u32[]{:S(2)}) collective-permute-start(bf16[768,2048]{1,0:T(8,128)(2,1)} %bitcast.15), channel_id=1, source_target_pairs={{0,1},{1,0},{2,3},{3,2},{4,5},{5,4},{6,7},{7,6},{8,9},{9,8},{10,11... | collective-permute-start | bytes 9437192 | tf_op jit(solution)/shard_map/ppermute | solution.py:265
  3.1 15.5 %collective-permute-start.5 = (bf16[2064,128]{1,0:T(8,128)(2,1)}, bf16[2064,128]{1,0:T(8,128)(2,1)}, u32[]{:S(2)}, u32[]{:S(2)}) collective-permute-start(bf16[2064,128]{1,0:T(8,128)(2,1)} %get-tuple-element.26.a_ref), channel_id=1, source_target_pairs={{0,4},{1,5},{4,8},{5,9},{8,12},{9,13},{12,14},{13,15},{14,10},{15,... | collective-permute-start | bytes 1585160 | tf_op jit(solution)/shard_map/ppermute | solution.py:246
  6.2 14.2 %collective-permute-start.7 = (bf16[2064,128]{1,0:T(8,128)(2,1)}, bf16[2064,128]{1,0:T(8,128)(2,1)}, u32[]{:S(2)}, u32[]{:S(2)}) collective-permute-start(bf16[2064,128]{1,0:T(8,128)(2,1)} %get-tuple-element.27.b_ref), channel_id=1, source_target_pairs={{0,2},{1,3},{4,0},{5,1},{8,4},{9,5},{12,8},{13,9},{14,12},{15,13},... | collective-permute-start | bytes 1585160 | tf_op jit(solution)/shard_map/ppermute | solution.py:246
  6.2 24.6 %collective-permute-start = (bf16[144,2048]{1,0:T(8,128)(2,1)}, bf16[144,2048]{1,0:T(8,128)(2,1)}, u32[]{:S(2)}, u32[]{:S(2)}) collective-permute-start(bf16[144,2048]{1,0:T(8,128)(2,1)} %get-tuple-element.25), channel_id=1, source_target_pairs={{0,16},{16,0},{1,17},{17,1},{2,18},{18,2},{3,19},{19,3},{4,20},{20... | collective-permute-start | bytes 1769480 | tf_op jit(solution)/shard_map/ppermute | solution.py:262
  18.6 15.2 %collective-permute-start.6 = (bf16[2064,128]{1,0:T(8,128)(2,1)}, bf16[2064,128]{1,0:T(8,128)(2,1)S(1)}, u32[]{:S(2)}, u32[]{:S(2)}) collective-permute-start(bf16[2064,128]{1,0:T(8,128)(2,1)} %collective-permute-done.5.a_ref), channel_id=1, source_target_pairs={{0,4},{1,5},{4,8},{5,9},{8,12},{9,13},{12,14},{13,15},{14,10},{15,... | collective-permute-start | bytes 1585160 | tf_op jit(solution)/shard_map/ppermute | solution.py:246
  20.4 14.9 %collective-permute-start.8 = (bf16[2064,128]{1,0:T(8,128)(2,1)}, bf16[2064,128]{1,0:T(8,128)(2,1)S(1)}, u32[]{:S(2)}, u32[]{:S(2)}) collective-permute-start(bf16[2064,128]{1,0:T(8,128)(2,1)} %collective-permute-done.7.b_ref), channel_id=1, source_target_pairs={{0,2},{1,3},{4,0},{5,1},{8,4},{9,5},{12,8},{13,9},{14,12},{15,13},... | collective-permute-start | bytes 1585160 | tf_op jit(solution)/shard_map/ppermute | solution.py:246
  28.7 12.2 %collective-permute-start.19 = (bf16[64,2048]{1,0:T(8,128)(2,1)S(1)}, bf16[64,2048]{1,0:T(8,128)(2,1)S(1)}, u32[]{:S(2)}, u32[]{:S(2)}) collective-permute-start(bf16[64,2048]{1,0:T(8,128)(2,1)S(1)} %get-tuple-element.58), channel_id=1, source_target_pairs={{0,4},{1,5},{4,8},{5,9},{8,12},{9,13},{12,14},{13,15},{14,10},{15,... | collective-permute-start | bytes 786440 | tf_op jit(solution)/shard_map/ppermute | solution.py:246
  30.5 10.4 %collective-permute-start.26 = (bf16[64,2048]{1,0:T(8,128)(2,1)S(1)}, bf16[64,2048]{1,0:T(8,128)(2,1)S(1)}, u32[]{:S(2)}, u32[]{:S(2)}) collective-permute-start(bf16[64,2048]{1,0:T(8,128)(2,1)S(1)} %get-tuple-element.57), channel_id=1, source_target_pairs={{0,2},{1,3},{4,0},{5,1},{8,4},{9,5},{12,8},{13,9},{14,12},{15,13},... | collective-permute-start | bytes 786440 | tf_op jit(solution)/shard_map/ppermute | solution.py:246
  35.3 16.9 %collective-permute-start.10 = (bf16[2064,128]{1,0:T(8,128)(2,1)S(1)}, bf16[2064,128]{1,0:T(8,128)(2,1)S(1)}, u32[]{:S(2)}, u32[]{:S(2)}) collective-permute-start(bf16[2064,128]{1,0:T(8,128)(2,1)S(1)} %collective-permute-done.8.b_ref), channel_id=1, source_target_pairs={{0,2},{1,3},{4,0},{5,1},{8,4},{9,5},{12,8},{13,9},{14,12},{15,13},... | collective-permute-start | bytes 1585160 | tf_op jit(solution)/shard_map/ppermute | solution.py:246
  35.8 16.5 %collective-permute-start.9 = (bf16[2064,128]{1,0:T(8,128)(2,1)S(1)}, bf16[2064,128]{1,0:T(8,128)(2,1)S(1)}, u32[]{:S(2)}, u32[]{:S(2)}) collective-permute-start(bf16[2064,128]{1,0:T(8,128)(2,1)S(1)} %collective-permute-done.6.a_ref), channel_id=1, source_target_pairs={{0,4},{1,5},{4,8},{5,9},{8,12},{9,13},{12,14},{13,15},{14,10},{15,... | collective-permute-start | bytes 1585160 | tf_op jit(solution)/shard_map/ppermute | solution.py:246
  41.1 16.8 %collective-permute-start.20 = (bf16[64,2048]{1,0:T(8,128)(2,1)S(1)}, bf16[64,2048]{1,0:T(8,128)(2,1)S(1)}, u32[]{:S(2)}, u32[]{:S(2)}) collective-permute-start(bf16[64,2048]{1,0:T(8,128)(2,1)S(1)} %get-tuple-element.56), channel_id=1, source_target_pairs={{0,4},{1,5},{4,8},{5,9},{8,12},{9,13},{12,14},{13,15},{14,10},{15,... | collective-permute-start | bytes 786440 | tf_op jit(solution)/shard_map/ppermute | solution.py:246
  42.7 15.2 %collective-permute-start.27 = (bf16[64,2048]{1,0:T(8,128)(2,1)S(1)}, bf16[64,2048]{1,0:T(8,128)(2,1)S(1)}, u32[]{:S(2)}, u32[]{:S(2)}) collective-permute-start(bf16[64,2048]{1,0:T(8,128)(2,1)S(1)} %get-tuple-element.55), channel_id=1, source_target_pairs={{0,2},{1,3},{4,0},{5,1},{8,4},{9,5},{12,8},{13,9},{14,12},{15,13},... | collective-permute-start | bytes 786440 | tf_op jit(solution)/shard_map/ppermute | solution.py:246
  52.3 15.4 %collective-permute-start.11 = (bf16[2064,128]{1,0:T(8,128)(2,1)S(1)}, bf16[2064,128]{1,0:T(8,128)(2,1)S(1)}, u32[]{:S(2)}, u32[]{:S(2)}) collective-permute-start(bf16[2064,128]{1,0:T(8,128)(2,1)S(1)} %collective-permute-done.9.a_ref), channel_id=1, source_target_pairs={{0,4},{1,5},{4,8},{5,9},{8,12},{9,13},{12,14},{13,15},{14,10},{15,... | collective-permute-start | bytes 1585160 | tf_op jit(solution)/shard_map/ppermute | solution.py:246
  53.9 15.6 %collective-permute-start.13 = (bf16[2064,128]{1,0:T(8,128)(2,1)S(1)}, bf16[2064,128]{1,0:T(8,128)(2,1)S(1)}, u32[]{:S(2)}, u32[]{:S(2)}) collective-permute-start(bf16[2064,128]{1,0:T(8,128)(2,1)S(1)} %collective-permute-done.10.b_ref), channel_id=1, source_target_pairs={{0,2},{1,3},{4,0},{5,1},{8,4},{9,5},{12,8},{13,9},{14,12},{15,13},... | collective-permute-start | bytes 1585160 | tf_op jit(solution)/shard_map/ppermute | solution.py:246
  58.0 15.2 %collective-permute-start.21 = (bf16[64,2048]{1,0:T(8,128)(2,1)S(1)}, bf16[64,2048]{1,0:T(8,128)(2,1)S(1)}, u32[]{:S(2)}, u32[]{:S(2)}) collective-permute-start(bf16[64,2048]{1,0:T(8,128)(2,1)S(1)} %get-tuple-element.54), channel_id=1, source_target_pairs={{0,4},{1,5},{4,8},{5,9},{8,12},{9,13},{12,14},{13,15},{14,10},{15,... | collective-permute-start | bytes 786440 | tf_op jit(solution)/shard_map/ppermute | solution.py:246
  59.6 15.2 %collective-permute-start.28 = (bf16[64,2048]{1,0:T(8,128)(2,1)S(1)}, bf16[64,2048]{1,0:T(8,128)(2,1)S(1)}, u32[]{:S(2)}, u32[]{:S(2)}) collective-permute-start(bf16[64,2048]{1,0:T(8,128)(2,1)S(1)} %get-tuple-element.53), channel_id=1, source_target_pairs={{0,2},{1,3},{4,0},{5,1},{8,4},{9,5},{12,8},{13,9},{14,12},{15,13},... | collective-permute-start | bytes 786440 | tf_op jit(solution)/shard_map/ppermute | solution.py:246
  60.1 16.9 %collective-permute-start.1 = (bf16[128,2048]{1,0:T(8,128)(2,1)S(1)}, bf16[128,2048]{1,0:T(8,128)(2,1)S(1)}, u32[]{:S(2)}, u32[]{:S(2)}) collective-permute-start(bf16[128,2048]{1,0:T(8,128)(2,1)S(1)} %bitcast.19), channel_id=1, source_target_pairs={{0,16},{16,0},{1,17},{17,1},{2,18},{18,2},{3,19},{19,3},{4,20},{20... | collective-permute-start | bytes 1572872 | tf_op jit(solution)/shard_map/ppermute | solution.py:262
  67.6 16.9 %collective-permute-start.12 = (bf16[2064,128]{1,0:T(8,128)(2,1)S(1)}, bf16[2064,128]{1,0:T(8,128)(2,1)S(1)}, u32[]{:S(2)}, u32[]{:S(2)}) collective-permute-start(bf16[2064,128]{1,0:T(8,128)(2,1)S(1)} %collective-permute-done.11.a_ref), channel_id=1, source_target_pairs={{0,4},{1,5},{4,8},{5,9},{8,12},{9,13},{12,14},{13,15},{14,10},{15,... | collective-permute-start | bytes 1585160 | tf_op jit(solution)/shard_map/ppermute | solution.py:246
  69.5 16.7 %collective-permute-start.14 = (bf16[2064,128]{1,0:T(8,128)(2,1)S(1)}, bf16[2064,128]{1,0:T(8,128)(2,1)S(1)}, u32[]{:S(2)}, u32[]{:S(2)}) collective-permute-start(bf16[2064,128]{1,0:T(8,128)(2,1)S(1)} %collective-permute-done.13.b_ref), channel_id=1, source_target_pairs={{0,2},{1,3},{4,0},{5,1},{8,4},{9,5},{12,8},{13,9},{14,12},{15,13},... | collective-permute-start | bytes 1585160 | tf_op jit(solution)/shard_map/ppermute | solution.py:246
  75.0 16.8 %collective-permute-start.22 = (bf16[64,2048]{1,0:T(8,128)(2,1)S(1)}, bf16[64,2048]{1,0:T(8,128)(2,1)S(1)}, u32[]{:S(2)}, u32[]{:S(2)}) collective-permute-start(bf16[64,2048]{1,0:T(8,128)(2,1)S(1)} %get-tuple-element.52), channel_id=1, source_target_pairs={{0,4},{1,5},{4,8},{5,9},{8,12},{9,13},{12,14},{13,15},{14,10},{15,... | collective-permute-start | bytes 786440 | tf_op jit(solution)/shard_map/ppermute | solution.py:246
  76.6 15.2 %collective-permute-start.29 = (bf16[64,2048]{1,0:T(8,128)(2,1)S(1)}, bf16[64,2048]{1,0:T(8,128)(2,1)S(1)}, u32[]{:S(2)}, u32[]{:S(2)}) collective-permute-start(bf16[64,2048]{1,0:T(8,128)(2,1)S(1)} %get-tuple-element.51), channel_id=1, source_target_pairs={{0,2},{1,3},{4,0},{5,1},{8,4},{9,5},{12,8},{13,9},{14,12},{15,13},... | collective-permute-start | bytes 786440 | tf_op jit(solution)/shard_map/ppermute | solution.py:246
  77.0 16.9 %collective-permute-start.4 = (bf16[128,2048]{1,0:T(8,128)(2,1)S(1)}, bf16[128,2048]{1,0:T(8,128)(2,1)S(1)}, u32[]{:S(2)}, u32[]{:S(2)}) collective-permute-start(bf16[128,2048]{1,0:T(8,128)(2,1)S(1)} %convert_element_type.77), channel_id=1, source_target_pairs={{0,16},{16,0},{1,17},{17,1},{2,18},{18,2},{3,19},{19,3},{4,20},{20... | collective-permute-start | bytes 1572872 | tf_op jit(solution)/shard_map/ppermute | solution.py:262
  86.2 15.4 %collective-permute-start.15 = (bf16[2064,128]{1,0:T(8,128)(2,1)S(1)}, bf16[2064,128]{1,0:T(8,128)(2,1)S(1)}, u32[]{:S(2)}, u32[]{:S(2)}) collective-permute-start(bf16[2064,128]{1,0:T(8,128)(2,1)S(1)} %collective-permute-done.12.a_ref), channel_id=1, source_target_pairs={{0,4},{1,5},{4,8},{5,9},{8,12},{9,13},{12,14},{13,15},{14,10},{15,... | collective-permute-start | bytes 1585160 | tf_op jit(solution)/shard_map/ppermute | solution.py:246
  87.7 15.4 %collective-permute-start.16 = (bf16[2064,128]{1,0:T(8,128)(2,1)S(1)}, bf16[2064,128]{1,0:T(8,128)(2,1)S(1)}, u32[]{:S(2)}, u32[]{:S(2)}) collective-permute-start(bf16[2064,128]{1,0:T(8,128)(2,1)S(1)} %collective-permute-done.14.b_ref), channel_id=1, source_target_pairs={{0,2},{1,3},{4,0},{5,1},{8,4},{9,5},{12,8},{13,9},{14,12},{15,13},... | collective-permute-start | bytes 1585160 | tf_op jit(solution)/shard_map/ppermute | solution.py:246
  91.9 16.8 %collective-permute-start.23 = (bf16[64,2048]{1,0:T(8,128)(2,1)S(1)}, bf16[64,2048]{1,0:T(8,128)(2,1)S(1)}, u32[]{:S(2)}, u32[]{:S(2)}) collective-permute-start(bf16[64,2048]{1,0:T(8,128)(2,1)S(1)} %get-tuple-element.50), channel_id=1, source_target_pairs={{0,4},{1,5},{4,8},{5,9},{8,12},{9,13},{12,14},{13,15},{14,10},{15,... | collective-permute-start | bytes 786440 | tf_op jit(solution)/shard_map/ppermute | solution.py:246
  93.5 15.2 %collective-permute-start.30 = (bf16[64,2048]{1,0:T(8,128)(2,1)S(1)}, bf16[64,2048]{1,0:T(8,128)(2,1)S(1)}, u32[]{:S(2)}, u32[]{:S(2)}) collective-permute-start(bf16[64,2048]{1,0:T(8,128)(2,1)S(1)} %get-tuple-element.49), channel_id=1, source_target_pairs={{0,2},{1,3},{4,0},{5,1},{8,4},{9,5},{12,8},{13,9},{14,12},{15,13},... | collective-permute-start | bytes 786440 | tf_op jit(solution)/shard_map/ppermute | solution.py:246
  103.1 15.4 %collective-permute-start.17 = (bf16[2064,128]{1,0:T(8,128)(2,1)S(1)}, bf16[2064,128]{1,0:T(8,128)(2,1)S(1)}, u32[]{:S(2)}, u32[]{:S(2)}) collective-permute-start(bf16[2064,128]{1,0:T(8,128)(2,1)S(1)} %collective-permute-done.15.a_ref), channel_id=1, source_target_pairs={{0,4},{1,5},{4,8},{5,9},{8,12},{9,13},{12,14},{13,15},{14,10},{15,... | collective-permute-start | bytes 1585160 | tf_op jit(solution)/shard_map/ppermute | solution.py:246
  104.7 15.4 %collective-permute-start.18 = (bf16[2064,128]{1,0:T(8,128)(2,1)S(1)}, bf16[2064,128]{1,0:T(8,128)(2,1)S(1)}, u32[]{:S(2)}, u32[]{:S(2)}) collective-permute-start(bf16[2064,128]{1,0:T(8,128)(2,1)S(1)} %collective-permute-done.16.b_ref), channel_id=1, source_target_pairs={{0,2},{1,3},{4,0},{5,1},{8,4},{9,5},{12,8},{13,9},{14,12},{15,13},... | collective-permute-start | bytes 1585160 | tf_op jit(solution)/shard_map/ppermute | solution.py:246
  108.9 14.7 %collective-permute-start.24 = (bf16[64,2048]{1,0:T(8,128)(2,1)S(1)}, bf16[64,2048]{1,0:T(8,128)(2,1)S(1)}, u32[]{:S(2)}, u32[]{:S(2)}) collective-permute-start(bf16[64,2048]{1,0:T(8,128)(2,1)S(1)} %get-tuple-element.48), channel_id=1, source_target_pairs={{0,4},{1,5},{4,8},{5,9},{8,12},{9,13},{12,14},{13,15},{14,10},{15,... | collective-permute-start | bytes 786440 | tf_op jit(solution)/shard_map/ppermute | solution.py:246
  110.5 13.2 %collective-permute-start.31 = (bf16[64,2048]{1,0:T(8,128)(2,1)S(1)}, bf16[64,2048]{1,0:T(8,128)(2,1)S(1)}, u32[]{:S(2)}, u32[]{:S(2)}) collective-permute-start(bf16[64,2048]{1,0:T(8,128)(2,1)S(1)} %get-tuple-element.47), channel_id=1, source_target_pairs={{0,2},{1,3},{4,0},{5,1},{8,4},{9,5},{12,8},{13,9},{14,12},{15,13},... | collective-permute-start | bytes 786440 | tf_op jit(solution)/shard_map/ppermute | solution.py:246
  123.9 10.7 %collective-permute-start.25 = (bf16[64,2048]{1,0:T(8,128)(2,1)S(1)}, bf16[64,2048]{1,0:T(8,128)(2,1)S(1)}, u32[]{:S(2)}, u32[]{:S(2)}) collective-permute-start(bf16[64,2048]{1,0:T(8,128)(2,1)S(1)} %get-tuple-element.46), channel_id=1, source_target_pairs={{0,20},{1,21},{4,24},{5,25},{8,28},{9,29},{12,30},{13,31},{14,26},... | collective-permute-start | bytes 786440 | tf_op jit(solution)/shard_map/ppermute | solution.py:250
  (8 other events, 73.9 us)

commit v9 on v8

--- a/solution.py
+++ b/solution.py
@@ -276,7 +276,7 @@
     weights = (*turn(u0, d0), *turn(u1, d1))
     own = expert_part(me, a, b, 2 * half, weights).astype(jnp.bfloat16)
     own_out, keep_out, grad_out = to_previous(own), to_previous(keep), to_previous(grad)
-    early = {3: own, 2: keep_out, 5: grad_out, 6: own_out}
+    early = {4: own, 2: keep_out, 3: grad_out, 6: own_out}
     sum_a = sum_b = None
     for step in range(1, chips):
         a, b = a1, b1

time: 138 us -> 138 us (level)
  no operation moved by 1% of the time
where the time goes in v9:
time: 138 us
  waiting for transfers between devices  53.9 us (39%)
  Pallas kernels  43.1 us (31%)
  starting transfers between devices  36.4 us (26%)
  local copies, waits for them, and re-layouts  3.51 us (3%)
    ppermute x26, waiting for transfers between devices, hop(): lax.ppermute(value, 'expert', [(2 * a + c, 2 * b + c) for a, b in moves f...  45.9 us
    pallas_call x8, Pallas kernels, expert_part(): pl.pallas_call(expert_kernel, out_shape=jax.ShapeDtypeStruct((rows, width...  29.7 us
    ppermute x26, starting transfers between devices, hop(): lax.ppermute(value, 'expert', [(2 * a + c, 2 * b + c) for a, b in moves f...  27.7 us
    ppermute x2, waiting for transfers between devices, last_hop(): lax.ppermute(value, ('pipe', 'expert'), [(s * experts + 2 * a + c, (s - 1...  7.95 us
    pallas_call x2, Pallas kernels, turn(): pl.pallas_call(turn_kernel, out_shape=[pltpu.VMEM(shape, up.dtype) for sh...  7.45 us
    ppermute x3, starting transfers between devices, to_previous(): lax.ppermute(value, 'pipe', [(s, (s - 1) % sections) for s in range(secti...  5.26 us
    unnamed x14, local copies, waits for them, and re-layouts  3.47 us
    ppermute x2, starting transfers between devices, last_hop(): lax.ppermute(value, ('pipe', 'expert'), [(s * experts + 2 * a + c, (s - 1...  2.98 us
  transfers between devices with their start and end apart: 33, of which 15 were waited for; matrix products, arithmetic and copies ran while one was open for 1% of the time, Pallas kernels for 30%

profile of v9, /device:TPU:0, one launch (start us, length us, event | category | flops | bytes accessed | tf_op | source)
XLA Modules:
  0.0 138.1 jit_solution(8831487962455463567)
XLA Ops:
  0.5 2.6 %pack.1 = (bf16[2064,128]{1,0:T(8,128)(2,1)}, bf16[2064,128]{1,0:T(8,128)(2,1)}, bf16[144,2048]{1,0:T(8,128)(2,1)}) custom-call(bf16[128,2048]{1,0:T(8,128)(2,1)} %bitcast.17, bf16[128,2048]{1,0:T(8,128)(2,1)} %bitcast.18, f32[1,2048]{1,0:T(1,128)} %gain_hbm.1, s32[8,128]{1,0:T(8,128)} %bitcast.20, bf16[8,128]{1,0:T(8,128)(2,1)} %bitcast.21), custom_call_target="tpu_custom_call" | custom-call | tf_op jit(solution)/shard_map/pack/pallas_call | solution.py:61
  3.1 3.1 %collective-permute-start.5 = (bf16[2064,128]{1,0:T(8,128)(2,1)}, bf16[2064,128]{1,0:T(8,128)(2,1)}, u32[]{:S(2)}, u32[]{:S(2)}) collective-permute-start(bf16[2064,128]{1,0:T(8,128)(2,1)} %get-tuple-element.26.a_ref), channel_id=1, source_target_pairs={{0,4},{1,5},{4,8},{5,9},{8,12},{9,13},{12,14},{13,15},{14,10},{15,... | collective-permute-start | bytes 1585160 | tf_op jit(solution)/shard_map/ppermute | solution.py:246
  6.2 2.0 %collective-permute-start = (bf16[144,2048]{1,0:T(8,128)(2,1)}, bf16[144,2048]{1,0:T(8,128)(2,1)}, u32[]{:S(2)}, u32[]{:S(2)}) collective-permute-start(bf16[144,2048]{1,0:T(8,128)(2,1)} %get-tuple-element.25), channel_id=1, source_target_pairs={{0,16},{16,0},{1,17},{17,1},{2,18},{18,2},{3,19},{19,3},{4,20},{20... | collective-permute-start | bytes 1769480 | tf_op jit(solution)/shard_map/ppermute | solution.py:262
  8.2 3.7 %turn.2 = (bf16[2048,768]{1,0:T(8,128)(2,1)S(1)}, bf16[768,2048]{1,0:T(8,128)(2,1)S(1)}, bf16[2048,768]{1,0:T(8,128)(2,1)S(1)}) custom-call(bf16[2048,768]{1,0:T(8,128)(2,1)} %bitcast.14, bf16[768,2048]{1,0:T(8,128)(2,1)} %bitcast.16), custom_call_target="tpu_custom_call" | custom-call | tf_op jit(solution)/shard_map/turn/pallas_call | solution.py:114
  11.9 1.7 %copy-done = bf16[768,2048]{1,0:T(8,128)(2,1)} copy-done((bf16[768,2048]{1,0:T(8,128)(2,1)}, bf16[768,2048]{1,0:T(8,128)(2,1)S(1)}, u32[]{:S(2)}) %copy-start) | copy-done | bytes 3145752
  13.6 1.7 %copy-done.2 = bf16[2048,768]{1,0:T(8,128)(2,1)} copy-done((bf16[2048,768]{1,0:T(8,128)(2,1)}, bf16[2048,768]{1,0:T(8,128)(2,1)S(1)}, u32[]{:S(2)}) %copy-start.2) | copy-done | bytes 3145752
  15.4 3.2 %collective-permute-done.5.a_ref = bf16[2064,128]{1,0:T(8,128)(2,1)} collective-permute-done((bf16[2064,128]{1,0:T(8,128)(2,1)}, bf16[2064,128]{1,0:T(8,128)(2,1)}, u32[]{:S(2)}, u32[]{:S(2)}) %collective-permute-start.5) | collective-permute-done | bytes 528416 | tf_op jit(solution)/shard_map/ppermute | solution.py:246
  18.6 1.8 %collective-permute-start.6 = (bf16[2064,128]{1,0:T(8,128)(2,1)}, bf16[2064,128]{1,0:T(8,128)(2,1)S(1)}, u32[]{:S(2)}, u32[]{:S(2)}) collective-permute-start(bf16[2064,128]{1,0:T(8,128)(2,1)} %collective-permute-done.5.a_ref), channel_id=1, source_target_pairs={{0,4},{1,5},{4,8},{5,9},{8,12},{9,13},{12,14},{13,15},{14,10},{15,... | collective-permute-start | bytes 1585160 | tf_op jit(solution)/shard_map/ppermute | solution.py:246
  20.6 3.7 %turn.3 = (bf16[2048,768]{1,0:T(8,128)(2,1)S(1)}, bf16[768,2048]{1,0:T(8,128)(2,1)S(1)}, bf16[2048,768]{1,0:T(8,128)(2,1)S(1)}) custom-call(bf16[2048,768]{1,0:T(8,128)(2,1)} %collective-permute-done.2.up_hbm, bf16[768,2048]{1,0:T(8,128)(2,1)} %collective-permute-done.3.down_hbm), custom_call_target="tpu_custom_call" | custom-call | tf_op jit(solution)/shard_map/turn/pallas_call | solution.py:114
  24.4 4.2 %expert_part.15 = f32[128,2048]{1,0:T(8,128)S(1)} custom-call(s32[2]{0:T(128)S(1)} %pad_add_fusion.me_ref, bf16[2064,128]{1,0:T(8,128)(2,1)} %collective-permute-done.5.a_ref, bf16[2064,128]{1,0:T(8,128)(2,1)} %collective-permute-done.7.b_ref, bf16[2048,768]{1,0:T(8,128)(2,1)S(1)} %get-tuple-element.28.refs_0_, bf16[768,2048]{1,0:T(8,128)(2,1)S(1)} %copy-done.1, ...), custom_call_target="tpu_custom_call" | custom-call | flops 2415919104 | bytes 14680064 | tf_op jit(solution)/shard_map/expert_part/pallas_call | solution.py:162
  28.7 1.9 %collective-permute-start.19 = (bf16[64,2048]{1,0:T(8,128)(2,1)S(1)}, bf16[64,2048]{1,0:T(8,128)(2,1)S(1)}, u32[]{:S(2)}, u32[]{:S(2)}) collective-permute-start(bf16[64,2048]{1,0:T(8,128)(2,1)S(1)} %get-tuple-element.58), channel_id=1, source_target_pairs={{0,4},{1,5},{4,8},{5,9},{8,12},{9,13},{12,14},{13,15},{14,10},{15,... | collective-permute-start | bytes 786440 | tf_op jit(solution)/shard_map/ppermute | solution.py:246
  30.8 1.8 %collective-permute-start.1 = (bf16[128,2048]{1,0:T(8,128)(2,1)S(1)}, bf16[128,2048]{1,0:T(8,128)(2,1)S(1)}, u32[]{:S(2)}, u32[]{:S(2)}) collective-permute-start(bf16[128,2048]{1,0:T(8,128)(2,1)S(1)} %bitcast.19), channel_id=1, source_target_pairs={{0,16},{16,0},{1,17},{17,1},{2,18},{18,2},{3,19},{19,3},{4,20},{20... | collective-permute-start | bytes 1572872 | tf_op jit(solution)/shard_map/ppermute | solution.py:262
  37.3 3.5 %expert_part.14 = f32[128,2048]{1,0:T(8,128)S(1)} custom-call(s32[2]{0:T(128)S(1)} %pad_add_fusion.me_ref, bf16[2064,128]{1,0:T(8,128)(2,1)S(1)} %collective-permute-done.6.a_ref, bf16[2064,128]{1,0:T(8,128)(2,1)S(1)} %collective-permute-done.8.b_ref, bf16[2048,768]{1,0:T(8,128)(2,1)S(1)} %get-tuple-element.28.refs_0_, bf16[768,2048]{1,0:T(8,128)(2,1)S(1)} %copy-done.1, ...), custom_call_target="tpu_custom_call" | custom-call | flops 2415919104 | bytes 14680064 | tf_op jit(solution)/shard_map/expert_part/pallas_call | solution.py:162
  41.0 1.6 %collective-permute-start.20 = (bf16[64,2048]{1,0:T(8,128)(2,1)S(1)}, bf16[64,2048]{1,0:T(8,128)(2,1)S(1)}, u32[]{:S(2)}, u32[]{:S(2)}) collective-permute-start(bf16[64,2048]{1,0:T(8,128)(2,1)S(1)} %get-tuple-element.56), channel_id=1, source_target_pairs={{0,4},{1,5},{4,8},{5,9},{8,12},{9,13},{12,14},{13,15},{14,10},{15,... | collective-permute-start | bytes 786440 | tf_op jit(solution)/shard_map/ppermute | solution.py:246
  43.1 9.1 %collective-permute-done.10.b_ref = bf16[2064,128]{1,0:T(8,128)(2,1)S(1)} collective-permute-done((bf16[2064,128]{1,0:T(8,128)(2,1)S(1)}, bf16[2064,128]{1,0:T(8,128)(2,1)S(1)}, u32[]{:S(2)}, u32[]{:S(2)}) %collective-permute-start.10) | collective-permute-done | bytes 528416 | tf_op jit(solution)/shard_map/ppermute | solution.py:246
  54.2 3.5 %expert_part.13 = f32[128,2048]{1,0:T(8,128)S(1)} custom-call(s32[2]{0:T(128)S(1)} %pad_add_fusion.me_ref, bf16[2064,128]{1,0:T(8,128)(2,1)S(1)} %collective-permute-done.9.a_ref, bf16[2064,128]{1,0:T(8,128)(2,1)S(1)} %collective-permute-done.10.b_ref, bf16[2048,768]{1,0:T(8,128)(2,1)S(1)} %get-tuple-element.28.refs_0_, bf16[768,2048]{1,0:T(8,128)(2,1)S(1)} %copy-done.1, ...), custom_call_target="tpu_custom_call" | custom-call | flops 2415919104 | bytes 14680064 | tf_op jit(solution)/shard_map/expert_part/pallas_call | solution.py:162
  58.0 1.6 %collective-permute-start.21 = (bf16[64,2048]{1,0:T(8,128)(2,1)S(1)}, bf16[64,2048]{1,0:T(8,128)(2,1)S(1)}, u32[]{:S(2)}, u32[]{:S(2)}) collective-permute-start(bf16[64,2048]{1,0:T(8,128)(2,1)S(1)} %get-tuple-element.54), channel_id=1, source_target_pairs={{0,4},{1,5},{4,8},{5,9},{8,12},{9,13},{12,14},{13,15},{14,10},{15,... | collective-permute-start | bytes 786440 | tf_op jit(solution)/shard_map/ppermute | solution.py:246
  60.0 4.1 %expert_part.8 = f32[128,2048]{1,0:T(8,128)S(1)} custom-call(s32[2]{0:T(128)S(1)} %pad_add_fusion.me_ref, bf16[2064,128]{1,0:T(8,128)(2,1)} %get-tuple-element.26.a_ref, bf16[2064,128]{1,0:T(8,128)(2,1)} %get-tuple-element.27.b_ref, bf16[2048,768]{1,0:T(8,128)(2,1)S(1)} %get-tuple-element.28.refs_0_, bf16[768,2048]{1,0:T(8,128)(2,1)S(1)} %copy-done.1, ...), custom_call_target="tpu_custom_call" | custom-call | flops 2415919104 | bytes 14680064 | tf_op jit(solution)/shard_map/expert_part/pallas_call | solution.py:162
  64.3 3.4 %collective-permute-done.11.a_ref = bf16[2064,128]{1,0:T(8,128)(2,1)S(1)} collective-permute-done((bf16[2064,128]{1,0:T(8,128)(2,1)S(1)}, bf16[2064,128]{1,0:T(8,128)(2,1)S(1)}, u32[]{:S(2)}, u32[]{:S(2)}) %collective-permute-start.11) | collective-permute-done | bytes 528416 | tf_op jit(solution)/shard_map/ppermute | solution.py:246
  71.2 3.5 %expert_part.12 = f32[128,2048]{1,0:T(8,128)S(1)} custom-call(s32[2]{0:T(128)S(1)} %pad_add_fusion.me_ref, bf16[2064,128]{1,0:T(8,128)(2,1)S(1)} %collective-permute-done.11.a_ref, bf16[2064,128]{1,0:T(8,128)(2,1)S(1)} %collective-permute-done.12.b_ref, bf16[2048,768]{1,0:T(8,128)(2,1)S(1)} %get-tuple-element.28.refs_0_, bf16[768,2048]{1,0:T(8,128)(2,1)S(1)} %copy-done.1, ...), custom_call_target="tpu_custom_call" | custom-call | flops 2415919104 | bytes 14680064 | tf_op jit(solution)/shard_map/expert_part/pallas_call | solution.py:162
  74.9 1.6 %collective-permute-start.22 = (bf16[64,2048]{1,0:T(8,128)(2,1)S(1)}, bf16[64,2048]{1,0:T(8,128)(2,1)S(1)}, u32[]{:S(2)}, u32[]{:S(2)}) collective-permute-start(bf16[64,2048]{1,0:T(8,128)(2,1)S(1)} %get-tuple-element.52), channel_id=1, source_target_pairs={{0,4},{1,5},{4,8},{5,9},{8,12},{9,13},{12,14},{13,15},{14,10},{15,... | collective-permute-start | bytes 786440 | tf_op jit(solution)/shard_map/ppermute | solution.py:246
  78.5 6.1 %collective-permute-done.13.a_ref = bf16[2064,128]{1,0:T(8,128)(2,1)S(1)} collective-permute-done((bf16[2064,128]{1,0:T(8,128)(2,1)S(1)}, bf16[2064,128]{1,0:T(8,128)(2,1)S(1)}, u32[]{:S(2)}, u32[]{:S(2)}) %collective-permute-start.13) | collective-permute-done | bytes 528416 | tf_op jit(solution)/shard_map/ppermute | solution.py:246
  84.6 1.8 %collective-permute-start.14 = (bf16[2064,128]{1,0:T(8,128)(2,1)S(1)}, bf16[2064,128]{1,0:T(8,128)(2,1)S(1)}, u32[]{:S(2)}, u32[]{:S(2)}) collective-permute-start(bf16[2064,128]{1,0:T(8,128)(2,1)S(1)} %collective-permute-done.13.a_ref), channel_id=1, source_target_pairs={{0,4},{1,5},{4,8},{5,9},{8,12},{9,13},{12,14},{13,15},{14,10},{15,... | collective-permute-start | bytes 1585160 | tf_op jit(solution)/shard_map/ppermute | solution.py:246
  86.6 3.6 %expert_part.11 = f32[128,2048]{1,0:T(8,128)S(1)} custom-call(s32[2]{0:T(128)S(1)} %pad_add_fusion.me_ref, bf16[2064,128]{1,0:T(8,128)(2,1)S(1)} %collective-permute-done.13.a_ref, bf16[2064,128]{1,0:T(8,128)(2,1)S(1)} %collective-permute-done.15.b_ref, bf16[2048,768]{1,0:T(8,128)(2,1)S(1)} %get-tuple-element.28.refs_0_, bf16[768,2048]{1,0:T(8,128)(2,1)S(1)} %copy-done.1, ...), custom_call_target="tpu_custom_call" | custom-call | flops 2415919104 | bytes 14680064 | tf_op jit(solution)/shard_map/expert_part/pallas_call | solution.py:162
  93.9 7.6 %collective-permute-done.14.a_ref = bf16[2064,128]{1,0:T(8,128)(2,1)S(1)} collective-permute-done((bf16[2064,128]{1,0:T(8,128)(2,1)S(1)}, bf16[2064,128]{1,0:T(8,128)(2,1)S(1)}, u32[]{:S(2)}, u32[]{:S(2)}) %collective-permute-start.14) | collective-permute-done | bytes 528416 | tf_op jit(solution)/shard_map/ppermute | solution.py:246
  105.1 3.5 %expert_part.10 = f32[128,2048]{1,0:T(8,128)S(1)} custom-call(s32[2]{0:T(128)S(1)} %pad_add_fusion.me_ref, bf16[2064,128]{1,0:T(8,128)(2,1)S(1)} %collective-permute-done.14.a_ref, bf16[2064,128]{1,0:T(8,128)(2,1)S(1)} %collective-permute-done.16.b_ref, bf16[2048,768]{1,0:T(8,128)(2,1)S(1)} %get-tuple-element.28.refs_0_, bf16[768,2048]{1,0:T(8,128)(2,1)S(1)} %copy-done.1, ...), custom_call_target="tpu_custom_call" | custom-call | flops 2415919104 | bytes 14680064 | tf_op jit(solution)/shard_map/expert_part/pallas_call | solution.py:162
  110.9 7.6 %collective-permute-done.17.a_ref = bf16[2064,128]{1,0:T(8,128)(2,1)S(1)} collective-permute-done((bf16[2064,128]{1,0:T(8,128)(2,1)S(1)}, bf16[2064,128]{1,0:T(8,128)(2,1)S(1)}, u32[]{:S(2)}, u32[]{:S(2)}) %collective-permute-start.17) | collective-permute-done | bytes 528416 | tf_op jit(solution)/shard_map/ppermute | solution.py:246
  120.0 3.6 %expert_part.9 = f32[128,2048]{1,0:T(8,128)S(1)} custom-call(s32[2]{0:T(128)S(1)} %pad_add_fusion.me_ref, bf16[2064,128]{1,0:T(8,128)(2,1)S(1)} %collective-permute-done.17.a_ref, bf16[2064,128]{1,0:T(8,128)(2,1)S(1)} %collective-permute-done.18.b_ref, bf16[2048,768]{1,0:T(8,128)(2,1)S(1)} %get-tuple-element.28.refs_0_, bf16[768,2048]{1,0:T(8,128)(2,1)S(1)} %copy-done.1, ...), custom_call_target="tpu_custom_call" | custom-call | flops 2415919104 | bytes 14680064 | tf_op jit(solution)/shard_map/expert_part/pallas_call | solution.py:162
  123.9 2.6 %collective-permute-start.25 = (bf16[64,2048]{1,0:T(8,128)(2,1)S(1)}, bf16[64,2048]{1,0:T(8,128)(2,1)S(1)}, u32[]{:S(2)}, u32[]{:S(2)}) collective-permute-start(bf16[64,2048]{1,0:T(8,128)(2,1)S(1)} %get-tuple-element.46), channel_id=1, source_target_pairs={{0,20},{1,21},{4,24},{5,25},{8,28},{9,29},{12,30},{13,31},{14,26},... | collective-permute-start | bytes 786440 | tf_op jit(solution)/shard_map/ppermute | solution.py:250
  126.8 2.1 %settle.1 = (f32[128,2048]{1,0:T(8,128)S(1)}, f32[128,2048]{1,0:T(8,128)S(1)}, f32[136,2048]{1,0:T(8,128)S(1)}) custom-call(bf16[144,2048]{1,0:T(8,128)(2,1)} %collective-permute-done.keep_hbm, bf16[128,2048]{1,0:T(8,128)(2,1)} %copy-done.4, bf16[128,2048]{1,0:T(8,128)(2,1)} %copy-done.5), custom_call_target="tpu_custom_call" | custom-call | tf_op jit(solution)/shard_map/settle/pallas_call | solution.py:204
  128.9 5.7 %collective-permute-done.25.a_ref = bf16[64,2048]{1,0:T(8,128)(2,1)S(1)} collective-permute-done((bf16[64,2048]{1,0:T(8,128)(2,1)S(1)}, bf16[64,2048]{1,0:T(8,128)(2,1)S(1)}, u32[]{:S(2)}, u32[]{:S(2)}) %collective-permute-start.25) | collective-permute-done | bytes 262176 | tf_op jit(solution)/shard_map/ppermute | solution.py:250
  134.6 2.3 %collective-permute-done.32.b_ref = bf16[64,2048]{1,0:T(8,128)(2,1)S(1)} collective-permute-done((bf16[64,2048]{1,0:T(8,128)(2,1)S(1)}, bf16[64,2048]{1,0:T(8,128)(2,1)S(1)}, u32[]{:S(2)}, u32[]{:S(2)}) %collective-permute-start.32) | collective-permute-done | bytes 262176 | tf_op jit(solution)/shard_map/ppermute | solution.py:250
  (71 shorter events, 27.9 us)
Async XLA Ops:
  0.0 20.6 %collective-permute-start.2 = (bf16[2048,768]{1,0:T(8,128)(2,1)}, bf16[2048,768]{1,0:T(8,128)(2,1)}, u32[]{:S(2)}, u32[]{:S(2)}) collective-permute-start(bf16[2048,768]{1,0:T(8,128)(2,1)} %bitcast.13), channel_id=1, source_target_pairs={{0,1},{1,0},{2,3},{3,2},{4,5},{5,4},{6,7},{7,6},{8,9},{9,8},{10,11... | collective-permute-start | bytes 9437192 | tf_op jit(solution)/shard_map/ppermute | solution.py:265
  0.5 20.2 %collective-permute-start.3 = (bf16[768,2048]{1,0:T(8,128)(2,1)}, bf16[768,2048]{1,0:T(8,128)(2,1)}, u32[]{:S(2)}, u32[]{:S(2)}) collective-permute-start(bf16[768,2048]{1,0:T(8,128)(2,1)} %bitcast.15), channel_id=1, source_target_pairs={{0,1},{1,0},{2,3},{3,2},{4,5},{5,4},{6,7},{7,6},{8,9},{9,8},{10,11... | collective-permute-start | bytes 9437192 | tf_op jit(solution)/shard_map/ppermute | solution.py:265
  3.1 15.5 %collective-permute-start.5 = (bf16[2064,128]{1,0:T(8,128)(2,1)}, bf16[2064,128]{1,0:T(8,128)(2,1)}, u32[]{:S(2)}, u32[]{:S(2)}) collective-permute-start(bf16[2064,128]{1,0:T(8,128)(2,1)} %get-tuple-element.26.a_ref), channel_id=1, source_target_pairs={{0,4},{1,5},{4,8},{5,9},{8,12},{9,13},{12,14},{13,15},{14,10},{15,... | collective-permute-start | bytes 1585160 | tf_op jit(solution)/shard_map/ppermute | solution.py:246
  6.2 14.2 %collective-permute-start.7 = (bf16[2064,128]{1,0:T(8,128)(2,1)}, bf16[2064,128]{1,0:T(8,128)(2,1)}, u32[]{:S(2)}, u32[]{:S(2)}) collective-permute-start(bf16[2064,128]{1,0:T(8,128)(2,1)} %get-tuple-element.27.b_ref), channel_id=1, source_target_pairs={{0,2},{1,3},{4,0},{5,1},{8,4},{9,5},{12,8},{13,9},{14,12},{15,13},... | collective-permute-start | bytes 1585160 | tf_op jit(solution)/shard_map/ppermute | solution.py:246
  6.2 24.6 %collective-permute-start = (bf16[144,2048]{1,0:T(8,128)(2,1)}, bf16[144,2048]{1,0:T(8,128)(2,1)}, u32[]{:S(2)}, u32[]{:S(2)}) collective-permute-start(bf16[144,2048]{1,0:T(8,128)(2,1)} %get-tuple-element.25), channel_id=1, source_target_pairs={{0,16},{16,0},{1,17},{17,1},{2,18},{18,2},{3,19},{19,3},{4,20},{20... | collective-permute-start | bytes 1769480 | tf_op jit(solution)/shard_map/ppermute | solution.py:262
  18.6 15.2 %collective-permute-start.6 = (bf16[2064,128]{1,0:T(8,128)(2,1)}, bf16[2064,128]{1,0:T(8,128)(2,1)S(1)}, u32[]{:S(2)}, u32[]{:S(2)}) collective-permute-start(bf16[2064,128]{1,0:T(8,128)(2,1)} %collective-permute-done.5.a_ref), channel_id=1, source_target_pairs={{0,4},{1,5},{4,8},{5,9},{8,12},{9,13},{12,14},{13,15},{14,10},{15,... | collective-permute-start | bytes 1585160 | tf_op jit(solution)/shard_map/ppermute | solution.py:246
  20.4 14.8 %collective-permute-start.8 = (bf16[2064,128]{1,0:T(8,128)(2,1)}, bf16[2064,128]{1,0:T(8,128)(2,1)S(1)}, u32[]{:S(2)}, u32[]{:S(2)}) collective-permute-start(bf16[2064,128]{1,0:T(8,128)(2,1)} %collective-permute-done.7.b_ref), channel_id=1, source_target_pairs={{0,2},{1,3},{4,0},{5,1},{8,4},{9,5},{12,8},{13,9},{14,12},{15,13},... | collective-permute-start | bytes 1585160 | tf_op jit(solution)/shard_map/ppermute | solution.py:246
  28.7 12.1 %collective-permute-start.19 = (bf16[64,2048]{1,0:T(8,128)(2,1)S(1)}, bf16[64,2048]{1,0:T(8,128)(2,1)S(1)}, u32[]{:S(2)}, u32[]{:S(2)}) collective-permute-start(bf16[64,2048]{1,0:T(8,128)(2,1)S(1)} %get-tuple-element.58), channel_id=1, source_target_pairs={{0,4},{1,5},{4,8},{5,9},{8,12},{9,13},{12,14},{13,15},{14,10},{15,... | collective-permute-start | bytes 786440 | tf_op jit(solution)/shard_map/ppermute | solution.py:246
  30.8 12.3 %collective-permute-start.1 = (bf16[128,2048]{1,0:T(8,128)(2,1)S(1)}, bf16[128,2048]{1,0:T(8,128)(2,1)S(1)}, u32[]{:S(2)}, u32[]{:S(2)}) collective-permute-start(bf16[128,2048]{1,0:T(8,128)(2,1)S(1)} %bitcast.19), channel_id=1, source_target_pairs={{0,16},{16,0},{1,17},{17,1},{2,18},{18,2},{3,19},{19,3},{4,20},{20... | collective-permute-start | bytes 1572872 | tf_op jit(solution)/shard_map/ppermute | solution.py:262
  35.3 16.9 %collective-permute-start.10 = (bf16[2064,128]{1,0:T(8,128)(2,1)S(1)}, bf16[2064,128]{1,0:T(8,128)(2,1)S(1)}, u32[]{:S(2)}, u32[]{:S(2)}) collective-permute-start(bf16[2064,128]{1,0:T(8,128)(2,1)S(1)} %collective-permute-done.8.b_ref), channel_id=1, source_target_pairs={{0,2},{1,3},{4,0},{5,1},{8,4},{9,5},{12,8},{13,9},{14,12},{15,13},... | collective-permute-start | bytes 1585160 | tf_op jit(solution)/shard_map/ppermute | solution.py:246
  35.8 16.4 %collective-permute-start.9 = (bf16[2064,128]{1,0:T(8,128)(2,1)S(1)}, bf16[2064,128]{1,0:T(8,128)(2,1)S(1)}, u32[]{:S(2)}, u32[]{:S(2)}) collective-permute-start(bf16[2064,128]{1,0:T(8,128)(2,1)S(1)} %collective-permute-done.6.a_ref), channel_id=1, source_target_pairs={{0,4},{1,5},{4,8},{5,9},{8,12},{9,13},{12,14},{13,15},{14,10},{15,... | collective-permute-start | bytes 1585160 | tf_op jit(solution)/shard_map/ppermute | solution.py:246
  41.0 16.8 %collective-permute-start.20 = (bf16[64,2048]{1,0:T(8,128)(2,1)S(1)}, bf16[64,2048]{1,0:T(8,128)(2,1)S(1)}, u32[]{:S(2)}, u32[]{:S(2)}) collective-permute-start(bf16[64,2048]{1,0:T(8,128)(2,1)S(1)} %get-tuple-element.56), channel_id=1, source_target_pairs={{0,4},{1,5},{4,8},{5,9},{8,12},{9,13},{12,14},{13,15},{14,10},{15,... | collective-permute-start | bytes 786440 | tf_op jit(solution)/shard_map/ppermute | solution.py:246
  42.6 15.2 %collective-permute-start.27 = (bf16[64,2048]{1,0:T(8,128)(2,1)S(1)}, bf16[64,2048]{1,0:T(8,128)(2,1)S(1)}, u32[]{:S(2)}, u32[]{:S(2)}) collective-permute-start(bf16[64,2048]{1,0:T(8,128)(2,1)S(1)} %get-tuple-element.55), channel_id=1, source_target_pairs={{0,2},{1,3},{4,0},{5,1},{8,4},{9,5},{12,8},{13,9},{14,12},{15,13},... | collective-permute-start | bytes 786440 | tf_op jit(solution)/shard_map/ppermute | solution.py:246
  52.2 15.4 %collective-permute-start.11 = (bf16[2064,128]{1,0:T(8,128)(2,1)S(1)}, bf16[2064,128]{1,0:T(8,128)(2,1)S(1)}, u32[]{:S(2)}, u32[]{:S(2)}) collective-permute-start(bf16[2064,128]{1,0:T(8,128)(2,1)S(1)} %collective-permute-done.9.a_ref), channel_id=1, source_target_pairs={{0,4},{1,5},{4,8},{5,9},{8,12},{9,13},{12,14},{13,15},{14,10},{15,... | collective-permute-start | bytes 1585160 | tf_op jit(solution)/shard_map/ppermute | solution.py:246
  53.8 15.4 %collective-permute-start.12 = (bf16[2064,128]{1,0:T(8,128)(2,1)S(1)}, bf16[2064,128]{1,0:T(8,128)(2,1)S(1)}, u32[]{:S(2)}, u32[]{:S(2)}) collective-permute-start(bf16[2064,128]{1,0:T(8,128)(2,1)S(1)} %collective-permute-done.10.b_ref), channel_id=1, source_target_pairs={{0,2},{1,3},{4,0},{5,1},{8,4},{9,5},{12,8},{13,9},{14,12},{15,13},... | collective-permute-start | bytes 1585160 | tf_op jit(solution)/shard_map/ppermute | solution.py:246
  58.0 16.8 %collective-permute-start.21 = (bf16[64,2048]{1,0:T(8,128)(2,1)S(1)}, bf16[64,2048]{1,0:T(8,128)(2,1)S(1)}, u32[]{:S(2)}, u32[]{:S(2)}) collective-permute-start(bf16[64,2048]{1,0:T(8,128)(2,1)S(1)} %get-tuple-element.54), channel_id=1, source_target_pairs={{0,4},{1,5},{4,8},{5,9},{8,12},{9,13},{12,14},{13,15},{14,10},{15,... | collective-permute-start | bytes 786440 | tf_op jit(solution)/shard_map/ppermute | solution.py:246
  59.6 15.2 %collective-permute-start.28 = (bf16[64,2048]{1,0:T(8,128)(2,1)S(1)}, bf16[64,2048]{1,0:T(8,128)(2,1)S(1)}, u32[]{:S(2)}, u32[]{:S(2)}) collective-permute-start(bf16[64,2048]{1,0:T(8,128)(2,1)S(1)} %get-tuple-element.53), channel_id=1, source_target_pairs={{0,2},{1,3},{4,0},{5,1},{8,4},{9,5},{12,8},{13,9},{14,12},{15,13},... | collective-permute-start | bytes 786440 | tf_op jit(solution)/shard_map/ppermute | solution.py:246
  69.1 15.4 %collective-permute-start.13 = (bf16[2064,128]{1,0:T(8,128)(2,1)S(1)}, bf16[2064,128]{1,0:T(8,128)(2,1)S(1)}, u32[]{:S(2)}, u32[]{:S(2)}) collective-permute-start(bf16[2064,128]{1,0:T(8,128)(2,1)S(1)} %collective-permute-done.11.a_ref), channel_id=1, source_target_pairs={{0,4},{1,5},{4,8},{5,9},{8,12},{9,13},{12,14},{13,15},{14,10},{15,... | collective-permute-start | bytes 1585160 | tf_op jit(solution)/shard_map/ppermute | solution.py:246
  70.7 15.7 %collective-permute-start.15 = (bf16[2064,128]{1,0:T(8,128)(2,1)S(1)}, bf16[2064,128]{1,0:T(8,128)(2,1)S(1)}, u32[]{:S(2)}, u32[]{:S(2)}) collective-permute-start(bf16[2064,128]{1,0:T(8,128)(2,1)S(1)} %collective-permute-done.12.b_ref), channel_id=1, source_target_pairs={{0,2},{1,3},{4,0},{5,1},{8,4},{9,5},{12,8},{13,9},{14,12},{15,13},... | collective-permute-start | bytes 1585160 | tf_op jit(solution)/shard_map/ppermute | solution.py:246
  74.9 15.3 %collective-permute-start.22 = (bf16[64,2048]{1,0:T(8,128)(2,1)S(1)}, bf16[64,2048]{1,0:T(8,128)(2,1)S(1)}, u32[]{:S(2)}, u32[]{:S(2)}) collective-permute-start(bf16[64,2048]{1,0:T(8,128)(2,1)S(1)} %get-tuple-element.52), channel_id=1, source_target_pairs={{0,4},{1,5},{4,8},{5,9},{8,12},{9,13},{12,14},{13,15},{14,10},{15,... | collective-permute-start | bytes 786440 | tf_op jit(solution)/shard_map/ppermute | solution.py:246
  76.5 15.2 %collective-permute-start.29 = (bf16[64,2048]{1,0:T(8,128)(2,1)S(1)}, bf16[64,2048]{1,0:T(8,128)(2,1)S(1)}, u32[]{:S(2)}, u32[]{:S(2)}) collective-permute-start(bf16[64,2048]{1,0:T(8,128)(2,1)S(1)} %get-tuple-element.51), channel_id=1, source_target_pairs={{0,2},{1,3},{4,0},{5,1},{8,4},{9,5},{12,8},{13,9},{14,12},{15,13},... | collective-permute-start | bytes 786440 | tf_op jit(solution)/shard_map/ppermute | solution.py:246
  77.0 16.9 %collective-permute-start.4 = (bf16[128,2048]{1,0:T(8,128)(2,1)S(1)}, bf16[128,2048]{1,0:T(8,128)(2,1)S(1)}, u32[]{:S(2)}, u32[]{:S(2)}) collective-permute-start(bf16[128,2048]{1,0:T(8,128)(2,1)S(1)} %convert_element_type.77), channel_id=1, source_target_pairs={{0,16},{16,0},{1,17},{17,1},{2,18},{18,2},{3,19},{19,3},{4,20},{20... | collective-permute-start | bytes 1572872 | tf_op jit(solution)/shard_map/ppermute | solution.py:262
  84.6 16.9 %collective-permute-start.14 = (bf16[2064,128]{1,0:T(8,128)(2,1)S(1)}, bf16[2064,128]{1,0:T(8,128)(2,1)S(1)}, u32[]{:S(2)}, u32[]{:S(2)}) collective-permute-start(bf16[2064,128]{1,0:T(8,128)(2,1)S(1)} %collective-permute-done.13.a_ref), channel_id=1, source_target_pairs={{0,4},{1,5},{4,8},{5,9},{8,12},{9,13},{12,14},{13,15},{14,10},{15,... | collective-permute-start | bytes 1585160 | tf_op jit(solution)/shard_map/ppermute | solution.py:246
  86.4 16.6 %collective-permute-start.16 = (bf16[2064,128]{1,0:T(8,128)(2,1)S(1)}, bf16[2064,128]{1,0:T(8,128)(2,1)S(1)}, u32[]{:S(2)}, u32[]{:S(2)}) collective-permute-start(bf16[2064,128]{1,0:T(8,128)(2,1)S(1)} %collective-permute-done.15.b_ref), channel_id=1, source_target_pairs={{0,2},{1,3},{4,0},{5,1},{8,4},{9,5},{12,8},{13,9},{14,12},{15,13},... | collective-permute-start | bytes 1585160 | tf_op jit(solution)/shard_map/ppermute | solution.py:246
  91.8 16.8 %collective-permute-start.23 = (bf16[64,2048]{1,0:T(8,128)(2,1)S(1)}, bf16[64,2048]{1,0:T(8,128)(2,1)S(1)}, u32[]{:S(2)}, u32[]{:S(2)}) collective-permute-start(bf16[64,2048]{1,0:T(8,128)(2,1)S(1)} %get-tuple-element.50), channel_id=1, source_target_pairs={{0,4},{1,5},{4,8},{5,9},{8,12},{9,13},{12,14},{13,15},{14,10},{15,... | collective-permute-start | bytes 786440 | tf_op jit(solution)/shard_map/ppermute | solution.py:246
  93.5 15.2 %collective-permute-start.30 = (bf16[64,2048]{1,0:T(8,128)(2,1)S(1)}, bf16[64,2048]{1,0:T(8,128)(2,1)S(1)}, u32[]{:S(2)}, u32[]{:S(2)}) collective-permute-start(bf16[64,2048]{1,0:T(8,128)(2,1)S(1)} %get-tuple-element.49), channel_id=1, source_target_pairs={{0,2},{1,3},{4,0},{5,1},{8,4},{9,5},{12,8},{13,9},{14,12},{15,13},... | collective-permute-start | bytes 786440 | tf_op jit(solution)/shard_map/ppermute | solution.py:246
  103.0 15.4 %collective-permute-start.17 = (bf16[2064,128]{1,0:T(8,128)(2,1)S(1)}, bf16[2064,128]{1,0:T(8,128)(2,1)S(1)}, u32[]{:S(2)}, u32[]{:S(2)}) collective-permute-start(bf16[2064,128]{1,0:T(8,128)(2,1)S(1)} %collective-permute-done.14.a_ref), channel_id=1, source_target_pairs={{0,4},{1,5},{4,8},{5,9},{8,12},{9,13},{12,14},{13,15},{14,10},{15,... | collective-permute-start | bytes 1585160 | tf_op jit(solution)/shard_map/ppermute | solution.py:246
  104.6 15.4 %collective-permute-start.18 = (bf16[2064,128]{1,0:T(8,128)(2,1)S(1)}, bf16[2064,128]{1,0:T(8,128)(2,1)S(1)}, u32[]{:S(2)}, u32[]{:S(2)}) collective-permute-start(bf16[2064,128]{1,0:T(8,128)(2,1)S(1)} %collective-permute-done.16.b_ref), channel_id=1, source_target_pairs={{0,2},{1,3},{4,0},{5,1},{8,4},{9,5},{12,8},{13,9},{14,12},{15,13},... | collective-permute-start | bytes 1585160 | tf_op jit(solution)/shard_map/ppermute | solution.py:246
  108.8 14.8 %collective-permute-start.24 = (bf16[64,2048]{1,0:T(8,128)(2,1)S(1)}, bf16[64,2048]{1,0:T(8,128)(2,1)S(1)}, u32[]{:S(2)}, u32[]{:S(2)}) collective-permute-start(bf16[64,2048]{1,0:T(8,128)(2,1)S(1)} %get-tuple-element.48), channel_id=1, source_target_pairs={{0,4},{1,5},{4,8},{5,9},{8,12},{9,13},{12,14},{13,15},{14,10},{15,... | collective-permute-start | bytes 786440 | tf_op jit(solution)/shard_map/ppermute | solution.py:246
  110.4 13.3 %collective-permute-start.31 = (bf16[64,2048]{1,0:T(8,128)(2,1)S(1)}, bf16[64,2048]{1,0:T(8,128)(2,1)S(1)}, u32[]{:S(2)}, u32[]{:S(2)}) collective-permute-start(bf16[64,2048]{1,0:T(8,128)(2,1)S(1)} %get-tuple-element.47), channel_id=1, source_target_pairs={{0,2},{1,3},{4,0},{5,1},{8,4},{9,5},{12,8},{13,9},{14,12},{15,13},... | collective-permute-start | bytes 786440 | tf_op jit(solution)/shard_map/ppermute | solution.py:246
  123.9 10.8 %collective-permute-start.25 = (bf16[64,2048]{1,0:T(8,128)(2,1)S(1)}, bf16[64,2048]{1,0:T(8,128)(2,1)S(1)}, u32[]{:S(2)}, u32[]{:S(2)}) collective-permute-start(bf16[64,2048]{1,0:T(8,128)(2,1)S(1)} %get-tuple-element.46), channel_id=1, source_target_pairs={{0,20},{1,21},{4,24},{5,25},{8,28},{9,29},{12,30},{13,31},{14,26},... | collective-permute-start | bytes 786440 | tf_op jit(solution)/shard_map/ppermute | solution.py:250
  126.4 10.5 %collective-permute-start.32 = (bf16[64,2048]{1,0:T(8,128)(2,1)S(1)}, bf16[64,2048]{1,0:T(8,128)(2,1)S(1)}, u32[]{:S(2)}, u32[]{:S(2)}) collective-permute-start(bf16[64,2048]{1,0:T(8,128)(2,1)S(1)} %get-tuple-element.45), channel_id=1, source_target_pairs={{0,18},{1,19},{4,16},{5,17},{8,20},{9,21},{12,24},{13,25},{14,28},... | collective-permute-start | bytes 786440 | tf_op jit(solution)/shard_map/ppermute | solution.py:250
  (8 other events, 67.4 us)
